TPU v7x, 512 devices: a whole 4x8x8 slice. The times are simulated.
512 devices in a mesh: section: 8 (over z_hi, x), rows: 64 (over z_lo, y, core).
Axes of the slice: x: 4, y: 8, z: 8 (z_hi: 2, z_lo: 4; z = z_hi * 4 + z_lo), core: 2. Of those that a mesh axis runs over, the one named last changes fastest.
Arguments:
- frames_in: bfloat16 [8, 2, 128, 64, 256], P(None, None, 'rows'), may hold values from -6 to 6
- layer_weights: bfloat16 [8, 2, 3, 3, 256, 256], P('section'), may hold values from -0.09375 to 0.09375
Outputs:
- layer_outputs: bfloat16 [8, 8, 2, 128, 64, 256], P('section', None, None, 'rows')
All inputs are finite; a program needn't handle non-finite values.
Results may differ from a plain program's by a relative error of at most 0.009.
Values may be sent and summed in bfloat16 or wider, within the bound.
No kernel may reach another device: no remote copies, remote signals or barrier semaphores. Data moves between devices by JAX's collectives and lax.ppermute only.
A program may use at most 64 MiB of HBM per device.

v0:
```python
import jax
import jax.numpy as jnp
from jax import lax
from jax.sharding import PartitionSpec as P


def with_halo(cells, sides, width):
    for axis, dim in sides:
        count = lax.axis_size(axis)
        ends = count - 1
        head = lax.slice_in_dim(cells, 0, width, axis=dim)
        tail = lax.slice_in_dim(cells, cells.shape[dim] - width, cells.shape[dim], axis=dim)
        cells = jnp.concatenate(
            [
                lax.ppermute(tail, axis, [(i, (i + 1) % count) for i in range(ends)]),
                cells,
                lax.ppermute(head, axis, [((i + 1) % count, i) for i in range(ends)]),
            ],
            axis=dim,
        )
    return cells


def passed_along(block, axis, distance):
    devices = range(lax.axis_size(axis))
    route = [(i - distance, i) for i in devices if i - distance in devices]
    return lax.ppermute(block, axis, route)


def normalize(clip):
    values = clip.astype(jnp.float32)
    scale = lax.rsqrt(jnp.mean(values * values, axis=-1, keepdims=True) + 1e-06)
    return (values * scale).astype(jnp.bfloat16)


def local(frames_in, layer_weights):
    sections = lax.axis_size("section")
    section = lax.axis_index("section")
    kernel = layer_weights[0]
    count, frames, slab, width, chans = frames_in.shape
    pieces = 1
    span = frames // pieces
    total = count * pieces
    ticks = total + sections - 1

    def one_tick(step, carry):
        received, previous, outputs = carry
        order = step - section
        valid = jnp.logical_and(order >= 0, order < total)
        placed = jnp.clip(order, 0, total - 1)
        clip_index = placed // pieces
        first = placed % pieces * span
        zero = jnp.int32(0)
        fresh = lax.dynamic_slice(
            frames_in, (clip_index, first, zero, zero, zero), (1, span, slab, width, chans)
        )[0]
        current = jnp.where(section == 0, fresh, received)
        normed = normalize(current)
        padded = with_halo(normed, (("rows", 1),), 1)
        padded = jnp.pad(padded, ((0, 0), (0, 0), (1, 1), (0, 0)))
        before = jnp.where(placed % pieces == 0, jnp.zeros_like(previous), previous)
        stacked = jnp.concatenate([before[None], padded], axis=0)
        conv = lax.conv_general_dilated(
            stacked[None],
            kernel,
            (1, 1, 1),
            "VALID",
            dimension_numbers=("NDHWC", "DHWIO", "NDHWC"),
            preferred_element_type=jnp.float32,
        )[0]
        result = (current.astype(jnp.float32) + jax.nn.silu(conv)).astype(jnp.bfloat16)
        corner = (clip_index, first, zero, zero, zero)
        older = lax.dynamic_slice(outputs, corner, (1, span, slab, width, chans))
        outputs = lax.dynamic_update_slice(outputs, jnp.where(valid, result[None], older), corner)
        passed = passed_along(result, "section", 1)
        return (passed, padded[-1], outputs)

    start = (
        jnp.zeros((span, slab, width, chans), jnp.bfloat16),
        jnp.zeros((slab + 2, width + 2, chans), jnp.bfloat16),
        jnp.zeros((count, frames, slab, width, chans), jnp.bfloat16),
    )
    received, previous, outputs = lax.fori_loop(0, ticks, one_tick, start)
    return outputs[None]


def solution(mesh):
    placed = (P(None, None, "rows", None, None), P("section", None, None, None, None, None))
    return jax.shard_map(
        local,
        mesh=mesh,
        in_specs=placed,
        out_specs=P("section", None, None, "rows", None, None),
        check_vma=False,
    )
```

profile of v0, /device:TPU:384, one launch (start us, length us, event | category | flops | bytes accessed | tf_op | source)
XLA Modules:
  0.0 434.7 jit_solution(8399601235501337074)
XLA Ops:
  0.7 433.1 %while.19 = (s32[]{:T(128)}, bf16[2,2,64,256]{3,1,2,0:T(2,128)(2,1)S(1)}, bf16[8,2,2,64,256]{4,3,2,1,0:T(8,128)(2,1)S(1)}, pred[]{:T(512)}, s32[]{:T(128)}, /*in...) while((s32[]{:T(128)}, ...), condition=%wide.region_2.3_spmd, body=%wide.region_0.2_spmd.sunk | while | flops 683778304 | bytes 19866012 | solution.py:83
  9.7 5.9 %collective-permute-done.1 = bf16[2,1,64,256]{3,1,2,0:T(2,128)(2,1)S(1)} collective-permute-done((bf16[2,1,64,256]{3,1,2,0:T(2,128)(2,1)S(1)}, bf16[2,1,64,256]{3,1,2,0:T(2,128)(2,1)S(1)}, u32[]{:S(2)}, u32[]{:S(2)}) %collective-permute-start.1) | collective-permute-done | bytes 65568 | tf_op jit(solution)/shard_map/while/body/eval_jaxpr/ppermute | solution.py:15
  22.6 9.4 %collective-permute-done.2 = bf16[2,2,64,256]{3,1,2,0:T(2,128)(2,1)S(1)} collective-permute-done((bf16[2,2,64,256]{3,1,2,0:T(2,128)(2,1)S(1)}, bf16[2,2,64,256]{3,1,2,0:T(2,128)(2,1)S(1)}, u32[]{:S(2)}, u32[]{:S(2)}) %collective-permute-start.2) | collective-permute-done | bytes 131104 | tf_op jit(solution)/shard_map/while/body/eval_jaxpr/ppermute | solution.py:27
  38.1 5.9 %collective-permute-done.1 = bf16[2,1,64,256]{3,1,2,0:T(2,128)(2,1)S(1)} collective-permute-done((bf16[2,1,64,256]{3,1,2,0:T(2,128)(2,1)S(1)}, bf16[2,1,64,256]{3,1,2,0:T(2,128)(2,1)S(1)}, u32[]{:S(2)}, u32[]{:S(2)}) %collective-permute-start.1) | collective-permute-done | bytes 65568 | tf_op jit(solution)/shard_map/while/body/eval_jaxpr/ppermute | solution.py:15
  49.6 10.9 %collective-permute-done.2 = bf16[2,2,64,256]{3,1,2,0:T(2,128)(2,1)S(1)} collective-permute-done((bf16[2,2,64,256]{3,1,2,0:T(2,128)(2,1)S(1)}, bf16[2,2,64,256]{3,1,2,0:T(2,128)(2,1)S(1)}, u32[]{:S(2)}, u32[]{:S(2)}) %collective-permute-start.2) | collective-permute-done | bytes 131104 | tf_op jit(solution)/shard_map/while/body/eval_jaxpr/ppermute | solution.py:27
  68.6 5.9 %collective-permute-done.1 = bf16[2,1,64,256]{3,1,2,0:T(2,128)(2,1)S(1)} collective-permute-done((bf16[2,1,64,256]{3,1,2,0:T(2,128)(2,1)S(1)}, bf16[2,1,64,256]{3,1,2,0:T(2,128)(2,1)S(1)}, u32[]{:S(2)}, u32[]{:S(2)}) %collective-permute-start.1) | collective-permute-done | bytes 65568 | tf_op jit(solution)/shard_map/while/body/eval_jaxpr/ppermute | solution.py:15
  80.0 10.9 %collective-permute-done.2 = bf16[2,2,64,256]{3,1,2,0:T(2,128)(2,1)S(1)} collective-permute-done((bf16[2,2,64,256]{3,1,2,0:T(2,128)(2,1)S(1)}, bf16[2,2,64,256]{3,1,2,0:T(2,128)(2,1)S(1)}, u32[]{:S(2)}, u32[]{:S(2)}) %collective-permute-start.2) | collective-permute-done | bytes 131104 | tf_op jit(solution)/shard_map/while/body/eval_jaxpr/ppermute | solution.py:27
  97.0 5.9 %collective-permute-done.1 = bf16[2,1,64,256]{3,1,2,0:T(2,128)(2,1)S(1)} collective-permute-done((bf16[2,1,64,256]{3,1,2,0:T(2,128)(2,1)S(1)}, bf16[2,1,64,256]{3,1,2,0:T(2,128)(2,1)S(1)}, u32[]{:S(2)}, u32[]{:S(2)}) %collective-permute-start.1) | collective-permute-done | bytes 65568 | tf_op jit(solution)/shard_map/while/body/eval_jaxpr/ppermute | solution.py:15
  108.4 10.9 %collective-permute-done.2 = bf16[2,2,64,256]{3,1,2,0:T(2,128)(2,1)S(1)} collective-permute-done((bf16[2,2,64,256]{3,1,2,0:T(2,128)(2,1)S(1)}, bf16[2,2,64,256]{3,1,2,0:T(2,128)(2,1)S(1)}, u32[]{:S(2)}, u32[]{:S(2)}) %collective-permute-start.2) | collective-permute-done | bytes 131104 | tf_op jit(solution)/shard_map/while/body/eval_jaxpr/ppermute | solution.py:27
  125.5 5.9 %collective-permute-done.1 = bf16[2,1,64,256]{3,1,2,0:T(2,128)(2,1)S(1)} collective-permute-done((bf16[2,1,64,256]{3,1,2,0:T(2,128)(2,1)S(1)}, bf16[2,1,64,256]{3,1,2,0:T(2,128)(2,1)S(1)}, u32[]{:S(2)}, u32[]{:S(2)}) %collective-permute-start.1) | collective-permute-done | bytes 65568 | tf_op jit(solution)/shard_map/while/body/eval_jaxpr/ppermute | solution.py:15
  136.9 10.9 %collective-permute-done.2 = bf16[2,2,64,256]{3,1,2,0:T(2,128)(2,1)S(1)} collective-permute-done((bf16[2,2,64,256]{3,1,2,0:T(2,128)(2,1)S(1)}, bf16[2,2,64,256]{3,1,2,0:T(2,128)(2,1)S(1)}, u32[]{:S(2)}, u32[]{:S(2)}) %collective-permute-start.2) | collective-permute-done | bytes 131104 | tf_op jit(solution)/shard_map/while/body/eval_jaxpr/ppermute | solution.py:27
  165.3 10.9 %collective-permute-done.2 = bf16[2,2,64,256]{3,1,2,0:T(2,128)(2,1)S(1)} collective-permute-done((bf16[2,2,64,256]{3,1,2,0:T(2,128)(2,1)S(1)}, bf16[2,2,64,256]{3,1,2,0:T(2,128)(2,1)S(1)}, u32[]{:S(2)}, u32[]{:S(2)}) %collective-permute-start.2) | collective-permute-done | bytes 131104 | tf_op jit(solution)/shard_map/while/body/eval_jaxpr/ppermute | solution.py:27
  193.8 10.9 %collective-permute-done.2 = bf16[2,2,64,256]{3,1,2,0:T(2,128)(2,1)S(1)} collective-permute-done((bf16[2,2,64,256]{3,1,2,0:T(2,128)(2,1)S(1)}, bf16[2,2,64,256]{3,1,2,0:T(2,128)(2,1)S(1)}, u32[]{:S(2)}, u32[]{:S(2)}) %collective-permute-start.2) | collective-permute-done | bytes 131104 | tf_op jit(solution)/shard_map/while/body/eval_jaxpr/ppermute | solution.py:27
  210.8 5.9 %collective-permute-done.1 = bf16[2,1,64,256]{3,1,2,0:T(2,128)(2,1)S(1)} collective-permute-done((bf16[2,1,64,256]{3,1,2,0:T(2,128)(2,1)S(1)}, bf16[2,1,64,256]{3,1,2,0:T(2,128)(2,1)S(1)}, u32[]{:S(2)}, u32[]{:S(2)}) %collective-permute-start.1) | collective-permute-done | bytes 65568 | tf_op jit(solution)/shard_map/while/body/eval_jaxpr/ppermute | solution.py:15
  222.2 10.9 %collective-permute-done.2 = bf16[2,2,64,256]{3,1,2,0:T(2,128)(2,1)S(1)} collective-permute-done((bf16[2,2,64,256]{3,1,2,0:T(2,128)(2,1)S(1)}, bf16[2,2,64,256]{3,1,2,0:T(2,128)(2,1)S(1)}, u32[]{:S(2)}, u32[]{:S(2)}) %collective-permute-start.2) | collective-permute-done | bytes 131104 | tf_op jit(solution)/shard_map/while/body/eval_jaxpr/ppermute | solution.py:27
  239.3 5.9 %collective-permute-done.1 = bf16[2,1,64,256]{3,1,2,0:T(2,128)(2,1)S(1)} collective-permute-done((bf16[2,1,64,256]{3,1,2,0:T(2,128)(2,1)S(1)}, bf16[2,1,64,256]{3,1,2,0:T(2,128)(2,1)S(1)}, u32[]{:S(2)}, u32[]{:S(2)}) %collective-permute-start.1) | collective-permute-done | bytes 65568 | tf_op jit(solution)/shard_map/while/body/eval_jaxpr/ppermute | solution.py:15
  250.7 10.9 %collective-permute-done.2 = bf16[2,2,64,256]{3,1,2,0:T(2,128)(2,1)S(1)} collective-permute-done((bf16[2,2,64,256]{3,1,2,0:T(2,128)(2,1)S(1)}, bf16[2,2,64,256]{3,1,2,0:T(2,128)(2,1)S(1)}, u32[]{:S(2)}, u32[]{:S(2)}) %collective-permute-start.2) | collective-permute-done | bytes 131104 | tf_op jit(solution)/shard_map/while/body/eval_jaxpr/ppermute | solution.py:27
  267.7 5.9 %collective-permute-done.1 = bf16[2,1,64,256]{3,1,2,0:T(2,128)(2,1)S(1)} collective-permute-done((bf16[2,1,64,256]{3,1,2,0:T(2,128)(2,1)S(1)}, bf16[2,1,64,256]{3,1,2,0:T(2,128)(2,1)S(1)}, u32[]{:S(2)}, u32[]{:S(2)}) %collective-permute-start.1) | collective-permute-done | bytes 65568 | tf_op jit(solution)/shard_map/while/body/eval_jaxpr/ppermute | solution.py:15
  279.1 10.9 %collective-permute-done.2 = bf16[2,2,64,256]{3,1,2,0:T(2,128)(2,1)S(1)} collective-permute-done((bf16[2,2,64,256]{3,1,2,0:T(2,128)(2,1)S(1)}, bf16[2,2,64,256]{3,1,2,0:T(2,128)(2,1)S(1)}, u32[]{:S(2)}, u32[]{:S(2)}) %collective-permute-start.2) | collective-permute-done | bytes 131104 | tf_op jit(solution)/shard_map/while/body/eval_jaxpr/ppermute | solution.py:27
  307.6 10.9 %collective-permute-done.2 = bf16[2,2,64,256]{3,1,2,0:T(2,128)(2,1)S(1)} collective-permute-done((bf16[2,2,64,256]{3,1,2,0:T(2,128)(2,1)S(1)}, bf16[2,2,64,256]{3,1,2,0:T(2,128)(2,1)S(1)}, u32[]{:S(2)}, u32[]{:S(2)}) %collective-permute-start.2) | collective-permute-done | bytes 131104 | tf_op jit(solution)/shard_map/while/body/eval_jaxpr/ppermute | solution.py:27
  336.1 12.3 %collective-permute-done.2 = bf16[2,2,64,256]{3,1,2,0:T(2,128)(2,1)S(1)} collective-permute-done((bf16[2,2,64,256]{3,1,2,0:T(2,128)(2,1)S(1)}, bf16[2,2,64,256]{3,1,2,0:T(2,128)(2,1)S(1)}, u32[]{:S(2)}, u32[]{:S(2)}) %collective-permute-start.2) | collective-permute-done | bytes 131104 | tf_op jit(solution)/shard_map/while/body/eval_jaxpr/ppermute | solution.py:27
  365.9 10.9 %collective-permute-done.2 = bf16[2,2,64,256]{3,1,2,0:T(2,128)(2,1)S(1)} collective-permute-done((bf16[2,2,64,256]{3,1,2,0:T(2,128)(2,1)S(1)}, bf16[2,2,64,256]{3,1,2,0:T(2,128)(2,1)S(1)}, u32[]{:S(2)}, u32[]{:S(2)}) %collective-permute-start.2) | collective-permute-done | bytes 131104 | tf_op jit(solution)/shard_map/while/body/eval_jaxpr/ppermute | solution.py:27
  394.4 10.9 %collective-permute-done.2 = bf16[2,2,64,256]{3,1,2,0:T(2,128)(2,1)S(1)} collective-permute-done((bf16[2,2,64,256]{3,1,2,0:T(2,128)(2,1)S(1)}, bf16[2,2,64,256]{3,1,2,0:T(2,128)(2,1)S(1)}, u32[]{:S(2)}, u32[]{:S(2)}) %collective-permute-start.2) | collective-permute-done | bytes 131104 | tf_op jit(solution)/shard_map/while/body/eval_jaxpr/ppermute | solution.py:27
  422.8 10.9 %collective-permute-done.2 = bf16[2,2,64,256]{3,1,2,0:T(2,128)(2,1)S(1)} collective-permute-done((bf16[2,2,64,256]{3,1,2,0:T(2,128)(2,1)S(1)}, bf16[2,2,64,256]{3,1,2,0:T(2,128)(2,1)S(1)}, u32[]{:S(2)}, u32[]{:S(2)}) %collective-permute-start.2) | collective-permute-done | bytes 131104 | tf_op jit(solution)/shard_map/while/body/eval_jaxpr/ppermute | solution.py:27
  (313 shorter events, 221.8 us)
Async XLA Ops:
  7.2 8.4 %collective-permute-start.1 = (bf16[2,1,64,256]{3,1,2,0:T(2,128)(2,1)S(1)}, bf16[2,1,64,256]{3,1,2,0:T(2,128)(2,1)S(1)}, u32[]{:S(2)}, u32[]{:S(2)}) collective-permute-start(bf16[2,1,64,256]{3,1,2,0:T(2,128)(2,1)S(1)} %get-tuple-element.304), channel_id=1, source_target_pairs={{0,1},{1,2},{2,3},{3,4},{4,5},{5,6},{6,7},{7,8},{8,9},{9,10},{10,1... | collective-permute-start | bytes 196616 | tf_op jit(solution)/shard_map/while/body/eval_jaxpr/ppermute | solution.py:15
  19.1 12.9 %collective-permute-start.2 = (bf16[2,2,64,256]{3,1,2,0:T(2,128)(2,1)S(1)}, bf16[2,2,64,256]{3,1,2,0:T(2,128)(2,1)S(1)}, u32[]{:S(2)}, u32[]{:S(2)}) collective-permute-start(bf16[2,2,64,256]{3,1,2,0:T(2,128)(2,1)S(1)} %get-tuple-element.305), channel_id=1, source_target_pairs={{0,64},{64,128},{128,192},{192,256},{256,320},{320,384},{384,448},... | collective-permute-start | bytes 393224 | tf_op jit(solution)/shard_map/while/body/eval_jaxpr/ppermute | solution.py:27
  35.6 8.4 %collective-permute-start.1 = (bf16[2,1,64,256]{3,1,2,0:T(2,128)(2,1)S(1)}, bf16[2,1,64,256]{3,1,2,0:T(2,128)(2,1)S(1)}, u32[]{:S(2)}, u32[]{:S(2)}) collective-permute-start(bf16[2,1,64,256]{3,1,2,0:T(2,128)(2,1)S(1)} %get-tuple-element.304), channel_id=1, source_target_pairs={{0,1},{1,2},{2,3},{3,4},{4,5},{5,6},{6,7},{7,8},{8,9},{9,10},{10,1... | collective-permute-start | bytes 196616 | tf_op jit(solution)/shard_map/while/body/eval_jaxpr/ppermute | solution.py:15
  47.6 12.9 %collective-permute-start.2 = (bf16[2,2,64,256]{3,1,2,0:T(2,128)(2,1)S(1)}, bf16[2,2,64,256]{3,1,2,0:T(2,128)(2,1)S(1)}, u32[]{:S(2)}, u32[]{:S(2)}) collective-permute-start(bf16[2,2,64,256]{3,1,2,0:T(2,128)(2,1)S(1)} %get-tuple-element.305), channel_id=1, source_target_pairs={{0,64},{64,128},{128,192},{192,256},{256,320},{320,384},{384,448},... | collective-permute-start | bytes 393224 | tf_op jit(solution)/shard_map/while/body/eval_jaxpr/ppermute | solution.py:27
  66.1 8.4 %collective-permute-start.1 = (bf16[2,1,64,256]{3,1,2,0:T(2,128)(2,1)S(1)}, bf16[2,1,64,256]{3,1,2,0:T(2,128)(2,1)S(1)}, u32[]{:S(2)}, u32[]{:S(2)}) collective-permute-start(bf16[2,1,64,256]{3,1,2,0:T(2,128)(2,1)S(1)} %get-tuple-element.304), channel_id=1, source_target_pairs={{0,1},{1,2},{2,3},{3,4},{4,5},{5,6},{6,7},{7,8},{8,9},{9,10},{10,1... | collective-permute-start | bytes 196616 | tf_op jit(solution)/shard_map/while/body/eval_jaxpr/ppermute | solution.py:15
  78.0 12.9 %collective-permute-start.2 = (bf16[2,2,64,256]{3,1,2,0:T(2,128)(2,1)S(1)}, bf16[2,2,64,256]{3,1,2,0:T(2,128)(2,1)S(1)}, u32[]{:S(2)}, u32[]{:S(2)}) collective-permute-start(bf16[2,2,64,256]{3,1,2,0:T(2,128)(2,1)S(1)} %get-tuple-element.305), channel_id=1, source_target_pairs={{0,64},{64,128},{128,192},{192,256},{256,320},{320,384},{384,448},... | collective-permute-start | bytes 393224 | tf_op jit(solution)/shard_map/while/body/eval_jaxpr/ppermute | solution.py:27
  94.5 8.4 %collective-permute-start.1 = (bf16[2,1,64,256]{3,1,2,0:T(2,128)(2,1)S(1)}, bf16[2,1,64,256]{3,1,2,0:T(2,128)(2,1)S(1)}, u32[]{:S(2)}, u32[]{:S(2)}) collective-permute-start(bf16[2,1,64,256]{3,1,2,0:T(2,128)(2,1)S(1)} %get-tuple-element.304), channel_id=1, source_target_pairs={{0,1},{1,2},{2,3},{3,4},{4,5},{5,6},{6,7},{7,8},{8,9},{9,10},{10,1... | collective-permute-start | bytes 196616 | tf_op jit(solution)/shard_map/while/body/eval_jaxpr/ppermute | solution.py:15
  106.5 12.9 %collective-permute-start.2 = (bf16[2,2,64,256]{3,1,2,0:T(2,128)(2,1)S(1)}, bf16[2,2,64,256]{3,1,2,0:T(2,128)(2,1)S(1)}, u32[]{:S(2)}, u32[]{:S(2)}) collective-permute-start(bf16[2,2,64,256]{3,1,2,0:T(2,128)(2,1)S(1)} %get-tuple-element.305), channel_id=1, source_target_pairs={{0,64},{64,128},{128,192},{192,256},{256,320},{320,384},{384,448},... | collective-permute-start | bytes 393224 | tf_op jit(solution)/shard_map/while/body/eval_jaxpr/ppermute | solution.py:27
  123.0 8.4 %collective-permute-start.1 = (bf16[2,1,64,256]{3,1,2,0:T(2,128)(2,1)S(1)}, bf16[2,1,64,256]{3,1,2,0:T(2,128)(2,1)S(1)}, u32[]{:S(2)}, u32[]{:S(2)}) collective-permute-start(bf16[2,1,64,256]{3,1,2,0:T(2,128)(2,1)S(1)} %get-tuple-element.304), channel_id=1, source_target_pairs={{0,1},{1,2},{2,3},{3,4},{4,5},{5,6},{6,7},{7,8},{8,9},{9,10},{10,1... | collective-permute-start | bytes 196616 | tf_op jit(solution)/shard_map/while/body/eval_jaxpr/ppermute | solution.py:15
  134.9 12.9 %collective-permute-start.2 = (bf16[2,2,64,256]{3,1,2,0:T(2,128)(2,1)S(1)}, bf16[2,2,64,256]{3,1,2,0:T(2,128)(2,1)S(1)}, u32[]{:S(2)}, u32[]{:S(2)}) collective-permute-start(bf16[2,2,64,256]{3,1,2,0:T(2,128)(2,1)S(1)} %get-tuple-element.305), channel_id=1, source_target_pairs={{0,64},{64,128},{128,192},{192,256},{256,320},{320,384},{384,448},... | collective-permute-start | bytes 393224 | tf_op jit(solution)/shard_map/while/body/eval_jaxpr/ppermute | solution.py:27
  163.4 12.9 %collective-permute-start.2 = (bf16[2,2,64,256]{3,1,2,0:T(2,128)(2,1)S(1)}, bf16[2,2,64,256]{3,1,2,0:T(2,128)(2,1)S(1)}, u32[]{:S(2)}, u32[]{:S(2)}) collective-permute-start(bf16[2,2,64,256]{3,1,2,0:T(2,128)(2,1)S(1)} %get-tuple-element.305), channel_id=1, source_target_pairs={{0,64},{64,128},{128,192},{192,256},{256,320},{320,384},{384,448},... | collective-permute-start | bytes 393224 | tf_op jit(solution)/shard_map/while/body/eval_jaxpr/ppermute | solution.py:27
  191.8 12.9 %collective-permute-start.2 = (bf16[2,2,64,256]{3,1,2,0:T(2,128)(2,1)S(1)}, bf16[2,2,64,256]{3,1,2,0:T(2,128)(2,1)S(1)}, u32[]{:S(2)}, u32[]{:S(2)}) collective-permute-start(bf16[2,2,64,256]{3,1,2,0:T(2,128)(2,1)S(1)} %get-tuple-element.305), channel_id=1, source_target_pairs={{0,64},{64,128},{128,192},{192,256},{256,320},{320,384},{384,448},... | collective-permute-start | bytes 393224 | tf_op jit(solution)/shard_map/while/body/eval_jaxpr/ppermute | solution.py:27
  208.3 8.4 %collective-permute-start.1 = (bf16[2,1,64,256]{3,1,2,0:T(2,128)(2,1)S(1)}, bf16[2,1,64,256]{3,1,2,0:T(2,128)(2,1)S(1)}, u32[]{:S(2)}, u32[]{:S(2)}) collective-permute-start(bf16[2,1,64,256]{3,1,2,0:T(2,128)(2,1)S(1)} %get-tuple-element.304), channel_id=1, source_target_pairs={{0,1},{1,2},{2,3},{3,4},{4,5},{5,6},{6,7},{7,8},{8,9},{9,10},{10,1... | collective-permute-start | bytes 196616 | tf_op jit(solution)/shard_map/while/body/eval_jaxpr/ppermute | solution.py:15
  220.3 12.9 %collective-permute-start.2 = (bf16[2,2,64,256]{3,1,2,0:T(2,128)(2,1)S(1)}, bf16[2,2,64,256]{3,1,2,0:T(2,128)(2,1)S(1)}, u32[]{:S(2)}, u32[]{:S(2)}) collective-permute-start(bf16[2,2,64,256]{3,1,2,0:T(2,128)(2,1)S(1)} %get-tuple-element.305), channel_id=1, source_target_pairs={{0,64},{64,128},{128,192},{192,256},{256,320},{320,384},{384,448},... | collective-permute-start | bytes 393224 | tf_op jit(solution)/shard_map/while/body/eval_jaxpr/ppermute | solution.py:27
  236.8 8.4 %collective-permute-start.1 = (bf16[2,1,64,256]{3,1,2,0:T(2,128)(2,1)S(1)}, bf16[2,1,64,256]{3,1,2,0:T(2,128)(2,1)S(1)}, u32[]{:S(2)}, u32[]{:S(2)}) collective-permute-start(bf16[2,1,64,256]{3,1,2,0:T(2,128)(2,1)S(1)} %get-tuple-element.304), channel_id=1, source_target_pairs={{0,1},{1,2},{2,3},{3,4},{4,5},{5,6},{6,7},{7,8},{8,9},{9,10},{10,1... | collective-permute-start | bytes 196616 | tf_op jit(solution)/shard_map/while/body/eval_jaxpr/ppermute | solution.py:15
  248.7 12.9 %collective-permute-start.2 = (bf16[2,2,64,256]{3,1,2,0:T(2,128)(2,1)S(1)}, bf16[2,2,64,256]{3,1,2,0:T(2,128)(2,1)S(1)}, u32[]{:S(2)}, u32[]{:S(2)}) collective-permute-start(bf16[2,2,64,256]{3,1,2,0:T(2,128)(2,1)S(1)} %get-tuple-element.305), channel_id=1, source_target_pairs={{0,64},{64,128},{128,192},{192,256},{256,320},{320,384},{384,448},... | collective-permute-start | bytes 393224 | tf_op jit(solution)/shard_map/while/body/eval_jaxpr/ppermute | solution.py:27
  265.2 8.4 %collective-permute-start.1 = (bf16[2,1,64,256]{3,1,2,0:T(2,128)(2,1)S(1)}, bf16[2,1,64,256]{3,1,2,0:T(2,128)(2,1)S(1)}, u32[]{:S(2)}, u32[]{:S(2)}) collective-permute-start(bf16[2,1,64,256]{3,1,2,0:T(2,128)(2,1)S(1)} %get-tuple-element.304), channel_id=1, source_target_pairs={{0,1},{1,2},{2,3},{3,4},{4,5},{5,6},{6,7},{7,8},{8,9},{9,10},{10,1... | collective-permute-start | bytes 196616 | tf_op jit(solution)/shard_map/while/body/eval_jaxpr/ppermute | solution.py:15
  277.2 12.9 %collective-permute-start.2 = (bf16[2,2,64,256]{3,1,2,0:T(2,128)(2,1)S(1)}, bf16[2,2,64,256]{3,1,2,0:T(2,128)(2,1)S(1)}, u32[]{:S(2)}, u32[]{:S(2)}) collective-permute-start(bf16[2,2,64,256]{3,1,2,0:T(2,128)(2,1)S(1)} %get-tuple-element.305), channel_id=1, source_target_pairs={{0,64},{64,128},{128,192},{192,256},{256,320},{320,384},{384,448},... | collective-permute-start | bytes 393224 | tf_op jit(solution)/shard_map/while/body/eval_jaxpr/ppermute | solution.py:27
  293.7 8.4 %collective-permute-start.1 = (bf16[2,1,64,256]{3,1,2,0:T(2,128)(2,1)S(1)}, bf16[2,1,64,256]{3,1,2,0:T(2,128)(2,1)S(1)}, u32[]{:S(2)}, u32[]{:S(2)}) collective-permute-start(bf16[2,1,64,256]{3,1,2,0:T(2,128)(2,1)S(1)} %get-tuple-element.304), channel_id=1, source_target_pairs={{0,1},{1,2},{2,3},{3,4},{4,5},{5,6},{6,7},{7,8},{8,9},{9,10},{10,1... | collective-permute-start | bytes 196616 | tf_op jit(solution)/shard_map/while/body/eval_jaxpr/ppermute | solution.py:15
  305.6 12.9 %collective-permute-start.2 = (bf16[2,2,64,256]{3,1,2,0:T(2,128)(2,1)S(1)}, bf16[2,2,64,256]{3,1,2,0:T(2,128)(2,1)S(1)}, u32[]{:S(2)}, u32[]{:S(2)}) collective-permute-start(bf16[2,2,64,256]{3,1,2,0:T(2,128)(2,1)S(1)} %get-tuple-element.305), channel_id=1, source_target_pairs={{0,64},{64,128},{128,192},{192,256},{256,320},{320,384},{384,448},... | collective-permute-start | bytes 393224 | tf_op jit(solution)/shard_map/while/body/eval_jaxpr/ppermute | solution.py:27
  334.1 14.3 %collective-permute-start.2 = (bf16[2,2,64,256]{3,1,2,0:T(2,128)(2,1)S(1)}, bf16[2,2,64,256]{3,1,2,0:T(2,128)(2,1)S(1)}, u32[]{:S(2)}, u32[]{:S(2)}) collective-permute-start(bf16[2,2,64,256]{3,1,2,0:T(2,128)(2,1)S(1)} %get-tuple-element.305), channel_id=1, source_target_pairs={{0,64},{64,128},{128,192},{192,256},{256,320},{320,384},{384,448},... | collective-permute-start | bytes 393224 | tf_op jit(solution)/shard_map/while/body/eval_jaxpr/ppermute | solution.py:27
  364.0 12.9 %collective-permute-start.2 = (bf16[2,2,64,256]{3,1,2,0:T(2,128)(2,1)S(1)}, bf16[2,2,64,256]{3,1,2,0:T(2,128)(2,1)S(1)}, u32[]{:S(2)}, u32[]{:S(2)}) collective-permute-start(bf16[2,2,64,256]{3,1,2,0:T(2,128)(2,1)S(1)} %get-tuple-element.305), channel_id=1, source_target_pairs={{0,64},{64,128},{128,192},{192,256},{256,320},{320,384},{384,448},... | collective-permute-start | bytes 393224 | tf_op jit(solution)/shard_map/while/body/eval_jaxpr/ppermute | solution.py:27
  392.4 12.9 %collective-permute-start.2 = (bf16[2,2,64,256]{3,1,2,0:T(2,128)(2,1)S(1)}, bf16[2,2,64,256]{3,1,2,0:T(2,128)(2,1)S(1)}, u32[]{:S(2)}, u32[]{:S(2)}) collective-permute-start(bf16[2,2,64,256]{3,1,2,0:T(2,128)(2,1)S(1)} %get-tuple-element.305), channel_id=1, source_target_pairs={{0,64},{64,128},{128,192},{192,256},{256,320},{320,384},{384,448},... | collective-permute-start | bytes 393224 | tf_op jit(solution)/shard_map/while/body/eval_jaxpr/ppermute | solution.py:27
  420.9 12.9 %collective-permute-start.2 = (bf16[2,2,64,256]{3,1,2,0:T(2,128)(2,1)S(1)}, bf16[2,2,64,256]{3,1,2,0:T(2,128)(2,1)S(1)}, u32[]{:S(2)}, u32[]{:S(2)}) collective-permute-start(bf16[2,2,64,256]{3,1,2,0:T(2,128)(2,1)S(1)} %get-tuple-element.305), channel_id=1, source_target_pairs={{0,64},{64,128},{128,192},{192,256},{256,320},{320,384},{384,448},... | collective-permute-start | bytes 393224 | tf_op jit(solution)/shard_map/while/body/eval_jaxpr/ppermute | solution.py:27
  (38 other events, 148.3 us)
where the time goes:
time: 437 us; the launch traced here: 435 us
  waiting for transfers between devices  254 us (58%)
  starting transfers between devices  99.1 us (23%)
  local copies, waits for them, and re-layouts  45.3 us (10%)
  other arithmetic  21.2 us (5%)
  matrix products  12.8 us (3%)
    ppermute x15, waiting for transfers between devices, passed_along(): return lax.ppermute(block, axis, route)  164 us
    ppermute x15, waiting for transfers between devices, with_halo(): lax.ppermute(tail, axis, [(i, (i + 1) % count) for i in range(ends)])  88.4 us
    ppermute x15, starting transfers between devices, with_halo(): lax.ppermute(tail, axis, [(i, (i + 1) % count) for i in range(ends)])  35.1 us
    ppermute x15, starting transfers between devices, with_halo(): lax.ppermute(head, axis, [((i + 1) % count, i) for i in range(ends)])  33.7 us
    ppermute x15, starting transfers between devices, passed_along(): return lax.ppermute(block, axis, route)  30.3 us
    while x30, local copies, waits for them, and re-layouts  18.6 us
    dynamic_slice x15, local copies, waits for them, and re-layouts, one_tick(): older = lax.dynamic_slice(outputs, corner, (1, span, slab, width, chans))  13.8 us
    conv_general_dilated x15, matrix products, one_tick(): lax.conv_general_dilated(stacked[None], kernel, (1, 1, 1), 'VALID', dimen...  12.8 us
  transfers between devices with their start and end apart: 45, of which 45 were waited for; matrix products, arithmetic and copies ran while one was open for 0% of the time, Pallas kernels for 0%

commit v1 on v0

v1 whole, which is shorter than its diff:
```python
import jax
import jax.numpy as jnp
from jax import lax
from jax.experimental import pallas as pl
from jax.experimental.pallas import tpu as pltpu
from jax.sharding import PartitionSpec as P

DEPTH = 4
CHUNK = 2


def stage_kernel(meta, top, mid, bot, own, left_mine, left_theirs, right_mine, right_theirs, far_mine, far_theirs,
                 kept, last, weights, cells, wide, sems):
    x, core, chip, piece, chips = meta[0], meta[1], meta[2], meta[3], meta[4]
    depth, _, taps, chans = weights.shape
    frames, slab, width, _ = mid.shape
    rows = 3 * slab
    part = taps // 4
    other = 1 - core

    def copy(src, dst, sem):
        pltpu.make_async_copy(src, dst, sem).start()

    for layer in range(depth):
        step = lax.rem(layer - x + depth, depth)
        sem = sems.at[layer]

        @pl.when(step == 0)
        def _():
            copy(own, weights.at[layer], sem)

        @pl.when(step == 1)
        def _():
            copy(right_mine, weights.at[layer, core], sem)
            copy(right_theirs, weights.at[layer, other], sem)

        @pl.when(step == 3)
        def _():
            copy(left_mine, weights.at[layer, core], sem)
            copy(left_theirs, weights.at[layer, other], sem)

        @pl.when(step == 2)
        def _():
            for place, shift in enumerate((0, 3, 1, 2)):
                at = pl.ds(pl.multiple_of(lax.rem(piece + shift, 4) * part, part), part)
                copy(far_mine.at[place], weights.at[layer, core, at], sem)
                copy(far_theirs.at[place], weights.at[layer, other, at], sem)

    cells[:, 0:slab] = top[...]
    cells[:, slab:2 * slab] = mid[...]
    cells[:, 2 * slab:] = bot[...]
    column = lax.broadcasted_iota(jnp.int32, (width, chans), 0)

    for layer in range(depth):
        def normalize(row, carry):
            place = chip * slab - slab + row
            inside = jnp.logical_and(place >= 0, place < chips * slab)
            for frame in range(frames):
                values = cells[frame, row].astype(jnp.float32)
                scale = lax.rsqrt(jnp.mean(values * values, axis=-1, keepdims=True) + 1e-06)
                normed = jnp.where(inside, values * scale, 0.0)
                before = jnp.where(column == 0, 0.0, pltpu.roll(normed, 1, 0))
                after = jnp.where(column == width - 1, 0.0, pltpu.roll(normed, width - 1, 0))
                wide[frame, row, :, 0:chans] = before.astype(jnp.bfloat16)
                wide[frame, row, :, chans:2 * chans] = normed.astype(jnp.bfloat16)
                wide[frame, row, :, 2 * chans:] = after.astype(jnp.bfloat16)
            return carry

        lax.fori_loop(layer, rows - layer, normalize, 0)
        pltpu.make_async_copy(own, weights.at[layer], sems.at[layer]).wait()

        def convolve(index, carry):
            row = layer + 1 + index * CHUNK
            size = CHUNK * width
            total = jnp.zeros((frames * size, chans), jnp.float32)
            older = jnp.zeros((size, chans), jnp.float32)
            for tap in range(3):
                at = pl.ds(tap * 3 * chans, 3 * chans)
                both = wide[:, pl.ds(row - 1 + tap, CHUNK)].reshape(frames * size, 3 * chans)
                total += jnp.dot(both, weights[layer, 1, at], preferred_element_type=jnp.float32)
                older += jnp.dot(both[:size], weights[layer, 0, at], preferred_element_type=jnp.float32)
            for frame in range(frames):
                conv = total[frame * size:(frame + 1) * size]
                if frame:
                    conv = conv + older
                conv = conv.reshape(CHUNK, width, chans)
                values = cells[frame, pl.ds(row, CHUNK)].astype(jnp.float32)
                cells[frame, pl.ds(row, CHUNK)] = (values + conv / (1.0 + jnp.exp(-conv))).astype(jnp.bfloat16)
            return carry

        lax.fori_loop(0, (rows - 2 * layer - 2) // CHUNK, convolve, 0)
        half = slab // 2
        kept[core, layer] = cells[:, slab:slab + half]
        kept[other, layer] = cells[:, slab + half:2 * slab]
    last[...] = cells[:, slab:2 * slab]


def run_stage(meta, top, mid, bot, kernels):
    frames, slab, width, chans = mid.shape
    taps = kernels[0].shape[1]
    vmem = pl.BlockSpec(memory_space=pltpu.VMEM)
    hbm = pl.BlockSpec(memory_space=pl.ANY)
    bf16 = jnp.bfloat16
    return pl.pallas_call(
        stage_kernel,
        out_shape=(
            jax.ShapeDtypeStruct((2, DEPTH, frames, slab // 2, width, chans), bf16),
            jax.ShapeDtypeStruct((frames, slab, width, chans), bf16),
        ),
        in_specs=[pl.BlockSpec(memory_space=pltpu.SMEM)] + [vmem] * 3 + [hbm] * len(kernels),
        out_specs=(vmem, vmem),
        scratch_shapes=[
            pltpu.VMEM((DEPTH, 2, taps, chans), bf16),
            pltpu.VMEM((frames, 3 * slab, width, chans), bf16),
            pltpu.VMEM((frames, 3 * slab, width, 3 * chans), bf16),
            pltpu.SemaphoreType.DMA((DEPTH,)),
        ],
        compiler_params=pltpu.CompilerParams(vmem_limit_bytes=40 * 1024 * 1024),
        cost_estimate=pl.CostEstimate(flops=7 * 10**9, bytes_accessed=12 * 10**6, transcendentals=10**6),
        name="stage",
    )(meta, top, mid, bot, *kernels)


def place_kernel(meta, *refs):
    sources, out, sems = refs[:-2], refs[-2], refs[-1]
    x, core = meta[0], meta[1]
    copies = []
    for shift in range(4):
        group = lax.rem(x - shift + 4, 4)
        for which in range(2):
            clip = 2 * group + (core if which == 0 else 1 - core)
            source = sources[2 * shift + which]
            copies.append(pltpu.make_async_copy(source, out.at[clip], sems.at[2 * shift + which]))
    for one in copies:
        one.start()
    for one in copies:
        one.wait()


def place(meta, sources):
    shape = sources[0].shape
    hbm = pl.BlockSpec(memory_space=pl.ANY)
    return pl.pallas_call(
        place_kernel,
        out_shape=jax.ShapeDtypeStruct((8,) + shape, jnp.bfloat16),
        in_specs=[pl.BlockSpec(memory_space=pltpu.SMEM)] + [hbm] * 8,
        out_specs=hbm,
        scratch_shapes=[pltpu.SemaphoreType.DMA((8,))],
        name="place",
    )(meta, *sources)


def route(move, keep=lambda zh, x, zl, y, c: True):
    pairs = []
    for zh in range(2):
        for x in range(4):
            for zl in range(4):
                for y in range(8):
                    for c in range(2):
                        here = (zh, x, zl, y, c)
                        there = move(*here)
                        if there is not None and keep(*here):
                            pairs.append(tuple((((d[0] * 4 + d[1]) * 4 + d[2]) * 8 + d[3]) * 2 + d[4] for d in (here, there)))
    return pairs


def next_chip(step):
    def move(zh, x, zl, y, c):
        chip = zl * 8 + y + step
        return (zh, x, chip // 8, chip % 8, c) if 0 <= chip < 32 else None
    return move


def send(array, move, keep=lambda *here: True):
    return lax.ppermute(array, ("section", "rows"), route(move, keep))


def along_x(step):
    return lambda zh, x, zl, y, c: (zh, (x + step) % 4, zl, y, c)


def along_y(step):
    return lambda zh, x, zl, y, c: (zh, x, zl, (y + step) % 8, c)


def sibling(zh, x, zl, y, c):
    return (zh, x, zl, y, 1 - c)


def local(frames_in, layer_weights):
    section, row = lax.axis_index("section"), lax.axis_index("rows")
    x, upper = section % 4, section // 4
    core, chip = row % 2, row // 2
    piece = chip % 4
    meta = jnp.stack([x, core, chip, piece, jnp.int32(32)]).astype(jnp.int32)
    chans = frames_in.shape[-1]

    own = layer_weights.reshape(2, 9 * chans, chans)
    mine = lax.dynamic_index_in_dim(own, core, 0, keepdims=False)
    part = mine.shape[0] // 4
    quarter = lax.dynamic_slice_in_dim(mine, piece * part, part, 0)

    far = send(quarter, along_x(2))
    left_mine = send(mine, along_x(1))
    right_mine = send(mine, along_x(-1))

    give = lax.dynamic_index_in_dim(frames_in, 2 * x + 1 - core, 0, keepdims=False)
    keep = lax.dynamic_index_in_dim(frames_in, 2 * x + core, 0, keepdims=False)
    got = send(give, sibling)
    mid = jnp.where(core == 0, jnp.concatenate([keep, got], 1), jnp.concatenate([got, keep], 1))
    top = send(mid, next_chip(1))
    bot = send(mid, next_chip(-1))

    far_mine = jnp.stack([far, send(far, along_y(1)), send(far, along_y(-1)), send(far, along_y(2))])
    far_theirs = send(far_mine, sibling)
    left_theirs = send(left_mine, sibling)
    right_theirs = send(right_mine, sibling)
    kernels = (own, left_mine, left_theirs, right_mine, right_theirs, far_mine, far_theirs)

    first, reached = run_stage(meta, top, mid, bot, kernels)

    mid = send(reached, lambda zh, x, zl, y, c: (1, x, zl, y, c), lambda zh, *_: zh == 0)
    top = send(mid, next_chip(1), lambda zh, *_: zh == 1)
    bot = send(mid, next_chip(-1), lambda zh, *_: zh == 1)
    second, _ = run_stage(meta, top, mid, bot, kernels)

    done = jnp.where(upper == 0, first, second)
    theirs = send(done[1], sibling)
    both = (done[0], theirs)
    sources = [lax.dynamic_index_in_dim(one, x, 0, keepdims=False) for one in both]
    for step in (1, 2, 3):
        layer = (x + step) % 4
        pair = jnp.stack([lax.dynamic_index_in_dim(one, layer, 0, keepdims=False) for one in both])
        got = send(pair, along_x(step))
        sources += [got[0], got[1]]
    return place(meta, sources)[None]


def solution(mesh):
    placed = (P(None, None, "rows", None, None), P("section", None, None, None, None, None))
    return jax.shard_map(
        local,
        mesh=mesh,
        in_specs=placed,
        out_specs=P("section", None, None, "rows", None, None),
        check_vma=False,
    )
```

time: 437 us -> 218 us (0.50)
  the two profiles are of different devices: /device:TPU:384 before, /device:TPU:455 now
where the time goes in v1:
time: 218 us
  waiting for transfers between devices  82.7 us (38%)
  Pallas kernels  64.3 us (29%)
  starting transfers between devices  59.2 us (27%)
  local copies, waits for them, and re-layouts  10.5 us (5%)
    ppermute x19, waiting for transfers between devices, send(): return lax.ppermute(array, ('section', 'rows'), route(move, keep))  82.7 us
    ppermute x19, starting transfers between devices, send(): return lax.ppermute(array, ('section', 'rows'), route(move, keep))  59.2 us
    pallas_call x1, Pallas kernels, place(): pl.pallas_call(place_kernel, out_shape=jax.ShapeDtypeStruct((8,) + shape,...  33.6 us
    pallas_call x2, Pallas kernels, run_stage(): pl.pallas_call(stage_kernel, out_shape=(jax.ShapeDtypeStruct((2, DEPTH, f...  30.7 us
  transfers between devices with their start and end apart: 19, of which 13 were waited for; matrix products, arithmetic and copies ran while one was open for 2% of the time, Pallas kernels for 0%

profile of v1, /device:TPU:455, one launch (start us, length us, event | category | flops | bytes accessed | tf_op | source)
XLA Modules:
  0.0 217.5 jit_solution(4401481833380454949)
XLA Ops:
  1.4 2.5 %collective-permute-start.5 = (bf16[2304,256]{1,0:T(8,128)(2,1)S(1)}, bf16[2304,256]{1,0:T(8,128)(2,1)}, u32[]{:S(2)}, u32[]{:S(2)}) collective-permute-start(bf16[2304,256]{1,0:T(8,128)(2,1)S(1)} %dynamic-slice_bitcast_fusion), channel_id=1, source_target_pairs={{0,192},{1,193},{2,194},{3,195},{4,196},{5,197},{6,198},{7,199},{8... | collective-permute-start | bytes 3538952 | tf_op jit(solution)/shard_map/ppermute | solution.py:175
  3.8 4.0 %collective-permute-start.3 = (bf16[2304,256]{1,0:T(8,128)(2,1)S(1)}, bf16[2304,256]{1,0:T(8,128)(2,1)}, u32[]{:S(2)}, u32[]{:S(2)}) collective-permute-start(bf16[2304,256]{1,0:T(8,128)(2,1)S(1)} %dynamic-slice_bitcast_fusion), channel_id=1, source_target_pairs={{0,64},{1,65},{2,66},{3,67},{4,68},{5,69},{6,70},{7,71},{8,72},{9,... | collective-permute-start | bytes 3538952 | tf_op jit(solution)/shard_map/ppermute | solution.py:175
  10.9 25.5 %collective-permute-done.7 = bf16[576,256]{1,0:T(8,128)(2,1)S(1)} collective-permute-done((bf16[576,256]{1,0:T(8,128)(2,1)S(1)}, bf16[576,256]{1,0:T(8,128)(2,1)S(1)}, u32[]{:S(2)}, u32[]{:S(2)}) %collective-permute-start.7) | collective-permute-done | bytes 294944 | tf_op jit(solution)/shard_map/ppermute | solution.py:175
  36.4 4.2 %collective-permute-start.10 = (bf16[576,256]{1,0:T(8,128)(2,1)S(1)}, bf16[576,256]{1,0:T(8,128)(2,1)S(1)}, u32[]{:S(2)}, u32[]{:S(2)}) collective-permute-start(bf16[576,256]{1,0:T(8,128)(2,1)S(1)} %collective-permute-done.7), channel_id=1, source_target_pairs={{0,4},{1,5},{2,6},{3,7},{4,8},{5,9},{6,10},{7,11},{8,12},{9,13},{1... | collective-permute-start | bytes 884744 | tf_op jit(solution)/shard_map/ppermute | solution.py:175
  40.6 3.3 %collective-permute-start.9 = (bf16[576,256]{1,0:T(8,128)(2,1)S(1)}, bf16[576,256]{1,0:T(8,128)(2,1)S(1)}, u32[]{:S(2)}, u32[]{:S(2)}) collective-permute-start(bf16[576,256]{1,0:T(8,128)(2,1)S(1)} %collective-permute-done.7), channel_id=1, source_target_pairs={{0,14},{1,15},{2,0},{3,1},{4,2},{5,3},{6,4},{7,5},{8,6},{9,7},{10,... | collective-permute-start | bytes 884744 | tf_op jit(solution)/shard_map/ppermute | solution.py:175
  45.9 5.5 %collective-permute-done.10 = bf16[576,256]{1,0:T(8,128)(2,1)S(1)} collective-permute-done((bf16[576,256]{1,0:T(8,128)(2,1)S(1)}, bf16[576,256]{1,0:T(8,128)(2,1)S(1)}, u32[]{:S(2)}, u32[]{:S(2)}) %collective-permute-start.10) | collective-permute-done | bytes 294944 | tf_op jit(solution)/shard_map/ppermute | solution.py:175
  51.4 10.0 %collective-permute-done.8 = bf16[576,256]{1,0:T(8,128)(2,1)S(1)} collective-permute-done((bf16[576,256]{1,0:T(8,128)(2,1)S(1)}, bf16[576,256]{1,0:T(8,128)(2,1)S(1)}, u32[]{:S(2)}, u32[]{:S(2)}) %collective-permute-start.8) | collective-permute-done | bytes 294944 | tf_op jit(solution)/shard_map/ppermute | solution.py:175
  61.5 3.1 %collective-permute-start.11 = (bf16[4,576,256]{2,1,0:T(8,128)(2,1)S(1)}, bf16[4,576,256]{2,1,0:T(8,128)(2,1)}, u32[]{:S(2)}, u32[]{:S(2)}) collective-permute-start(bf16[4,576,256]{2,1,0:T(8,128)(2,1)S(1)} %pad_maximum_fusion.far_mine), channel_id=1, source_target_pairs={{0,1},{1,0},{2,3},{3,2},{4,5},{5,4},{6,7},{7,6},{8,9},{9,8},{10,11... | collective-permute-start | bytes 3538952 | tf_op jit(solution)/shard_map/ppermute | solution.py:175
  73.3 2.6 %collective-permute-start.2 = (bf16[2,4,64,256]{3,2,1,0:T(8,128)(2,1)S(1)}, bf16[2,4,64,256]{3,2,1,0:T(8,128)(2,1)S(1)}, u32[]{:S(2)}, u32[]{:S(2)}) collective-permute-start(bf16[2,4,64,256]{3,2,1,0:T(8,128)(2,1)S(1)} %maximum_select_fusion.mid), channel_id=1, source_target_pairs={{2,0},{3,1},{4,2},{5,3},{6,4},{7,5},{8,6},{9,7},{10,8},{11,9},{12,... | collective-permute-start | bytes 786440 | tf_op jit(solution)/shard_map/ppermute | solution.py:175
  75.8 2.7 %collective-permute-start.1 = (bf16[2,4,64,256]{3,2,1,0:T(8,128)(2,1)S(1)}, bf16[2,4,64,256]{3,2,1,0:T(8,128)(2,1)S(1)}, u32[]{:S(2)}, u32[]{:S(2)}) collective-permute-start(bf16[2,4,64,256]{3,2,1,0:T(8,128)(2,1)S(1)} %maximum_select_fusion.mid), channel_id=1, source_target_pairs={{0,2},{1,3},{2,4},{3,5},{4,6},{5,7},{6,8},{7,9},{8,10},{9,11},{10,... | collective-permute-start | bytes 786440 | tf_op jit(solution)/shard_map/ppermute | solution.py:175
  78.6 4.3 %collective-permute-done.2.bot = bf16[2,4,64,256]{3,2,1,0:T(8,128)(2,1)S(1)} collective-permute-done((bf16[2,4,64,256]{3,2,1,0:T(8,128)(2,1)S(1)}, bf16[2,4,64,256]{3,2,1,0:T(8,128)(2,1)S(1)}, u32[]{:S(2)}, u32[]{:S(2)}) %collective-permute-start.2) | collective-permute-done | bytes 262176 | tf_op jit(solution)/shard_map/ppermute | solution.py:175
  82.9 4.4 %collective-permute-done.1.top = bf16[2,4,64,256]{3,2,1,0:T(8,128)(2,1)S(1)} collective-permute-done((bf16[2,4,64,256]{3,2,1,0:T(8,128)(2,1)S(1)}, bf16[2,4,64,256]{3,2,1,0:T(8,128)(2,1)S(1)}, u32[]{:S(2)}, u32[]{:S(2)}) %collective-permute-start.1) | collective-permute-done | bytes 262176 | tf_op jit(solution)/shard_map/ppermute | solution.py:175
  89.0 15.0 %stage.2 = (bf16[2,4,2,2,64,256]{5,4,3,2,1,0:T(8,128)(2,1)S(1)}, bf16[2,4,64,256]{3,2,1,0:T(8,128)(2,1)S(1)}) custom-call(s32[5]{0:T(128)S(1)} %stack.49.meta, bf16[2,4,64,256]{3,2,1,0:T(8,128)(2,1)S(1)} %collective-permute-done.1.top, bf16[2,4,64,256]{3,2,1,0:T(8,128)(2,1)S(1)} %maximum_select_fusion.mid, ...), custom_call_target="tpu_custom_call" | custom-call | flops 7000000000 | bytes 12000000 | tf_op jit(solution)/shard_map/stage/pallas_call | solution.py:104
  105.3 11.0 %collective-permute-done.12.mid = bf16[2,4,64,256]{3,2,1,0:T(8,128)(2,1)S(1)} collective-permute-done((bf16[2,4,64,256]{3,2,1,0:T(8,128)(2,1)S(1)}, bf16[2,4,64,256]{3,2,1,0:T(8,128)(2,1)S(1)}, u32[]{:S(2)}, u32[]{:S(2)}) %collective-permute-start.12) | collective-permute-done | bytes 262176 | tf_op jit(solution)/shard_map/ppermute | solution.py:175
  116.3 8.6 %collective-permute-start.14 = (bf16[2,4,64,256]{3,2,1,0:T(8,128)(2,1)S(1)}, bf16[2,4,64,256]{3,2,1,0:T(8,128)(2,1)S(1)}, u32[]{:S(2)}, u32[]{:S(2)}) collective-permute-start(bf16[2,4,64,256]{3,2,1,0:T(8,128)(2,1)S(1)} %collective-permute-done.12.mid), channel_id=1, source_target_pairs={{258,256},{259,257},{260,258},{261,259},{262,260},{263,261},{264,2... | collective-permute-start | bytes 786440 | tf_op jit(solution)/shard_map/ppermute | solution.py:175
  126.8 3.2 %collective-permute-done.14.bot = bf16[2,4,64,256]{3,2,1,0:T(8,128)(2,1)S(1)} collective-permute-done((bf16[2,4,64,256]{3,2,1,0:T(8,128)(2,1)S(1)}, bf16[2,4,64,256]{3,2,1,0:T(8,128)(2,1)S(1)}, u32[]{:S(2)}, u32[]{:S(2)}) %collective-permute-start.14) | collective-permute-done | bytes 262176 | tf_op jit(solution)/shard_map/ppermute | solution.py:175
  130.1 5.9 %collective-permute-done.13.top = bf16[2,4,64,256]{3,2,1,0:T(8,128)(2,1)S(1)} collective-permute-done((bf16[2,4,64,256]{3,2,1,0:T(8,128)(2,1)S(1)}, bf16[2,4,64,256]{3,2,1,0:T(8,128)(2,1)S(1)}, u32[]{:S(2)}, u32[]{:S(2)}) %collective-permute-start.13) | collective-permute-done | bytes 262176 | tf_op jit(solution)/shard_map/ppermute | solution.py:175
  137.6 15.7 %stage.3 = (bf16[2,4,2,2,64,256]{5,4,3,2,1,0:T(8,128)(2,1)S(1)}, bf16[2,4,64,256]{3,2,1,0:T(8,128)(2,1)}) custom-call(s32[5]{0:T(128)S(1)} %stack.49.meta, bf16[2,4,64,256]{3,2,1,0:T(8,128)(2,1)S(1)} %collective-permute-done.13.top, bf16[2,4,64,256]{3,2,1,0:T(8,128)(2,1)S(1)} %collective-permute-done.12.mid, ...), custom_call_target="tpu_custom_call" | custom-call | flops 7000000000 | bytes 12000000 | tf_op jit(solution)/shard_map/stage/pallas_call | solution.py:104
  153.5 3.6 %collective-permute-start.15 = (bf16[4,2,2,64,256]{4,3,2,1,0:T(8,128)(2,1)S(1)}, bf16[4,2,2,64,256]{4,3,2,1,0:T(8,128)(2,1)S(1)}, u32[]{:S(2)}, u32[]{:S(2)}) collective-permute-start(bf16[4,2,2,64,256]{4,3,2,1,0:T(8,128)(2,1)S(1)} %get-tuple-element.11), channel_id=1, source_target_pairs={{0,1},{1,0},{2,3},{3,2},{4,5},{5,4},{6,7},{7,6},{8,9},{9,8},{10,11... | collective-permute-start | bytes 1572872 | tf_op jit(solution)/shard_map/ppermute | solution.py:175
  159.4 6.5 %collective-permute-start.16 = (bf16[2,2,2,64,256]{4,3,2,1,0:T(8,128)(2,1)S(1)}, bf16[2,2,2,64,256]{4,3,2,1,0:T(8,128)(2,1)S(1)}, u32[]{:S(2)}, u32[]{:S(2)}) collective-permute-start(bf16[2,2,2,64,256]{4,3,2,1,0:T(8,128)(2,1)S(1)} %pad_maximum_fusion.1), channel_id=1, source_target_pairs={{0,64},{1,65},{2,66},{3,67},{4,68},{5,69},{6,70},{7,71},{8,72},{9,... | collective-permute-start | bytes 786440 | tf_op jit(solution)/shard_map/ppermute | solution.py:175
  165.9 2.8 %collective-permute-start.17 = (bf16[2,2,2,64,256]{4,3,2,1,0:T(8,128)(2,1)S(1)}, bf16[2,2,2,64,256]{4,3,2,1,0:T(8,128)(2,1)S(1)}, u32[]{:S(2)}, u32[]{:S(2)}) collective-permute-start(bf16[2,2,2,64,256]{4,3,2,1,0:T(8,128)(2,1)S(1)} %pad_maximum_fusion.2), channel_id=1, source_target_pairs={{0,128},{1,129},{2,130},{3,131},{4,132},{5,133},{6,134},{7,135},{8... | collective-permute-start | bytes 786440 | tf_op jit(solution)/shard_map/ppermute | solution.py:175
  172.3 4.3 %collective-permute-done.17 = bf16[2,2,2,64,256]{4,3,2,1,0:T(8,128)(2,1)S(1)} collective-permute-done((bf16[2,2,2,64,256]{4,3,2,1,0:T(8,128)(2,1)S(1)}, bf16[2,2,2,64,256]{4,3,2,1,0:T(8,128)(2,1)S(1)}, u32[]{:S(2)}, u32[]{:S(2)}) %collective-permute-start.17) | collective-permute-done | bytes 262176 | tf_op jit(solution)/shard_map/ppermute | solution.py:175
  177.3 5.9 %collective-permute-done.18 = bf16[2,2,2,64,256]{4,3,2,1,0:T(8,128)(2,1)S(1)} collective-permute-done((bf16[2,2,2,64,256]{4,3,2,1,0:T(8,128)(2,1)S(1)}, bf16[2,2,2,64,256]{4,3,2,1,0:T(8,128)(2,1)S(1)}, u32[]{:S(2)}, u32[]{:S(2)}) %collective-permute-start.18) | collective-permute-done | bytes 262176 | tf_op jit(solution)/shard_map/ppermute | solution.py:175
  183.9 33.6 %place.1 = bf16[8,2,2,64,256]{4,3,2,1,0:T(8,128)(2,1)} custom-call(s32[5]{0:T(128)} %copy-done.2, bf16[2,2,64,256]{3,2,1,0:T(8,128)(2,1)} %get-tuple-element.18.refs_0_, bf16[2,2,64,256]{3,2,1,0:T(8,128)(2,1)} %get-tuple-element.22.refs_1_, bf16[2,2,64,256]{3,2,1,0:T(8,128)(2,1)} %get-tuple-element.28.refs_2_, ...), custom_call_target="tpu_custom_call" | custom-call | tf_op jit(solution)/shard_map/place/pallas_call | solution.py:143
  (39 shorter events, 29.0 us)
Async XLA Ops:
  1.4 63.3 %collective-permute-start.5 = (bf16[2304,256]{1,0:T(8,128)(2,1)S(1)}, bf16[2304,256]{1,0:T(8,128)(2,1)}, u32[]{:S(2)}, u32[]{:S(2)}) collective-permute-start(bf16[2304,256]{1,0:T(8,128)(2,1)S(1)} %dynamic-slice_bitcast_fusion), channel_id=1, source_target_pairs={{0,192},{1,193},{2,194},{3,195},{4,196},{5,197},{6,198},{7,199},{8... | collective-permute-start | bytes 3538952 | tf_op jit(solution)/shard_map/ppermute | solution.py:175
  3.8 62.7 %collective-permute-start.3 = (bf16[2304,256]{1,0:T(8,128)(2,1)S(1)}, bf16[2304,256]{1,0:T(8,128)(2,1)}, u32[]{:S(2)}, u32[]{:S(2)}) collective-permute-start(bf16[2304,256]{1,0:T(8,128)(2,1)S(1)} %dynamic-slice_bitcast_fusion), channel_id=1, source_target_pairs={{0,64},{1,65},{2,66},{3,67},{4,68},{5,69},{6,70},{7,71},{8,72},{9,... | collective-permute-start | bytes 3538952 | tf_op jit(solution)/shard_map/ppermute | solution.py:175
  9.0 27.4 %collective-permute-start.7 = (bf16[576,256]{1,0:T(8,128)(2,1)S(1)}, bf16[576,256]{1,0:T(8,128)(2,1)S(1)}, u32[]{:S(2)}, u32[]{:S(2)}) collective-permute-start(bf16[576,256]{1,0:T(8,128)(2,1)S(1)} %dynamic-slice_bitcast_fusion.1), channel_id=1, source_target_pairs={{0,128},{1,129},{2,130},{3,131},{4,132},{5,133},{6,134},{7,135},{8... | collective-permute-start | bytes 884744 | tf_op jit(solution)/shard_map/ppermute | solution.py:175
  36.4 15.0 %collective-permute-start.10 = (bf16[576,256]{1,0:T(8,128)(2,1)S(1)}, bf16[576,256]{1,0:T(8,128)(2,1)S(1)}, u32[]{:S(2)}, u32[]{:S(2)}) collective-permute-start(bf16[576,256]{1,0:T(8,128)(2,1)S(1)} %collective-permute-done.7), channel_id=1, source_target_pairs={{0,4},{1,5},{2,6},{3,7},{4,8},{5,9},{6,10},{7,11},{8,12},{9,13},{1... | collective-permute-start | bytes 884744 | tf_op jit(solution)/shard_map/ppermute | solution.py:175
  40.6 10.8 %collective-permute-start.9 = (bf16[576,256]{1,0:T(8,128)(2,1)S(1)}, bf16[576,256]{1,0:T(8,128)(2,1)S(1)}, u32[]{:S(2)}, u32[]{:S(2)}) collective-permute-start(bf16[576,256]{1,0:T(8,128)(2,1)S(1)} %collective-permute-done.7), channel_id=1, source_target_pairs={{0,14},{1,15},{2,0},{3,1},{4,2},{5,3},{6,4},{7,5},{8,6},{9,7},{10,... | collective-permute-start | bytes 884744 | tf_op jit(solution)/shard_map/ppermute | solution.py:175
  43.9 17.5 %collective-permute-start.8 = (bf16[576,256]{1,0:T(8,128)(2,1)S(1)}, bf16[576,256]{1,0:T(8,128)(2,1)S(1)}, u32[]{:S(2)}, u32[]{:S(2)}) collective-permute-start(bf16[576,256]{1,0:T(8,128)(2,1)S(1)} %collective-permute-done.7), channel_id=1, source_target_pairs={{0,2},{1,3},{2,4},{3,5},{4,6},{5,7},{6,8},{7,9},{8,10},{9,11},{10,... | collective-permute-start | bytes 884744 | tf_op jit(solution)/shard_map/ppermute | solution.py:175
  61.5 25.8 %collective-permute-start.11 = (bf16[4,576,256]{2,1,0:T(8,128)(2,1)S(1)}, bf16[4,576,256]{2,1,0:T(8,128)(2,1)}, u32[]{:S(2)}, u32[]{:S(2)}) collective-permute-start(bf16[4,576,256]{2,1,0:T(8,128)(2,1)S(1)} %pad_maximum_fusion.far_mine), channel_id=1, source_target_pairs={{0,1},{1,0},{2,3},{3,2},{4,5},{5,4},{6,7},{7,6},{8,9},{9,8},{10,11... | collective-permute-start | bytes 3538952 | tf_op jit(solution)/shard_map/ppermute | solution.py:175
  64.6 22.7 %collective-permute-start.6 = (bf16[2304,256]{1,0:T(8,128)(2,1)}, bf16[2304,256]{1,0:T(8,128)(2,1)}, u32[]{:S(2)}, u32[]{:S(2)}) collective-permute-start(bf16[2304,256]{1,0:T(8,128)(2,1)} %collective-permute-done.5.right_mine), channel_id=1, source_target_pairs={{0,1},{1,0},{2,3},{3,2},{4,5},{5,4},{6,7},{7,6},{8,9},{9,8},{10,11... | collective-permute-start | bytes 3538952 | tf_op jit(solution)/shard_map/ppermute | solution.py:175
  66.5 20.7 %collective-permute-start.4 = (bf16[2304,256]{1,0:T(8,128)(2,1)}, bf16[2304,256]{1,0:T(8,128)(2,1)}, u32[]{:S(2)}, u32[]{:S(2)}) collective-permute-start(bf16[2304,256]{1,0:T(8,128)(2,1)} %collective-permute-done.3.left_mine), channel_id=1, source_target_pairs={{0,1},{1,0},{2,3},{3,2},{4,5},{5,4},{6,7},{7,6},{8,9},{9,8},{10,11... | collective-permute-start | bytes 3538952 | tf_op jit(solution)/shard_map/ppermute | solution.py:175
  70.0 3.2 %collective-permute-start = (bf16[2,2,64,256]{3,2,1,0:T(8,128)(2,1)S(1)}, bf16[2,2,64,256]{3,2,1,0:T(8,128)(2,1)S(1)}, u32[]{:S(2)}, u32[]{:S(2)}) collective-permute-start(bf16[2,2,64,256]{3,2,1,0:T(8,128)(2,1)S(1)} %get-tuple-element.14), channel_id=1, source_target_pairs={{0,1},{1,0},{2,3},{3,2},{4,5},{5,4},{6,7},{7,6},{8,9},{9,8},{10,11... | collective-permute-start | bytes 393224 | tf_op jit(solution)/shard_map/ppermute | solution.py:175
  73.3 9.6 %collective-permute-start.2 = (bf16[2,4,64,256]{3,2,1,0:T(8,128)(2,1)S(1)}, bf16[2,4,64,256]{3,2,1,0:T(8,128)(2,1)S(1)}, u32[]{:S(2)}, u32[]{:S(2)}) collective-permute-start(bf16[2,4,64,256]{3,2,1,0:T(8,128)(2,1)S(1)} %maximum_select_fusion.mid), channel_id=1, source_target_pairs={{2,0},{3,1},{4,2},{5,3},{6,4},{7,5},{8,6},{9,7},{10,8},{11,9},{12,... | collective-permute-start | bytes 786440 | tf_op jit(solution)/shard_map/ppermute | solution.py:175
  75.8 11.4 %collective-permute-start.1 = (bf16[2,4,64,256]{3,2,1,0:T(8,128)(2,1)S(1)}, bf16[2,4,64,256]{3,2,1,0:T(8,128)(2,1)S(1)}, u32[]{:S(2)}, u32[]{:S(2)}) collective-permute-start(bf16[2,4,64,256]{3,2,1,0:T(8,128)(2,1)S(1)} %maximum_select_fusion.mid), channel_id=1, source_target_pairs={{0,2},{1,3},{2,4},{3,5},{4,6},{5,7},{6,8},{7,9},{8,10},{9,11},{10,... | collective-permute-start | bytes 786440 | tf_op jit(solution)/shard_map/ppermute | solution.py:175
  78.6 57.3 %copy-start.2 = (s32[5]{0:T(128)}, s32[5]{0:T(128)S(1)}, u32[]{:S(2)}) copy-start(s32[5]{0:T(128)S(1)} %stack.49.meta) | copy-start | bytes 64
  87.3 1.7 copy-start
  104.0 12.3 %collective-permute-start.12 = (bf16[2,4,64,256]{3,2,1,0:T(8,128)(2,1)S(1)}, bf16[2,4,64,256]{3,2,1,0:T(8,128)(2,1)S(1)}, u32[]{:S(2)}, u32[]{:S(2)}) collective-permute-start(bf16[2,4,64,256]{3,2,1,0:T(8,128)(2,1)S(1)} %get-tuple-element.9), channel_id=1, source_target_pairs={{0,256},{1,257},{2,258},{3,259},{4,260},{5,261},{6,262},{7,263},{8... | collective-permute-start | bytes 786440 | tf_op jit(solution)/shard_map/ppermute | solution.py:175
  116.3 13.8 %collective-permute-start.14 = (bf16[2,4,64,256]{3,2,1,0:T(8,128)(2,1)S(1)}, bf16[2,4,64,256]{3,2,1,0:T(8,128)(2,1)S(1)}, u32[]{:S(2)}, u32[]{:S(2)}) collective-permute-start(bf16[2,4,64,256]{3,2,1,0:T(8,128)(2,1)S(1)} %collective-permute-done.12.mid), channel_id=1, source_target_pairs={{258,256},{259,257},{260,258},{261,259},{262,260},{263,261},{264,2... | collective-permute-start | bytes 786440 | tf_op jit(solution)/shard_map/ppermute | solution.py:175
  124.9 11.1 %collective-permute-start.13 = (bf16[2,4,64,256]{3,2,1,0:T(8,128)(2,1)S(1)}, bf16[2,4,64,256]{3,2,1,0:T(8,128)(2,1)S(1)}, u32[]{:S(2)}, u32[]{:S(2)}) collective-permute-start(bf16[2,4,64,256]{3,2,1,0:T(8,128)(2,1)S(1)} %collective-permute-done.12.mid), channel_id=1, source_target_pairs={{256,258},{257,259},{258,260},{259,261},{260,262},{261,263},{262,2... | collective-permute-start | bytes 786440 | tf_op jit(solution)/shard_map/ppermute | solution.py:175
  136.0 1.7 copy-start.1
  153.5 5.1 %collective-permute-start.15 = (bf16[4,2,2,64,256]{4,3,2,1,0:T(8,128)(2,1)S(1)}, bf16[4,2,2,64,256]{4,3,2,1,0:T(8,128)(2,1)S(1)}, u32[]{:S(2)}, u32[]{:S(2)}) collective-permute-start(bf16[4,2,2,64,256]{4,3,2,1,0:T(8,128)(2,1)S(1)} %get-tuple-element.11), channel_id=1, source_target_pairs={{0,1},{1,0},{2,3},{3,2},{4,5},{5,4},{6,7},{7,6},{8,9},{9,8},{10,11... | collective-permute-start | bytes 1572872 | tf_op jit(solution)/shard_map/ppermute | solution.py:175
  159.4 12.2 %collective-permute-start.16 = (bf16[2,2,2,64,256]{4,3,2,1,0:T(8,128)(2,1)S(1)}, bf16[2,2,2,64,256]{4,3,2,1,0:T(8,128)(2,1)S(1)}, u32[]{:S(2)}, u32[]{:S(2)}) collective-permute-start(bf16[2,2,2,64,256]{4,3,2,1,0:T(8,128)(2,1)S(1)} %pad_maximum_fusion.1), channel_id=1, source_target_pairs={{0,64},{1,65},{2,66},{3,67},{4,68},{5,69},{6,70},{7,71},{8,72},{9,... | collective-permute-start | bytes 786440 | tf_op jit(solution)/shard_map/ppermute | solution.py:175
  165.9 10.6 %collective-permute-start.17 = (bf16[2,2,2,64,256]{4,3,2,1,0:T(8,128)(2,1)S(1)}, bf16[2,2,2,64,256]{4,3,2,1,0:T(8,128)(2,1)S(1)}, u32[]{:S(2)}, u32[]{:S(2)}) collective-permute-start(bf16[2,2,2,64,256]{4,3,2,1,0:T(8,128)(2,1)S(1)} %pad_maximum_fusion.2), channel_id=1, source_target_pairs={{0,128},{1,129},{2,130},{3,131},{4,132},{5,133},{6,134},{7,135},{8... | collective-permute-start | bytes 786440 | tf_op jit(solution)/shard_map/ppermute | solution.py:175
  168.8 14.4 %collective-permute-start.18 = (bf16[2,2,2,64,256]{4,3,2,1,0:T(8,128)(2,1)S(1)}, bf16[2,2,2,64,256]{4,3,2,1,0:T(8,128)(2,1)S(1)}, u32[]{:S(2)}, u32[]{:S(2)}) collective-permute-start(bf16[2,2,2,64,256]{4,3,2,1,0:T(8,128)(2,1)S(1)} %pad_maximum_fusion.3), channel_id=1, source_target_pairs={{0,192},{1,193},{2,194},{3,195},{4,196},{5,197},{6,198},{7,199},{8... | collective-permute-start | bytes 786440 | tf_op jit(solution)/shard_map/ppermute | solution.py:175

commit v2 on v1

--- a/solution.py
+++ b/solution.py
@@ -9,7 +9,7 @@
 CHUNK = 2
 
 
-def stage_kernel(meta, top, mid, bot, own, left_mine, left_theirs, right_mine, right_theirs, far_mine, far_theirs,
+def stage_kernel(meta, top, mid, bot, own_mine, own_theirs, left_mine, left_theirs, right_mine, right_theirs, far_mine, far_theirs,
                  kept, last, weights, cells, wide, sems):
     x, core, chip, piece, chips = meta[0], meta[1], meta[2], meta[3], meta[4]
     depth, _, taps, chans = weights.shape
@@ -27,7 +27,8 @@
 
         @pl.when(step == 0)
         def _():
-            copy(own, weights.at[layer], sem)
+            copy(own_mine, weights.at[layer, core], sem)
+            copy(own_theirs, weights.at[layer, other], sem)
 
         @pl.when(step == 1)
         def _():
@@ -67,7 +68,7 @@
             return carry
 
         lax.fori_loop(layer, rows - layer, normalize, 0)
-        pltpu.make_async_copy(own, weights.at[layer], sems.at[layer]).wait()
+        pltpu.make_async_copy(weights.at[layer], weights.at[layer], sems.at[layer]).wait()
 
         def convolve(index, carry):
             row = layer + 1 + index * CHUNK
@@ -97,7 +98,7 @@
 
 def run_stage(meta, top, mid, bot, kernels):
     frames, slab, width, chans = mid.shape
-    taps = kernels[0].shape[1]
+    taps = kernels[0].shape[0]
     vmem = pl.BlockSpec(memory_space=pltpu.VMEM)
     hbm = pl.BlockSpec(memory_space=pl.ANY)
     bf16 = jnp.bfloat16
@@ -121,33 +122,27 @@
     )(meta, top, mid, bot, *kernels)
 
 
-def place_kernel(meta, *refs):
-    sources, out, sems = refs[:-2], refs[-2], refs[-1]
+def place_kernel(meta, home, away, *refs):
+    arrived, out = refs[:-1], refs[-1]
     x, core = meta[0], meta[1]
-    copies = []
-    for shift in range(4):
+    out[2 * x + core] = home[...]
+    out[2 * x + 1 - core] = away[...]
+    for shift, pair in enumerate(arrived, 1):
         group = lax.rem(x - shift + 4, 4)
-        for which in range(2):
-            clip = 2 * group + (core if which == 0 else 1 - core)
-            source = sources[2 * shift + which]
-            copies.append(pltpu.make_async_copy(source, out.at[clip], sems.at[2 * shift + which]))
-    for one in copies:
-        one.start()
-    for one in copies:
-        one.wait()
-
-
-def place(meta, sources):
-    shape = sources[0].shape
-    hbm = pl.BlockSpec(memory_space=pl.ANY)
+        out[2 * group + core] = pair[0]
+        out[2 * group + 1 - core] = pair[1]
+
+
+def place(meta, home, away, arrived):
+    vmem = pl.BlockSpec(memory_space=pltpu.VMEM)
     return pl.pallas_call(
         place_kernel,
-        out_shape=jax.ShapeDtypeStruct((8,) + shape, jnp.bfloat16),
-        in_specs=[pl.BlockSpec(memory_space=pltpu.SMEM)] + [hbm] * 8,
-        out_specs=hbm,
-        scratch_shapes=[pltpu.SemaphoreType.DMA((8,))],
+        out_shape=jax.ShapeDtypeStruct((8,) + home.shape, jnp.bfloat16),
+        in_specs=[pl.BlockSpec(memory_space=pltpu.SMEM)] + [vmem] * (2 + len(arrived)),
+        out_specs=vmem,
+        compiler_params=pltpu.CompilerParams(vmem_limit_bytes=8 * 1024 * 1024),
         name="place",
-    )(meta, *sources)
+    )(meta, home, away, *arrived)
 
 
 def route(move, keep=lambda zh, x, zl, y, c: True):
@@ -196,26 +191,28 @@
     chans = frames_in.shape[-1]
 
     own = layer_weights.reshape(2, 9 * chans, chans)
-    mine = lax.dynamic_index_in_dim(own, core, 0, keepdims=False)
-    part = mine.shape[0] // 4
-    quarter = lax.dynamic_slice_in_dim(mine, piece * part, part, 0)
-
+    part = own.shape[1] // 4
+    quarter = lax.dynamic_slice(own, (core, piece * part, 0), (1, part, chans))[0]
     far = send(quarter, along_x(2))
-    left_mine = send(mine, along_x(1))
-    right_mine = send(mine, along_x(-1))
 
     give = lax.dynamic_index_in_dim(frames_in, 2 * x + 1 - core, 0, keepdims=False)
     keep = lax.dynamic_index_in_dim(frames_in, 2 * x + core, 0, keepdims=False)
     got = send(give, sibling)
+    mine = lax.dynamic_index_in_dim(own, core, 0, keepdims=False)
+    theirs = lax.dynamic_index_in_dim(own, 1 - core, 0, keepdims=False)
+    far, mine, got = lax.optimization_barrier((far, mine, got))
+    left_mine = send(mine, along_x(1))
+    right_mine = send(mine, along_x(-1))
     mid = jnp.where(core == 0, jnp.concatenate([keep, got], 1), jnp.concatenate([got, keep], 1))
     top = send(mid, next_chip(1))
     bot = send(mid, next_chip(-1))
 
+    far, top, bot = lax.optimization_barrier((far, top, bot))
     far_mine = jnp.stack([far, send(far, along_y(1)), send(far, along_y(-1)), send(far, along_y(2))])
     far_theirs = send(far_mine, sibling)
     left_theirs = send(left_mine, sibling)
     right_theirs = send(right_mine, sibling)
-    kernels = (own, left_mine, left_theirs, right_mine, right_theirs, far_mine, far_theirs)
+    kernels = (mine, theirs, left_mine, left_theirs, right_mine, right_theirs, far_mine, far_theirs)
 
     first, reached = run_stage(meta, top, mid, bot, kernels)
 
@@ -225,15 +222,14 @@
     second, _ = run_stage(meta, top, mid, bot, kernels)
 
     done = jnp.where(upper == 0, first, second)
-    theirs = send(done[1], sibling)
-    both = (done[0], theirs)
-    sources = [lax.dynamic_index_in_dim(one, x, 0, keepdims=False) for one in both]
+    both = (done[0], send(done[1], sibling))
+    home, away = [lax.dynamic_index_in_dim(one, x, 0, keepdims=False) for one in both]
+    arrived = []
     for step in (1, 2, 3):
         layer = (x + step) % 4
         pair = jnp.stack([lax.dynamic_index_in_dim(one, layer, 0, keepdims=False) for one in both])
-        got = send(pair, along_x(step))
-        sources += [got[0], got[1]]
-    return place(meta, sources)[None]
+        arrived.append(send(pair, along_x(step)))
+    return place(meta, home, away, arrived)[None]
 
 
 def solution(mesh):

time: 218 us -> 170 us (0.78)
  the two profiles are of different devices: /device:TPU:455 before, /device:TPU:391 now
where the time goes in v2:
time: 170 us
  waiting for transfers between devices  70.1 us (41%)
  starting transfers between devices  54.2 us (32%)
  Pallas kernels  33.5 us (20%)
  local copies, waits for them, and re-layouts  9.93 us (6%)
    ppermute x19, waiting for transfers between devices, send(): return lax.ppermute(array, ('section', 'rows'), route(move, keep))  70.1 us
    ppermute x19, starting transfers between devices, send(): return lax.ppermute(array, ('section', 'rows'), route(move, keep))  54.2 us
    pallas_call x2, Pallas kernels, run_stage(): pl.pallas_call(stage_kernel, out_shape=(jax.ShapeDtypeStruct((2, DEPTH, f...  31.9 us
    unnamed x18, local copies, waits for them, and re-layouts  5.93 us
  transfers between devices with their start and end apart: 19, of which 14 were waited for; matrix products, arithmetic and copies ran while one was open for 2% of the time, Pallas kernels for 0%

profile of v2, /device:TPU:391, one launch (start us, length us, event | category | flops | bytes accessed | tf_op | source)
XLA Modules:
  0.0 169.5 jit_solution(3902413381700478175)
XLA Ops:
  1.0 2.6 %collective-permute-start.1 = (bf16[2,2,64,256]{3,2,1,0:T(8,128)(2,1)S(1)}, bf16[2,2,64,256]{3,2,1,0:T(8,128)(2,1)S(1)}, u32[]{:S(2)}, u32[]{:S(2)}) collective-permute-start(bf16[2,2,64,256]{3,2,1,0:T(8,128)(2,1)S(1)} %get-tuple-element.28), channel_id=1, source_target_pairs={{0,1},{1,0},{2,3},{3,2},{4,5},{5,4},{6,7},{7,6},{8,9},{9,8},{10,11... | collective-permute-start | bytes 393224 | tf_op jit(solution)/shard_map/ppermute | solution.py:170
  4.6 3.0 %collective-permute-start = (bf16[576,256]{1,0:T(8,128)(2,1)S(1)}, bf16[576,256]{1,0:T(8,128)(2,1)S(1)}, u32[]{:S(2)}, u32[]{:S(2)}) collective-permute-start(bf16[576,256]{1,0:T(8,128)(2,1)S(1)} %dynamic-slice_bitcast_fusion.2), channel_id=1, source_target_pairs={{0,128},{1,129},{2,130},{3,131},{4,132},{5,133},{6,134},{7,135},{8... | collective-permute-start | bytes 884744 | tf_op jit(solution)/shard_map/ppermute | solution.py:170
  9.5 7.2 %collective-permute-done = bf16[576,256]{1,0:T(8,128)(2,1)S(1)} collective-permute-done((bf16[576,256]{1,0:T(8,128)(2,1)S(1)}, bf16[576,256]{1,0:T(8,128)(2,1)S(1)}, u32[]{:S(2)}, u32[]{:S(2)}) %collective-permute-start) | collective-permute-done | bytes 294944 | tf_op jit(solution)/shard_map/ppermute | solution.py:170
  16.6 2.4 %collective-permute-start.6 = (bf16[2304,256]{1,0:T(8,128)(2,1)S(1)}, bf16[2304,256]{1,0:T(8,128)(2,1)}, u32[]{:S(2)}, u32[]{:S(2)}) collective-permute-start(bf16[2304,256]{1,0:T(8,128)(2,1)S(1)} %get-tuple-element.18.own_mine), channel_id=1, source_target_pairs={{0,192},{1,193},{2,194},{3,195},{4,196},{5,197},{6,198},{7,199},{8... | collective-permute-start | bytes 3538952 | tf_op jit(solution)/shard_map/ppermute | solution.py:170
  19.1 4.0 %collective-permute-start.4 = (bf16[2304,256]{1,0:T(8,128)(2,1)S(1)}, bf16[2304,256]{1,0:T(8,128)(2,1)}, u32[]{:S(2)}, u32[]{:S(2)}) collective-permute-start(bf16[2304,256]{1,0:T(8,128)(2,1)S(1)} %get-tuple-element.18.own_mine), channel_id=1, source_target_pairs={{0,64},{1,65},{2,66},{3,67},{4,68},{5,69},{6,70},{7,71},{8,72},{9,... | collective-permute-start | bytes 3538952 | tf_op jit(solution)/shard_map/ppermute | solution.py:170
  23.2 5.1 %collective-permute-start.3 = (bf16[2,4,64,256]{3,2,1,0:T(8,128)(2,1)S(1)}, bf16[2,4,64,256]{3,2,1,0:T(8,128)(2,1)S(1)}, u32[]{:S(2)}, u32[]{:S(2)}) collective-permute-start(bf16[2,4,64,256]{3,2,1,0:T(8,128)(2,1)S(1)} %maximum_select_fusion.mid), channel_id=1, source_target_pairs={{2,0},{3,1},{4,2},{5,3},{6,4},{7,5},{8,6},{9,7},{10,8},{11,9},{12,... | collective-permute-start | bytes 786440 | tf_op jit(solution)/shard_map/ppermute | solution.py:170
  33.2 5.2 %collective-permute-done.2.top = bf16[2,4,64,256]{3,2,1,0:T(8,128)(2,1)S(1)} collective-permute-done((bf16[2,4,64,256]{3,2,1,0:T(8,128)(2,1)S(1)}, bf16[2,4,64,256]{3,2,1,0:T(8,128)(2,1)S(1)}, u32[]{:S(2)}, u32[]{:S(2)}) %collective-permute-start.2) | collective-permute-done | bytes 262176 | tf_op jit(solution)/shard_map/ppermute | solution.py:170
  41.1 2.6 %collective-permute-start.9 = (bf16[576,256]{1,0:T(8,128)(2,1)S(1)}, bf16[576,256]{1,0:T(8,128)(2,1)S(1)}, u32[]{:S(2)}, u32[]{:S(2)}) collective-permute-start(bf16[576,256]{1,0:T(8,128)(2,1)S(1)} %collective-permute-done), channel_id=1, source_target_pairs={{0,14},{1,15},{2,0},{3,1},{4,2},{5,3},{6,4},{7,5},{8,6},{9,7},{10,... | collective-permute-start | bytes 884744 | tf_op jit(solution)/shard_map/ppermute | solution.py:170
  43.7 2.7 %collective-permute-start.8 = (bf16[576,256]{1,0:T(8,128)(2,1)S(1)}, bf16[576,256]{1,0:T(8,128)(2,1)S(1)}, u32[]{:S(2)}, u32[]{:S(2)}) collective-permute-start(bf16[576,256]{1,0:T(8,128)(2,1)S(1)} %collective-permute-done), channel_id=1, source_target_pairs={{0,2},{1,3},{2,4},{3,5},{4,6},{5,7},{6,8},{7,9},{8,10},{9,11},{10,... | collective-permute-start | bytes 884744 | tf_op jit(solution)/shard_map/ppermute | solution.py:170
  46.4 9.9 %collective-permute-done.10 = bf16[576,256]{1,0:T(8,128)(2,1)S(1)} collective-permute-done((bf16[576,256]{1,0:T(8,128)(2,1)S(1)}, bf16[576,256]{1,0:T(8,128)(2,1)S(1)}, u32[]{:S(2)}, u32[]{:S(2)}) %collective-permute-start.10) | collective-permute-done | bytes 294944 | tf_op jit(solution)/shard_map/ppermute | solution.py:170
  56.3 4.2 %collective-permute-done.8 = bf16[576,256]{1,0:T(8,128)(2,1)S(1)} collective-permute-done((bf16[576,256]{1,0:T(8,128)(2,1)S(1)}, bf16[576,256]{1,0:T(8,128)(2,1)S(1)}, u32[]{:S(2)}, u32[]{:S(2)}) %collective-permute-start.8) | collective-permute-done | bytes 294944 | tf_op jit(solution)/shard_map/ppermute | solution.py:170
  61.6 3.7 %collective-permute-start.11 = (bf16[4,576,256]{2,1,0:T(8,128)(2,1)S(1)}, bf16[4,576,256]{2,1,0:T(8,128)(2,1)}, u32[]{:S(2)}, u32[]{:S(2)}) collective-permute-start(bf16[4,576,256]{2,1,0:T(8,128)(2,1)S(1)} %pad_maximum_fusion.far_mine), channel_id=1, source_target_pairs={{0,1},{1,0},{2,3},{3,2},{4,5},{5,4},{6,7},{7,6},{8,9},{9,8},{10,11... | collective-permute-start | bytes 3538952 | tf_op jit(solution)/shard_map/ppermute | solution.py:170
  67.3 2.4 %collective-permute-start.5 = (bf16[2304,256]{1,0:T(8,128)(2,1)}, bf16[2304,256]{1,0:T(8,128)(2,1)}, u32[]{:S(2)}, u32[]{:S(2)}) collective-permute-start(bf16[2304,256]{1,0:T(8,128)(2,1)} %collective-permute-done.4.left_mine), channel_id=1, source_target_pairs={{0,1},{1,0},{2,3},{3,2},{4,5},{5,4},{6,7},{7,6},{8,9},{9,8},{10,11... | collective-permute-start | bytes 3538952 | tf_op jit(solution)/shard_map/ppermute | solution.py:170
  75.4 15.3 %stage.2 = (bf16[2,4,2,2,64,256]{5,4,3,2,1,0:T(8,128)(2,1)S(1)}, bf16[2,4,64,256]{3,2,1,0:T(8,128)(2,1)S(1)}) custom-call(s32[5]{0:T(128)S(1)} %stack.49.meta, bf16[2,4,64,256]{3,2,1,0:T(8,128)(2,1)S(1)} %copy-done.7, bf16[2,4,64,256]{3,2,1,0:T(8,128)(2,1)S(1)} %copy-done.3, bf16[2,4,64,256]{3,2,1,0:T(8,128)(2,1)S(1)} %copy-done.5, ...), custom_call_target="tpu_custom_call" | custom-call | flops 7000000000 | bytes 12000000 | tf_op jit(solution)/shard_map/stage/pallas_call | solution.py:105
  93.0 17.0 %collective-permute-done.12.mid = bf16[2,4,64,256]{3,2,1,0:T(8,128)(2,1)} collective-permute-done((bf16[2,4,64,256]{3,2,1,0:T(8,128)(2,1)S(1)}, bf16[2,4,64,256]{3,2,1,0:T(8,128)(2,1)}, u32[]{:S(2)}, u32[]{:S(2)}) %collective-permute-start.12) | collective-permute-done | bytes 262176 | tf_op jit(solution)/shard_map/ppermute | solution.py:170
  110.0 5.1 %collective-permute-start.14 = (bf16[2,4,64,256]{3,2,1,0:T(8,128)(2,1)}, bf16[2,4,64,256]{3,2,1,0:T(8,128)(2,1)}, u32[]{:S(2)}, u32[]{:S(2)}) collective-permute-start(bf16[2,4,64,256]{3,2,1,0:T(8,128)(2,1)} %collective-permute-done.12.mid), channel_id=1, source_target_pairs={{258,256},{259,257},{260,258},{261,259},{262,260},{263,261},{264,2... | collective-permute-start | bytes 786440 | tf_op jit(solution)/shard_map/ppermute | solution.py:170
  117.0 2.7 %collective-permute-done.14.bot = bf16[2,4,64,256]{3,2,1,0:T(8,128)(2,1)} collective-permute-done((bf16[2,4,64,256]{3,2,1,0:T(8,128)(2,1)}, bf16[2,4,64,256]{3,2,1,0:T(8,128)(2,1)}, u32[]{:S(2)}, u32[]{:S(2)}) %collective-permute-start.14) | collective-permute-done | bytes 262176 | tf_op jit(solution)/shard_map/ppermute | solution.py:170
  119.8 5.9 %collective-permute-done.13.top = bf16[2,4,64,256]{3,2,1,0:T(8,128)(2,1)} collective-permute-done((bf16[2,4,64,256]{3,2,1,0:T(8,128)(2,1)}, bf16[2,4,64,256]{3,2,1,0:T(8,128)(2,1)}, u32[]{:S(2)}, u32[]{:S(2)}) %collective-permute-start.13) | collective-permute-done | bytes 262176 | tf_op jit(solution)/shard_map/ppermute | solution.py:170
  125.7 16.6 %stage.3 = (bf16[2,4,2,2,64,256]{5,4,3,2,1,0:T(8,128)(2,1)S(1)}, bf16[2,4,64,256]{3,2,1,0:T(8,128)(2,1)}) custom-call(s32[5]{0:T(128)S(1)} %stack.49.meta, bf16[2,4,64,256]{3,2,1,0:T(8,128)(2,1)} %collective-permute-done.13.top, bf16[2,4,64,256]{3,2,1,0:T(8,128)(2,1)} %collective-permute-done.12.mid, bf16[2,4,64,256]{3,2,1,0:T(8,128)(2,1)} %collective-permute-done.14.bot, ...), custom_call_target="tpu_custom_call" | custom-call | flops 7000000000 | bytes 12000000 | tf_op jit(solution)/shard_map/stage/pallas_call | solution.py:105
  142.5 4.3 %collective-permute-start.15 = (bf16[4,2,2,64,256]{4,3,2,1,0:T(8,128)(2,1)S(1)}, bf16[4,2,2,64,256]{4,3,2,1,0:T(8,128)(2,1)S(1)}, u32[]{:S(2)}, u32[]{:S(2)}) collective-permute-start(bf16[4,2,2,64,256]{4,3,2,1,0:T(8,128)(2,1)S(1)} %get-tuple-element.25), channel_id=1, source_target_pairs={{0,1},{1,0},{2,3},{3,2},{4,5},{5,4},{6,7},{7,6},{8,9},{9,8},{10,11... | collective-permute-start | bytes 1572872 | tf_op jit(solution)/shard_map/ppermute | solution.py:170
  150.7 2.7 %collective-permute-start.17 = (bf16[2,2,2,64,256]{4,3,2,1,0:T(8,128)(2,1)S(1)}, bf16[2,2,2,64,256]{4,3,2,1,0:T(8,128)(2,1)S(1)}, u32[]{:S(2)}, u32[]{:S(2)}) collective-permute-start(bf16[2,2,2,64,256]{4,3,2,1,0:T(8,128)(2,1)S(1)} %pad_maximum_fusion.2), channel_id=1, source_target_pairs={{0,128},{1,129},{2,130},{3,131},{4,132},{5,133},{6,134},{7,135},{8... | collective-permute-start | bytes 786440 | tf_op jit(solution)/shard_map/ppermute | solution.py:170
  153.5 2.3 %collective-permute-start.18 = (bf16[2,2,2,64,256]{4,3,2,1,0:T(8,128)(2,1)S(1)}, bf16[2,2,2,64,256]{4,3,2,1,0:T(8,128)(2,1)S(1)}, u32[]{:S(2)}, u32[]{:S(2)}) collective-permute-start(bf16[2,2,2,64,256]{4,3,2,1,0:T(8,128)(2,1)S(1)} %pad_maximum_fusion.3), channel_id=1, source_target_pairs={{0,192},{1,193},{2,194},{3,195},{4,196},{5,197},{6,198},{7,199},{8... | collective-permute-start | bytes 786440 | tf_op jit(solution)/shard_map/ppermute | solution.py:170
  157.9 3.5 %collective-permute-done.17.refs_1_ = bf16[2,2,2,64,256]{4,3,2,1,0:T(8,128)(2,1)S(1)} collective-permute-done((bf16[2,2,2,64,256]{4,3,2,1,0:T(8,128)(2,1)S(1)}, bf16[2,2,2,64,256]{4,3,2,1,0:T(8,128)(2,1)S(1)}, u32[]{:S(2)}, u32[]{:S(2)}) %collective-permute-start.17) | collective-permute-done | bytes 262176 | tf_op jit(solution)/shard_map/ppermute | solution.py:170
  161.3 6.6 %collective-permute-done.18.refs_2_ = bf16[2,2,2,64,256]{4,3,2,1,0:T(8,128)(2,1)S(1)} collective-permute-done((bf16[2,2,2,64,256]{4,3,2,1,0:T(8,128)(2,1)S(1)}, bf16[2,2,2,64,256]{4,3,2,1,0:T(8,128)(2,1)S(1)}, u32[]{:S(2)}, u32[]{:S(2)}) %collective-permute-start.18) | collective-permute-done | bytes 262176 | tf_op jit(solution)/shard_map/ppermute | solution.py:170
  (48 shorter events, 31.8 us)
Async XLA Ops:
  1.0 8.5 %collective-permute-start.1 = (bf16[2,2,64,256]{3,2,1,0:T(8,128)(2,1)S(1)}, bf16[2,2,64,256]{3,2,1,0:T(8,128)(2,1)S(1)}, u32[]{:S(2)}, u32[]{:S(2)}) collective-permute-start(bf16[2,2,64,256]{3,2,1,0:T(8,128)(2,1)S(1)} %get-tuple-element.28), channel_id=1, source_target_pairs={{0,1},{1,0},{2,3},{3,2},{4,5},{5,4},{6,7},{7,6},{8,9},{9,8},{10,11... | collective-permute-start | bytes 393224 | tf_op jit(solution)/shard_map/ppermute | solution.py:170
  4.6 12.0 %collective-permute-start = (bf16[576,256]{1,0:T(8,128)(2,1)S(1)}, bf16[576,256]{1,0:T(8,128)(2,1)S(1)}, u32[]{:S(2)}, u32[]{:S(2)}) collective-permute-start(bf16[576,256]{1,0:T(8,128)(2,1)S(1)} %dynamic-slice_bitcast_fusion.2), channel_id=1, source_target_pairs={{0,128},{1,129},{2,130},{3,131},{4,132},{5,133},{6,134},{7,135},{8... | collective-permute-start | bytes 884744 | tf_op jit(solution)/shard_map/ppermute | solution.py:170
  16.6 43.9 %copy-start.8 = (bf16[576,256]{1,0:T(8,128)(2,1)}, bf16[576,256]{1,0:T(8,128)(2,1)S(1)}, u32[]{:S(2)}) copy-start(bf16[576,256]{1,0:T(8,128)(2,1)S(1)} %collective-permute-done) | copy-start | bytes 884740
  16.6 48.7 %collective-permute-start.6 = (bf16[2304,256]{1,0:T(8,128)(2,1)S(1)}, bf16[2304,256]{1,0:T(8,128)(2,1)}, u32[]{:S(2)}, u32[]{:S(2)}) collective-permute-start(bf16[2304,256]{1,0:T(8,128)(2,1)S(1)} %get-tuple-element.18.own_mine), channel_id=1, source_target_pairs={{0,192},{1,193},{2,194},{3,195},{4,196},{5,197},{6,198},{7,199},{8... | collective-permute-start | bytes 3538952 | tf_op jit(solution)/shard_map/ppermute | solution.py:170
  19.1 48.2 %collective-permute-start.4 = (bf16[2304,256]{1,0:T(8,128)(2,1)S(1)}, bf16[2304,256]{1,0:T(8,128)(2,1)}, u32[]{:S(2)}, u32[]{:S(2)}) collective-permute-start(bf16[2304,256]{1,0:T(8,128)(2,1)S(1)} %get-tuple-element.18.own_mine), channel_id=1, source_target_pairs={{0,64},{1,65},{2,66},{3,67},{4,68},{5,69},{6,70},{7,71},{8,72},{9,... | collective-permute-start | bytes 3538952 | tf_op jit(solution)/shard_map/ppermute | solution.py:170
  23.2 9.3 %collective-permute-start.3 = (bf16[2,4,64,256]{3,2,1,0:T(8,128)(2,1)S(1)}, bf16[2,4,64,256]{3,2,1,0:T(8,128)(2,1)S(1)}, u32[]{:S(2)}, u32[]{:S(2)}) collective-permute-start(bf16[2,4,64,256]{3,2,1,0:T(8,128)(2,1)S(1)} %maximum_select_fusion.mid), channel_id=1, source_target_pairs={{2,0},{3,1},{4,2},{5,3},{6,4},{7,5},{8,6},{9,7},{10,8},{11,9},{12,... | collective-permute-start | bytes 786440 | tf_op jit(solution)/shard_map/ppermute | solution.py:170
  28.3 10.2 %collective-permute-start.2 = (bf16[2,4,64,256]{3,2,1,0:T(8,128)(2,1)S(1)}, bf16[2,4,64,256]{3,2,1,0:T(8,128)(2,1)S(1)}, u32[]{:S(2)}, u32[]{:S(2)}) collective-permute-start(bf16[2,4,64,256]{3,2,1,0:T(8,128)(2,1)S(1)} %maximum_select_fusion.mid), channel_id=1, source_target_pairs={{0,2},{1,3},{2,4},{3,5},{4,6},{5,7},{6,8},{7,9},{8,10},{9,11},{10,... | collective-permute-start | bytes 786440 | tf_op jit(solution)/shard_map/ppermute | solution.py:170
  39.2 17.2 %collective-permute-start.10 = (bf16[576,256]{1,0:T(8,128)(2,1)S(1)}, bf16[576,256]{1,0:T(8,128)(2,1)S(1)}, u32[]{:S(2)}, u32[]{:S(2)}) collective-permute-start(bf16[576,256]{1,0:T(8,128)(2,1)S(1)} %collective-permute-done), channel_id=1, source_target_pairs={{0,4},{1,5},{2,6},{3,7},{4,8},{5,9},{6,10},{7,11},{8,12},{9,13},{1... | collective-permute-start | bytes 884744 | tf_op jit(solution)/shard_map/ppermute | solution.py:170
  41.1 15.2 %collective-permute-start.9 = (bf16[576,256]{1,0:T(8,128)(2,1)S(1)}, bf16[576,256]{1,0:T(8,128)(2,1)S(1)}, u32[]{:S(2)}, u32[]{:S(2)}) collective-permute-start(bf16[576,256]{1,0:T(8,128)(2,1)S(1)} %collective-permute-done), channel_id=1, source_target_pairs={{0,14},{1,15},{2,0},{3,1},{4,2},{5,3},{6,4},{7,5},{8,6},{9,7},{10,... | collective-permute-start | bytes 884744 | tf_op jit(solution)/shard_map/ppermute | solution.py:170
  43.7 16.9 %collective-permute-start.8 = (bf16[576,256]{1,0:T(8,128)(2,1)S(1)}, bf16[576,256]{1,0:T(8,128)(2,1)S(1)}, u32[]{:S(2)}, u32[]{:S(2)}) collective-permute-start(bf16[576,256]{1,0:T(8,128)(2,1)S(1)} %collective-permute-done), channel_id=1, source_target_pairs={{0,2},{1,3},{2,4},{3,5},{4,6},{5,7},{6,8},{7,9},{8,10},{9,11},{10,... | collective-permute-start | bytes 884744 | tf_op jit(solution)/shard_map/ppermute | solution.py:170
  61.6 8.2 %collective-permute-start.11 = (bf16[4,576,256]{2,1,0:T(8,128)(2,1)S(1)}, bf16[4,576,256]{2,1,0:T(8,128)(2,1)}, u32[]{:S(2)}, u32[]{:S(2)}) collective-permute-start(bf16[4,576,256]{2,1,0:T(8,128)(2,1)S(1)} %pad_maximum_fusion.far_mine), channel_id=1, source_target_pairs={{0,1},{1,0},{2,3},{3,2},{4,5},{5,4},{6,7},{7,6},{8,9},{9,8},{10,11... | collective-permute-start | bytes 3538952 | tf_op jit(solution)/shard_map/ppermute | solution.py:170
  65.4 5.1 %collective-permute-start.7 = (bf16[2304,256]{1,0:T(8,128)(2,1)}, bf16[2304,256]{1,0:T(8,128)(2,1)}, u32[]{:S(2)}, u32[]{:S(2)}) collective-permute-start(bf16[2304,256]{1,0:T(8,128)(2,1)} %collective-permute-done.6.right_mine), channel_id=1, source_target_pairs={{0,1},{1,0},{2,3},{3,2},{4,5},{5,4},{6,7},{7,6},{8,9},{9,8},{10,11... | collective-permute-start | bytes 3538952 | tf_op jit(solution)/shard_map/ppermute | solution.py:170
  67.3 5.2 %collective-permute-start.5 = (bf16[2304,256]{1,0:T(8,128)(2,1)}, bf16[2304,256]{1,0:T(8,128)(2,1)}, u32[]{:S(2)}, u32[]{:S(2)}) collective-permute-start(bf16[2304,256]{1,0:T(8,128)(2,1)} %collective-permute-done.4.left_mine), channel_id=1, source_target_pairs={{0,1},{1,0},{2,3},{3,2},{4,5},{5,4},{6,7},{7,6},{8,9},{9,8},{10,11... | collective-permute-start | bytes 3538952 | tf_op jit(solution)/shard_map/ppermute | solution.py:170
  72.6 0.9 copy-start.3
  73.5 0.9 copy-start.5
  90.7 1.0 copy-start
  91.7 18.3 %collective-permute-start.12 = (bf16[2,4,64,256]{3,2,1,0:T(8,128)(2,1)S(1)}, bf16[2,4,64,256]{3,2,1,0:T(8,128)(2,1)}, u32[]{:S(2)}, u32[]{:S(2)}) collective-permute-start(bf16[2,4,64,256]{3,2,1,0:T(8,128)(2,1)S(1)} %get-tuple-element.21), channel_id=1, source_target_pairs={{0,256},{1,257},{2,258},{3,259},{4,260},{5,261},{6,262},{7,263},{8... | collective-permute-start | bytes 786440 | tf_op jit(solution)/shard_map/ppermute | solution.py:170
  110.0 9.8 %collective-permute-start.14 = (bf16[2,4,64,256]{3,2,1,0:T(8,128)(2,1)}, bf16[2,4,64,256]{3,2,1,0:T(8,128)(2,1)}, u32[]{:S(2)}, u32[]{:S(2)}) collective-permute-start(bf16[2,4,64,256]{3,2,1,0:T(8,128)(2,1)} %collective-permute-done.12.mid), channel_id=1, source_target_pairs={{258,256},{259,257},{260,258},{261,259},{262,260},{263,261},{264,2... | collective-permute-start | bytes 786440 | tf_op jit(solution)/shard_map/ppermute | solution.py:170
  115.1 10.6 %collective-permute-start.13 = (bf16[2,4,64,256]{3,2,1,0:T(8,128)(2,1)}, bf16[2,4,64,256]{3,2,1,0:T(8,128)(2,1)}, u32[]{:S(2)}, u32[]{:S(2)}) collective-permute-start(bf16[2,4,64,256]{3,2,1,0:T(8,128)(2,1)} %collective-permute-done.12.mid), channel_id=1, source_target_pairs={{256,258},{257,259},{258,260},{259,261},{260,262},{261,263},{262,2... | collective-permute-start | bytes 786440 | tf_op jit(solution)/shard_map/ppermute | solution.py:170
  117.0 25.3 %copy-start.1 = (bf16[2,4,2,2,64,256]{5,4,3,2,1,0:T(8,128)(2,1)S(1)}, bf16[2,4,2,2,64,256]{5,4,3,2,1,0:T(8,128)(2,1)}, u32[]{:S(2)}) copy-start(bf16[2,4,2,2,64,256]{5,4,3,2,1,0:T(8,128)(2,1)} %copy-done) | copy-start | bytes 3145732
  142.5 5.8 %collective-permute-start.15 = (bf16[4,2,2,64,256]{4,3,2,1,0:T(8,128)(2,1)S(1)}, bf16[4,2,2,64,256]{4,3,2,1,0:T(8,128)(2,1)S(1)}, u32[]{:S(2)}, u32[]{:S(2)}) collective-permute-start(bf16[4,2,2,64,256]{4,3,2,1,0:T(8,128)(2,1)S(1)} %get-tuple-element.25), channel_id=1, source_target_pairs={{0,1},{1,0},{2,3},{3,2},{4,5},{5,4},{6,7},{7,6},{8,9},{9,8},{10,11... | collective-permute-start | bytes 1572872 | tf_op jit(solution)/shard_map/ppermute | solution.py:170
  148.4 9.4 %collective-permute-start.16 = (bf16[2,2,2,64,256]{4,3,2,1,0:T(8,128)(2,1)S(1)}, bf16[2,2,2,64,256]{4,3,2,1,0:T(8,128)(2,1)S(1)}, u32[]{:S(2)}, u32[]{:S(2)}) collective-permute-start(bf16[2,2,2,64,256]{4,3,2,1,0:T(8,128)(2,1)S(1)} %pad_maximum_fusion.1), channel_id=1, source_target_pairs={{0,64},{1,65},{2,66},{3,67},{4,68},{5,69},{6,70},{7,71},{8,72},{9,... | collective-permute-start | bytes 786440 | tf_op jit(solution)/shard_map/ppermute | solution.py:170
  150.7 10.6 %collective-permute-start.17 = (bf16[2,2,2,64,256]{4,3,2,1,0:T(8,128)(2,1)S(1)}, bf16[2,2,2,64,256]{4,3,2,1,0:T(8,128)(2,1)S(1)}, u32[]{:S(2)}, u32[]{:S(2)}) collective-permute-start(bf16[2,2,2,64,256]{4,3,2,1,0:T(8,128)(2,1)S(1)} %pad_maximum_fusion.2), channel_id=1, source_target_pairs={{0,128},{1,129},{2,130},{3,131},{4,132},{5,133},{6,134},{7,135},{8... | collective-permute-start | bytes 786440 | tf_op jit(solution)/shard_map/ppermute | solution.py:170
  153.5 14.5 %collective-permute-start.18 = (bf16[2,2,2,64,256]{4,3,2,1,0:T(8,128)(2,1)S(1)}, bf16[2,2,2,64,256]{4,3,2,1,0:T(8,128)(2,1)S(1)}, u32[]{:S(2)}, u32[]{:S(2)}) collective-permute-start(bf16[2,2,2,64,256]{4,3,2,1,0:T(8,128)(2,1)S(1)} %pad_maximum_fusion.3), channel_id=1, source_target_pairs={{0,192},{1,193},{2,194},{3,195},{4,196},{5,197},{6,198},{7,199},{8... | collective-permute-start | bytes 786440 | tf_op jit(solution)/shard_map/ppermute | solution.py:170
  (4 other events, 3.1 us)

commit v3 on v2

v3 whole, which is shorter than its diff:
```python
import functools

import jax
import jax.numpy as jnp
from jax import lax
from jax.experimental import pallas as pl
from jax.experimental.pallas import tpu as pltpu
from jax.sharding import PartitionSpec as P

DEPTH = 4
SPLIT = 4


def frame_kernel(frame, meta, top, mid, bot, *refs):
    first = frame == 0
    refs = list(refs)
    pieces = refs[:8]
    older = refs[8]
    kept, last = (refs[9], refs[10]) if not first else (refs[8], refs[9])
    older = refs[8] if not first else refs[10]
    weights, cells, wide, sems = refs[11:]
    x, core, chip, piece, chips = meta[0], meta[1], meta[2], meta[3], meta[4]
    depth, _, taps, chans = weights.shape
    _, slab, width, _ = mid.shape
    rows = 3 * slab
    other = 1 - core
    used = (0, 1) if first else (1,)

    def fetch(layer, mine, theirs, places):
        for half in used:
            for source, owner in ((mine, core), (theirs, other)):
                @pl.when(owner == half)
                def _():
                    for at, block in places(source):
                        pltpu.make_async_copy(block, weights.at[layer, half, at], sems.at[layer]).start()

    def whole(source):
        return [(slice(None), source)]

    def quarters(source):
        part = taps // 4
        return [(pl.ds(pl.multiple_of(lax.rem(piece + shift, 4) * part, part), part), source.at[place])
                for place, shift in enumerate((0, 3, 1, 2))]

    for layer in range(depth):
        step = lax.rem(layer - x + depth, depth)
        for distance, at in ((0, 0), (1, 4), (3, 2), (2, 6)):
            @pl.when(step == distance)
            def _():
                fetch(layer, pieces[at], pieces[at + 1], quarters if distance == 2 else whole)

    column = lax.broadcasted_iota(jnp.int32, (width, chans), 0)

    def spread(row, stored, buffer):
        values = stored.astype(jnp.float32)
        place = chip * slab - slab + row
        inside = jnp.logical_and(place >= 0, place < chips * slab)
        scale = lax.rsqrt(jnp.mean(values * values, axis=-1, keepdims=True) + 1e-06)
        normed = values * jnp.where(inside, scale, 0.0)
        before = jnp.where(column == 0, 0.0, pltpu.roll(normed, 1, 0))
        after = jnp.where(column == width - 1, 0.0, pltpu.roll(normed, width - 1, 0))
        wide[buffer, row, :, 0:chans] = before.astype(jnp.bfloat16)
        wide[buffer, row, :, chans:2 * chans] = normed.astype(jnp.bfloat16)
        wide[buffer, row, :, 2 * chans:] = after.astype(jnp.bfloat16)

    index = min(frame, mid.shape[0] - 1)
    for row in range(rows):
        stored = (top, mid, bot)[row // slab][index, row % slab]
        cells[row] = stored
        spread(row, stored, 0)

    base = 0
    for layer in range(depth):
        now = layer % 2
        count = rows - 2 * layer - 2
        waited = weights.at[layer] if first else weights.at[layer, 1]
        pltpu.make_async_copy(waited, waited, sems.at[layer]).wait()
        edges = [0, count] if count <= SPLIT else [0, count // 2, count]
        for low, high in zip(edges[:-1], edges[1:]):
            size = high - low
            start = layer + 1 + low
            total = earlier = None
            for tap in range(3):
                at = pl.ds(tap * 3 * chans, 3 * chans)
                block = wide[now, start - 1 + tap:start - 1 + tap + size].reshape(size * width, 3 * chans)
                here = jnp.dot(block, weights[layer, 1, at], preferred_element_type=jnp.float32)
                total = here if total is None else total + here
                if first:
                    there = jnp.dot(block, weights[layer, 0, at], preferred_element_type=jnp.float32)
                    earlier = there if earlier is None else earlier + there
            if first:
                older[base + low:base + high] = earlier.reshape(size, width, chans)
            for row in range(size):
                conv = total[row * width:(row + 1) * width]
                if not first:
                    conv = conv + older[base + low + row]
                place = start + row
                values = cells[place].astype(jnp.float32)
                stored = (values + conv / (1.0 + jnp.exp(-conv))).astype(jnp.bfloat16)
                cells[place] = stored
                if layer < depth - 1:
                    spread(place, stored, 1 - now)
                inner = place - slab
                if 0 <= inner < slab:
                    kept[core if inner < slab // 2 else other, layer, inner % (slab // 2)] = stored
                    if layer == depth - 1:
                        last[0, inner] = stored
        base += count


def run_frame(frame, meta, top, mid, bot, kernels, older=None):
    _, slab, width, chans = mid.shape
    taps = kernels[0].shape[0]
    vmem = pl.BlockSpec(memory_space=pltpu.VMEM)
    hbm = pl.BlockSpec(memory_space=pl.ANY)
    bf16 = jnp.bfloat16
    sums = DEPTH * (3 * slab - DEPTH - 1)
    out = [
        jax.ShapeDtypeStruct((2, DEPTH, slab // 2, width, chans), bf16),
        jax.ShapeDtypeStruct((1, slab, width, chans), bf16),
    ]
    extra = []
    if frame == 0:
        out.append(jax.ShapeDtypeStruct((sums, width, chans), jnp.float32))
    else:
        extra.append(older)
    work = 2 * sums * width * 9 * chans * chans * (2 - frame)
    return pl.pallas_call(
        functools.partial(frame_kernel, frame),
        out_shape=tuple(out),
        in_specs=[pl.BlockSpec(memory_space=pltpu.SMEM)] + [vmem] * 3 + [hbm] * len(kernels) + [vmem] * len(extra),
        out_specs=(vmem,) * len(out),
        scratch_shapes=[
            pltpu.VMEM((DEPTH, 2, taps, chans), bf16),
            pltpu.VMEM((3 * slab, width, chans), bf16),
            pltpu.VMEM((2, 3 * slab, width, 3 * chans), bf16),
            pltpu.SemaphoreType.DMA((DEPTH,)),
        ],
        compiler_params=pltpu.CompilerParams(vmem_limit_bytes=36 * 1024 * 1024),
        cost_estimate=pl.CostEstimate(flops=work, bytes_accessed=8 * 10**6, transcendentals=10**6),
        name="frame%d" % frame,
    )(meta, top, mid, bot, *kernels, *extra)


def place_kernel(meta, home, away, *refs):
    arrived, out = refs[:-1], refs[-1]
    x, core = meta[0], meta[1]
    out[2 * x + core] = home[...]
    out[2 * x + 1 - core] = away[...]
    for shift, pair in enumerate(arrived, 1):
        group = lax.rem(x - shift + 4, 4)
        out[2 * group + core] = pair[0]
        out[2 * group + 1 - core] = pair[1]


def place(meta, home, away, arrived):
    vmem = pl.BlockSpec(memory_space=pltpu.VMEM)
    return pl.pallas_call(
        place_kernel,
        out_shape=jax.ShapeDtypeStruct((8,) + home.shape, jnp.bfloat16),
        in_specs=[pl.BlockSpec(memory_space=pltpu.SMEM)] + [vmem] * (2 + len(arrived)),
        out_specs=vmem,
        compiler_params=pltpu.CompilerParams(vmem_limit_bytes=8 * 1024 * 1024),
        name="place",
    )(meta, home, away, *arrived)


def route(move, keep=lambda zh, x, zl, y, c: True):
    pairs = []
    for zh in range(2):
        for x in range(4):
            for zl in range(4):
                for y in range(8):
                    for c in range(2):
                        here = (zh, x, zl, y, c)
                        there = move(*here)
                        if there is not None and keep(*here):
                            pairs.append(tuple((((d[0] * 4 + d[1]) * 4 + d[2]) * 8 + d[3]) * 2 + d[4] for d in (here, there)))
    return pairs


def next_chip(step):
    def move(zh, x, zl, y, c):
        chip = zl * 8 + y + step
        return (zh, x, chip // 8, chip % 8, c) if 0 <= chip < 32 else None
    return move


def send(array, move, keep=lambda *here: True):
    return lax.ppermute(array, ("section", "rows"), route(move, keep))


def along_x(step):
    return lambda zh, x, zl, y, c: (zh, (x + step) % 4, zl, y, c)


def along_y(step):
    return lambda zh, x, zl, y, c: (zh, x, zl, (y + step) % 8, c)


def two_along_y(zh, x, zl, y, c):
    return (zh, x, zl, (y + (2 if y % 2 == 0 else -2)) % 8, c)


def hop(zh, x, zl, y, c):
    return (1, x, zl, y, c) if zh == 0 else None


def is_upper(zh, x, zl, y, c):
    return zh == 1


def sibling(zh, x, zl, y, c):
    return (zh, x, zl, y, 1 - c)


def local(frames_in, layer_weights):
    section, row = lax.axis_index("section"), lax.axis_index("rows")
    x, upper = section % 4, section // 4
    core, chip = row % 2, row // 2
    piece = chip % 4
    meta = jnp.stack([x, core, chip, piece, jnp.int32(32)]).astype(jnp.int32)
    chans = frames_in.shape[-1]

    own = layer_weights.reshape(2, 9 * chans, chans)
    part = own.shape[1] // 4
    quarter = lax.dynamic_slice(own, (core, piece * part, 0), (1, part, chans))[0]
    far = send(quarter, along_x(2))

    give = lax.dynamic_index_in_dim(frames_in, 2 * x + 1 - core, 0, keepdims=False)
    keep = lax.dynamic_index_in_dim(frames_in, 2 * x + core, 0, keepdims=False)
    got = send(give, sibling)
    mine = lax.dynamic_index_in_dim(own, core, 0, keepdims=False)
    theirs = lax.dynamic_index_in_dim(own, 1 - core, 0, keepdims=False)
    far, mine, got = lax.optimization_barrier((far, mine, got))
    left_mine = send(mine, along_x(1))
    right_mine = send(mine, along_x(-1))
    mid = jnp.where(core == 0, jnp.concatenate([keep, got], 1), jnp.concatenate([got, keep], 1))
    top = send(mid, next_chip(1))
    bot = send(mid, next_chip(-1))

    parts = (far, send(far, along_y(1)), send(far, along_y(-1)), send(far, two_along_y))
    *parts, top, bot = lax.optimization_barrier((*parts, top, bot))
    far_mine = jnp.stack(parts)
    far_theirs = send(far_mine, sibling)
    left_theirs = send(left_mine, sibling)
    right_theirs = send(right_mine, sibling)
    kernels = (mine, theirs, left_mine, left_theirs, right_mine, right_theirs, far_mine, far_theirs)

    kept, reached, older = run_frame(0, meta, top, mid, bot, kernels)
    mid_0 = send(reached, hop)
    first = [kept]
    kept, reached = run_frame(1, meta, top, mid, bot, kernels, older)
    first.append(kept)
    mid_1 = send(reached, hop)

    second = []
    top, bot = send(mid_0, next_chip(1), is_upper), send(mid_0, next_chip(-1), is_upper)
    kept, _, older = run_frame(0, meta, top, mid_0, bot, kernels)
    second.append(kept)
    top, bot = send(mid_1, next_chip(1), is_upper), send(mid_1, next_chip(-1), is_upper)
    kept, _ = run_frame(1, meta, top, mid_1, bot, kernels, older)
    second.append(kept)

    first, second = jnp.stack(first, 2), jnp.stack(second, 2)
    done = jnp.where(upper == 0, first, second)
    both = (done[0], send(done[1], sibling))
    home, away = [lax.dynamic_index_in_dim(one, x, 0, keepdims=False) for one in both]
    arrived = []
    for step in (1, 2, 3):
        layer = (x + step) % 4
        pair = jnp.stack([lax.dynamic_index_in_dim(one, layer, 0, keepdims=False) for one in both])
        arrived.append(send(pair, along_x(step)))
    return place(meta, home, away, arrived)[None]


def solution(mesh):
    placed = (P(None, None, "rows", None, None), P("section", None, None, None, None, None))
    return jax.shard_map(
        local,
        mesh=mesh,
        in_specs=placed,
        out_specs=P("section", None, None, "rows", None, None),
        check_vma=False,
    )
```

time: 170 us -> 151 us (0.89)
  the two profiles are of different devices: /device:TPU:391 before, /device:TPU:327 now
where the time goes in v3:
time: 151 us; the launch traced here: 150 us
  starting transfers between devices  68.1 us (45%)
  waiting for transfers between devices  38.2 us (25%)
  Pallas kernels  31.9 us (21%)
  local copies, waits for them, and re-layouts  9.79 us (6%)
    ppermute x22, starting transfers between devices, send(): return lax.ppermute(array, ('section', 'rows'), route(move, keep))  68.1 us
    ppermute x22, waiting for transfers between devices, send(): return lax.ppermute(array, ('section', 'rows'), route(move, keep))  38.2 us
    pallas_call x4, Pallas kernels, run_frame(): pl.pallas_call(functools.partial(frame_kernel, frame), out_shape=tuple(ou...  30.3 us
    unnamed x22, local copies, waits for them, and re-layouts  5.79 us
  transfers between devices with their start and end apart: 22, of which 12 were waited for; matrix products, arithmetic and copies ran while one was open for 3% of the time, Pallas kernels for 10%

profile of v3, /device:TPU:327, one launch (start us, length us, event | category | flops | bytes accessed | tf_op | source)
XLA Modules:
  0.0 150.0 jit_solution(11852773451106530110)
XLA Ops:
  1.0 2.6 %collective-permute-start.1 = (bf16[2,2,64,256]{3,2,1,0:T(8,128)(2,1)S(1)}, bf16[2,2,64,256]{3,2,1,0:T(8,128)(2,1)S(1)}, u32[]{:S(2)}, u32[]{:S(2)}) collective-permute-start(bf16[2,2,64,256]{3,2,1,0:T(8,128)(2,1)S(1)} %get-tuple-element.44), channel_id=1, source_target_pairs={{0,1},{1,0},{2,3},{3,2},{4,5},{5,4},{6,7},{7,6},{8,9},{9,8},{10,11... | collective-permute-start | bytes 393224 | tf_op jit(solution)/shard_map/ppermute | solution.py:190
  4.6 3.0 %collective-permute-start = (bf16[576,256]{1,0:T(8,128)(2,1)S(1)}, bf16[576,256]{1,0:T(8,128)(2,1)S(1)}, u32[]{:S(2)}, u32[]{:S(2)}) collective-permute-start(bf16[576,256]{1,0:T(8,128)(2,1)S(1)} %dynamic-slice_bitcast_fusion.2), channel_id=1, source_target_pairs={{0,128},{1,129},{2,130},{3,131},{4,132},{5,133},{6,134},{7,135},{8... | collective-permute-start | bytes 884744 | tf_op jit(solution)/shard_map/ppermute | solution.py:190
  9.5 7.2 %collective-permute-done = bf16[576,256]{1,0:T(8,128)(2,1)S(1)} collective-permute-done((bf16[576,256]{1,0:T(8,128)(2,1)S(1)}, bf16[576,256]{1,0:T(8,128)(2,1)S(1)}, u32[]{:S(2)}, u32[]{:S(2)}) %collective-permute-start) | collective-permute-done | bytes 294944 | tf_op jit(solution)/shard_map/ppermute | solution.py:190
  16.6 2.4 %collective-permute-start.9 = (bf16[2304,256]{1,0:T(8,128)(2,1)S(1)}, bf16[2304,256]{1,0:T(8,128)(2,1)}, u32[]{:S(2)}, u32[]{:S(2)}) collective-permute-start(bf16[2304,256]{1,0:T(8,128)(2,1)S(1)} %get-tuple-element.26.refs_0_), channel_id=1, source_target_pairs={{0,192},{1,193},{2,194},{3,195},{4,196},{5,197},{6,198},{7,199},{8... | collective-permute-start | bytes 3538952 | tf_op jit(solution)/shard_map/ppermute | solution.py:190
  19.1 4.0 %collective-permute-start.7 = (bf16[2304,256]{1,0:T(8,128)(2,1)S(1)}, bf16[2304,256]{1,0:T(8,128)(2,1)}, u32[]{:S(2)}, u32[]{:S(2)}) collective-permute-start(bf16[2304,256]{1,0:T(8,128)(2,1)S(1)} %get-tuple-element.26.refs_0_), channel_id=1, source_target_pairs={{0,64},{1,65},{2,66},{3,67},{4,68},{5,69},{6,70},{7,71},{8,72},{9,... | collective-permute-start | bytes 3538952 | tf_op jit(solution)/shard_map/ppermute | solution.py:190
  23.2 5.1 %collective-permute-start.6 = (bf16[2,4,64,256]{3,2,1,0:T(8,128)(2,1)S(1)}, bf16[2,4,64,256]{3,2,1,0:T(8,128)(2,1)S(1)}, u32[]{:S(2)}, u32[]{:S(2)}) collective-permute-start(bf16[2,4,64,256]{3,2,1,0:T(8,128)(2,1)S(1)} %maximum_select_fusion.1.mid), channel_id=1, source_target_pairs={{2,0},{3,1},{4,2},{5,3},{6,4},{7,5},{8,6},{9,7},{10,8},{11,9},{12,... | collective-permute-start | bytes 786440 | tf_op jit(solution)/shard_map/ppermute | solution.py:190
  30.9 2.5 %collective-permute-start.4 = (bf16[576,256]{1,0:T(8,128)(2,1)S(1)}, bf16[576,256]{1,0:T(8,128)(2,1)S(1)}, u32[]{:S(2)}, u32[]{:S(2)}) collective-permute-start(bf16[576,256]{1,0:T(8,128)(2,1)S(1)} %collective-permute-done), channel_id=1, source_target_pairs={{0,4},{1,5},{2,14},{3,15},{4,8},{5,9},{6,2},{7,3},{8,12},{9,13},{1... | collective-permute-start | bytes 884744 | tf_op jit(solution)/shard_map/ppermute | solution.py:190
  34.2 5.3 %collective-permute-start.3 = (bf16[576,256]{1,0:T(8,128)(2,1)S(1)}, bf16[576,256]{1,0:T(8,128)(2,1)S(1)}, u32[]{:S(2)}, u32[]{:S(2)}) collective-permute-start(bf16[576,256]{1,0:T(8,128)(2,1)S(1)} %collective-permute-done), channel_id=1, source_target_pairs={{0,14},{1,15},{2,0},{3,1},{4,2},{5,3},{6,4},{7,5},{8,6},{9,7},{10,... | collective-permute-start | bytes 884744 | tf_op jit(solution)/shard_map/ppermute | solution.py:190
  40.5 2.4 %collective-permute-start.2 = (bf16[576,256]{1,0:T(8,128)(2,1)S(1)}, bf16[576,256]{1,0:T(8,128)(2,1)S(1)}, u32[]{:S(2)}, u32[]{:S(2)}) collective-permute-start(bf16[576,256]{1,0:T(8,128)(2,1)S(1)} %collective-permute-done), channel_id=1, source_target_pairs={{0,2},{1,3},{2,4},{3,5},{4,6},{5,7},{6,8},{7,9},{8,10},{9,11},{10,... | collective-permute-start | bytes 884744 | tf_op jit(solution)/shard_map/ppermute | solution.py:190
  44.1 5.8 %collective-permute-done.3 = bf16[576,256]{1,0:T(8,128)(2,1)S(1)} collective-permute-done((bf16[576,256]{1,0:T(8,128)(2,1)S(1)}, bf16[576,256]{1,0:T(8,128)(2,1)S(1)}, u32[]{:S(2)}, u32[]{:S(2)}) %collective-permute-start.3) | collective-permute-done | bytes 294944 | tf_op jit(solution)/shard_map/ppermute | solution.py:190
  51.0 10.6 %collective-permute-start.11 = (bf16[4,576,256]{2,1,0:T(8,128)(2,1)S(1)}, bf16[4,576,256]{2,1,0:T(8,128)(2,1)}, u32[]{:S(2)}, u32[]{:S(2)}) collective-permute-start(bf16[4,576,256]{2,1,0:T(8,128)(2,1)S(1)} %pad_maximum_fusion.refs_6_), channel_id=1, source_target_pairs={{0,1},{1,0},{2,3},{3,2},{4,5},{5,4},{6,7},{7,6},{8,9},{9,8},{10,11... | collective-permute-start | bytes 3538952 | tf_op jit(solution)/shard_map/ppermute | solution.py:190
  63.5 2.4 %collective-permute-start.8 = (bf16[2304,256]{1,0:T(8,128)(2,1)}, bf16[2304,256]{1,0:T(8,128)(2,1)}, u32[]{:S(2)}, u32[]{:S(2)}) collective-permute-start(bf16[2304,256]{1,0:T(8,128)(2,1)} %collective-permute-done.7.refs_2_), channel_id=1, source_target_pairs={{0,1},{1,0},{2,3},{3,2},{4,5},{5,4},{6,7},{7,6},{8,9},{9,8},{10,11... | collective-permute-start | bytes 3538952 | tf_op jit(solution)/shard_map/ppermute | solution.py:190
  71.6 7.7 %frame0.2 = (bf16[2,4,2,64,256]{4,3,2,1,0:T(8,128)(2,1)S(1)}, bf16[1,4,64,256]{3,2,1,0:T(8,128)(2,1)S(1)}, f32[28,64,256]{2,1,0:T(8,128)S(1)}) custom-call(s32[5]{0:T(128)S(1)} %stack.67.meta, bf16[2,4,64,256]{3,2,1,0:T(8,128)(2,1)S(1)} %copy-done.9, bf16[2,4,64,256]{3,2,1,0:T(8,128)(2,1)S(1)} %copy-done.1, bf16[2,4,64,256]{3,2,1,0:T(8,128)(2,1)S(1)} %copy-done.7, ...), custom_call_target="tpu_custom_call" | custom-call | flops 4227858432 | bytes 8000000 | tf_op jit(solution)/shard_map/frame0/pallas_call | solution.py:128
  80.6 6.7 %frame1.2 = (bf16[2,4,2,64,256]{4,3,2,1,0:T(8,128)(2,1)S(1)}, bf16[1,4,64,256]{3,2,1,0:T(8,128)(2,1)}) custom-call(s32[5]{0:T(128)S(1)} %stack.67.meta, bf16[2,4,64,256]{3,2,1,0:T(8,128)(2,1)S(1)} %copy-done.9, bf16[2,4,64,256]{3,2,1,0:T(8,128)(2,1)S(1)} %copy-done.1, bf16[2,4,64,256]{3,2,1,0:T(8,128)(2,1)S(1)} %copy-done.7, ...), custom_call_target="tpu_custom_call" | custom-call | flops 2113929216 | bytes 8000000 | tf_op jit(solution)/shard_map/frame1/pallas_call | solution.py:128
  89.3 3.4 %collective-permute-done.12.mid = bf16[1,4,64,256]{3,2,1,0:T(8,128)(2,1)} collective-permute-done((bf16[1,4,64,256]{3,2,1,0:T(8,128)(2,1)S(1)}, bf16[1,4,64,256]{3,2,1,0:T(8,128)(2,1)}, u32[]{:S(2)}, u32[]{:S(2)}) %collective-permute-start.12) | collective-permute-done | bytes 131104 | tf_op jit(solution)/shard_map/ppermute | solution.py:190
  94.6 3.4 %collective-permute-start.13 = (bf16[1,4,64,256]{3,2,1,0:T(8,128)(2,1)}, bf16[1,4,64,256]{3,2,1,0:T(8,128)(2,1)}, u32[]{:S(2)}, u32[]{:S(2)}) collective-permute-start(bf16[1,4,64,256]{3,2,1,0:T(8,128)(2,1)} %collective-permute-done.12.mid), channel_id=1, source_target_pairs={{256,258},{257,259},{258,260},{259,261},{260,262},{261,263},{262,2... | collective-permute-start | bytes 393224 | tf_op jit(solution)/shard_map/ppermute | solution.py:190
  98.0 4.3 %collective-permute-done.15.mid = bf16[1,4,64,256]{3,2,1,0:T(8,128)(2,1)} collective-permute-done((bf16[1,4,64,256]{3,2,1,0:T(8,128)(2,1)}, bf16[1,4,64,256]{3,2,1,0:T(8,128)(2,1)}, u32[]{:S(2)}, u32[]{:S(2)}) %collective-permute-start.15) | collective-permute-done | bytes 131104 | tf_op jit(solution)/shard_map/ppermute | solution.py:190
  104.2 3.4 %collective-permute-start.16 = (bf16[1,4,64,256]{3,2,1,0:T(8,128)(2,1)}, bf16[1,4,64,256]{3,2,1,0:T(8,128)(2,1)S(1)}, u32[]{:S(2)}, u32[]{:S(2)}) collective-permute-start(bf16[1,4,64,256]{3,2,1,0:T(8,128)(2,1)} %collective-permute-done.15.mid), channel_id=1, source_target_pairs={{256,258},{257,259},{258,260},{259,261},{260,262},{261,263},{262,2... | collective-permute-start | bytes 393224 | tf_op jit(solution)/shard_map/ppermute | solution.py:190
  107.6 8.9 %frame0.3 = (bf16[2,4,2,64,256]{4,3,2,1,0:T(8,128)(2,1)S(1)}, bf16[1,4,64,256]{3,2,1,0:T(8,128)(2,1)}, f32[28,64,256]{2,1,0:T(8,128)S(1)}) custom-call(s32[5]{0:T(128)S(1)} %stack.67.meta, bf16[1,4,64,256]{3,2,1,0:T(8,128)(2,1)} %collective-permute-done.13.top, bf16[1,4,64,256]{3,2,1,0:T(8,128)(2,1)} %collective-permute-done.12.mid, ...), custom_call_target="tpu_custom_call" | custom-call | flops 4227858432 | bytes 8000000 | tf_op jit(solution)/shard_map/frame0/pallas_call | solution.py:128
  116.5 7.1 %frame1.3 = (bf16[2,4,2,64,256]{4,3,2,1,0:T(8,128)(2,1)S(1)}, bf16[1,4,64,256]{3,2,1,0:T(8,128)(2,1)}) custom-call(s32[5]{0:T(128)S(1)} %stack.67.meta, bf16[1,4,64,256]{3,2,1,0:T(8,128)(2,1)S(1)} %collective-permute-done.16.top, bf16[1,4,64,256]{3,2,1,0:T(8,128)(2,1)} %collective-permute-done.15.mid, ...), custom_call_target="tpu_custom_call" | custom-call | flops 2113929216 | bytes 8000000 | tf_op jit(solution)/shard_map/frame1/pallas_call | solution.py:128
  123.9 3.7 %collective-permute-start.18 = (bf16[4,2,2,64,256]{4,3,2,1,0:T(8,128)(2,1)S(1)}, bf16[4,2,2,64,256]{4,3,2,1,0:T(8,128)(2,1)S(1)}, u32[]{:S(2)}, u32[]{:S(2)}) collective-permute-start(bf16[4,2,2,64,256]{4,3,2,1,0:T(8,128)(2,1)S(1)} %get-tuple-element.41), channel_id=1, source_target_pairs={{0,1},{1,0},{2,3},{3,2},{4,5},{5,4},{6,7},{7,6},{8,9},{9,8},{10,11... | collective-permute-start | bytes 1572872 | tf_op jit(solution)/shard_map/ppermute | solution.py:190
  133.4 3.1 %collective-permute-start.21 = (bf16[2,2,2,64,256]{4,3,2,1,0:T(8,128)(2,1)S(1)}, bf16[2,2,2,64,256]{4,3,2,1,0:T(8,128)(2,1)S(1)}, u32[]{:S(2)}, u32[]{:S(2)}) collective-permute-start(bf16[2,2,2,64,256]{4,3,2,1,0:T(8,128)(2,1)S(1)} %pad_maximum_fusion.3), channel_id=1, source_target_pairs={{0,192},{1,193},{2,194},{3,195},{4,196},{5,197},{6,198},{7,199},{8... | collective-permute-start | bytes 786440 | tf_op jit(solution)/shard_map/ppermute | solution.py:190
  138.6 3.5 %collective-permute-done.20.refs_1_ = bf16[2,2,2,64,256]{4,3,2,1,0:T(8,128)(2,1)S(1)} collective-permute-done((bf16[2,2,2,64,256]{4,3,2,1,0:T(8,128)(2,1)S(1)}, bf16[2,2,2,64,256]{4,3,2,1,0:T(8,128)(2,1)S(1)}, u32[]{:S(2)}, u32[]{:S(2)}) %collective-permute-start.20) | collective-permute-done | bytes 262176 | tf_op jit(solution)/shard_map/ppermute | solution.py:190
  142.1 6.3 %collective-permute-done.21.refs_2_ = bf16[2,2,2,64,256]{4,3,2,1,0:T(8,128)(2,1)S(1)} collective-permute-done((bf16[2,2,2,64,256]{4,3,2,1,0:T(8,128)(2,1)S(1)}, bf16[2,2,2,64,256]{4,3,2,1,0:T(8,128)(2,1)S(1)}, u32[]{:S(2)}, u32[]{:S(2)}) %collective-permute-start.21) | collective-permute-done | bytes 262176 | tf_op jit(solution)/shard_map/ppermute | solution.py:190
  (60 shorter events, 34.8 us)
Async XLA Ops:
  1.0 8.5 %collective-permute-start.1 = (bf16[2,2,64,256]{3,2,1,0:T(8,128)(2,1)S(1)}, bf16[2,2,64,256]{3,2,1,0:T(8,128)(2,1)S(1)}, u32[]{:S(2)}, u32[]{:S(2)}) collective-permute-start(bf16[2,2,64,256]{3,2,1,0:T(8,128)(2,1)S(1)} %get-tuple-element.44), channel_id=1, source_target_pairs={{0,1},{1,0},{2,3},{3,2},{4,5},{5,4},{6,7},{7,6},{8,9},{9,8},{10,11... | collective-permute-start | bytes 393224 | tf_op jit(solution)/shard_map/ppermute | solution.py:190
  4.6 12.0 %collective-permute-start = (bf16[576,256]{1,0:T(8,128)(2,1)S(1)}, bf16[576,256]{1,0:T(8,128)(2,1)S(1)}, u32[]{:S(2)}, u32[]{:S(2)}) collective-permute-start(bf16[576,256]{1,0:T(8,128)(2,1)S(1)} %dynamic-slice_bitcast_fusion.2), channel_id=1, source_target_pairs={{0,128},{1,129},{2,130},{3,131},{4,132},{5,133},{6,134},{7,135},{8... | collective-permute-start | bytes 884744 | tf_op jit(solution)/shard_map/ppermute | solution.py:190
  16.6 33.2 %copy-start.10 = (bf16[576,256]{1,0:T(8,128)(2,1)}, bf16[576,256]{1,0:T(8,128)(2,1)S(1)}, u32[]{:S(2)}) copy-start(bf16[576,256]{1,0:T(8,128)(2,1)S(1)} %collective-permute-done) | copy-start | bytes 884740
  16.6 44.9 %collective-permute-start.9 = (bf16[2304,256]{1,0:T(8,128)(2,1)S(1)}, bf16[2304,256]{1,0:T(8,128)(2,1)}, u32[]{:S(2)}, u32[]{:S(2)}) collective-permute-start(bf16[2304,256]{1,0:T(8,128)(2,1)S(1)} %get-tuple-element.26.refs_0_), channel_id=1, source_target_pairs={{0,192},{1,193},{2,194},{3,195},{4,196},{5,197},{6,198},{7,199},{8... | collective-permute-start | bytes 3538952 | tf_op jit(solution)/shard_map/ppermute | solution.py:190
  19.1 44.4 %collective-permute-start.7 = (bf16[2304,256]{1,0:T(8,128)(2,1)S(1)}, bf16[2304,256]{1,0:T(8,128)(2,1)}, u32[]{:S(2)}, u32[]{:S(2)}) collective-permute-start(bf16[2304,256]{1,0:T(8,128)(2,1)S(1)} %get-tuple-element.26.refs_0_), channel_id=1, source_target_pairs={{0,64},{1,65},{2,66},{3,67},{4,68},{5,69},{6,70},{7,71},{8,72},{9,... | collective-permute-start | bytes 3538952 | tf_op jit(solution)/shard_map/ppermute | solution.py:190
  23.2 10.2 %collective-permute-start.6 = (bf16[2,4,64,256]{3,2,1,0:T(8,128)(2,1)S(1)}, bf16[2,4,64,256]{3,2,1,0:T(8,128)(2,1)S(1)}, u32[]{:S(2)}, u32[]{:S(2)}) collective-permute-start(bf16[2,4,64,256]{3,2,1,0:T(8,128)(2,1)S(1)} %maximum_select_fusion.1.mid), channel_id=1, source_target_pairs={{2,0},{3,1},{4,2},{5,3},{6,4},{7,5},{8,6},{9,7},{10,8},{11,9},{12,... | collective-permute-start | bytes 786440 | tf_op jit(solution)/shard_map/ppermute | solution.py:190
  28.3 11.5 %collective-permute-start.5 = (bf16[2,4,64,256]{3,2,1,0:T(8,128)(2,1)S(1)}, bf16[2,4,64,256]{3,2,1,0:T(8,128)(2,1)S(1)}, u32[]{:S(2)}, u32[]{:S(2)}) collective-permute-start(bf16[2,4,64,256]{3,2,1,0:T(8,128)(2,1)S(1)} %maximum_select_fusion.1.mid), channel_id=1, source_target_pairs={{0,2},{1,3},{2,4},{3,5},{4,6},{5,7},{6,8},{7,9},{8,10},{9,11},{10,... | collective-permute-start | bytes 786440 | tf_op jit(solution)/shard_map/ppermute | solution.py:190
  30.9 13.1 %collective-permute-start.4 = (bf16[576,256]{1,0:T(8,128)(2,1)S(1)}, bf16[576,256]{1,0:T(8,128)(2,1)S(1)}, u32[]{:S(2)}, u32[]{:S(2)}) collective-permute-start(bf16[576,256]{1,0:T(8,128)(2,1)S(1)} %collective-permute-done), channel_id=1, source_target_pairs={{0,4},{1,5},{2,14},{3,15},{4,8},{5,9},{6,2},{7,3},{8,12},{9,13},{1... | collective-permute-start | bytes 884744 | tf_op jit(solution)/shard_map/ppermute | solution.py:190
  34.2 15.7 %collective-permute-start.3 = (bf16[576,256]{1,0:T(8,128)(2,1)S(1)}, bf16[576,256]{1,0:T(8,128)(2,1)S(1)}, u32[]{:S(2)}, u32[]{:S(2)}) collective-permute-start(bf16[576,256]{1,0:T(8,128)(2,1)S(1)} %collective-permute-done), channel_id=1, source_target_pairs={{0,14},{1,15},{2,0},{3,1},{4,2},{5,3},{6,4},{7,5},{8,6},{9,7},{10,... | collective-permute-start | bytes 884744 | tf_op jit(solution)/shard_map/ppermute | solution.py:190
  40.5 9.4 %collective-permute-start.2 = (bf16[576,256]{1,0:T(8,128)(2,1)S(1)}, bf16[576,256]{1,0:T(8,128)(2,1)S(1)}, u32[]{:S(2)}, u32[]{:S(2)}) collective-permute-start(bf16[576,256]{1,0:T(8,128)(2,1)S(1)} %collective-permute-done), channel_id=1, source_target_pairs={{0,2},{1,3},{2,4},{3,5},{4,6},{5,7},{6,8},{7,9},{8,10},{9,11},{10,... | collective-permute-start | bytes 884744 | tf_op jit(solution)/shard_map/ppermute | solution.py:190
  51.0 15.0 %collective-permute-start.11 = (bf16[4,576,256]{2,1,0:T(8,128)(2,1)S(1)}, bf16[4,576,256]{2,1,0:T(8,128)(2,1)}, u32[]{:S(2)}, u32[]{:S(2)}) collective-permute-start(bf16[4,576,256]{2,1,0:T(8,128)(2,1)S(1)} %pad_maximum_fusion.refs_6_), channel_id=1, source_target_pairs={{0,1},{1,0},{2,3},{3,2},{4,5},{5,4},{6,7},{7,6},{8,9},{9,8},{10,11... | collective-permute-start | bytes 3538952 | tf_op jit(solution)/shard_map/ppermute | solution.py:190
  61.5 5.1 %collective-permute-start.10 = (bf16[2304,256]{1,0:T(8,128)(2,1)}, bf16[2304,256]{1,0:T(8,128)(2,1)}, u32[]{:S(2)}, u32[]{:S(2)}) collective-permute-start(bf16[2304,256]{1,0:T(8,128)(2,1)} %collective-permute-done.9.refs_4_), channel_id=1, source_target_pairs={{0,1},{1,0},{2,3},{3,2},{4,5},{5,4},{6,7},{7,6},{8,9},{9,8},{10,11... | collective-permute-start | bytes 3538952 | tf_op jit(solution)/shard_map/ppermute | solution.py:190
  63.5 5.2 %collective-permute-start.8 = (bf16[2304,256]{1,0:T(8,128)(2,1)}, bf16[2304,256]{1,0:T(8,128)(2,1)}, u32[]{:S(2)}, u32[]{:S(2)}) collective-permute-start(bf16[2304,256]{1,0:T(8,128)(2,1)} %collective-permute-done.7.refs_2_), channel_id=1, source_target_pairs={{0,1},{1,0},{2,3},{3,2},{4,5},{5,4},{6,7},{7,6},{8,9},{9,8},{10,11... | collective-permute-start | bytes 3538952 | tf_op jit(solution)/shard_map/ppermute | solution.py:190
  79.3 8.0 %copy-start.2 = (bf16[2,4,2,64,256]{4,3,2,1,0:T(8,128)(2,1)}, bf16[2,4,2,64,256]{4,3,2,1,0:T(8,128)(2,1)S(1)}, u32[]{:S(2)}) copy-start(bf16[2,4,2,64,256]{4,3,2,1,0:T(8,128)(2,1)S(1)} %get-tuple-element.31) | copy-start | bytes 1572868
  79.3 13.4 %collective-permute-start.12 = (bf16[1,4,64,256]{3,2,1,0:T(8,128)(2,1)S(1)}, bf16[1,4,64,256]{3,2,1,0:T(8,128)(2,1)}, u32[]{:S(2)}, u32[]{:S(2)}) collective-permute-start(bf16[1,4,64,256]{3,2,1,0:T(8,128)(2,1)S(1)} %get-tuple-element.34), channel_id=1, source_target_pairs={{0,256},{1,257},{2,258},{3,259},{4,260},{5,261},{6,262},{7,263},{8... | collective-permute-start | bytes 393224 | tf_op jit(solution)/shard_map/ppermute | solution.py:190
  88.0 14.3 %collective-permute-start.15 = (bf16[1,4,64,256]{3,2,1,0:T(8,128)(2,1)}, bf16[1,4,64,256]{3,2,1,0:T(8,128)(2,1)}, u32[]{:S(2)}, u32[]{:S(2)}) collective-permute-start(bf16[1,4,64,256]{3,2,1,0:T(8,128)(2,1)} %get-tuple-element.36), channel_id=1, source_target_pairs={{0,256},{1,257},{2,258},{3,259},{4,260},{5,261},{6,262},{7,263},{8... | collective-permute-start | bytes 393224 | tf_op jit(solution)/shard_map/ppermute | solution.py:190
  92.7 14.9 %collective-permute-start.14 = (bf16[1,4,64,256]{3,2,1,0:T(8,128)(2,1)}, bf16[1,4,64,256]{3,2,1,0:T(8,128)(2,1)}, u32[]{:S(2)}, u32[]{:S(2)}) collective-permute-start(bf16[1,4,64,256]{3,2,1,0:T(8,128)(2,1)} %collective-permute-done.12.mid), channel_id=1, source_target_pairs={{258,256},{259,257},{260,258},{261,259},{262,260},{263,261},{264,2... | collective-permute-start | bytes 393224 | tf_op jit(solution)/shard_map/ppermute | solution.py:190
  94.6 13.0 %collective-permute-start.13 = (bf16[1,4,64,256]{3,2,1,0:T(8,128)(2,1)}, bf16[1,4,64,256]{3,2,1,0:T(8,128)(2,1)}, u32[]{:S(2)}, u32[]{:S(2)}) collective-permute-start(bf16[1,4,64,256]{3,2,1,0:T(8,128)(2,1)} %collective-permute-done.12.mid), channel_id=1, source_target_pairs={{256,258},{257,259},{258,260},{259,261},{260,262},{261,263},{262,2... | collective-permute-start | bytes 393224 | tf_op jit(solution)/shard_map/ppermute | solution.py:190
  102.3 14.2 %collective-permute-start.17 = (bf16[1,4,64,256]{3,2,1,0:T(8,128)(2,1)}, bf16[1,4,64,256]{3,2,1,0:T(8,128)(2,1)S(1)}, u32[]{:S(2)}, u32[]{:S(2)}) collective-permute-start(bf16[1,4,64,256]{3,2,1,0:T(8,128)(2,1)} %collective-permute-done.15.mid), channel_id=1, source_target_pairs={{258,256},{259,257},{260,258},{261,259},{262,260},{263,261},{264,2... | collective-permute-start | bytes 393224 | tf_op jit(solution)/shard_map/ppermute | solution.py:190
  104.2 12.3 %collective-permute-start.16 = (bf16[1,4,64,256]{3,2,1,0:T(8,128)(2,1)}, bf16[1,4,64,256]{3,2,1,0:T(8,128)(2,1)S(1)}, u32[]{:S(2)}, u32[]{:S(2)}) collective-permute-start(bf16[1,4,64,256]{3,2,1,0:T(8,128)(2,1)} %collective-permute-done.15.mid), channel_id=1, source_target_pairs={{256,258},{257,259},{258,260},{259,261},{260,262},{261,263},{262,2... | collective-permute-start | bytes 393224 | tf_op jit(solution)/shard_map/ppermute | solution.py:190
  123.9 5.2 %collective-permute-start.18 = (bf16[4,2,2,64,256]{4,3,2,1,0:T(8,128)(2,1)S(1)}, bf16[4,2,2,64,256]{4,3,2,1,0:T(8,128)(2,1)S(1)}, u32[]{:S(2)}, u32[]{:S(2)}) collective-permute-start(bf16[4,2,2,64,256]{4,3,2,1,0:T(8,128)(2,1)S(1)} %get-tuple-element.41), channel_id=1, source_target_pairs={{0,1},{1,0},{2,3},{3,2},{4,5},{5,4},{6,7},{7,6},{8,9},{9,8},{10,11... | collective-permute-start | bytes 1572872 | tf_op jit(solution)/shard_map/ppermute | solution.py:190
  129.2 9.4 %collective-permute-start.19 = (bf16[2,2,2,64,256]{4,3,2,1,0:T(8,128)(2,1)S(1)}, bf16[2,2,2,64,256]{4,3,2,1,0:T(8,128)(2,1)S(1)}, u32[]{:S(2)}, u32[]{:S(2)}) collective-permute-start(bf16[2,2,2,64,256]{4,3,2,1,0:T(8,128)(2,1)S(1)} %pad_maximum_fusion.1), channel_id=1, source_target_pairs={{0,64},{1,65},{2,66},{3,67},{4,68},{5,69},{6,70},{7,71},{8,72},{9,... | collective-permute-start | bytes 786440 | tf_op jit(solution)/shard_map/ppermute | solution.py:190
  131.2 11.0 %collective-permute-start.20 = (bf16[2,2,2,64,256]{4,3,2,1,0:T(8,128)(2,1)S(1)}, bf16[2,2,2,64,256]{4,3,2,1,0:T(8,128)(2,1)S(1)}, u32[]{:S(2)}, u32[]{:S(2)}) collective-permute-start(bf16[2,2,2,64,256]{4,3,2,1,0:T(8,128)(2,1)S(1)} %pad_maximum_fusion.2), channel_id=1, source_target_pairs={{0,128},{1,129},{2,130},{3,131},{4,132},{5,133},{6,134},{7,135},{8... | collective-permute-start | bytes 786440 | tf_op jit(solution)/shard_map/ppermute | solution.py:190
  133.4 15.0 %collective-permute-start.21 = (bf16[2,2,2,64,256]{4,3,2,1,0:T(8,128)(2,1)S(1)}, bf16[2,2,2,64,256]{4,3,2,1,0:T(8,128)(2,1)S(1)}, u32[]{:S(2)}, u32[]{:S(2)}) collective-permute-start(bf16[2,2,2,64,256]{4,3,2,1,0:T(8,128)(2,1)S(1)} %pad_maximum_fusion.3), channel_id=1, source_target_pairs={{0,192},{1,193},{2,194},{3,195},{4,196},{5,197},{6,198},{7,199},{8... | collective-permute-start | bytes 786440 | tf_op jit(solution)/shard_map/ppermute | solution.py:190
  (9 other events, 20.1 us)

commit v4 on v3

--- a/solution.py
+++ b/solution.py
@@ -18,13 +18,17 @@
     older = refs[8]
     kept, last = (refs[9], refs[10]) if not first else (refs[8], refs[9])
     older = refs[8] if not first else refs[10]
-    weights, cells, wide, sems = refs[11:]
+    weights, cells, wide, sems, row_sem = refs[11:]
     x, core, chip, piece, chips = meta[0], meta[1], meta[2], meta[3], meta[4]
     depth, _, taps, chans = weights.shape
     _, slab, width, _ = mid.shape
     rows = 3 * slab
     other = 1 - core
     used = (0, 1) if first else (1,)
+
+    index = min(frame, mid.shape[0] - 1)
+    for place, source in enumerate((top, mid, bot)):
+        pltpu.make_async_copy(source.at[index], cells.at[pl.ds(place * slab, slab)], row_sem).start()
 
     def fetch(layer, mine, theirs, places):
         for half in used:
@@ -63,11 +67,9 @@
         wide[buffer, row, :, chans:2 * chans] = normed.astype(jnp.bfloat16)
         wide[buffer, row, :, 2 * chans:] = after.astype(jnp.bfloat16)
 
-    index = min(frame, mid.shape[0] - 1)
+    pltpu.make_async_copy(cells, cells, row_sem).wait()
     for row in range(rows):
-        stored = (top, mid, bot)[row // slab][index, row % slab]
-        cells[row] = stored
-        spread(row, stored, 0)
+        spread(row, cells[row], 0)
 
     base = 0
     for layer in range(depth):
@@ -128,15 +130,16 @@
     return pl.pallas_call(
         functools.partial(frame_kernel, frame),
         out_shape=tuple(out),
-        in_specs=[pl.BlockSpec(memory_space=pltpu.SMEM)] + [vmem] * 3 + [hbm] * len(kernels) + [vmem] * len(extra),
+        in_specs=[pl.BlockSpec(memory_space=pltpu.SMEM)] + [hbm] * (3 + len(kernels)) + [vmem] * len(extra),
         out_specs=(vmem,) * len(out),
         scratch_shapes=[
             pltpu.VMEM((DEPTH, 2, taps, chans), bf16),
             pltpu.VMEM((3 * slab, width, chans), bf16),
             pltpu.VMEM((2, 3 * slab, width, 3 * chans), bf16),
             pltpu.SemaphoreType.DMA((DEPTH,)),
+            pltpu.SemaphoreType.DMA,
         ],
-        compiler_params=pltpu.CompilerParams(vmem_limit_bytes=36 * 1024 * 1024),
+        compiler_params=pltpu.CompilerParams(vmem_limit_bytes=50 * 1024 * 1024),
         cost_estimate=pl.CostEstimate(flops=work, bytes_accessed=8 * 10**6, transcendentals=10**6),
         name="frame%d" % frame,
     )(meta, top, mid, bot, *kernels, *extra)
@@ -228,6 +231,7 @@
     far = send(quarter, along_x(2))
 
     give = lax.dynamic_index_in_dim(frames_in, 2 * x + 1 - core, 0, keepdims=False)
+    give, quarter = lax.optimization_barrier((give, quarter))
     keep = lax.dynamic_index_in_dim(frames_in, 2 * x + core, 0, keepdims=False)
     got = send(give, sibling)
     mine = lax.dynamic_index_in_dim(own, core, 0, keepdims=False)
@@ -235,11 +239,13 @@
     far, mine, got = lax.optimization_barrier((far, mine, got))
     left_mine = send(mine, along_x(1))
     right_mine = send(mine, along_x(-1))
+    parts = (far, send(far, along_y(1)), send(far, along_y(-1)), send(far, two_along_y))
+    got, early = lax.optimization_barrier((got, parts[2]))
+    parts = (far, parts[1], early, parts[3])
     mid = jnp.where(core == 0, jnp.concatenate([keep, got], 1), jnp.concatenate([got, keep], 1))
     top = send(mid, next_chip(1))
     bot = send(mid, next_chip(-1))
 
-    parts = (far, send(far, along_y(1)), send(far, along_y(-1)), send(far, two_along_y))
     *parts, top, bot = lax.optimization_barrier((*parts, top, bot))
     far_mine = jnp.stack(parts)
     far_theirs = send(far_mine, sibling)

time: 151 us -> 151 us (level)
  the two profiles are of different devices: /device:TPU:327 before, /device:TPU:391 now
where the time goes in v4:
time: 151 us; the launch traced here: 150 us
  starting transfers between devices  71.3 us (47%)
  Pallas kernels  36.9 us (24%)
  waiting for transfers between devices  33.2 us (22%)
  local copies, waits for them, and re-layouts  5.79 us (4%)
  other arithmetic  2.73 us (2%)
    ppermute x22, starting transfers between devices, send(): return lax.ppermute(array, ('section', 'rows'), route(move, keep))  71.3 us
    pallas_call x4, Pallas kernels, run_frame(): pl.pallas_call(functools.partial(frame_kernel, frame), out_shape=tuple(ou...  35.3 us
    ppermute x22, waiting for transfers between devices, send(): return lax.ppermute(array, ('section', 'rows'), route(move, keep))  33.2 us
  transfers between devices with their start and end apart: 22, of which 11 were waited for; matrix products, arithmetic and copies ran while one was open for 4% of the time, Pallas kernels for 12%

profile of v4, /device:TPU:391, one launch (start us, length us, event | category | flops | bytes accessed | tf_op | source)
XLA Modules:
  0.0 150.4 jit_solution(2014746353131118344)
XLA Ops:
  1.0 3.0 %collective-permute-start = (bf16[576,256]{1,0:T(8,128)(2,1)S(1)}, bf16[576,256]{1,0:T(8,128)(2,1)}, u32[]{:S(2)}, u32[]{:S(2)}) collective-permute-start(bf16[576,256]{1,0:T(8,128)(2,1)S(1)} %dynamic-slice_bitcast_fusion.2), channel_id=1, source_target_pairs={{0,128},{1,129},{2,130},{3,131},{4,132},{5,133},{6,134},{7,135},{8... | collective-permute-start | bytes 884744 | tf_op jit(solution)/shard_map/ppermute | solution.py:193
  5.0 2.9 %collective-permute-start.1 = (bf16[2,2,64,256]{3,2,1,0:T(8,128)(2,1)S(1)}, bf16[2,2,64,256]{3,2,1,0:T(8,128)(2,1)S(1)}, u32[]{:S(2)}, u32[]{:S(2)}) collective-permute-start(bf16[2,2,64,256]{3,2,1,0:T(8,128)(2,1)S(1)} %get-tuple-element.25), channel_id=1, source_target_pairs={{0,1},{1,0},{2,3},{3,2},{4,5},{5,4},{6,7},{7,6},{8,9},{9,8},{10,11... | collective-permute-start | bytes 393224 | tf_op jit(solution)/shard_map/ppermute | solution.py:193
  9.7 2.6 %collective-permute-done = bf16[576,256]{1,0:T(8,128)(2,1)} collective-permute-done((bf16[576,256]{1,0:T(8,128)(2,1)S(1)}, bf16[576,256]{1,0:T(8,128)(2,1)}, u32[]{:S(2)}, u32[]{:S(2)}) %collective-permute-start) | collective-permute-done | bytes 294944 | tf_op jit(solution)/shard_map/ppermute | solution.py:193
  12.4 2.4 %collective-permute-start.9 = (bf16[2304,256]{1,0:T(8,128)(2,1)S(1)}, bf16[2304,256]{1,0:T(8,128)(2,1)}, u32[]{:S(2)}, u32[]{:S(2)}) collective-permute-start(bf16[2304,256]{1,0:T(8,128)(2,1)S(1)} %get-tuple-element.32.refs_0_), channel_id=1, source_target_pairs={{0,192},{1,193},{2,194},{3,195},{4,196},{5,197},{6,198},{7,199},{8... | collective-permute-start | bytes 3538952 | tf_op jit(solution)/shard_map/ppermute | solution.py:193
  14.8 4.0 %collective-permute-start.7 = (bf16[2304,256]{1,0:T(8,128)(2,1)S(1)}, bf16[2304,256]{1,0:T(8,128)(2,1)}, u32[]{:S(2)}, u32[]{:S(2)}) collective-permute-start(bf16[2304,256]{1,0:T(8,128)(2,1)S(1)} %get-tuple-element.32.refs_0_), channel_id=1, source_target_pairs={{0,64},{1,65},{2,66},{3,67},{4,68},{5,69},{6,70},{7,71},{8,72},{9,... | collective-permute-start | bytes 3538952 | tf_op jit(solution)/shard_map/ppermute | solution.py:193
  18.9 5.1 %collective-permute-start.3 = (bf16[576,256]{1,0:T(8,128)(2,1)}, bf16[576,256]{1,0:T(8,128)(2,1)S(1)}, u32[]{:S(2)}, u32[]{:S(2)}) collective-permute-start(bf16[576,256]{1,0:T(8,128)(2,1)} %collective-permute-done), channel_id=1, source_target_pairs={{0,14},{1,15},{2,0},{3,1},{4,2},{5,3},{6,4},{7,5},{8,6},{9,7},{10,... | collective-permute-start | bytes 884744 | tf_op jit(solution)/shard_map/ppermute | solution.py:193
  25.9 4.1 %collective-permute-start.2 = (bf16[576,256]{1,0:T(8,128)(2,1)}, bf16[576,256]{1,0:T(8,128)(2,1)S(1)}, u32[]{:S(2)}, u32[]{:S(2)}) collective-permute-start(bf16[576,256]{1,0:T(8,128)(2,1)} %collective-permute-done), channel_id=1, source_target_pairs={{0,2},{1,3},{2,4},{3,5},{4,6},{5,7},{6,8},{7,9},{8,10},{9,11},{10,... | collective-permute-start | bytes 884744 | tf_op jit(solution)/shard_map/ppermute | solution.py:193
  30.1 3.7 %collective-permute-start.6 = (bf16[2,4,64,256]{3,2,1,0:T(8,128)(2,1)S(1)}, bf16[2,4,64,256]{3,2,1,0:T(8,128)(2,1)S(1)}, u32[]{:S(2)}, u32[]{:S(2)}) collective-permute-start(bf16[2,4,64,256]{3,2,1,0:T(8,128)(2,1)S(1)} %maximum_select_fusion.1.mid), channel_id=1, source_target_pairs={{2,0},{3,1},{4,2},{5,3},{6,4},{7,5},{8,6},{9,7},{10,8},{11,9},{12,... | collective-permute-start | bytes 786440 | tf_op jit(solution)/shard_map/ppermute | solution.py:193
  34.5 3.5 %collective-permute-start.5 = (bf16[2,4,64,256]{3,2,1,0:T(8,128)(2,1)S(1)}, bf16[2,4,64,256]{3,2,1,0:T(8,128)(2,1)S(1)}, u32[]{:S(2)}, u32[]{:S(2)}) collective-permute-start(bf16[2,4,64,256]{3,2,1,0:T(8,128)(2,1)S(1)} %maximum_select_fusion.1.mid), channel_id=1, source_target_pairs={{0,2},{1,3},{2,4},{3,5},{4,6},{5,7},{6,8},{7,9},{8,10},{9,11},{10,... | collective-permute-start | bytes 786440 | tf_op jit(solution)/shard_map/ppermute | solution.py:193
  38.0 5.2 %collective-permute-done.2 = bf16[576,256]{1,0:T(8,128)(2,1)S(1)} collective-permute-done((bf16[576,256]{1,0:T(8,128)(2,1)}, bf16[576,256]{1,0:T(8,128)(2,1)S(1)}, u32[]{:S(2)}, u32[]{:S(2)}) %collective-permute-start.2) | collective-permute-done | bytes 294944 | tf_op jit(solution)/shard_map/ppermute | solution.py:193
  43.2 2.8 %collective-permute-done.5.top = bf16[2,4,64,256]{3,2,1,0:T(8,128)(2,1)S(1)} collective-permute-done((bf16[2,4,64,256]{3,2,1,0:T(8,128)(2,1)S(1)}, bf16[2,4,64,256]{3,2,1,0:T(8,128)(2,1)S(1)}, u32[]{:S(2)}, u32[]{:S(2)}) %collective-permute-start.5) | collective-permute-done | bytes 262176 | tf_op jit(solution)/shard_map/ppermute | solution.py:193
  46.0 2.4 %pad_maximum_fusion.refs_6_ = bf16[4,576,256]{2,1,0:T(8,128)(2,1)} fusion(bf16[1,576,256]{2,1,0:T(8,128)(2,1)} %bitcast.13, bf16[1,576,256]{2,1,0:T(8,128)(2,1)} %bitcast.42, bf16[1,576,256]{2,1,0:T(8,128)(2,1)S(1)} %bitcast.43, bf16[1,576,256]{2,1,0:T(8,128)(2,1)} %bitcast.10), kind=kLoop, calls=%fused_computation | loop fusion | flops 1769472 | bytes 2359296 | tf_op jit(solution)/shard_map/stack | solution.py:250
  48.5 11.2 %collective-permute-start.11 = (bf16[4,576,256]{2,1,0:T(8,128)(2,1)}, bf16[4,576,256]{2,1,0:T(8,128)(2,1)}, u32[]{:S(2)}, u32[]{:S(2)}) collective-permute-start(bf16[4,576,256]{2,1,0:T(8,128)(2,1)} %pad_maximum_fusion.refs_6_), channel_id=1, source_target_pairs={{0,1},{1,0},{2,3},{3,2},{4,5},{5,4},{6,7},{7,6},{8,9},{9,8},{10,11... | collective-permute-start | bytes 3538952 | tf_op jit(solution)/shard_map/ppermute | solution.py:193
  67.8 9.5 %frame0.2 = (bf16[2,4,2,64,256]{4,3,2,1,0:T(8,128)(2,1)S(1)}, bf16[1,4,64,256]{3,2,1,0:T(8,128)(2,1)S(1)}, f32[28,64,256]{2,1,0:T(8,128)}) custom-call(s32[5]{0:T(128)S(1)} %stack.67.meta, bf16[2,4,64,256]{3,2,1,0:T(8,128)(2,1)S(1)} %copy-done.3, bf16[2,4,64,256]{3,2,1,0:T(8,128)(2,1)S(1)} %maximum_select_fusion.1.mid, ...), custom_call_target="tpu_custom_call" | custom-call | flops 4227858432 | bytes 8000000 | tf_op jit(solution)/shard_map/frame0/pallas_call | solution.py:130
  78.6 8.1 %frame1.2 = (bf16[2,4,2,64,256]{4,3,2,1,0:T(8,128)(2,1)S(1)}, bf16[1,4,64,256]{3,2,1,0:T(8,128)(2,1)}) custom-call(s32[5]{0:T(128)S(1)} %stack.67.meta, bf16[2,4,64,256]{3,2,1,0:T(8,128)(2,1)S(1)} %copy-done.3, bf16[2,4,64,256]{3,2,1,0:T(8,128)(2,1)S(1)} %maximum_select_fusion.1.mid, bf16[2,4,64,256]{3,2,1,0:T(8,128)(2,1)S(1)} %collective-permute-done.6.bot, ...), custom_call_target="tpu_custom_call" | custom-call | flops 2113929216 | bytes 8000000 | tf_op jit(solution)/shard_map/frame1/pallas_call | solution.py:130
  88.8 3.2 %collective-permute-start.14 = (bf16[1,4,64,256]{3,2,1,0:T(8,128)(2,1)S(1)}, bf16[1,4,64,256]{3,2,1,0:T(8,128)(2,1)S(1)}, u32[]{:S(2)}, u32[]{:S(2)}) collective-permute-start(bf16[1,4,64,256]{3,2,1,0:T(8,128)(2,1)S(1)} %collective-permute-done.12.mid), channel_id=1, source_target_pairs={{258,256},{259,257},{260,258},{261,259},{262,260},{263,261},{264,2... | collective-permute-start | bytes 393224 | tf_op jit(solution)/shard_map/ppermute | solution.py:193
  94.1 5.8 %collective-permute-done.15.mid = bf16[1,4,64,256]{3,2,1,0:T(8,128)(2,1)S(1)} collective-permute-done((bf16[1,4,64,256]{3,2,1,0:T(8,128)(2,1)}, bf16[1,4,64,256]{3,2,1,0:T(8,128)(2,1)S(1)}, u32[]{:S(2)}, u32[]{:S(2)}) %collective-permute-start.15) | collective-permute-done | bytes 131104 | tf_op jit(solution)/shard_map/ppermute | solution.py:193
  100.0 3.9 %collective-permute-start.17 = (bf16[1,4,64,256]{3,2,1,0:T(8,128)(2,1)S(1)}, bf16[1,4,64,256]{3,2,1,0:T(8,128)(2,1)S(1)}, u32[]{:S(2)}, u32[]{:S(2)}) collective-permute-start(bf16[1,4,64,256]{3,2,1,0:T(8,128)(2,1)S(1)} %collective-permute-done.15.mid), channel_id=1, source_target_pairs={{258,256},{259,257},{260,258},{261,259},{262,260},{263,261},{264,2... | collective-permute-start | bytes 393224 | tf_op jit(solution)/shard_map/ppermute | solution.py:193
  105.8 9.5 %frame0.3 = (bf16[2,4,2,64,256]{4,3,2,1,0:T(8,128)(2,1)S(1)}, bf16[1,4,64,256]{3,2,1,0:T(8,128)(2,1)}, f32[28,64,256]{2,1,0:T(8,128)}) custom-call(s32[5]{0:T(128)S(1)} %stack.67.meta, bf16[1,4,64,256]{3,2,1,0:T(8,128)(2,1)S(1)} %collective-permute-done.13.top, bf16[1,4,64,256]{3,2,1,0:T(8,128)(2,1)S(1)} %collective-permute-done.12.mid, ...), custom_call_target="tpu_custom_call" | custom-call | flops 4227858432 | bytes 8000000 | tf_op jit(solution)/shard_map/frame0/pallas_call | solution.py:130
  115.4 8.2 %frame1.3 = (bf16[2,4,2,64,256]{4,3,2,1,0:T(8,128)(2,1)S(1)}, bf16[1,4,64,256]{3,2,1,0:T(8,128)(2,1)}) custom-call(s32[5]{0:T(128)S(1)} %stack.67.meta, bf16[1,4,64,256]{3,2,1,0:T(8,128)(2,1)S(1)} %collective-permute-done.16.top, bf16[1,4,64,256]{3,2,1,0:T(8,128)(2,1)S(1)} %collective-permute-done.15.mid, ...), custom_call_target="tpu_custom_call" | custom-call | flops 2113929216 | bytes 8000000 | tf_op jit(solution)/shard_map/frame1/pallas_call | solution.py:130
  123.9 4.1 %collective-permute-start.18 = (bf16[4,2,2,64,256]{4,3,2,1,0:T(8,128)(2,1)S(1)}, bf16[4,2,2,64,256]{4,3,2,1,0:T(8,128)(2,1)S(1)}, u32[]{:S(2)}, u32[]{:S(2)}) collective-permute-start(bf16[4,2,2,64,256]{4,3,2,1,0:T(8,128)(2,1)S(1)} %get-tuple-element.47), channel_id=1, source_target_pairs={{0,1},{1,0},{2,3},{3,2},{4,5},{5,4},{6,7},{7,6},{8,9},{9,8},{10,11... | collective-permute-start | bytes 1572872 | tf_op jit(solution)/shard_map/ppermute | solution.py:193
  131.6 2.9 %collective-permute-start.20 = (bf16[2,2,2,64,256]{4,3,2,1,0:T(8,128)(2,1)S(1)}, bf16[2,2,2,64,256]{4,3,2,1,0:T(8,128)(2,1)S(1)}, u32[]{:S(2)}, u32[]{:S(2)}) collective-permute-start(bf16[2,2,2,64,256]{4,3,2,1,0:T(8,128)(2,1)S(1)} %pad_maximum_fusion.2), channel_id=1, source_target_pairs={{0,128},{1,129},{2,130},{3,131},{4,132},{5,133},{6,134},{7,135},{8... | collective-permute-start | bytes 786440 | tf_op jit(solution)/shard_map/ppermute | solution.py:193
  139.0 3.5 %collective-permute-done.20.refs_1_ = bf16[2,2,2,64,256]{4,3,2,1,0:T(8,128)(2,1)S(1)} collective-permute-done((bf16[2,2,2,64,256]{4,3,2,1,0:T(8,128)(2,1)S(1)}, bf16[2,2,2,64,256]{4,3,2,1,0:T(8,128)(2,1)S(1)}, u32[]{:S(2)}, u32[]{:S(2)}) %collective-permute-start.20) | collective-permute-done | bytes 262176 | tf_op jit(solution)/shard_map/ppermute | solution.py:193
  142.5 6.3 %collective-permute-done.21.refs_2_ = bf16[2,2,2,64,256]{4,3,2,1,0:T(8,128)(2,1)S(1)} collective-permute-done((bf16[2,2,2,64,256]{4,3,2,1,0:T(8,128)(2,1)S(1)}, bf16[2,2,2,64,256]{4,3,2,1,0:T(8,128)(2,1)S(1)}, u32[]{:S(2)}, u32[]{:S(2)}) %collective-permute-start.21) | collective-permute-done | bytes 262176 | tf_op jit(solution)/shard_map/ppermute | solution.py:193
  (48 shorter events, 31.6 us)
Async XLA Ops:
  1.0 11.4 %collective-permute-start = (bf16[576,256]{1,0:T(8,128)(2,1)S(1)}, bf16[576,256]{1,0:T(8,128)(2,1)}, u32[]{:S(2)}, u32[]{:S(2)}) collective-permute-start(bf16[576,256]{1,0:T(8,128)(2,1)S(1)} %dynamic-slice_bitcast_fusion.2), channel_id=1, source_target_pairs={{0,128},{1,129},{2,130},{3,131},{4,132},{5,133},{6,134},{7,135},{8... | collective-permute-start | bytes 884744 | tf_op jit(solution)/shard_map/ppermute | solution.py:193
  5.0 4.7 %collective-permute-start.1 = (bf16[2,2,64,256]{3,2,1,0:T(8,128)(2,1)S(1)}, bf16[2,2,64,256]{3,2,1,0:T(8,128)(2,1)S(1)}, u32[]{:S(2)}, u32[]{:S(2)}) collective-permute-start(bf16[2,2,64,256]{3,2,1,0:T(8,128)(2,1)S(1)} %get-tuple-element.25), channel_id=1, source_target_pairs={{0,1},{1,0},{2,3},{3,2},{4,5},{5,4},{6,7},{7,6},{8,9},{9,8},{10,11... | collective-permute-start | bytes 393224 | tf_op jit(solution)/shard_map/ppermute | solution.py:193
  12.4 47.3 %collective-permute-start.9 = (bf16[2304,256]{1,0:T(8,128)(2,1)S(1)}, bf16[2304,256]{1,0:T(8,128)(2,1)}, u32[]{:S(2)}, u32[]{:S(2)}) collective-permute-start(bf16[2304,256]{1,0:T(8,128)(2,1)S(1)} %get-tuple-element.32.refs_0_), channel_id=1, source_target_pairs={{0,192},{1,193},{2,194},{3,195},{4,196},{5,197},{6,198},{7,199},{8... | collective-permute-start | bytes 3538952 | tf_op jit(solution)/shard_map/ppermute | solution.py:193
  14.8 46.8 %collective-permute-start.7 = (bf16[2304,256]{1,0:T(8,128)(2,1)S(1)}, bf16[2304,256]{1,0:T(8,128)(2,1)}, u32[]{:S(2)}, u32[]{:S(2)}) collective-permute-start(bf16[2304,256]{1,0:T(8,128)(2,1)S(1)} %get-tuple-element.32.refs_0_), channel_id=1, source_target_pairs={{0,64},{1,65},{2,66},{3,67},{4,68},{5,69},{6,70},{7,71},{8,72},{9,... | collective-permute-start | bytes 3538952 | tf_op jit(solution)/shard_map/ppermute | solution.py:193
  18.9 11.2 %collective-permute-start.3 = (bf16[576,256]{1,0:T(8,128)(2,1)}, bf16[576,256]{1,0:T(8,128)(2,1)S(1)}, u32[]{:S(2)}, u32[]{:S(2)}) collective-permute-start(bf16[576,256]{1,0:T(8,128)(2,1)} %collective-permute-done), channel_id=1, source_target_pairs={{0,14},{1,15},{2,0},{3,1},{4,2},{5,3},{6,4},{7,5},{8,6},{9,7},{10,... | collective-permute-start | bytes 884744 | tf_op jit(solution)/shard_map/ppermute | solution.py:193
  24.0 10.5 %collective-permute-start.4 = (bf16[576,256]{1,0:T(8,128)(2,1)}, bf16[576,256]{1,0:T(8,128)(2,1)}, u32[]{:S(2)}, u32[]{:S(2)}) collective-permute-start(bf16[576,256]{1,0:T(8,128)(2,1)} %collective-permute-done), channel_id=1, source_target_pairs={{0,4},{1,5},{2,14},{3,15},{4,8},{5,9},{6,2},{7,3},{8,12},{9,13},{1... | collective-permute-start | bytes 884744 | tf_op jit(solution)/shard_map/ppermute | solution.py:193
  25.9 17.3 %collective-permute-start.2 = (bf16[576,256]{1,0:T(8,128)(2,1)}, bf16[576,256]{1,0:T(8,128)(2,1)S(1)}, u32[]{:S(2)}, u32[]{:S(2)}) collective-permute-start(bf16[576,256]{1,0:T(8,128)(2,1)} %collective-permute-done), channel_id=1, source_target_pairs={{0,2},{1,3},{2,4},{3,5},{4,6},{5,7},{6,8},{7,9},{8,10},{9,11},{10,... | collective-permute-start | bytes 884744 | tf_op jit(solution)/shard_map/ppermute | solution.py:193
  30.1 3.7 %copy-start.4 = (bf16[576,256]{1,0:T(8,128)(2,1)}, bf16[576,256]{1,0:T(8,128)(2,1)S(1)}, u32[]{:S(2)}) copy-start(bf16[576,256]{1,0:T(8,128)(2,1)S(1)} %collective-permute-done.3) | copy-start | bytes 884740
  30.1 13.1 %collective-permute-start.6 = (bf16[2,4,64,256]{3,2,1,0:T(8,128)(2,1)S(1)}, bf16[2,4,64,256]{3,2,1,0:T(8,128)(2,1)S(1)}, u32[]{:S(2)}, u32[]{:S(2)}) collective-permute-start(bf16[2,4,64,256]{3,2,1,0:T(8,128)(2,1)S(1)} %maximum_select_fusion.1.mid), channel_id=1, source_target_pairs={{2,0},{3,1},{4,2},{5,3},{6,4},{7,5},{8,6},{9,7},{10,8},{11,9},{12,... | collective-permute-start | bytes 786440 | tf_op jit(solution)/shard_map/ppermute | solution.py:193
  34.5 11.6 %collective-permute-start.5 = (bf16[2,4,64,256]{3,2,1,0:T(8,128)(2,1)S(1)}, bf16[2,4,64,256]{3,2,1,0:T(8,128)(2,1)S(1)}, u32[]{:S(2)}, u32[]{:S(2)}) collective-permute-start(bf16[2,4,64,256]{3,2,1,0:T(8,128)(2,1)S(1)} %maximum_select_fusion.1.mid), channel_id=1, source_target_pairs={{0,2},{1,3},{2,4},{3,5},{4,6},{5,7},{6,8},{7,9},{8,10},{9,11},{10,... | collective-permute-start | bytes 786440 | tf_op jit(solution)/shard_map/ppermute | solution.py:193
  48.5 15.7 %collective-permute-start.11 = (bf16[4,576,256]{2,1,0:T(8,128)(2,1)}, bf16[4,576,256]{2,1,0:T(8,128)(2,1)}, u32[]{:S(2)}, u32[]{:S(2)}) collective-permute-start(bf16[4,576,256]{2,1,0:T(8,128)(2,1)} %pad_maximum_fusion.refs_6_), channel_id=1, source_target_pairs={{0,1},{1,0},{2,3},{3,2},{4,5},{5,4},{6,7},{7,6},{8,9},{9,8},{10,11... | collective-permute-start | bytes 3538952 | tf_op jit(solution)/shard_map/ppermute | solution.py:193
  59.7 5.1 %collective-permute-start.10 = (bf16[2304,256]{1,0:T(8,128)(2,1)}, bf16[2304,256]{1,0:T(8,128)(2,1)}, u32[]{:S(2)}, u32[]{:S(2)}) collective-permute-start(bf16[2304,256]{1,0:T(8,128)(2,1)} %collective-permute-done.9.refs_4_), channel_id=1, source_target_pairs={{0,1},{1,0},{2,3},{3,2},{4,5},{5,4},{6,7},{7,6},{8,9},{9,8},{10,11... | collective-permute-start | bytes 3538952 | tf_op jit(solution)/shard_map/ppermute | solution.py:193
  61.6 5.2 %collective-permute-start.8 = (bf16[2304,256]{1,0:T(8,128)(2,1)}, bf16[2304,256]{1,0:T(8,128)(2,1)}, u32[]{:S(2)}, u32[]{:S(2)}) collective-permute-start(bf16[2304,256]{1,0:T(8,128)(2,1)} %collective-permute-done.7.refs_2_), channel_id=1, source_target_pairs={{0,1},{1,0},{2,3},{3,2},{4,5},{5,4},{6,7},{7,6},{8,9},{9,8},{10,11... | collective-permute-start | bytes 3538952 | tf_op jit(solution)/shard_map/ppermute | solution.py:193
  77.3 11.5 %collective-permute-start.12 = (bf16[1,4,64,256]{3,2,1,0:T(8,128)(2,1)S(1)}, bf16[1,4,64,256]{3,2,1,0:T(8,128)(2,1)S(1)}, u32[]{:S(2)}, u32[]{:S(2)}) collective-permute-start(bf16[1,4,64,256]{3,2,1,0:T(8,128)(2,1)S(1)} %get-tuple-element.40), channel_id=1, source_target_pairs={{0,256},{1,257},{2,258},{3,259},{4,260},{5,261},{6,262},{7,263},{8... | collective-permute-start | bytes 393224 | tf_op jit(solution)/shard_map/ppermute | solution.py:193
  87.5 12.4 %collective-permute-start.15 = (bf16[1,4,64,256]{3,2,1,0:T(8,128)(2,1)}, bf16[1,4,64,256]{3,2,1,0:T(8,128)(2,1)S(1)}, u32[]{:S(2)}, u32[]{:S(2)}) collective-permute-start(bf16[1,4,64,256]{3,2,1,0:T(8,128)(2,1)} %get-tuple-element.42), channel_id=1, source_target_pairs={{0,256},{1,257},{2,258},{3,259},{4,260},{5,261},{6,262},{7,263},{8... | collective-permute-start | bytes 393224 | tf_op jit(solution)/shard_map/ppermute | solution.py:193
  88.8 17.0 %collective-permute-start.14 = (bf16[1,4,64,256]{3,2,1,0:T(8,128)(2,1)S(1)}, bf16[1,4,64,256]{3,2,1,0:T(8,128)(2,1)S(1)}, u32[]{:S(2)}, u32[]{:S(2)}) collective-permute-start(bf16[1,4,64,256]{3,2,1,0:T(8,128)(2,1)S(1)} %collective-permute-done.12.mid), channel_id=1, source_target_pairs={{258,256},{259,257},{260,258},{261,259},{262,260},{263,261},{264,2... | collective-permute-start | bytes 393224 | tf_op jit(solution)/shard_map/ppermute | solution.py:193
  92.1 13.8 %collective-permute-start.13 = (bf16[1,4,64,256]{3,2,1,0:T(8,128)(2,1)S(1)}, bf16[1,4,64,256]{3,2,1,0:T(8,128)(2,1)S(1)}, u32[]{:S(2)}, u32[]{:S(2)}) collective-permute-start(bf16[1,4,64,256]{3,2,1,0:T(8,128)(2,1)S(1)} %collective-permute-done.12.mid), channel_id=1, source_target_pairs={{256,258},{257,259},{258,260},{259,261},{260,262},{261,263},{262,2... | collective-permute-start | bytes 393224 | tf_op jit(solution)/shard_map/ppermute | solution.py:193
  100.0 15.4 %collective-permute-start.17 = (bf16[1,4,64,256]{3,2,1,0:T(8,128)(2,1)S(1)}, bf16[1,4,64,256]{3,2,1,0:T(8,128)(2,1)S(1)}, u32[]{:S(2)}, u32[]{:S(2)}) collective-permute-start(bf16[1,4,64,256]{3,2,1,0:T(8,128)(2,1)S(1)} %collective-permute-done.15.mid), channel_id=1, source_target_pairs={{258,256},{259,257},{260,258},{261,259},{262,260},{263,261},{264,2... | collective-permute-start | bytes 393224 | tf_op jit(solution)/shard_map/ppermute | solution.py:193
  103.9 11.5 %collective-permute-start.16 = (bf16[1,4,64,256]{3,2,1,0:T(8,128)(2,1)S(1)}, bf16[1,4,64,256]{3,2,1,0:T(8,128)(2,1)S(1)}, u32[]{:S(2)}, u32[]{:S(2)}) collective-permute-start(bf16[1,4,64,256]{3,2,1,0:T(8,128)(2,1)S(1)} %collective-permute-done.15.mid), channel_id=1, source_target_pairs={{256,258},{257,259},{258,260},{259,261},{260,262},{261,263},{262,2... | collective-permute-start | bytes 393224 | tf_op jit(solution)/shard_map/ppermute | solution.py:193
  115.4 8.2 %copy-start.1 = (bf16[2,4,2,64,256]{4,3,2,1,0:T(8,128)(2,1)S(1)}, bf16[2,4,2,64,256]{4,3,2,1,0:T(8,128)(2,1)}, u32[]{:S(2)}) copy-start(bf16[2,4,2,64,256]{4,3,2,1,0:T(8,128)(2,1)} %copy-done) | copy-start | bytes 1572868
  123.9 5.6 %collective-permute-start.18 = (bf16[4,2,2,64,256]{4,3,2,1,0:T(8,128)(2,1)S(1)}, bf16[4,2,2,64,256]{4,3,2,1,0:T(8,128)(2,1)S(1)}, u32[]{:S(2)}, u32[]{:S(2)}) collective-permute-start(bf16[4,2,2,64,256]{4,3,2,1,0:T(8,128)(2,1)S(1)} %get-tuple-element.47), channel_id=1, source_target_pairs={{0,1},{1,0},{2,3},{3,2},{4,5},{5,4},{6,7},{7,6},{8,9},{9,8},{10,11... | collective-permute-start | bytes 1572872 | tf_op jit(solution)/shard_map/ppermute | solution.py:193
  129.6 9.4 %collective-permute-start.19 = (bf16[2,2,2,64,256]{4,3,2,1,0:T(8,128)(2,1)S(1)}, bf16[2,2,2,64,256]{4,3,2,1,0:T(8,128)(2,1)S(1)}, u32[]{:S(2)}, u32[]{:S(2)}) collective-permute-start(bf16[2,2,2,64,256]{4,3,2,1,0:T(8,128)(2,1)S(1)} %pad_maximum_fusion.1), channel_id=1, source_target_pairs={{0,64},{1,65},{2,66},{3,67},{4,68},{5,69},{6,70},{7,71},{8,72},{9,... | collective-permute-start | bytes 786440 | tf_op jit(solution)/shard_map/ppermute | solution.py:193
  131.6 11.0 %collective-permute-start.20 = (bf16[2,2,2,64,256]{4,3,2,1,0:T(8,128)(2,1)S(1)}, bf16[2,2,2,64,256]{4,3,2,1,0:T(8,128)(2,1)S(1)}, u32[]{:S(2)}, u32[]{:S(2)}) collective-permute-start(bf16[2,2,2,64,256]{4,3,2,1,0:T(8,128)(2,1)S(1)} %pad_maximum_fusion.2), channel_id=1, source_target_pairs={{0,128},{1,129},{2,130},{3,131},{4,132},{5,133},{6,134},{7,135},{8... | collective-permute-start | bytes 786440 | tf_op jit(solution)/shard_map/ppermute | solution.py:193
  134.5 14.3 %collective-permute-start.21 = (bf16[2,2,2,64,256]{4,3,2,1,0:T(8,128)(2,1)S(1)}, bf16[2,2,2,64,256]{4,3,2,1,0:T(8,128)(2,1)S(1)}, u32[]{:S(2)}, u32[]{:S(2)}) collective-permute-start(bf16[2,2,2,64,256]{4,3,2,1,0:T(8,128)(2,1)S(1)} %pad_maximum_fusion.3), channel_id=1, source_target_pairs={{0,192},{1,193},{2,194},{3,195},{4,196},{5,197},{6,198},{7,199},{8... | collective-permute-start | bytes 786440 | tf_op jit(solution)/shard_map/ppermute | solution.py:193
  (3 other events, 4.2 us)

commit v5 on v3

--- a/solution.py
+++ b/solution.py
@@ -9,30 +9,39 @@
 
 DEPTH = 4
 SPLIT = 4
-
-
-def frame_kernel(frame, meta, top, mid, bot, *refs):
+LIMIT = 50
+
+
+def frame_kernel(frame, builds, slabs, meta, *refs):
     first = frame == 0
-    refs = list(refs)
-    pieces = refs[:8]
-    older = refs[8]
-    kept, last = (refs[9], refs[10]) if not first else (refs[8], refs[9])
-    older = refs[8] if not first else refs[10]
-    weights, cells, wide, sems = refs[11:]
+    inputs, refs = refs[:slabs], list(refs[slabs:])
+    fetches = inputs[0].shape[0] > 1
+    if builds:
+        pieces, refs = refs[:8], refs[8:]
+    else:
+        weights = refs.pop(0)
+    older = refs.pop(0) if not first else None
+    kept, last = refs.pop(0), refs.pop(0)
+    older = refs.pop(0) if first else older
+    if builds:
+        weights = refs.pop(0)
+    later = refs.pop(0) if fetches else None
+    cells, wide, sems, row_sems = refs
     x, core, chip, piece, chips = meta[0], meta[1], meta[2], meta[3], meta[4]
     depth, _, taps, chans = weights.shape
-    _, slab, width, _ = mid.shape
-    rows = 3 * slab
+    rows, width, _ = cells.shape
+    slab = rows // 3
     other = 1 - core
-    used = (0, 1) if first else (1,)
+    if fetches:
+        for place, source in enumerate(inputs):
+            at = pl.ds(place * slab, slab)
+            pltpu.make_async_copy(source.at[0], cells.at[at], row_sems.at[0]).start()
+            pltpu.make_async_copy(source.at[1], later.at[0, at], row_sems.at[1]).start()
 
     def fetch(layer, mine, theirs, places):
-        for half in used:
-            for source, owner in ((mine, core), (theirs, other)):
-                @pl.when(owner == half)
-                def _():
-                    for at, block in places(source):
-                        pltpu.make_async_copy(block, weights.at[layer, half, at], sems.at[layer]).start()
+        for source, owner in ((mine, core), (theirs, other)):
+            for at, block in places(source):
+                pltpu.make_async_copy(block, weights.at[layer, owner, at], sems.at[layer]).start()
 
     def whole(source):
         return [(slice(None), source)]
@@ -42,12 +51,13 @@
         return [(pl.ds(pl.multiple_of(lax.rem(piece + shift, 4) * part, part), part), source.at[place])
                 for place, shift in enumerate((0, 3, 1, 2))]
 
-    for layer in range(depth):
-        step = lax.rem(layer - x + depth, depth)
-        for distance, at in ((0, 0), (1, 4), (3, 2), (2, 6)):
-            @pl.when(step == distance)
-            def _():
-                fetch(layer, pieces[at], pieces[at + 1], quarters if distance == 2 else whole)
+    if builds:
+        for layer in range(depth):
+            step = lax.rem(layer - x + depth, depth)
+            for distance, at in ((0, 0), (1, 4), (3, 2), (2, 6)):
+                @pl.when(step == distance)
+                def _():
+                    fetch(layer, pieces[at], pieces[at + 1], quarters if distance == 2 else whole)
 
     column = lax.broadcasted_iota(jnp.int32, (width, chans), 0)
 
@@ -63,18 +73,23 @@
         wide[buffer, row, :, chans:2 * chans] = normed.astype(jnp.bfloat16)
         wide[buffer, row, :, 2 * chans:] = after.astype(jnp.bfloat16)
 
-    index = min(frame, mid.shape[0] - 1)
+    if fetches:
+        pltpu.make_async_copy(cells, cells, row_sems.at[0]).wait()
     for row in range(rows):
-        stored = (top, mid, bot)[row // slab][index, row % slab]
-        cells[row] = stored
+        if fetches:
+            stored = cells[row]
+        else:
+            depth_of = inputs[0].shape[1]
+            stored = inputs[row // depth_of][0, row % depth_of]
+            cells[row] = stored
         spread(row, stored, 0)
 
     base = 0
     for layer in range(depth):
         now = layer % 2
         count = rows - 2 * layer - 2
-        waited = weights.at[layer] if first else weights.at[layer, 1]
-        pltpu.make_async_copy(waited, waited, sems.at[layer]).wait()
+        if builds:
+            pltpu.make_async_copy(weights.at[layer], weights.at[layer], sems.at[layer]).wait()
         edges = [0, count] if count <= SPLIT else [0, count // 2, count]
         for low, high in zip(edges[:-1], edges[1:]):
             size = high - low
@@ -106,15 +121,23 @@
                     if layer == depth - 1:
                         last[0, inner] = stored
         base += count
-
-
-def run_frame(frame, meta, top, mid, bot, kernels, older=None):
-    _, slab, width, chans = mid.shape
-    taps = kernels[0].shape[0]
+    if fetches:
+        pltpu.make_async_copy(later.at[0], later.at[0], row_sems.at[1]).wait()
+
+
+def run_frame(frame, meta, inputs, kernels, older=None):
+    _, _, width, chans = inputs[0].shape
+    slab = sum(one.shape[1] for one in inputs) // 3
+    fetches = inputs[0].shape[0] > 1
+    builds = isinstance(kernels, tuple)
+    if not builds:
+        kernels = (kernels,)
+    taps = kernels[0].shape[-2]
     vmem = pl.BlockSpec(memory_space=pltpu.VMEM)
     hbm = pl.BlockSpec(memory_space=pl.ANY)
     bf16 = jnp.bfloat16
     sums = DEPTH * (3 * slab - DEPTH - 1)
+    gathered = jax.ShapeDtypeStruct((DEPTH, 2, taps, chans), bf16)
     out = [
         jax.ShapeDtypeStruct((2, DEPTH, slab // 2, width, chans), bf16),
         jax.ShapeDtypeStruct((1, slab, width, chans), bf16),
@@ -124,22 +147,28 @@
         out.append(jax.ShapeDtypeStruct((sums, width, chans), jnp.float32))
     else:
         extra.append(older)
+    if builds:
+        out.append(gathered)
+    if fetches:
+        out.append(jax.ShapeDtypeStruct((1, 3 * slab, width, chans), bf16))
     work = 2 * sums * width * 9 * chans * chans * (2 - frame)
     return pl.pallas_call(
-        functools.partial(frame_kernel, frame),
+        functools.partial(frame_kernel, frame, builds, len(inputs)),
         out_shape=tuple(out),
-        in_specs=[pl.BlockSpec(memory_space=pltpu.SMEM)] + [vmem] * 3 + [hbm] * len(kernels) + [vmem] * len(extra),
+        in_specs=[pl.BlockSpec(memory_space=pltpu.SMEM)]
+        + [hbm if fetches else vmem] * len(inputs)
+        + [hbm if builds else vmem] * len(kernels) + [vmem] * len(extra),
         out_specs=(vmem,) * len(out),
         scratch_shapes=[
-            pltpu.VMEM((DEPTH, 2, taps, chans), bf16),
             pltpu.VMEM((3 * slab, width, chans), bf16),
             pltpu.VMEM((2, 3 * slab, width, 3 * chans), bf16),
             pltpu.SemaphoreType.DMA((DEPTH,)),
+            pltpu.SemaphoreType.DMA((2,)),
         ],
-        compiler_params=pltpu.CompilerParams(vmem_limit_bytes=36 * 1024 * 1024),
+        compiler_params=pltpu.CompilerParams(vmem_limit_bytes=LIMIT * 1024 * 1024),
         cost_estimate=pl.CostEstimate(flops=work, bytes_accessed=8 * 10**6, transcendentals=10**6),
         name="frame%d" % frame,
-    )(meta, top, mid, bot, *kernels, *extra)
+    )(meta, *inputs, *kernels, *extra)
 
 
 def place_kernel(meta, home, away, *refs):
@@ -228,6 +257,7 @@
     far = send(quarter, along_x(2))
 
     give = lax.dynamic_index_in_dim(frames_in, 2 * x + 1 - core, 0, keepdims=False)
+    give, quarter = lax.optimization_barrier((give, quarter))
     keep = lax.dynamic_index_in_dim(frames_in, 2 * x + core, 0, keepdims=False)
     got = send(give, sibling)
     mine = lax.dynamic_index_in_dim(own, core, 0, keepdims=False)
@@ -235,11 +265,11 @@
     far, mine, got = lax.optimization_barrier((far, mine, got))
     left_mine = send(mine, along_x(1))
     right_mine = send(mine, along_x(-1))
+    parts = (far, send(far, along_y(1)), send(far, along_y(-1)), send(far, two_along_y))
     mid = jnp.where(core == 0, jnp.concatenate([keep, got], 1), jnp.concatenate([got, keep], 1))
     top = send(mid, next_chip(1))
     bot = send(mid, next_chip(-1))
 
-    parts = (far, send(far, along_y(1)), send(far, along_y(-1)), send(far, two_along_y))
     *parts, top, bot = lax.optimization_barrier((*parts, top, bot))
     far_mine = jnp.stack(parts)
     far_theirs = send(far_mine, sibling)
@@ -247,19 +277,19 @@
     right_theirs = send(right_mine, sibling)
     kernels = (mine, theirs, left_mine, left_theirs, right_mine, right_theirs, far_mine, far_theirs)
 
-    kept, reached, older = run_frame(0, meta, top, mid, bot, kernels)
+    kept, reached, older, weights, later = run_frame(0, meta, (top, mid, bot), kernels)
     mid_0 = send(reached, hop)
     first = [kept]
-    kept, reached = run_frame(1, meta, top, mid, bot, kernels, older)
+    kept, reached = run_frame(1, meta, (later,), weights, older)
     first.append(kept)
     mid_1 = send(reached, hop)
 
     second = []
     top, bot = send(mid_0, next_chip(1), is_upper), send(mid_0, next_chip(-1), is_upper)
-    kept, _, older = run_frame(0, meta, top, mid_0, bot, kernels)
+    kept, _, older, weights = run_frame(0, meta, (top, mid_0, bot), kernels)
     second.append(kept)
     top, bot = send(mid_1, next_chip(1), is_upper), send(mid_1, next_chip(-1), is_upper)
-    kept, _ = run_frame(1, meta, top, mid_1, bot, kernels, older)
+    kept, _ = run_frame(1, meta, (top, mid_1, bot), weights, older)
     second.append(kept)
 
     first, second = jnp.stack(first, 2), jnp.stack(second, 2)

time: 151 us -> 157 us (1.040)
  Pallas kernels: 31.9 us -> 43.3 us
  waiting for transfers between devices: 38.2 us -> 35.6 us
  local copies, waits for them, and re-layouts: 9.79 us -> 8.02 us
    pallas_call x4, Pallas kernels: 30.3 us -> 41.7 us  [run_frame(): pl.pallas_call(functools.partial(frame_kernel, frame, builds, len(inputs)...]
    unnamed x22 -> x6, local copies, waits for them, and re-layouts: 5.79 us -> 2.99 us
    ppermute x22, waiting for transfers between devices: 38.2 us -> 35.6 us  [send(): return lax.ppermute(array, ('section', 'rows'), route(move, keep))]
  transfers between devices with their start and end apart: 22 -> 22, of which waited for: 12 -> 13; matrix products, arithmetic and copies ran while one was open for 3% -> 3% of each run, Pallas kernels for 10% -> 13%
where the time goes in v5:
time: 157 us; the launch traced here: 156 us
  starting transfers between devices  66.8 us (43%)
  Pallas kernels  43.3 us (28%)
  waiting for transfers between devices  35.6 us (23%)
  local copies, waits for them, and re-layouts  8.02 us (5%)
    ppermute x22, starting transfers between devices, send(): return lax.ppermute(array, ('section', 'rows'), route(move, keep))  66.8 us
    pallas_call x4, Pallas kernels, run_frame(): pl.pallas_call(functools.partial(frame_kernel, frame, builds, len(inputs)...  41.7 us
    ppermute x22, waiting for transfers between devices, send(): return lax.ppermute(array, ('section', 'rows'), route(move, keep))  35.6 us
  transfers between devices with their start and end apart: 22, of which 13 were waited for; matrix products, arithmetic and copies ran while one was open for 3% of the time, Pallas kernels for 13%

profile of v5, /device:TPU:327, one launch (start us, length us, event | category | flops | bytes accessed | tf_op | source)
XLA Modules:
  0.0 155.7 jit_solution(11261032841479404866)
XLA Ops:
  1.0 3.0 %collective-permute-start = (bf16[576,256]{1,0:T(8,128)(2,1)S(1)}, bf16[576,256]{1,0:T(8,128)(2,1)S(1)}, u32[]{:S(2)}, u32[]{:S(2)}) collective-permute-start(bf16[576,256]{1,0:T(8,128)(2,1)S(1)} %dynamic-slice_bitcast_fusion.2), channel_id=1, source_target_pairs={{0,128},{1,129},{2,130},{3,131},{4,132},{5,133},{6,134},{7,135},{8... | collective-permute-start | bytes 884744 | tf_op jit(solution)/shard_map/ppermute | solution.py:219
  5.0 2.9 %collective-permute-start.1 = (bf16[2,2,64,256]{3,2,1,0:T(8,128)(2,1)S(1)}, bf16[2,2,64,256]{3,2,1,0:T(8,128)(2,1)S(1)}, u32[]{:S(2)}, u32[]{:S(2)}) collective-permute-start(bf16[2,2,64,256]{3,2,1,0:T(8,128)(2,1)S(1)} %get-tuple-element.26), channel_id=1, source_target_pairs={{0,1},{1,0},{2,3},{3,2},{4,5},{5,4},{6,7},{7,6},{8,9},{9,8},{10,11... | collective-permute-start | bytes 393224 | tf_op jit(solution)/shard_map/ppermute | solution.py:219
  7.9 2.8 %dynamic-slice_bitcast_fusion = (bf16[2304,256]{1,0:T(8,128)(2,1)}, bf16[2304,256]{1,0:T(8,128)(2,1)S(1)}) fusion(bf16[2,2304,256]{2,1,0:T(8,128)(2,1)} %bitcast.41, s32[]{:T(128)S(6)} %select_n.97, s32[]{:T(128)S(6)} %select_n.91), kind=kLoop, calls=%fused_computation.1 | loop fusion | bytes 4718600 | tf_op jit(solution)/shard_map/jit(dynamic_index_in_dim)/squeeze | solution.py:264
  12.3 2.4 %collective-permute-start.9 = (bf16[2304,256]{1,0:T(8,128)(2,1)S(1)}, bf16[2304,256]{1,0:T(8,128)(2,1)}, u32[]{:S(2)}, u32[]{:S(2)}) collective-permute-start(bf16[2304,256]{1,0:T(8,128)(2,1)S(1)} %get-tuple-element.31.refs_3_), channel_id=1, source_target_pairs={{0,192},{1,193},{2,194},{3,195},{4,196},{5,197},{6,198},{7,199},{8... | collective-permute-start | bytes 3538952 | tf_op jit(solution)/shard_map/ppermute | solution.py:219
  14.7 4.0 %collective-permute-start.7 = (bf16[2304,256]{1,0:T(8,128)(2,1)S(1)}, bf16[2304,256]{1,0:T(8,128)(2,1)}, u32[]{:S(2)}, u32[]{:S(2)}) collective-permute-start(bf16[2304,256]{1,0:T(8,128)(2,1)S(1)} %get-tuple-element.31.refs_3_), channel_id=1, source_target_pairs={{0,64},{1,65},{2,66},{3,67},{4,68},{5,69},{6,70},{7,71},{8,72},{9,... | collective-permute-start | bytes 3538952 | tf_op jit(solution)/shard_map/ppermute | solution.py:219
  18.8 5.1 %collective-permute-start.6 = (bf16[2,4,64,256]{3,2,1,0:T(8,128)(2,1)S(1)}, bf16[2,4,64,256]{3,2,1,0:T(8,128)(2,1)S(1)}, u32[]{:S(2)}, u32[]{:S(2)}) collective-permute-start(bf16[2,4,64,256]{3,2,1,0:T(8,128)(2,1)S(1)} %maximum_select_fusion.1.refs_1_), channel_id=1, source_target_pairs={{2,0},{3,1},{4,2},{5,3},{6,4},{7,5},{8,6},{9,7},{10,8},{11,9},{12,... | collective-permute-start | bytes 786440 | tf_op jit(solution)/shard_map/ppermute | solution.py:219
  25.8 2.5 %collective-permute-start.4 = (bf16[576,256]{1,0:T(8,128)(2,1)S(1)}, bf16[576,256]{1,0:T(8,128)(2,1)S(1)}, u32[]{:S(2)}, u32[]{:S(2)}) collective-permute-start(bf16[576,256]{1,0:T(8,128)(2,1)S(1)} %collective-permute-done), channel_id=1, source_target_pairs={{0,4},{1,5},{2,14},{3,15},{4,8},{5,9},{6,2},{7,3},{8,12},{9,13},{1... | collective-permute-start | bytes 884744 | tf_op jit(solution)/shard_map/ppermute | solution.py:219
  28.3 5.2 %collective-permute-start.3 = (bf16[576,256]{1,0:T(8,128)(2,1)S(1)}, bf16[576,256]{1,0:T(8,128)(2,1)S(1)}, u32[]{:S(2)}, u32[]{:S(2)}) collective-permute-start(bf16[576,256]{1,0:T(8,128)(2,1)S(1)} %collective-permute-done), channel_id=1, source_target_pairs={{0,14},{1,15},{2,0},{3,1},{4,2},{5,3},{6,4},{7,5},{8,6},{9,7},{10,... | collective-permute-start | bytes 884744 | tf_op jit(solution)/shard_map/ppermute | solution.py:219
  33.6 2.5 %collective-permute-done.5.refs_0_ = bf16[2,4,64,256]{3,2,1,0:T(8,128)(2,1)S(1)} collective-permute-done((bf16[2,4,64,256]{3,2,1,0:T(8,128)(2,1)S(1)}, bf16[2,4,64,256]{3,2,1,0:T(8,128)(2,1)S(1)}, u32[]{:S(2)}, u32[]{:S(2)}) %collective-permute-start.5) | collective-permute-done | bytes 262176 | tf_op jit(solution)/shard_map/ppermute | solution.py:219
  38.8 5.6 %collective-permute-done.3 = bf16[576,256]{1,0:T(8,128)(2,1)S(1)} collective-permute-done((bf16[576,256]{1,0:T(8,128)(2,1)S(1)}, bf16[576,256]{1,0:T(8,128)(2,1)S(1)}, u32[]{:S(2)}, u32[]{:S(2)}) %collective-permute-start.3) | collective-permute-done | bytes 294944 | tf_op jit(solution)/shard_map/ppermute | solution.py:219
  46.9 10.1 %collective-permute-start.11 = (bf16[4,576,256]{2,1,0:T(8,128)(2,1)}, bf16[4,576,256]{2,1,0:T(8,128)(2,1)}, u32[]{:S(2)}, u32[]{:S(2)}) collective-permute-start(bf16[4,576,256]{2,1,0:T(8,128)(2,1)} %pad_maximum_fusion.refs_9_), channel_id=1, source_target_pairs={{0,1},{1,0},{2,3},{3,2},{4,5},{5,4},{6,7},{7,6},{8,9},{9,8},{10,11... | collective-permute-start | bytes 3538952 | tf_op jit(solution)/shard_map/ppermute | solution.py:219
  59.0 2.4 %collective-permute-start.8 = (bf16[2304,256]{1,0:T(8,128)(2,1)}, bf16[2304,256]{1,0:T(8,128)(2,1)}, u32[]{:S(2)}, u32[]{:S(2)}) collective-permute-start(bf16[2304,256]{1,0:T(8,128)(2,1)} %collective-permute-done.7.refs_5_), channel_id=1, source_target_pairs={{0,1},{1,0},{2,3},{3,2},{4,5},{5,4},{6,7},{7,6},{8,9},{9,8},{10,11... | collective-permute-start | bytes 3538952 | tf_op jit(solution)/shard_map/ppermute | solution.py:219
  64.2 12.9 %frame0.2 = (bf16[2,4,2,64,256]{4,3,2,1,0:T(8,128)(2,1)S(1)}, bf16[1,4,64,256]{3,2,1,0:T(8,128)(2,1)S(1)}, f32[28,64,256]{2,1,0:T(8,128)}, bf16[4,2,2304,256]{3,2,1,0:T(8,128)(2,1)}, bf16[1,12,64,256]{3,2,1,0:T(8,128)(2,1)S(1)}) custom-call(s32[5]{0:T(128)S(1)} %stack.67.meta, bf16[2,4,64,256]{3,2,1,0:T(8,128)(2,1)S(1)} %collective-permute-done.5.refs_0_, ...), custom_call_target="tpu_custom_call" | custom-call | flops 4227858432 | bytes 8000000 | tf_op jit(solution)/shard_map/frame0/pallas_call | solution.py:155
  79.9 8.2 %frame1.2 = (bf16[2,4,2,64,256]{4,3,2,1,0:T(8,128)(2,1)S(1)}, bf16[1,4,64,256]{3,2,1,0:T(8,128)(2,1)}) custom-call(s32[5]{0:T(128)S(1)} %stack.67.meta, bf16[1,12,64,256]{3,2,1,0:T(8,128)(2,1)S(1)} %get-tuple-element.37.refs_0_, bf16[4,2,2304,256]{3,2,1,0:T(8,128)(2,1)} %get-tuple-element.38.refs_1_, f32[28,64,256]{2,1,0:T(8,128)S(1)} %copy-done.1), custom_call_target="tpu_custom_call" | custom-call | flops 2113929216 | bytes 8000000 | tf_op jit(solution)/shard_map/frame1/pallas_call | solution.py:155
  92.8 3.4 %collective-permute-start.13 = (bf16[1,4,64,256]{3,2,1,0:T(8,128)(2,1)}, bf16[1,4,64,256]{3,2,1,0:T(8,128)(2,1)}, u32[]{:S(2)}, u32[]{:S(2)}) collective-permute-start(bf16[1,4,64,256]{3,2,1,0:T(8,128)(2,1)} %collective-permute-done.12.refs_1_), channel_id=1, source_target_pairs={{256,258},{257,259},{258,260},{259,261},{260,262},{261,263},{262,2... | collective-permute-start | bytes 393224 | tf_op jit(solution)/shard_map/ppermute | solution.py:219
  96.2 6.4 %collective-permute-done.15.refs_1_ = bf16[1,4,64,256]{3,2,1,0:T(8,128)(2,1)S(1)} collective-permute-done((bf16[1,4,64,256]{3,2,1,0:T(8,128)(2,1)}, bf16[1,4,64,256]{3,2,1,0:T(8,128)(2,1)S(1)}, u32[]{:S(2)}, u32[]{:S(2)}) %collective-permute-start.15) | collective-permute-done | bytes 131104 | tf_op jit(solution)/shard_map/ppermute | solution.py:219
  104.5 3.4 %collective-permute-start.16 = (bf16[1,4,64,256]{3,2,1,0:T(8,128)(2,1)S(1)}, bf16[1,4,64,256]{3,2,1,0:T(8,128)(2,1)S(1)}, u32[]{:S(2)}, u32[]{:S(2)}) collective-permute-start(bf16[1,4,64,256]{3,2,1,0:T(8,128)(2,1)S(1)} %collective-permute-done.15.refs_1_), channel_id=1, source_target_pairs={{256,258},{257,259},{258,260},{259,261},{260,262},{261,263},{262,2... | collective-permute-start | bytes 393224 | tf_op jit(solution)/shard_map/ppermute | solution.py:219
  107.9 12.6 %frame0.3 = (bf16[2,4,2,64,256]{4,3,2,1,0:T(8,128)(2,1)S(1)}, bf16[1,4,64,256]{3,2,1,0:T(8,128)(2,1)}, f32[28,64,256]{2,1,0:T(8,128)}, bf16[4,2,2304,256]{3,2,1,0:T(8,128)(2,1)}) custom-call(s32[5]{0:T(128)S(1)} %stack.67.meta, bf16[1,4,64,256]{3,2,1,0:T(8,128)(2,1)} %collective-permute-done.13.refs_0_, ...), custom_call_target="tpu_custom_call" | custom-call | flops 4227858432 | bytes 8000000 | tf_op jit(solution)/shard_map/frame0/pallas_call | solution.py:155
  122.0 8.1 %frame1.3 = (bf16[2,4,2,64,256]{4,3,2,1,0:T(8,128)(2,1)S(1)}, bf16[1,4,64,256]{3,2,1,0:T(8,128)(2,1)}) custom-call(s32[5]{0:T(128)S(1)} %stack.67.meta, bf16[1,4,64,256]{3,2,1,0:T(8,128)(2,1)S(1)} %collective-permute-done.16.refs_0_, bf16[1,4,64,256]{3,2,1,0:T(8,128)(2,1)S(1)} %collective-permute-done.15.refs_1_, ...), custom_call_target="tpu_custom_call" | custom-call | flops 2113929216 | bytes 8000000 | tf_op jit(solution)/shard_map/frame1/pallas_call | solution.py:155
  130.4 2.9 %collective-permute-start.18 = (bf16[4,2,2,64,256]{4,3,2,1,0:T(8,128)(2,1)S(1)}, bf16[4,2,2,64,256]{4,3,2,1,0:T(8,128)(2,1)S(1)}, u32[]{:S(2)}, u32[]{:S(2)}) collective-permute-start(bf16[4,2,2,64,256]{4,3,2,1,0:T(8,128)(2,1)S(1)} %get-tuple-element.49), channel_id=1, source_target_pairs={{0,1},{1,0},{2,3},{3,2},{4,5},{5,4},{6,7},{7,6},{8,9},{9,8},{10,11... | collective-permute-start | bytes 1572872 | tf_op jit(solution)/shard_map/ppermute | solution.py:219
  136.9 3.0 %collective-permute-start.20 = (bf16[2,2,2,64,256]{4,3,2,1,0:T(8,128)(2,1)S(1)}, bf16[2,2,2,64,256]{4,3,2,1,0:T(8,128)(2,1)S(1)}, u32[]{:S(2)}, u32[]{:S(2)}) collective-permute-start(bf16[2,2,2,64,256]{4,3,2,1,0:T(8,128)(2,1)S(1)} %pad_maximum_fusion.2), channel_id=1, source_target_pairs={{0,128},{1,129},{2,130},{3,131},{4,132},{5,133},{6,134},{7,135},{8... | collective-permute-start | bytes 786440 | tf_op jit(solution)/shard_map/ppermute | solution.py:219
  139.9 2.3 %collective-permute-start.21 = (bf16[2,2,2,64,256]{4,3,2,1,0:T(8,128)(2,1)S(1)}, bf16[2,2,2,64,256]{4,3,2,1,0:T(8,128)(2,1)S(1)}, u32[]{:S(2)}, u32[]{:S(2)}) collective-permute-start(bf16[2,2,2,64,256]{4,3,2,1,0:T(8,128)(2,1)S(1)} %pad_maximum_fusion.3), channel_id=1, source_target_pairs={{0,192},{1,193},{2,194},{3,195},{4,196},{5,197},{6,198},{7,199},{8... | collective-permute-start | bytes 786440 | tf_op jit(solution)/shard_map/ppermute | solution.py:219
  144.3 3.5 %collective-permute-done.20.refs_1_ = bf16[2,2,2,64,256]{4,3,2,1,0:T(8,128)(2,1)S(1)} collective-permute-done((bf16[2,2,2,64,256]{4,3,2,1,0:T(8,128)(2,1)S(1)}, bf16[2,2,2,64,256]{4,3,2,1,0:T(8,128)(2,1)S(1)}, u32[]{:S(2)}, u32[]{:S(2)}) %collective-permute-start.20) | collective-permute-done | bytes 262176 | tf_op jit(solution)/shard_map/ppermute | solution.py:219
  147.8 6.3 %collective-permute-done.21.refs_2_ = bf16[2,2,2,64,256]{4,3,2,1,0:T(8,128)(2,1)S(1)} collective-permute-done((bf16[2,2,2,64,256]{4,3,2,1,0:T(8,128)(2,1)S(1)}, bf16[2,2,2,64,256]{4,3,2,1,0:T(8,128)(2,1)S(1)}, u32[]{:S(2)}, u32[]{:S(2)}) %collective-permute-start.21) | collective-permute-done | bytes 262176 | tf_op jit(solution)/shard_map/ppermute | solution.py:219
  (44 shorter events, 33.6 us)
Async XLA Ops:
  1.0 11.3 %collective-permute-start = (bf16[576,256]{1,0:T(8,128)(2,1)S(1)}, bf16[576,256]{1,0:T(8,128)(2,1)S(1)}, u32[]{:S(2)}, u32[]{:S(2)}) collective-permute-start(bf16[576,256]{1,0:T(8,128)(2,1)S(1)} %dynamic-slice_bitcast_fusion.2), channel_id=1, source_target_pairs={{0,128},{1,129},{2,130},{3,131},{4,132},{5,133},{6,134},{7,135},{8... | collective-permute-start | bytes 884744 | tf_op jit(solution)/shard_map/ppermute | solution.py:219
  5.0 5.7 %collective-permute-start.1 = (bf16[2,2,64,256]{3,2,1,0:T(8,128)(2,1)S(1)}, bf16[2,2,64,256]{3,2,1,0:T(8,128)(2,1)S(1)}, u32[]{:S(2)}, u32[]{:S(2)}) collective-permute-start(bf16[2,2,64,256]{3,2,1,0:T(8,128)(2,1)S(1)} %get-tuple-element.26), channel_id=1, source_target_pairs={{0,1},{1,0},{2,3},{3,2},{4,5},{5,4},{6,7},{7,6},{8,9},{9,8},{10,11... | collective-permute-start | bytes 393224 | tf_op jit(solution)/shard_map/ppermute | solution.py:219
  12.3 44.7 %collective-permute-start.9 = (bf16[2304,256]{1,0:T(8,128)(2,1)S(1)}, bf16[2304,256]{1,0:T(8,128)(2,1)}, u32[]{:S(2)}, u32[]{:S(2)}) collective-permute-start(bf16[2304,256]{1,0:T(8,128)(2,1)S(1)} %get-tuple-element.31.refs_3_), channel_id=1, source_target_pairs={{0,192},{1,193},{2,194},{3,195},{4,196},{5,197},{6,198},{7,199},{8... | collective-permute-start | bytes 3538952 | tf_op jit(solution)/shard_map/ppermute | solution.py:219
  14.7 44.2 %collective-permute-start.7 = (bf16[2304,256]{1,0:T(8,128)(2,1)S(1)}, bf16[2304,256]{1,0:T(8,128)(2,1)}, u32[]{:S(2)}, u32[]{:S(2)}) collective-permute-start(bf16[2304,256]{1,0:T(8,128)(2,1)S(1)} %get-tuple-element.31.refs_3_), channel_id=1, source_target_pairs={{0,64},{1,65},{2,66},{3,67},{4,68},{5,69},{6,70},{7,71},{8,72},{9,... | collective-permute-start | bytes 3538952 | tf_op jit(solution)/shard_map/ppermute | solution.py:219
  18.8 9.5 %collective-permute-start.6 = (bf16[2,4,64,256]{3,2,1,0:T(8,128)(2,1)S(1)}, bf16[2,4,64,256]{3,2,1,0:T(8,128)(2,1)S(1)}, u32[]{:S(2)}, u32[]{:S(2)}) collective-permute-start(bf16[2,4,64,256]{3,2,1,0:T(8,128)(2,1)S(1)} %maximum_select_fusion.1.refs_1_), channel_id=1, source_target_pairs={{2,0},{3,1},{4,2},{5,3},{6,4},{7,5},{8,6},{9,7},{10,8},{11,9},{12,... | collective-permute-start | bytes 786440 | tf_op jit(solution)/shard_map/ppermute | solution.py:219
  23.9 12.2 %collective-permute-start.5 = (bf16[2,4,64,256]{3,2,1,0:T(8,128)(2,1)S(1)}, bf16[2,4,64,256]{3,2,1,0:T(8,128)(2,1)S(1)}, u32[]{:S(2)}, u32[]{:S(2)}) collective-permute-start(bf16[2,4,64,256]{3,2,1,0:T(8,128)(2,1)S(1)} %maximum_select_fusion.1.refs_1_), channel_id=1, source_target_pairs={{0,2},{1,3},{2,4},{3,5},{4,6},{5,7},{6,8},{7,9},{8,10},{9,11},{10,... | collective-permute-start | bytes 786440 | tf_op jit(solution)/shard_map/ppermute | solution.py:219
  25.8 12.9 %collective-permute-start.4 = (bf16[576,256]{1,0:T(8,128)(2,1)S(1)}, bf16[576,256]{1,0:T(8,128)(2,1)S(1)}, u32[]{:S(2)}, u32[]{:S(2)}) collective-permute-start(bf16[576,256]{1,0:T(8,128)(2,1)S(1)} %collective-permute-done), channel_id=1, source_target_pairs={{0,4},{1,5},{2,14},{3,15},{4,8},{5,9},{6,2},{7,3},{8,12},{9,13},{1... | collective-permute-start | bytes 884744 | tf_op jit(solution)/shard_map/ppermute | solution.py:219
  28.3 16.1 %collective-permute-start.3 = (bf16[576,256]{1,0:T(8,128)(2,1)S(1)}, bf16[576,256]{1,0:T(8,128)(2,1)S(1)}, u32[]{:S(2)}, u32[]{:S(2)}) collective-permute-start(bf16[576,256]{1,0:T(8,128)(2,1)S(1)} %collective-permute-done), channel_id=1, source_target_pairs={{0,14},{1,15},{2,0},{3,1},{4,2},{5,3},{6,4},{7,5},{8,6},{9,7},{10,... | collective-permute-start | bytes 884744 | tf_op jit(solution)/shard_map/ppermute | solution.py:219
  36.1 9.6 %collective-permute-start.2 = (bf16[576,256]{1,0:T(8,128)(2,1)S(1)}, bf16[576,256]{1,0:T(8,128)(2,1)S(1)}, u32[]{:S(2)}, u32[]{:S(2)}) collective-permute-start(bf16[576,256]{1,0:T(8,128)(2,1)S(1)} %collective-permute-done), channel_id=1, source_target_pairs={{0,2},{1,3},{2,4},{3,5},{4,6},{5,7},{6,8},{7,9},{8,10},{9,11},{10,... | collective-permute-start | bytes 884744 | tf_op jit(solution)/shard_map/ppermute | solution.py:219
  46.9 14.6 %collective-permute-start.11 = (bf16[4,576,256]{2,1,0:T(8,128)(2,1)}, bf16[4,576,256]{2,1,0:T(8,128)(2,1)}, u32[]{:S(2)}, u32[]{:S(2)}) collective-permute-start(bf16[4,576,256]{2,1,0:T(8,128)(2,1)} %pad_maximum_fusion.refs_9_), channel_id=1, source_target_pairs={{0,1},{1,0},{2,3},{3,2},{4,5},{5,4},{6,7},{7,6},{8,9},{9,8},{10,11... | collective-permute-start | bytes 3538952 | tf_op jit(solution)/shard_map/ppermute | solution.py:219
  57.0 5.1 %collective-permute-start.10 = (bf16[2304,256]{1,0:T(8,128)(2,1)}, bf16[2304,256]{1,0:T(8,128)(2,1)}, u32[]{:S(2)}, u32[]{:S(2)}) collective-permute-start(bf16[2304,256]{1,0:T(8,128)(2,1)} %collective-permute-done.9.refs_7_), channel_id=1, source_target_pairs={{0,1},{1,0},{2,3},{3,2},{4,5},{5,4},{6,7},{7,6},{8,9},{9,8},{10,11... | collective-permute-start | bytes 3538952 | tf_op jit(solution)/shard_map/ppermute | solution.py:219
  59.0 5.2 %collective-permute-start.8 = (bf16[2304,256]{1,0:T(8,128)(2,1)}, bf16[2304,256]{1,0:T(8,128)(2,1)}, u32[]{:S(2)}, u32[]{:S(2)}) collective-permute-start(bf16[2304,256]{1,0:T(8,128)(2,1)} %collective-permute-done.7.refs_5_), channel_id=1, source_target_pairs={{0,1},{1,0},{2,3},{3,2},{4,5},{5,4},{6,7},{7,6},{8,9},{9,8},{10,11... | collective-permute-start | bytes 3538952 | tf_op jit(solution)/shard_map/ppermute | solution.py:219
  77.1 13.8 %collective-permute-start.12 = (bf16[1,4,64,256]{3,2,1,0:T(8,128)(2,1)S(1)}, bf16[1,4,64,256]{3,2,1,0:T(8,128)(2,1)}, u32[]{:S(2)}, u32[]{:S(2)}) collective-permute-start(bf16[1,4,64,256]{3,2,1,0:T(8,128)(2,1)S(1)} %get-tuple-element.41), channel_id=1, source_target_pairs={{0,256},{1,257},{2,258},{3,259},{4,260},{5,261},{6,262},{7,263},{8... | collective-permute-start | bytes 393224 | tf_op jit(solution)/shard_map/ppermute | solution.py:219
  78.4 1.5 copy-start.1
  79.9 28.0 %copy-start.2 = (bf16[2304,256]{1,0:T(8,128)(2,1)S(1)}, bf16[2304,256]{1,0:T(8,128)(2,1)}, u32[]{:S(2)}) copy-start(bf16[2304,256]{1,0:T(8,128)(2,1)} %get-tuple-element.47.refs_4_) | copy-start | bytes 3538948
  88.1 14.5 %collective-permute-start.15 = (bf16[1,4,64,256]{3,2,1,0:T(8,128)(2,1)}, bf16[1,4,64,256]{3,2,1,0:T(8,128)(2,1)S(1)}, u32[]{:S(2)}, u32[]{:S(2)}) collective-permute-start(bf16[1,4,64,256]{3,2,1,0:T(8,128)(2,1)} %get-tuple-element.43), channel_id=1, source_target_pairs={{0,256},{1,257},{2,258},{3,259},{4,260},{5,261},{6,262},{7,263},{8... | collective-permute-start | bytes 393224 | tf_op jit(solution)/shard_map/ppermute | solution.py:219
  90.9 17.0 %collective-permute-start.14 = (bf16[1,4,64,256]{3,2,1,0:T(8,128)(2,1)}, bf16[1,4,64,256]{3,2,1,0:T(8,128)(2,1)}, u32[]{:S(2)}, u32[]{:S(2)}) collective-permute-start(bf16[1,4,64,256]{3,2,1,0:T(8,128)(2,1)} %collective-permute-done.12.refs_1_), channel_id=1, source_target_pairs={{258,256},{259,257},{260,258},{261,259},{262,260},{263,261},{264,2... | collective-permute-start | bytes 393224 | tf_op jit(solution)/shard_map/ppermute | solution.py:219
  92.8 15.1 %collective-permute-start.13 = (bf16[1,4,64,256]{3,2,1,0:T(8,128)(2,1)}, bf16[1,4,64,256]{3,2,1,0:T(8,128)(2,1)}, u32[]{:S(2)}, u32[]{:S(2)}) collective-permute-start(bf16[1,4,64,256]{3,2,1,0:T(8,128)(2,1)} %collective-permute-done.12.refs_1_), channel_id=1, source_target_pairs={{256,258},{257,259},{258,260},{259,261},{260,262},{261,263},{262,2... | collective-permute-start | bytes 393224 | tf_op jit(solution)/shard_map/ppermute | solution.py:219
  102.6 17.9 %collective-permute-start.17 = (bf16[1,4,64,256]{3,2,1,0:T(8,128)(2,1)S(1)}, bf16[1,4,64,256]{3,2,1,0:T(8,128)(2,1)S(1)}, u32[]{:S(2)}, u32[]{:S(2)}) collective-permute-start(bf16[1,4,64,256]{3,2,1,0:T(8,128)(2,1)S(1)} %collective-permute-done.15.refs_1_), channel_id=1, source_target_pairs={{258,256},{259,257},{260,258},{261,259},{262,260},{263,261},{264,2... | collective-permute-start | bytes 393224 | tf_op jit(solution)/shard_map/ppermute | solution.py:219
  104.5 16.0 %collective-permute-start.16 = (bf16[1,4,64,256]{3,2,1,0:T(8,128)(2,1)S(1)}, bf16[1,4,64,256]{3,2,1,0:T(8,128)(2,1)S(1)}, u32[]{:S(2)}, u32[]{:S(2)}) collective-permute-start(bf16[1,4,64,256]{3,2,1,0:T(8,128)(2,1)S(1)} %collective-permute-done.15.refs_1_), channel_id=1, source_target_pairs={{256,258},{257,259},{258,260},{259,261},{260,262},{261,263},{262,2... | collective-permute-start | bytes 393224 | tf_op jit(solution)/shard_map/ppermute | solution.py:219
  130.4 4.5 %collective-permute-start.18 = (bf16[4,2,2,64,256]{4,3,2,1,0:T(8,128)(2,1)S(1)}, bf16[4,2,2,64,256]{4,3,2,1,0:T(8,128)(2,1)S(1)}, u32[]{:S(2)}, u32[]{:S(2)}) collective-permute-start(bf16[4,2,2,64,256]{4,3,2,1,0:T(8,128)(2,1)S(1)} %get-tuple-element.49), channel_id=1, source_target_pairs={{0,1},{1,0},{2,3},{3,2},{4,5},{5,4},{6,7},{7,6},{8,9},{9,8},{10,11... | collective-permute-start | bytes 1572872 | tf_op jit(solution)/shard_map/ppermute | solution.py:219
  134.9 9.4 %collective-permute-start.19 = (bf16[2,2,2,64,256]{4,3,2,1,0:T(8,128)(2,1)S(1)}, bf16[2,2,2,64,256]{4,3,2,1,0:T(8,128)(2,1)S(1)}, u32[]{:S(2)}, u32[]{:S(2)}) collective-permute-start(bf16[2,2,2,64,256]{4,3,2,1,0:T(8,128)(2,1)S(1)} %pad_maximum_fusion.1), channel_id=1, source_target_pairs={{0,64},{1,65},{2,66},{3,67},{4,68},{5,69},{6,70},{7,71},{8,72},{9,... | collective-permute-start | bytes 786440 | tf_op jit(solution)/shard_map/ppermute | solution.py:219
  136.9 11.0 %collective-permute-start.20 = (bf16[2,2,2,64,256]{4,3,2,1,0:T(8,128)(2,1)S(1)}, bf16[2,2,2,64,256]{4,3,2,1,0:T(8,128)(2,1)S(1)}, u32[]{:S(2)}, u32[]{:S(2)}) collective-permute-start(bf16[2,2,2,64,256]{4,3,2,1,0:T(8,128)(2,1)S(1)} %pad_maximum_fusion.2), channel_id=1, source_target_pairs={{0,128},{1,129},{2,130},{3,131},{4,132},{5,133},{6,134},{7,135},{8... | collective-permute-start | bytes 786440 | tf_op jit(solution)/shard_map/ppermute | solution.py:219
  139.9 14.2 %collective-permute-start.21 = (bf16[2,2,2,64,256]{4,3,2,1,0:T(8,128)(2,1)S(1)}, bf16[2,2,2,64,256]{4,3,2,1,0:T(8,128)(2,1)S(1)}, u32[]{:S(2)}, u32[]{:S(2)}) collective-permute-start(bf16[2,2,2,64,256]{4,3,2,1,0:T(8,128)(2,1)S(1)} %pad_maximum_fusion.3), channel_id=1, source_target_pairs={{0,192},{1,193},{2,194},{3,195},{4,196},{5,197},{6,198},{7,199},{8... | collective-permute-start | bytes 786440 | tf_op jit(solution)/shard_map/ppermute | solution.py:219
  (1 other events, 1.5 us)

commit v6 on v5

--- a/solution.py
+++ b/solution.py
@@ -9,7 +9,7 @@
 
 DEPTH = 4
 SPLIT = 4
-LIMIT = 50
+LIMIT = 24
 
 
 def frame_kernel(frame, builds, slabs, meta, *refs):
@@ -257,27 +257,26 @@
     far = send(quarter, along_x(2))
 
     give = lax.dynamic_index_in_dim(frames_in, 2 * x + 1 - core, 0, keepdims=False)
-    give, quarter = lax.optimization_barrier((give, quarter))
     keep = lax.dynamic_index_in_dim(frames_in, 2 * x + core, 0, keepdims=False)
     got = send(give, sibling)
     mine = lax.dynamic_index_in_dim(own, core, 0, keepdims=False)
     theirs = lax.dynamic_index_in_dim(own, 1 - core, 0, keepdims=False)
-    far, mine, got = lax.optimization_barrier((far, mine, got))
+    mid = jnp.where(core == 0, jnp.concatenate([keep, got], 1), jnp.concatenate([got, keep], 1))
+    top = send(mid, next_chip(1))
+    bot = send(mid, next_chip(-1))
+
+    far, mine, top, bot = lax.optimization_barrier((far, mine, top, bot))
     left_mine = send(mine, along_x(1))
     right_mine = send(mine, along_x(-1))
     parts = (far, send(far, along_y(1)), send(far, along_y(-1)), send(far, two_along_y))
-    mid = jnp.where(core == 0, jnp.concatenate([keep, got], 1), jnp.concatenate([got, keep], 1))
-    top = send(mid, next_chip(1))
-    bot = send(mid, next_chip(-1))
-
-    *parts, top, bot = lax.optimization_barrier((*parts, top, bot))
     far_mine = jnp.stack(parts)
     far_theirs = send(far_mine, sibling)
     left_theirs = send(left_mine, sibling)
     right_theirs = send(right_mine, sibling)
     kernels = (mine, theirs, left_mine, left_theirs, right_mine, right_theirs, far_mine, far_theirs)
 
-    kept, reached, older, weights, later = run_frame(0, meta, (top, mid, bot), kernels)
+    rows = tuple(pltpu.with_memory_space_constraint(one, pltpu.HBM) for one in (top, mid, bot))
+    kept, reached, older, weights, later = run_frame(0, meta, rows, kernels)
     mid_0 = send(reached, hop)
     first = [kept]
     kept, reached = run_frame(1, meta, (later,), weights, older)

time: 157 us -> 140 us (0.89)
  Pallas kernels: 43.3 us -> 28.8 us
  waiting for transfers between devices: 35.6 us -> 43.9 us
  starting transfers between devices: 66.8 us -> 60 us
  local copies, waits for them, and re-layouts: 8.02 us -> 4.82 us
    pallas_call x4, Pallas kernels: 41.7 us -> 27.2 us  [run_frame(): pl.pallas_call(functools.partial(frame_kernel, frame, builds, len(inputs)...]
    ppermute x22, waiting for transfers between devices: 35.6 us -> 43.9 us  [send(): return lax.ppermute(array, ('section', 'rows'), route(move, keep))]
    ppermute x22, starting transfers between devices: 66.8 us -> 60 us  [send(): return lax.ppermute(array, ('section', 'rows'), route(move, keep))]
    unnamed x6 -> x16, local copies, waits for them, and re-layouts: 2.99 us -> 0.82 us
  transfers between devices with their start and end apart: 22 -> 22, of which waited for: 13 -> 14; matrix products, arithmetic and copies ran while one was open for 3% -> 3% of each run, Pallas kernels for 13% -> 10%
where the time goes in v6:
time: 140 us; the launch traced here: 139 us
  starting transfers between devices  60 us (43%)
  waiting for transfers between devices  43.9 us (31%)
  Pallas kernels  28.8 us (21%)
  local copies, waits for them, and re-layouts  4.82 us (3%)
    ppermute x22, starting transfers between devices, send(): return lax.ppermute(array, ('section', 'rows'), route(move, keep))  60 us
    ppermute x22, waiting for transfers between devices, send(): return lax.ppermute(array, ('section', 'rows'), route(move, keep))  43.9 us
    pallas_call x4, Pallas kernels, run_frame(): pl.pallas_call(functools.partial(frame_kernel, frame, builds, len(inputs)...  27.2 us
  transfers between devices with their start and end apart: 22, of which 14 were waited for; matrix products, arithmetic and copies ran while one was open for 3% of the time, Pallas kernels for 10%

profile of v6, /device:TPU:327, one launch (start us, length us, event | category | flops | bytes accessed | tf_op | source)
XLA Modules:
  0.0 139.5 jit_solution(7073481990139226965)
XLA Ops:
  1.0 2.6 %collective-permute-start.1 = (bf16[2,2,64,256]{3,2,1,0:T(8,128)(2,1)S(1)}, bf16[2,2,64,256]{3,2,1,0:T(8,128)(2,1)S(1)}, u32[]{:S(2)}, u32[]{:S(2)}) collective-permute-start(bf16[2,2,64,256]{3,2,1,0:T(8,128)(2,1)S(1)} %get-tuple-element.40), channel_id=1, source_target_pairs={{0,1},{1,0},{2,3},{3,2},{4,5},{5,4},{6,7},{7,6},{8,9},{9,8},{10,11... | collective-permute-start | bytes 393224 | tf_op jit(solution)/shard_map/ppermute | solution.py:219
  4.6 3.0 %collective-permute-start = (bf16[576,256]{1,0:T(8,128)(2,1)S(1)}, bf16[576,256]{1,0:T(8,128)(2,1)S(1)}, u32[]{:S(2)}, u32[]{:S(2)}) collective-permute-start(bf16[576,256]{1,0:T(8,128)(2,1)S(1)} %dynamic-slice_bitcast_fusion.2), channel_id=1, source_target_pairs={{0,128},{1,129},{2,130},{3,131},{4,132},{5,133},{6,134},{7,135},{8... | collective-permute-start | bytes 884744 | tf_op jit(solution)/shard_map/ppermute | solution.py:219
  7.7 5.1 %collective-permute-start.3 = (bf16[2,4,64,256]{3,2,1,0:T(8,128)(2,1)S(1)}, bf16[2,4,64,256]{3,2,1,0:T(8,128)(2,1)S(1)}, u32[]{:S(2)}, u32[]{:S(2)}) collective-permute-start(bf16[2,4,64,256]{3,2,1,0:T(8,128)(2,1)S(1)} %maximum_select_fusion.1.refs_1_), channel_id=1, source_target_pairs={{2,0},{3,1},{4,2},{5,3},{6,4},{7,5},{8,6},{9,7},{10,8},{11,9},{12,... | collective-permute-start | bytes 786440 | tf_op jit(solution)/shard_map/ppermute | solution.py:219
  18.2 5.9 %collective-permute-done.2.refs_0_ = bf16[2,4,64,256]{3,2,1,0:T(8,128)(2,1)S(1)} collective-permute-done((bf16[2,4,64,256]{3,2,1,0:T(8,128)(2,1)S(1)}, bf16[2,4,64,256]{3,2,1,0:T(8,128)(2,1)S(1)}, u32[]{:S(2)}, u32[]{:S(2)}) %collective-permute-start.2) | collective-permute-done | bytes 262176 | tf_op jit(solution)/shard_map/ppermute | solution.py:219
  26.0 4.6 %collective-permute-start.4 = (bf16[2304,256]{1,0:T(8,128)(2,1)S(1)}, bf16[2304,256]{1,0:T(8,128)(2,1)}, u32[]{:S(2)}, u32[]{:S(2)}) collective-permute-start(bf16[2304,256]{1,0:T(8,128)(2,1)S(1)} %get-tuple-element.22.refs_3_), channel_id=1, source_target_pairs={{0,64},{1,65},{2,66},{3,67},{4,68},{5,69},{6,70},{7,71},{8,72},{9,... | collective-permute-start | bytes 3538952 | tf_op jit(solution)/shard_map/ppermute | solution.py:219
  32.5 2.7 %collective-permute-start.9 = (bf16[576,256]{1,0:T(8,128)(2,1)S(1)}, bf16[576,256]{1,0:T(8,128)(2,1)S(1)}, u32[]{:S(2)}, u32[]{:S(2)}) collective-permute-start(bf16[576,256]{1,0:T(8,128)(2,1)S(1)} %collective-permute-done), channel_id=1, source_target_pairs={{0,14},{1,15},{2,0},{3,1},{4,2},{5,3},{6,4},{7,5},{8,6},{9,7},{10,... | collective-permute-start | bytes 884744 | tf_op jit(solution)/shard_map/ppermute | solution.py:219
  35.3 2.6 %collective-permute-start.8 = (bf16[576,256]{1,0:T(8,128)(2,1)S(1)}, bf16[576,256]{1,0:T(8,128)(2,1)S(1)}, u32[]{:S(2)}, u32[]{:S(2)}) collective-permute-start(bf16[576,256]{1,0:T(8,128)(2,1)S(1)} %collective-permute-done), channel_id=1, source_target_pairs={{0,2},{1,3},{2,4},{3,5},{4,6},{5,7},{6,8},{7,9},{8,10},{9,11},{10,... | collective-permute-start | bytes 884744 | tf_op jit(solution)/shard_map/ppermute | solution.py:219
  37.8 3.3 %collective-permute-done.10 = bf16[576,256]{1,0:T(8,128)(2,1)S(1)} collective-permute-done((bf16[576,256]{1,0:T(8,128)(2,1)S(1)}, bf16[576,256]{1,0:T(8,128)(2,1)S(1)}, u32[]{:S(2)}, u32[]{:S(2)}) %collective-permute-start.10) | collective-permute-done | bytes 294944 | tf_op jit(solution)/shard_map/ppermute | solution.py:219
  41.1 3.9 %collective-permute-done.9 = bf16[576,256]{1,0:T(8,128)(2,1)S(1)} collective-permute-done((bf16[576,256]{1,0:T(8,128)(2,1)S(1)}, bf16[576,256]{1,0:T(8,128)(2,1)S(1)}, u32[]{:S(2)}, u32[]{:S(2)}) %collective-permute-start.9) | collective-permute-done | bytes 294944 | tf_op jit(solution)/shard_map/ppermute | solution.py:219
  45.0 4.2 %collective-permute-done.8 = bf16[576,256]{1,0:T(8,128)(2,1)S(1)} collective-permute-done((bf16[576,256]{1,0:T(8,128)(2,1)S(1)}, bf16[576,256]{1,0:T(8,128)(2,1)S(1)}, u32[]{:S(2)}, u32[]{:S(2)}) %collective-permute-start.8) | collective-permute-done | bytes 294944 | tf_op jit(solution)/shard_map/ppermute | solution.py:219
  50.4 3.0 %collective-permute-start.11 = (bf16[4,576,256]{2,1,0:T(8,128)(2,1)S(1)}, bf16[4,576,256]{2,1,0:T(8,128)(2,1)}, u32[]{:S(2)}, u32[]{:S(2)}) collective-permute-start(bf16[4,576,256]{2,1,0:T(8,128)(2,1)S(1)} %pad_maximum_fusion.refs_9_), channel_id=1, source_target_pairs={{0,1},{1,0},{2,3},{3,2},{4,5},{5,4},{6,7},{7,6},{8,9},{9,8},{10,11... | collective-permute-start | bytes 3538952 | tf_op jit(solution)/shard_map/ppermute | solution.py:219
  53.4 4.2 %collective-permute-start.7 = (bf16[2304,256]{1,0:T(8,128)(2,1)}, bf16[2304,256]{1,0:T(8,128)(2,1)}, u32[]{:S(2)}, u32[]{:S(2)}) collective-permute-start(bf16[2304,256]{1,0:T(8,128)(2,1)} %collective-permute-done.6.refs_7_), channel_id=1, source_target_pairs={{0,1},{1,0},{2,3},{3,2},{4,5},{5,4},{6,7},{7,6},{8,9},{9,8},{10,11... | collective-permute-start | bytes 3538952 | tf_op jit(solution)/shard_map/ppermute | solution.py:219
  62.7 8.1 %frame0.2 = (bf16[2,4,2,64,256]{4,3,2,1,0:T(8,128)(2,1)S(1)}, bf16[1,4,64,256]{3,2,1,0:T(8,128)(2,1)S(1)}, f32[28,64,256]{2,1,0:T(8,128)S(1)}, bf16[4,2,2304,256...) custom-call(s32[5]{0:T(128)S(1)} %stack.67.meta, bf16[2,4,64,256]{3,2,1,0:T(8,128)(2,1)} %copy-done.7, ...), custom_call_target="tpu_custom_call" | custom-call | flops 4227858432 | bytes 8000000 | tf_op jit(solution)/shard_map/frame0/pallas_call | solution.py:155
  72.1 4.9 %frame1.2 = (bf16[2,4,2,64,256]{4,3,2,1,0:T(8,128)(2,1)S(1)}, bf16[1,4,64,256]{3,2,1,0:T(8,128)(2,1)}) custom-call(s32[5]{0:T(128)S(1)} %stack.67.meta, bf16[1,12,64,256]{3,2,1,0:T(8,128)(2,1)S(1)} %get-tuple-element.25.refs_0_, bf16[4,2,2304,256]{3,2,1,0:T(8,128)(2,1)S(1)} %get-tuple-element.26.refs_1_, f32[28,64,256]{2,1,0:T(8,128)S(1)} %get-tuple-element.27.refs_2_), custom_call_target="tpu_custom_call" | custom-call | flops 2113929216 | bytes 8000000 | tf_op jit(solution)/shard_map/frame1/pallas_call | solution.py:155
  79.1 5.4 %collective-permute-done.12.refs_1_ = bf16[1,4,64,256]{3,2,1,0:T(8,128)(2,1)} collective-permute-done((bf16[1,4,64,256]{3,2,1,0:T(8,128)(2,1)S(1)}, bf16[1,4,64,256]{3,2,1,0:T(8,128)(2,1)}, u32[]{:S(2)}, u32[]{:S(2)}) %collective-permute-start.12) | collective-permute-done | bytes 131104 | tf_op jit(solution)/shard_map/ppermute | solution.py:219
  86.4 3.4 %collective-permute-start.13 = (bf16[1,4,64,256]{3,2,1,0:T(8,128)(2,1)}, bf16[1,4,64,256]{3,2,1,0:T(8,128)(2,1)}, u32[]{:S(2)}, u32[]{:S(2)}) collective-permute-start(bf16[1,4,64,256]{3,2,1,0:T(8,128)(2,1)} %collective-permute-done.12.refs_1_), channel_id=1, source_target_pairs={{256,258},{257,259},{258,260},{259,261},{260,262},{261,263},{262,2... | collective-permute-start | bytes 393224 | tf_op jit(solution)/shard_map/ppermute | solution.py:219
  94.2 3.4 %collective-permute-start.16 = (bf16[1,4,64,256]{3,2,1,0:T(8,128)(2,1)}, bf16[1,4,64,256]{3,2,1,0:T(8,128)(2,1)S(1)}, u32[]{:S(2)}, u32[]{:S(2)}) collective-permute-start(bf16[1,4,64,256]{3,2,1,0:T(8,128)(2,1)} %collective-permute-done.15.refs_1_), channel_id=1, source_target_pairs={{256,258},{257,259},{258,260},{259,261},{260,262},{261,263},{262,2... | collective-permute-start | bytes 393224 | tf_op jit(solution)/shard_map/ppermute | solution.py:219
  97.6 8.9 %frame0.3 = (bf16[2,4,2,64,256]{4,3,2,1,0:T(8,128)(2,1)S(1)}, bf16[1,4,64,256]{3,2,1,0:T(8,128)(2,1)}, f32[28,64,256]{2,1,0:T(8,128)S(1)}, bf16[4,2,2304,256]{3,2,1,0:T(8,128)(2,1)S(1)}) custom-call(s32[5]{0:T(128)S(1)} %stack.67.meta, bf16[1,4,64,256]{3,2,1,0:T(8,128)(2,1)} %collective-permute-done.13.refs_0_, ...), custom_call_target="tpu_custom_call" | custom-call | flops 4227858432 | bytes 8000000 | tf_op jit(solution)/shard_map/frame0/pallas_call | solution.py:155
  106.6 5.3 %frame1.3 = (bf16[2,4,2,64,256]{4,3,2,1,0:T(8,128)(2,1)S(1)}, bf16[1,4,64,256]{3,2,1,0:T(8,128)(2,1)}) custom-call(s32[5]{0:T(128)S(1)} %stack.67.meta, bf16[1,4,64,256]{3,2,1,0:T(8,128)(2,1)S(1)} %collective-permute-done.16.refs_0_, bf16[1,4,64,256]{3,2,1,0:T(8,128)(2,1)} %collective-permute-done.15.refs_1_, ...), custom_call_target="tpu_custom_call" | custom-call | flops 2113929216 | bytes 8000000 | tf_op jit(solution)/shard_map/frame1/pallas_call | solution.py:155
  112.2 3.4 %collective-permute-start.18 = (bf16[4,2,2,64,256]{4,3,2,1,0:T(8,128)(2,1)S(1)}, bf16[4,2,2,64,256]{4,3,2,1,0:T(8,128)(2,1)S(1)}, u32[]{:S(2)}, u32[]{:S(2)}) collective-permute-start(bf16[4,2,2,64,256]{4,3,2,1,0:T(8,128)(2,1)S(1)} %get-tuple-element.37), channel_id=1, source_target_pairs={{0,1},{1,0},{2,3},{3,2},{4,5},{5,4},{6,7},{7,6},{8,9},{9,8},{10,11... | collective-permute-start | bytes 1572872 | tf_op jit(solution)/shard_map/ppermute | solution.py:219
  117.3 3.3 %collective-permute-start.19 = (bf16[2,2,2,64,256]{4,3,2,1,0:T(8,128)(2,1)S(1)}, bf16[2,2,2,64,256]{4,3,2,1,0:T(8,128)(2,1)S(1)}, u32[]{:S(2)}, u32[]{:S(2)}) collective-permute-start(bf16[2,2,2,64,256]{4,3,2,1,0:T(8,128)(2,1)S(1)} %pad_maximum_fusion.1), channel_id=1, source_target_pairs={{0,64},{1,65},{2,66},{3,67},{4,68},{5,69},{6,70},{7,71},{8,72},{9,... | collective-permute-start | bytes 786440 | tf_op jit(solution)/shard_map/ppermute | solution.py:219
  122.6 2.7 %collective-permute-start.21 = (bf16[2,2,2,64,256]{4,3,2,1,0:T(8,128)(2,1)S(1)}, bf16[2,2,2,64,256]{4,3,2,1,0:T(8,128)(2,1)S(1)}, u32[]{:S(2)}, u32[]{:S(2)}) collective-permute-start(bf16[2,2,2,64,256]{4,3,2,1,0:T(8,128)(2,1)S(1)} %pad_maximum_fusion.3), channel_id=1, source_target_pairs={{0,192},{1,193},{2,194},{3,195},{4,196},{5,197},{6,198},{7,199},{8... | collective-permute-start | bytes 786440 | tf_op jit(solution)/shard_map/ppermute | solution.py:219
  126.7 4.6 %collective-permute-done.20.refs_1_ = bf16[2,2,2,64,256]{4,3,2,1,0:T(8,128)(2,1)S(1)} collective-permute-done((bf16[2,2,2,64,256]{4,3,2,1,0:T(8,128)(2,1)S(1)}, bf16[2,2,2,64,256]{4,3,2,1,0:T(8,128)(2,1)S(1)}, u32[]{:S(2)}, u32[]{:S(2)}) %collective-permute-start.20) | collective-permute-done | bytes 262176 | tf_op jit(solution)/shard_map/ppermute | solution.py:219
  131.3 6.6 %collective-permute-done.21.refs_2_ = bf16[2,2,2,64,256]{4,3,2,1,0:T(8,128)(2,1)S(1)} collective-permute-done((bf16[2,2,2,64,256]{4,3,2,1,0:T(8,128)(2,1)S(1)}, bf16[2,2,2,64,256]{4,3,2,1,0:T(8,128)(2,1)S(1)}, u32[]{:S(2)}, u32[]{:S(2)}) %collective-permute-start.21) | collective-permute-done | bytes 262176 | tf_op jit(solution)/shard_map/ppermute | solution.py:219
  (54 shorter events, 33.8 us)
Async XLA Ops:
  1.0 6.7 %collective-permute-start.1 = (bf16[2,2,64,256]{3,2,1,0:T(8,128)(2,1)S(1)}, bf16[2,2,64,256]{3,2,1,0:T(8,128)(2,1)S(1)}, u32[]{:S(2)}, u32[]{:S(2)}) collective-permute-start(bf16[2,2,64,256]{3,2,1,0:T(8,128)(2,1)S(1)} %get-tuple-element.40), channel_id=1, source_target_pairs={{0,1},{1,0},{2,3},{3,2},{4,5},{5,4},{6,7},{7,6},{8,9},{9,8},{10,11... | collective-permute-start | bytes 393224 | tf_op jit(solution)/shard_map/ppermute | solution.py:219
  4.6 12.0 %collective-permute-start = (bf16[576,256]{1,0:T(8,128)(2,1)S(1)}, bf16[576,256]{1,0:T(8,128)(2,1)S(1)}, u32[]{:S(2)}, u32[]{:S(2)}) collective-permute-start(bf16[576,256]{1,0:T(8,128)(2,1)S(1)} %dynamic-slice_bitcast_fusion.2), channel_id=1, source_target_pairs={{0,128},{1,129},{2,130},{3,131},{4,132},{5,133},{6,134},{7,135},{8... | collective-permute-start | bytes 884744 | tf_op jit(solution)/shard_map/ppermute | solution.py:219
  7.7 10.5 %collective-permute-start.3 = (bf16[2,4,64,256]{3,2,1,0:T(8,128)(2,1)S(1)}, bf16[2,4,64,256]{3,2,1,0:T(8,128)(2,1)S(1)}, u32[]{:S(2)}, u32[]{:S(2)}) collective-permute-start(bf16[2,4,64,256]{3,2,1,0:T(8,128)(2,1)S(1)} %maximum_select_fusion.1.refs_1_), channel_id=1, source_target_pairs={{2,0},{3,1},{4,2},{5,3},{6,4},{7,5},{8,6},{9,7},{10,8},{11,9},{12,... | collective-permute-start | bytes 786440 | tf_op jit(solution)/shard_map/ppermute | solution.py:219
  12.8 11.3 %collective-permute-start.2 = (bf16[2,4,64,256]{3,2,1,0:T(8,128)(2,1)S(1)}, bf16[2,4,64,256]{3,2,1,0:T(8,128)(2,1)S(1)}, u32[]{:S(2)}, u32[]{:S(2)}) collective-permute-start(bf16[2,4,64,256]{3,2,1,0:T(8,128)(2,1)S(1)} %maximum_select_fusion.1.refs_1_), channel_id=1, source_target_pairs={{0,2},{1,3},{2,4},{3,5},{4,6},{5,7},{6,8},{7,9},{8,10},{9,11},{10,... | collective-permute-start | bytes 786440 | tf_op jit(solution)/shard_map/ppermute | solution.py:219
  16.6 32.6 %copy-start.4 = (bf16[576,256]{1,0:T(8,128)(2,1)}, bf16[576,256]{1,0:T(8,128)(2,1)S(1)}, u32[]{:S(2)}) copy-start(bf16[576,256]{1,0:T(8,128)(2,1)S(1)} %collective-permute-done) | copy-start | bytes 884740
  18.2 32.2 %copy-start.6 = (bf16[2,4,64,256]{3,2,1,0:T(8,128)(2,1)}, bf16[2,4,64,256]{3,2,1,0:T(8,128)(2,1)S(1)}, u32[]{:S(2)}) copy-start(bf16[2,4,64,256]{3,2,1,0:T(8,128)(2,1)S(1)} %collective-permute-done.3.refs_2_) | copy-start | bytes 786436
  24.1 29.3 %collective-permute-start.6 = (bf16[2304,256]{1,0:T(8,128)(2,1)S(1)}, bf16[2304,256]{1,0:T(8,128)(2,1)}, u32[]{:S(2)}, u32[]{:S(2)}) collective-permute-start(bf16[2304,256]{1,0:T(8,128)(2,1)S(1)} %get-tuple-element.22.refs_3_), channel_id=1, source_target_pairs={{0,192},{1,193},{2,194},{3,195},{4,196},{5,197},{6,198},{7,199},{8... | collective-permute-start | bytes 3538952 | tf_op jit(solution)/shard_map/ppermute | solution.py:219
  26.0 31.6 %collective-permute-start.4 = (bf16[2304,256]{1,0:T(8,128)(2,1)S(1)}, bf16[2304,256]{1,0:T(8,128)(2,1)}, u32[]{:S(2)}, u32[]{:S(2)}) collective-permute-start(bf16[2304,256]{1,0:T(8,128)(2,1)S(1)} %get-tuple-element.22.refs_3_), channel_id=1, source_target_pairs={{0,64},{1,65},{2,66},{3,67},{4,68},{5,69},{6,70},{7,71},{8,72},{9,... | collective-permute-start | bytes 3538952 | tf_op jit(solution)/shard_map/ppermute | solution.py:219
  30.6 10.5 %collective-permute-start.10 = (bf16[576,256]{1,0:T(8,128)(2,1)S(1)}, bf16[576,256]{1,0:T(8,128)(2,1)S(1)}, u32[]{:S(2)}, u32[]{:S(2)}) collective-permute-start(bf16[576,256]{1,0:T(8,128)(2,1)S(1)} %collective-permute-done), channel_id=1, source_target_pairs={{0,4},{1,5},{2,14},{3,15},{4,8},{5,9},{6,2},{7,3},{8,12},{9,13},{1... | collective-permute-start | bytes 884744 | tf_op jit(solution)/shard_map/ppermute | solution.py:219
  32.5 12.5 %collective-permute-start.9 = (bf16[576,256]{1,0:T(8,128)(2,1)S(1)}, bf16[576,256]{1,0:T(8,128)(2,1)S(1)}, u32[]{:S(2)}, u32[]{:S(2)}) collective-permute-start(bf16[576,256]{1,0:T(8,128)(2,1)S(1)} %collective-permute-done), channel_id=1, source_target_pairs={{0,14},{1,15},{2,0},{3,1},{4,2},{5,3},{6,4},{7,5},{8,6},{9,7},{10,... | collective-permute-start | bytes 884744 | tf_op jit(solution)/shard_map/ppermute | solution.py:219
  35.3 14.0 %collective-permute-start.8 = (bf16[576,256]{1,0:T(8,128)(2,1)S(1)}, bf16[576,256]{1,0:T(8,128)(2,1)S(1)}, u32[]{:S(2)}, u32[]{:S(2)}) collective-permute-start(bf16[576,256]{1,0:T(8,128)(2,1)S(1)} %collective-permute-done), channel_id=1, source_target_pairs={{0,2},{1,3},{2,4},{3,5},{4,6},{5,7},{6,8},{7,9},{8,10},{9,11},{10,... | collective-permute-start | bytes 884744 | tf_op jit(solution)/shard_map/ppermute | solution.py:219
  50.4 9.2 %collective-permute-start.11 = (bf16[4,576,256]{2,1,0:T(8,128)(2,1)S(1)}, bf16[4,576,256]{2,1,0:T(8,128)(2,1)}, u32[]{:S(2)}, u32[]{:S(2)}) collective-permute-start(bf16[4,576,256]{2,1,0:T(8,128)(2,1)S(1)} %pad_maximum_fusion.refs_9_), channel_id=1, source_target_pairs={{0,1},{1,0},{2,3},{3,2},{4,5},{5,4},{6,7},{7,6},{8,9},{9,8},{10,11... | collective-permute-start | bytes 3538952 | tf_op jit(solution)/shard_map/ppermute | solution.py:219
  53.4 7.0 %collective-permute-start.7 = (bf16[2304,256]{1,0:T(8,128)(2,1)}, bf16[2304,256]{1,0:T(8,128)(2,1)}, u32[]{:S(2)}, u32[]{:S(2)}) collective-permute-start(bf16[2304,256]{1,0:T(8,128)(2,1)} %collective-permute-done.6.refs_7_), channel_id=1, source_target_pairs={{0,1},{1,0},{2,3},{3,2},{4,5},{5,4},{6,7},{7,6},{8,9},{9,8},{10,11... | collective-permute-start | bytes 3538952 | tf_op jit(solution)/shard_map/ppermute | solution.py:219
  57.6 5.1 %collective-permute-start.5 = (bf16[2304,256]{1,0:T(8,128)(2,1)}, bf16[2304,256]{1,0:T(8,128)(2,1)}, u32[]{:S(2)}, u32[]{:S(2)}) collective-permute-start(bf16[2304,256]{1,0:T(8,128)(2,1)} %collective-permute-done.4.refs_5_), channel_id=1, source_target_pairs={{0,1},{1,0},{2,3},{3,2},{4,5},{5,4},{6,7},{7,6},{8,9},{9,8},{10,11... | collective-permute-start | bytes 3538952 | tf_op jit(solution)/shard_map/ppermute | solution.py:219
  70.8 13.7 %collective-permute-start.12 = (bf16[1,4,64,256]{3,2,1,0:T(8,128)(2,1)S(1)}, bf16[1,4,64,256]{3,2,1,0:T(8,128)(2,1)}, u32[]{:S(2)}, u32[]{:S(2)}) collective-permute-start(bf16[1,4,64,256]{3,2,1,0:T(8,128)(2,1)S(1)} %get-tuple-element.29), channel_id=1, source_target_pairs={{0,256},{1,257},{2,258},{3,259},{4,260},{5,261},{6,262},{7,263},{8... | collective-permute-start | bytes 393224 | tf_op jit(solution)/shard_map/ppermute | solution.py:219
  77.8 14.5 %collective-permute-start.15 = (bf16[1,4,64,256]{3,2,1,0:T(8,128)(2,1)}, bf16[1,4,64,256]{3,2,1,0:T(8,128)(2,1)}, u32[]{:S(2)}, u32[]{:S(2)}) collective-permute-start(bf16[1,4,64,256]{3,2,1,0:T(8,128)(2,1)} %get-tuple-element.31), channel_id=1, source_target_pairs={{0,256},{1,257},{2,258},{3,259},{4,260},{5,261},{6,262},{7,263},{8... | collective-permute-start | bytes 393224 | tf_op jit(solution)/shard_map/ppermute | solution.py:219
  84.5 13.2 %collective-permute-start.14 = (bf16[1,4,64,256]{3,2,1,0:T(8,128)(2,1)}, bf16[1,4,64,256]{3,2,1,0:T(8,128)(2,1)}, u32[]{:S(2)}, u32[]{:S(2)}) collective-permute-start(bf16[1,4,64,256]{3,2,1,0:T(8,128)(2,1)} %collective-permute-done.12.refs_1_), channel_id=1, source_target_pairs={{258,256},{259,257},{260,258},{261,259},{262,260},{263,261},{264,2... | collective-permute-start | bytes 393224 | tf_op jit(solution)/shard_map/ppermute | solution.py:219
  86.4 11.2 %collective-permute-start.13 = (bf16[1,4,64,256]{3,2,1,0:T(8,128)(2,1)}, bf16[1,4,64,256]{3,2,1,0:T(8,128)(2,1)}, u32[]{:S(2)}, u32[]{:S(2)}) collective-permute-start(bf16[1,4,64,256]{3,2,1,0:T(8,128)(2,1)} %collective-permute-done.12.refs_1_), channel_id=1, source_target_pairs={{256,258},{257,259},{258,260},{259,261},{260,262},{261,263},{262,2... | collective-permute-start | bytes 393224 | tf_op jit(solution)/shard_map/ppermute | solution.py:219
  92.3 14.2 %collective-permute-start.17 = (bf16[1,4,64,256]{3,2,1,0:T(8,128)(2,1)}, bf16[1,4,64,256]{3,2,1,0:T(8,128)(2,1)S(1)}, u32[]{:S(2)}, u32[]{:S(2)}) collective-permute-start(bf16[1,4,64,256]{3,2,1,0:T(8,128)(2,1)} %collective-permute-done.15.refs_1_), channel_id=1, source_target_pairs={{258,256},{259,257},{260,258},{261,259},{262,260},{263,261},{264,2... | collective-permute-start | bytes 393224 | tf_op jit(solution)/shard_map/ppermute | solution.py:219
  94.2 12.3 %collective-permute-start.16 = (bf16[1,4,64,256]{3,2,1,0:T(8,128)(2,1)}, bf16[1,4,64,256]{3,2,1,0:T(8,128)(2,1)S(1)}, u32[]{:S(2)}, u32[]{:S(2)}) collective-permute-start(bf16[1,4,64,256]{3,2,1,0:T(8,128)(2,1)} %collective-permute-done.15.refs_1_), channel_id=1, source_target_pairs={{256,258},{257,259},{258,260},{259,261},{260,262},{261,263},{262,2... | collective-permute-start | bytes 393224 | tf_op jit(solution)/shard_map/ppermute | solution.py:219
  112.2 5.0 %collective-permute-start.18 = (bf16[4,2,2,64,256]{4,3,2,1,0:T(8,128)(2,1)S(1)}, bf16[4,2,2,64,256]{4,3,2,1,0:T(8,128)(2,1)S(1)}, u32[]{:S(2)}, u32[]{:S(2)}) collective-permute-start(bf16[4,2,2,64,256]{4,3,2,1,0:T(8,128)(2,1)S(1)} %get-tuple-element.37), channel_id=1, source_target_pairs={{0,1},{1,0},{2,3},{3,2},{4,5},{5,4},{6,7},{7,6},{8,9},{9,8},{10,11... | collective-permute-start | bytes 1572872 | tf_op jit(solution)/shard_map/ppermute | solution.py:219
  117.3 9.4 %collective-permute-start.19 = (bf16[2,2,2,64,256]{4,3,2,1,0:T(8,128)(2,1)S(1)}, bf16[2,2,2,64,256]{4,3,2,1,0:T(8,128)(2,1)S(1)}, u32[]{:S(2)}, u32[]{:S(2)}) collective-permute-start(bf16[2,2,2,64,256]{4,3,2,1,0:T(8,128)(2,1)S(1)} %pad_maximum_fusion.1), channel_id=1, source_target_pairs={{0,64},{1,65},{2,66},{3,67},{4,68},{5,69},{6,70},{7,71},{8,72},{9,... | collective-permute-start | bytes 786440 | tf_op jit(solution)/shard_map/ppermute | solution.py:219
  120.6 10.6 %collective-permute-start.20 = (bf16[2,2,2,64,256]{4,3,2,1,0:T(8,128)(2,1)S(1)}, bf16[2,2,2,64,256]{4,3,2,1,0:T(8,128)(2,1)S(1)}, u32[]{:S(2)}, u32[]{:S(2)}) collective-permute-start(bf16[2,2,2,64,256]{4,3,2,1,0:T(8,128)(2,1)S(1)} %pad_maximum_fusion.2), channel_id=1, source_target_pairs={{0,128},{1,129},{2,130},{3,131},{4,132},{5,133},{6,134},{7,135},{8... | collective-permute-start | bytes 786440 | tf_op jit(solution)/shard_map/ppermute | solution.py:219
  122.6 15.3 %collective-permute-start.21 = (bf16[2,2,2,64,256]{4,3,2,1,0:T(8,128)(2,1)S(1)}, bf16[2,2,2,64,256]{4,3,2,1,0:T(8,128)(2,1)S(1)}, u32[]{:S(2)}, u32[]{:S(2)}) collective-permute-start(bf16[2,2,2,64,256]{4,3,2,1,0:T(8,128)(2,1)S(1)} %pad_maximum_fusion.3), channel_id=1, source_target_pairs={{0,192},{1,193},{2,194},{3,195},{4,196},{5,197},{6,198},{7,199},{8... | collective-permute-start | bytes 786440 | tf_op jit(solution)/shard_map/ppermute | solution.py:219
  (6 other events, 52.8 us)

commit v7 on v6

--- a/solution.py
+++ b/solution.py
@@ -10,6 +10,49 @@
 DEPTH = 4
 SPLIT = 4
 LIMIT = 24
+
+
+def fetch_weights(meta, pieces, weights, sems):
+    x, core, piece = meta[0], meta[1], meta[3]
+    depth, _, taps, _ = weights.shape
+    part = taps // 4
+
+    def whole(source):
+        return [(slice(None), source)]
+
+    def quarters(source):
+        return [(pl.ds(pl.multiple_of(lax.rem(piece + shift, 4) * part, part), part), source.at[place])
+                for place, shift in enumerate((0, 3, 1, 2))]
+
+    for layer in range(depth):
+        step = lax.rem(layer - x + depth, depth)
+        for distance, at in ((0, 0), (1, 4), (3, 2), (2, 6)):
+            @pl.when(step == distance)
+            def _():
+                for source, owner in ((pieces[at], core), (pieces[at + 1], 1 - core)):
+                    for rows, block in (quarters if distance == 2 else whole)(source):
+                        pltpu.make_async_copy(block, weights.at[layer, owner, rows], sems.at[layer]).start()
+
+
+def gather_kernel(meta, *refs):
+    pieces, weights, sems = refs[:8], refs[8], refs[9]
+    fetch_weights(meta, pieces, weights, sems)
+    for layer in range(DEPTH):
+        pltpu.make_async_copy(weights.at[layer], weights.at[layer], sems.at[layer]).wait()
+
+
+def gather(meta, kernels):
+    taps, chans = kernels[0].shape
+    return pl.pallas_call(
+        gather_kernel,
+        out_shape=jax.ShapeDtypeStruct((DEPTH, 2, taps, chans), jnp.bfloat16),
+        in_specs=[pl.BlockSpec(memory_space=pltpu.SMEM)] + [pl.BlockSpec(memory_space=pl.ANY)] * 8,
+        out_specs=pl.BlockSpec(memory_space=pltpu.VMEM),
+        scratch_shapes=[pltpu.SemaphoreType.DMA((DEPTH,))],
+        compiler_params=pltpu.CompilerParams(vmem_limit_bytes=LIMIT * 1024 * 1024),
+        cost_estimate=pl.CostEstimate(flops=0, bytes_accessed=19 * 10**6, transcendentals=0),
+        name="gather",
+    )(meta, *kernels)
 
 
 def frame_kernel(frame, builds, slabs, meta, *refs):
@@ -38,26 +81,8 @@
             pltpu.make_async_copy(source.at[0], cells.at[at], row_sems.at[0]).start()
             pltpu.make_async_copy(source.at[1], later.at[0, at], row_sems.at[1]).start()
 
-    def fetch(layer, mine, theirs, places):
-        for source, owner in ((mine, core), (theirs, other)):
-            for at, block in places(source):
-                pltpu.make_async_copy(block, weights.at[layer, owner, at], sems.at[layer]).start()
-
-    def whole(source):
-        return [(slice(None), source)]
-
-    def quarters(source):
-        part = taps // 4
-        return [(pl.ds(pl.multiple_of(lax.rem(piece + shift, 4) * part, part), part), source.at[place])
-                for place, shift in enumerate((0, 3, 1, 2))]
-
     if builds:
-        for layer in range(depth):
-            step = lax.rem(layer - x + depth, depth)
-            for distance, at in ((0, 0), (1, 4), (3, 2), (2, 6)):
-                @pl.when(step == distance)
-                def _():
-                    fetch(layer, pieces[at], pieces[at + 1], quarters if distance == 2 else whole)
+        fetch_weights(meta, pieces, weights, sems)
 
     column = lax.broadcasted_iota(jnp.int32, (width, chans), 0)
 
@@ -265,10 +290,11 @@
     top = send(mid, next_chip(1))
     bot = send(mid, next_chip(-1))
 
-    far, mine, top, bot = lax.optimization_barrier((far, mine, top, bot))
+    far, mine, bot = lax.optimization_barrier((far, mine, bot))
     left_mine = send(mine, along_x(1))
     right_mine = send(mine, along_x(-1))
     parts = (far, send(far, along_y(1)), send(far, along_y(-1)), send(far, two_along_y))
+    *parts, top = lax.optimization_barrier((*parts, top))
     far_mine = jnp.stack(parts)
     far_theirs = send(far_mine, sibling)
     left_theirs = send(left_mine, sibling)
@@ -283,9 +309,12 @@
     first.append(kept)
     mid_1 = send(reached, hop)
 
+    later_meta, _ = lax.optimization_barrier((meta, mid_0))
+    weights = gather(later_meta, kernels)
+    mid_1, weights = lax.optimization_barrier((mid_1, weights))
     second = []
     top, bot = send(mid_0, next_chip(1), is_upper), send(mid_0, next_chip(-1), is_upper)
-    kept, _, older, weights = run_frame(0, meta, (top, mid_0, bot), kernels)
+    kept, _, older = run_frame(0, meta, (top, mid_0, bot), weights)
     second.append(kept)
     top, bot = send(mid_1, next_chip(1), is_upper), send(mid_1, next_chip(-1), is_upper)
     kept, _ = run_frame(1, meta, (top, mid_1, bot), weights, older)

time: 140 us -> 144 us (1.029)
  starting transfers between devices: 60 us -> 67.3 us
  waiting for transfers between devices: 43.9 us -> 38.9 us
    ppermute x22, starting transfers between devices: 60 us -> 67.3 us  [send(): return lax.ppermute(array, ('section', 'rows'), route(move, keep))]
    ppermute x22, waiting for transfers between devices: 43.9 us -> 38.9 us  [send(): return lax.ppermute(array, ('section', 'rows'), route(move, keep))]
    pallas_call x0 -> x1, Pallas kernels: none -> 3.37 us  [gather(): pl.pallas_call(gather_kernel, out_shape=jax.ShapeDtypeStruct((DEPTH, 2, t...]
    pallas_call x4, Pallas kernels: 27.2 us -> 24.9 us  [run_frame(): pl.pallas_call(functools.partial(frame_kernel, frame, builds, len(inputs)...]
  transfers between devices with their start and end apart: 22 -> 22, of which waited for: 14 -> 11; matrix products, arithmetic and copies ran while one was open for 3% -> 3% of each run, Pallas kernels for 10% -> 10%
where the time goes in v7:
time: 144 us; the launch traced here: 143 us
  starting transfers between devices  67.3 us (47%)
  waiting for transfers between devices  38.9 us (27%)
  Pallas kernels  29.8 us (21%)
  local copies, waits for them, and re-layouts  4.82 us (3%)
    ppermute x22, starting transfers between devices, send(): return lax.ppermute(array, ('section', 'rows'), route(move, keep))  67.3 us
    ppermute x22, waiting for transfers between devices, send(): return lax.ppermute(array, ('section', 'rows'), route(move, keep))  38.9 us
    pallas_call x4, Pallas kernels, run_frame(): pl.pallas_call(functools.partial(frame_kernel, frame, builds, len(inputs)...  24.9 us
    pallas_call x1, Pallas kernels, gather(): pl.pallas_call(gather_kernel, out_shape=jax.ShapeDtypeStruct((DEPTH, 2, t...  3.37 us
  transfers between devices with their start and end apart: 22, of which 11 were waited for; matrix products, arithmetic and copies ran while one was open for 3% of the time, Pallas kernels for 10%

profile of v7, /device:TPU:327, one launch (start us, length us, event | category | flops | bytes accessed | tf_op | source)
XLA Modules:
  0.0 142.8 jit_solution(8658397349044744038)
XLA Ops:
  1.0 2.6 %collective-permute-start.1 = (bf16[2,2,64,256]{3,2,1,0:T(8,128)(2,1)S(1)}, bf16[2,2,64,256]{3,2,1,0:T(8,128)(2,1)S(1)}, u32[]{:S(2)}, u32[]{:S(2)}) collective-permute-start(bf16[2,2,64,256]{3,2,1,0:T(8,128)(2,1)S(1)} %get-tuple-element.52), channel_id=1, source_target_pairs={{0,1},{1,0},{2,3},{3,2},{4,5},{5,4},{6,7},{7,6},{8,9},{9,8},{10,11... | collective-permute-start | bytes 393224 | tf_op jit(solution)/shard_map/ppermute | solution.py:244
  4.6 3.0 %collective-permute-start = (bf16[576,256]{1,0:T(8,128)(2,1)S(1)}, bf16[576,256]{1,0:T(8,128)(2,1)S(1)}, u32[]{:S(2)}, u32[]{:S(2)}) collective-permute-start(bf16[576,256]{1,0:T(8,128)(2,1)S(1)} %dynamic-slice_bitcast_fusion.2), channel_id=1, source_target_pairs={{0,128},{1,129},{2,130},{3,131},{4,132},{5,133},{6,134},{7,135},{8... | collective-permute-start | bytes 884744 | tf_op jit(solution)/shard_map/ppermute | solution.py:244
  7.7 5.1 %collective-permute-start.2 = (bf16[2,4,64,256]{3,2,1,0:T(8,128)(2,1)S(1)}, bf16[2,4,64,256]{3,2,1,0:T(8,128)(2,1)S(1)}, u32[]{:S(2)}, u32[]{:S(2)}) collective-permute-start(bf16[2,4,64,256]{3,2,1,0:T(8,128)(2,1)S(1)} %maximum_select_fusion.1.refs_1_), channel_id=1, source_target_pairs={{2,0},{3,1},{4,2},{5,3},{6,4},{7,5},{8,6},{9,7},{10,8},{11,9},{12,... | collective-permute-start | bytes 786440 | tf_op jit(solution)/shard_map/ppermute | solution.py:244
  18.2 3.7 %collective-permute-start.7 = (bf16[2304,256]{1,0:T(8,128)(2,1)S(1)}, bf16[2304,256]{1,0:T(8,128)(2,1)}, u32[]{:S(2)}, u32[]{:S(2)}) collective-permute-start(bf16[2304,256]{1,0:T(8,128)(2,1)S(1)} %get-tuple-element.29.refs_3_.refs_0_), channel_id=1, source_target_pairs={{0,64},{1,65},{2,66},{3,67},{4,68},{5,69},{6,70},{7,71},{8,72},{9,... | collective-permute-start | bytes 3538952 | tf_op jit(solution)/shard_map/ppermute | solution.py:244
  23.9 2.2 %collective-permute-start.6 = (bf16[2,4,64,256]{3,2,1,0:T(8,128)(2,1)S(1)}, bf16[2,4,64,256]{3,2,1,0:T(8,128)(2,1)}, u32[]{:S(2)}, u32[]{:S(2)}) collective-permute-start(bf16[2,4,64,256]{3,2,1,0:T(8,128)(2,1)S(1)} %maximum_select_fusion.1.refs_1_), channel_id=1, source_target_pairs={{0,2},{1,3},{2,4},{3,5},{4,6},{5,7},{6,8},{7,9},{8,10},{9,11},{10,... | collective-permute-start | bytes 786440 | tf_op jit(solution)/shard_map/ppermute | solution.py:244
  26.1 3.2 %collective-permute-start.3 = (bf16[576,256]{1,0:T(8,128)(2,1)S(1)}, bf16[576,256]{1,0:T(8,128)(2,1)S(1)}, u32[]{:S(2)}, u32[]{:S(2)}) collective-permute-start(bf16[576,256]{1,0:T(8,128)(2,1)S(1)} %collective-permute-done), channel_id=1, source_target_pairs={{0,2},{1,3},{2,4},{3,5},{4,6},{5,7},{6,8},{7,9},{8,10},{9,11},{10,... | collective-permute-start | bytes 884744 | tf_op jit(solution)/shard_map/ppermute | solution.py:244
  29.3 4.6 %collective-permute-start.4 = (bf16[576,256]{1,0:T(8,128)(2,1)S(1)}, bf16[576,256]{1,0:T(8,128)(2,1)S(1)}, u32[]{:S(2)}, u32[]{:S(2)}) collective-permute-start(bf16[576,256]{1,0:T(8,128)(2,1)S(1)} %collective-permute-done), channel_id=1, source_target_pairs={{0,14},{1,15},{2,0},{3,1},{4,2},{5,3},{6,4},{7,5},{8,6},{9,7},{10,... | collective-permute-start | bytes 884744 | tf_op jit(solution)/shard_map/ppermute | solution.py:244
  37.3 4.4 %collective-permute-done.3 = bf16[576,256]{1,0:T(8,128)(2,1)S(1)} collective-permute-done((bf16[576,256]{1,0:T(8,128)(2,1)S(1)}, bf16[576,256]{1,0:T(8,128)(2,1)S(1)}, u32[]{:S(2)}, u32[]{:S(2)}) %collective-permute-start.3) | collective-permute-done | bytes 294944 | tf_op jit(solution)/shard_map/ppermute | solution.py:244
  41.7 7.1 %collective-permute-done.5 = bf16[576,256]{1,0:T(8,128)(2,1)S(1)} collective-permute-done((bf16[576,256]{1,0:T(8,128)(2,1)S(1)}, bf16[576,256]{1,0:T(8,128)(2,1)S(1)}, u32[]{:S(2)}, u32[]{:S(2)}) %collective-permute-start.5) | collective-permute-done | bytes 294944 | tf_op jit(solution)/shard_map/ppermute | solution.py:244
  50.0 4.2 %collective-permute-start.11 = (bf16[4,576,256]{2,1,0:T(8,128)(2,1)S(1)}, bf16[4,576,256]{2,1,0:T(8,128)(2,1)}, u32[]{:S(2)}, u32[]{:S(2)}) collective-permute-start(bf16[4,576,256]{2,1,0:T(8,128)(2,1)S(1)} %pad_maximum_fusion.refs_9_.refs_6_), channel_id=1, source_target_pairs={{0,1},{1,0},{2,3},{3,2},{4,5},{5,4},{6,7},{7,6},{8,9},{9,8},{10,11... | collective-permute-start | bytes 3538952 | tf_op jit(solution)/shard_map/ppermute | solution.py:244
  56.2 2.4 %collective-permute-start.10 = (bf16[2304,256]{1,0:T(8,128)(2,1)}, bf16[2304,256]{1,0:T(8,128)(2,1)}, u32[]{:S(2)}, u32[]{:S(2)}) collective-permute-start(bf16[2304,256]{1,0:T(8,128)(2,1)} %collective-permute-done.9.refs_7_.refs_4_), channel_id=1, source_target_pairs={{0,1},{1,0},{2,3},{3,2},{4,5},{5,4},{6,7},{7,6},{8,9},{9,8},{10,11... | collective-permute-start | bytes 3538952 | tf_op jit(solution)/shard_map/ppermute | solution.py:244
  61.4 8.1 %frame0.2 = (bf16[2,4,2,64,256]{4,3,2,1,0:T(8,128)(2,1)S(1)}, bf16[1,4,64,256]{3,2,1,0:T(8,128)(2,1)S(1)}, f32[28,64,256]{2,1,0:T(8,128)S(1)}, bf16[4,2,2304,256...) custom-call(s32[5]{0:T(128)S(1)} %stack.67.meta, bf16[2,4,64,256]{3,2,1,0:T(8,128)(2,1)} %collective-permute-done.6.refs_0_, ...), custom_call_target="tpu_custom_call" | custom-call | flops 4227858432 | bytes 8000000 | tf_op jit(solution)/shard_map/frame0/pallas_call | solution.py:180
  70.8 4.9 %frame1.2 = (bf16[2,4,2,64,256]{4,3,2,1,0:T(8,128)(2,1)S(1)}, bf16[1,4,64,256]{3,2,1,0:T(8,128)(2,1)}) custom-call(s32[5]{0:T(128)S(1)} %stack.67.meta, bf16[1,12,64,256]{3,2,1,0:T(8,128)(2,1)S(1)} %get-tuple-element.35.refs_0_, bf16[4,2,2304,256]{3,2,1,0:T(8,128)(2,1)S(1)} %get-tuple-element.36.refs_1_, f32[28,64,256]{2,1,0:T(8,128)S(1)} %get-tuple-element.37.refs_2_), custom_call_target="tpu_custom_call" | custom-call | flops 2113929216 | bytes 8000000 | tf_op jit(solution)/shard_map/frame1/pallas_call | solution.py:180
  77.8 5.4 %collective-permute-done.12.refs_1_ = bf16[1,4,64,256]{3,2,1,0:T(8,128)(2,1)} collective-permute-done((bf16[1,4,64,256]{3,2,1,0:T(8,128)(2,1)S(1)}, bf16[1,4,64,256]{3,2,1,0:T(8,128)(2,1)}, u32[]{:S(2)}, u32[]{:S(2)}) %collective-permute-start.12) | collective-permute-done | bytes 131104 | tf_op jit(solution)/shard_map/ppermute | solution.py:244
  85.1 5.5 %collective-permute-start.14 = (bf16[1,4,64,256]{3,2,1,0:T(8,128)(2,1)}, bf16[1,4,64,256]{3,2,1,0:T(8,128)(2,1)}, u32[]{:S(2)}, u32[]{:S(2)}) collective-permute-start(bf16[1,4,64,256]{3,2,1,0:T(8,128)(2,1)} %collective-permute-done.12.refs_1_), channel_id=1, source_target_pairs={{258,256},{259,257},{260,258},{261,259},{262,260},{263,261},{264,2... | collective-permute-start | bytes 393224 | tf_op jit(solution)/shard_map/ppermute | solution.py:244
  90.6 3.4 %gather.1.refs_3_ = bf16[4,2,2304,256]{3,2,1,0:T(8,128)(2,1)S(1)} custom-call(s32[5]{0:T(128)S(1)} %stack.67.meta, bf16[2304,256]{1,0:T(8,128)(2,1)S(1)} %get-tuple-element.29.refs_3_.refs_0_, bf16[2304,256]{1,0:T(8,128)(2,1)S(1)} %get-tuple-element.47.refs_4_.refs_1_, bf16[2304,256]{1,0:T(8,128)(2,1)} %collective-permute-done.7.refs_5_.refs_2_, ...), custom_call_target="tpu_custom_call" | custom-call | bytes 19000000 | tf_op jit(solution)/shard_map/gather/pallas_call | solution.py:46
  95.9 5.7 %collective-permute-start.17 = (bf16[1,4,64,256]{3,2,1,0:T(8,128)(2,1)}, bf16[1,4,64,256]{3,2,1,0:T(8,128)(2,1)S(1)}, u32[]{:S(2)}, u32[]{:S(2)}) collective-permute-start(bf16[1,4,64,256]{3,2,1,0:T(8,128)(2,1)} %collective-permute-done.15.refs_1_), channel_id=1, source_target_pairs={{258,256},{259,257},{260,258},{261,259},{262,260},{263,261},{264,2... | collective-permute-start | bytes 393224 | tf_op jit(solution)/shard_map/ppermute | solution.py:244
  101.6 6.5 %frame0.3 = (bf16[2,4,2,64,256]{4,3,2,1,0:T(8,128)(2,1)S(1)}, bf16[1,4,64,256]{3,2,1,0:T(8,128)(2,1)}, f32[28,64,256]{2,1,0:T(8,128)S(1)}) custom-call(s32[5]{0:T(128)S(1)} %stack.67.meta, bf16[1,4,64,256]{3,2,1,0:T(8,128)(2,1)} %collective-permute-done.13.refs_0_, bf16[1,4,64,256]{3,2,1,0:T(8,128)(2,1)} %collective-permute-done.12.refs_1_, ...), custom_call_target="tpu_custom_call" | custom-call | flops 4227858432 | bytes 8000000 | tf_op jit(solution)/shard_map/frame0/pallas_call | solution.py:180
  108.2 5.3 %frame1.3 = (bf16[2,4,2,64,256]{4,3,2,1,0:T(8,128)(2,1)S(1)}, bf16[1,4,64,256]{3,2,1,0:T(8,128)(2,1)}) custom-call(s32[5]{0:T(128)S(1)} %stack.67.meta, bf16[1,4,64,256]{3,2,1,0:T(8,128)(2,1)S(1)} %collective-permute-done.16.refs_0_, bf16[1,4,64,256]{3,2,1,0:T(8,128)(2,1)} %collective-permute-done.15.refs_1_, ...), custom_call_target="tpu_custom_call" | custom-call | flops 2113929216 | bytes 8000000 | tf_op jit(solution)/shard_map/frame1/pallas_call | solution.py:180
  113.8 4.0 %collective-permute-start.18 = (bf16[4,2,2,64,256]{4,3,2,1,0:T(8,128)(2,1)S(1)}, bf16[4,2,2,64,256]{4,3,2,1,0:T(8,128)(2,1)S(1)}, u32[]{:S(2)}, u32[]{:S(2)}) collective-permute-start(bf16[4,2,2,64,256]{4,3,2,1,0:T(8,128)(2,1)S(1)} %get-tuple-element.49), channel_id=1, source_target_pairs={{0,1},{1,0},{2,3},{3,2},{4,5},{5,4},{6,7},{7,6},{8,9},{9,8},{10,11... | collective-permute-start | bytes 1572872 | tf_op jit(solution)/shard_map/ppermute | solution.py:244
  119.4 4.5 %collective-permute-start.19 = (bf16[2,2,2,64,256]{4,3,2,1,0:T(8,128)(2,1)S(1)}, bf16[2,2,2,64,256]{4,3,2,1,0:T(8,128)(2,1)S(1)}, u32[]{:S(2)}, u32[]{:S(2)}) collective-permute-start(bf16[2,2,2,64,256]{4,3,2,1,0:T(8,128)(2,1)S(1)} %pad_maximum_fusion.1), channel_id=1, source_target_pairs={{0,64},{1,65},{2,66},{3,67},{4,68},{5,69},{6,70},{7,71},{8,72},{9,... | collective-permute-start | bytes 786440 | tf_op jit(solution)/shard_map/ppermute | solution.py:244
  125.9 2.5 %collective-permute-start.21 = (bf16[2,2,2,64,256]{4,3,2,1,0:T(8,128)(2,1)S(1)}, bf16[2,2,2,64,256]{4,3,2,1,0:T(8,128)(2,1)S(1)}, u32[]{:S(2)}, u32[]{:S(2)}) collective-permute-start(bf16[2,2,2,64,256]{4,3,2,1,0:T(8,128)(2,1)S(1)} %pad_maximum_fusion.3), channel_id=1, source_target_pairs={{0,192},{1,193},{2,194},{3,195},{4,196},{5,197},{6,198},{7,199},{8... | collective-permute-start | bytes 786440 | tf_op jit(solution)/shard_map/ppermute | solution.py:244
  128.4 6.3 %collective-permute-done.19.refs_0_ = bf16[2,2,2,64,256]{4,3,2,1,0:T(8,128)(2,1)S(1)} collective-permute-done((bf16[2,2,2,64,256]{4,3,2,1,0:T(8,128)(2,1)S(1)}, bf16[2,2,2,64,256]{4,3,2,1,0:T(8,128)(2,1)S(1)}, u32[]{:S(2)}, u32[]{:S(2)}) %collective-permute-start.19) | collective-permute-done | bytes 262176 | tf_op jit(solution)/shard_map/ppermute | solution.py:244
  134.7 6.5 %collective-permute-done.21.refs_2_ = bf16[2,2,2,64,256]{4,3,2,1,0:T(8,128)(2,1)S(1)} collective-permute-done((bf16[2,2,2,64,256]{4,3,2,1,0:T(8,128)(2,1)S(1)}, bf16[2,2,2,64,256]{4,3,2,1,0:T(8,128)(2,1)S(1)}, u32[]{:S(2)}, u32[]{:S(2)}) %collective-permute-start.21) | collective-permute-done | bytes 262176 | tf_op jit(solution)/shard_map/ppermute | solution.py:244
  (53 shorter events, 31.0 us)
Async XLA Ops:
  1.0 6.7 %collective-permute-start.1 = (bf16[2,2,64,256]{3,2,1,0:T(8,128)(2,1)S(1)}, bf16[2,2,64,256]{3,2,1,0:T(8,128)(2,1)S(1)}, u32[]{:S(2)}, u32[]{:S(2)}) collective-permute-start(bf16[2,2,64,256]{3,2,1,0:T(8,128)(2,1)S(1)} %get-tuple-element.52), channel_id=1, source_target_pairs={{0,1},{1,0},{2,3},{3,2},{4,5},{5,4},{6,7},{7,6},{8,9},{9,8},{10,11... | collective-permute-start | bytes 393224 | tf_op jit(solution)/shard_map/ppermute | solution.py:244
  4.6 12.0 %collective-permute-start = (bf16[576,256]{1,0:T(8,128)(2,1)S(1)}, bf16[576,256]{1,0:T(8,128)(2,1)S(1)}, u32[]{:S(2)}, u32[]{:S(2)}) collective-permute-start(bf16[576,256]{1,0:T(8,128)(2,1)S(1)} %dynamic-slice_bitcast_fusion.2), channel_id=1, source_target_pairs={{0,128},{1,129},{2,130},{3,131},{4,132},{5,133},{6,134},{7,135},{8... | collective-permute-start | bytes 884744 | tf_op jit(solution)/shard_map/ppermute | solution.py:244
  7.7 10.5 %collective-permute-start.2 = (bf16[2,4,64,256]{3,2,1,0:T(8,128)(2,1)S(1)}, bf16[2,4,64,256]{3,2,1,0:T(8,128)(2,1)S(1)}, u32[]{:S(2)}, u32[]{:S(2)}) collective-permute-start(bf16[2,4,64,256]{3,2,1,0:T(8,128)(2,1)S(1)} %maximum_select_fusion.1.refs_1_), channel_id=1, source_target_pairs={{2,0},{3,1},{4,2},{5,3},{6,4},{7,5},{8,6},{9,7},{10,8},{11,9},{12,... | collective-permute-start | bytes 786440 | tf_op jit(solution)/shard_map/ppermute | solution.py:244
  16.6 32.2 %copy-start.4 = (bf16[576,256]{1,0:T(8,128)(2,1)}, bf16[576,256]{1,0:T(8,128)(2,1)S(1)}, u32[]{:S(2)}) copy-start(bf16[576,256]{1,0:T(8,128)(2,1)S(1)} %collective-permute-done) | copy-start | bytes 884740
  18.2 31.8 %copy-start.6 = (bf16[2,4,64,256]{3,2,1,0:T(8,128)(2,1)}, bf16[2,4,64,256]{3,2,1,0:T(8,128)(2,1)S(1)}, u32[]{:S(2)}) copy-start(bf16[2,4,64,256]{3,2,1,0:T(8,128)(2,1)S(1)} %collective-permute-done.2.refs_2_) | copy-start | bytes 786436
  18.2 36.0 %collective-permute-start.7 = (bf16[2304,256]{1,0:T(8,128)(2,1)S(1)}, bf16[2304,256]{1,0:T(8,128)(2,1)}, u32[]{:S(2)}, u32[]{:S(2)}) collective-permute-start(bf16[2304,256]{1,0:T(8,128)(2,1)S(1)} %get-tuple-element.29.refs_3_.refs_0_), channel_id=1, source_target_pairs={{0,64},{1,65},{2,66},{3,67},{4,68},{5,69},{6,70},{7,71},{8,72},{9,... | collective-permute-start | bytes 3538952 | tf_op jit(solution)/shard_map/ppermute | solution.py:244
  21.9 34.2 %collective-permute-start.9 = (bf16[2304,256]{1,0:T(8,128)(2,1)S(1)}, bf16[2304,256]{1,0:T(8,128)(2,1)}, u32[]{:S(2)}, u32[]{:S(2)}) collective-permute-start(bf16[2304,256]{1,0:T(8,128)(2,1)S(1)} %get-tuple-element.29.refs_3_.refs_0_), channel_id=1, source_target_pairs={{0,192},{1,193},{2,194},{3,195},{4,196},{5,197},{6,198},{7,199},{8... | collective-permute-start | bytes 3538952 | tf_op jit(solution)/shard_map/ppermute | solution.py:244
  23.9 11.5 %collective-permute-start.6 = (bf16[2,4,64,256]{3,2,1,0:T(8,128)(2,1)S(1)}, bf16[2,4,64,256]{3,2,1,0:T(8,128)(2,1)}, u32[]{:S(2)}, u32[]{:S(2)}) collective-permute-start(bf16[2,4,64,256]{3,2,1,0:T(8,128)(2,1)S(1)} %maximum_select_fusion.1.refs_1_), channel_id=1, source_target_pairs={{0,2},{1,3},{2,4},{3,5},{4,6},{5,7},{6,8},{7,9},{8,10},{9,11},{10,... | collective-permute-start | bytes 786440 | tf_op jit(solution)/shard_map/ppermute | solution.py:244
  26.1 15.6 %collective-permute-start.3 = (bf16[576,256]{1,0:T(8,128)(2,1)S(1)}, bf16[576,256]{1,0:T(8,128)(2,1)S(1)}, u32[]{:S(2)}, u32[]{:S(2)}) collective-permute-start(bf16[576,256]{1,0:T(8,128)(2,1)S(1)} %collective-permute-done), channel_id=1, source_target_pairs={{0,2},{1,3},{2,4},{3,5},{4,6},{5,7},{6,8},{7,9},{8,10},{9,11},{10,... | collective-permute-start | bytes 884744 | tf_op jit(solution)/shard_map/ppermute | solution.py:244
  29.3 12.4 %collective-permute-start.4 = (bf16[576,256]{1,0:T(8,128)(2,1)S(1)}, bf16[576,256]{1,0:T(8,128)(2,1)S(1)}, u32[]{:S(2)}, u32[]{:S(2)}) collective-permute-start(bf16[576,256]{1,0:T(8,128)(2,1)S(1)} %collective-permute-done), channel_id=1, source_target_pairs={{0,14},{1,15},{2,0},{3,1},{4,2},{5,3},{6,4},{7,5},{8,6},{9,7},{10,... | collective-permute-start | bytes 884744 | tf_op jit(solution)/shard_map/ppermute | solution.py:244
  35.4 13.4 %collective-permute-start.5 = (bf16[576,256]{1,0:T(8,128)(2,1)S(1)}, bf16[576,256]{1,0:T(8,128)(2,1)S(1)}, u32[]{:S(2)}, u32[]{:S(2)}) collective-permute-start(bf16[576,256]{1,0:T(8,128)(2,1)S(1)} %collective-permute-done), channel_id=1, source_target_pairs={{0,4},{1,5},{2,14},{3,15},{4,8},{5,9},{6,2},{7,3},{8,12},{9,13},{1... | collective-permute-start | bytes 884744 | tf_op jit(solution)/shard_map/ppermute | solution.py:244
  50.0 8.7 %collective-permute-start.11 = (bf16[4,576,256]{2,1,0:T(8,128)(2,1)S(1)}, bf16[4,576,256]{2,1,0:T(8,128)(2,1)}, u32[]{:S(2)}, u32[]{:S(2)}) collective-permute-start(bf16[4,576,256]{2,1,0:T(8,128)(2,1)S(1)} %pad_maximum_fusion.refs_9_.refs_6_), channel_id=1, source_target_pairs={{0,1},{1,0},{2,3},{3,2},{4,5},{5,4},{6,7},{7,6},{8,9},{9,8},{10,11... | collective-permute-start | bytes 3538952 | tf_op jit(solution)/shard_map/ppermute | solution.py:244
  54.2 5.1 %collective-permute-start.8 = (bf16[2304,256]{1,0:T(8,128)(2,1)}, bf16[2304,256]{1,0:T(8,128)(2,1)}, u32[]{:S(2)}, u32[]{:S(2)}) collective-permute-start(bf16[2304,256]{1,0:T(8,128)(2,1)} %collective-permute-done.7.refs_5_.refs_2_), channel_id=1, source_target_pairs={{0,1},{1,0},{2,3},{3,2},{4,5},{5,4},{6,7},{7,6},{8,9},{9,8},{10,11... | collective-permute-start | bytes 3538952 | tf_op jit(solution)/shard_map/ppermute | solution.py:244
  56.2 5.2 %collective-permute-start.10 = (bf16[2304,256]{1,0:T(8,128)(2,1)}, bf16[2304,256]{1,0:T(8,128)(2,1)}, u32[]{:S(2)}, u32[]{:S(2)}) collective-permute-start(bf16[2304,256]{1,0:T(8,128)(2,1)} %collective-permute-done.9.refs_7_.refs_4_), channel_id=1, source_target_pairs={{0,1},{1,0},{2,3},{3,2},{4,5},{5,4},{6,7},{7,6},{8,9},{9,8},{10,11... | collective-permute-start | bytes 3538952 | tf_op jit(solution)/shard_map/ppermute | solution.py:244
  69.5 13.7 %collective-permute-start.12 = (bf16[1,4,64,256]{3,2,1,0:T(8,128)(2,1)S(1)}, bf16[1,4,64,256]{3,2,1,0:T(8,128)(2,1)}, u32[]{:S(2)}, u32[]{:S(2)}) collective-permute-start(bf16[1,4,64,256]{3,2,1,0:T(8,128)(2,1)S(1)} %get-tuple-element.39), channel_id=1, source_target_pairs={{0,256},{1,257},{2,258},{3,259},{4,260},{5,261},{6,262},{7,263},{8... | collective-permute-start | bytes 393224 | tf_op jit(solution)/shard_map/ppermute | solution.py:244
  76.5 17.5 %collective-permute-start.15 = (bf16[1,4,64,256]{3,2,1,0:T(8,128)(2,1)}, bf16[1,4,64,256]{3,2,1,0:T(8,128)(2,1)}, u32[]{:S(2)}, u32[]{:S(2)}) collective-permute-start(bf16[1,4,64,256]{3,2,1,0:T(8,128)(2,1)} %get-tuple-element.40), channel_id=1, source_target_pairs={{0,256},{1,257},{2,258},{3,259},{4,260},{5,261},{6,262},{7,263},{8... | collective-permute-start | bytes 393224 | tf_op jit(solution)/shard_map/ppermute | solution.py:244
  83.2 18.4 %collective-permute-start.13 = (bf16[1,4,64,256]{3,2,1,0:T(8,128)(2,1)}, bf16[1,4,64,256]{3,2,1,0:T(8,128)(2,1)}, u32[]{:S(2)}, u32[]{:S(2)}) collective-permute-start(bf16[1,4,64,256]{3,2,1,0:T(8,128)(2,1)} %collective-permute-done.12.refs_1_), channel_id=1, source_target_pairs={{256,258},{257,259},{258,260},{259,261},{260,262},{261,263},{262,2... | collective-permute-start | bytes 393224 | tf_op jit(solution)/shard_map/ppermute | solution.py:244
  85.1 16.5 %collective-permute-start.14 = (bf16[1,4,64,256]{3,2,1,0:T(8,128)(2,1)}, bf16[1,4,64,256]{3,2,1,0:T(8,128)(2,1)}, u32[]{:S(2)}, u32[]{:S(2)}) collective-permute-start(bf16[1,4,64,256]{3,2,1,0:T(8,128)(2,1)} %collective-permute-done.12.refs_1_), channel_id=1, source_target_pairs={{258,256},{259,257},{260,258},{261,259},{262,260},{263,261},{264,2... | collective-permute-start | bytes 393224 | tf_op jit(solution)/shard_map/ppermute | solution.py:244
  94.0 14.2 %collective-permute-start.16 = (bf16[1,4,64,256]{3,2,1,0:T(8,128)(2,1)}, bf16[1,4,64,256]{3,2,1,0:T(8,128)(2,1)S(1)}, u32[]{:S(2)}, u32[]{:S(2)}) collective-permute-start(bf16[1,4,64,256]{3,2,1,0:T(8,128)(2,1)} %collective-permute-done.15.refs_1_), channel_id=1, source_target_pairs={{256,258},{257,259},{258,260},{259,261},{260,262},{261,263},{262,2... | collective-permute-start | bytes 393224 | tf_op jit(solution)/shard_map/ppermute | solution.py:244
  95.9 12.2 %collective-permute-start.17 = (bf16[1,4,64,256]{3,2,1,0:T(8,128)(2,1)}, bf16[1,4,64,256]{3,2,1,0:T(8,128)(2,1)S(1)}, u32[]{:S(2)}, u32[]{:S(2)}) collective-permute-start(bf16[1,4,64,256]{3,2,1,0:T(8,128)(2,1)} %collective-permute-done.15.refs_1_), channel_id=1, source_target_pairs={{258,256},{259,257},{260,258},{261,259},{262,260},{263,261},{264,2... | collective-permute-start | bytes 393224 | tf_op jit(solution)/shard_map/ppermute | solution.py:244
  113.8 5.5 %collective-permute-start.18 = (bf16[4,2,2,64,256]{4,3,2,1,0:T(8,128)(2,1)S(1)}, bf16[4,2,2,64,256]{4,3,2,1,0:T(8,128)(2,1)S(1)}, u32[]{:S(2)}, u32[]{:S(2)}) collective-permute-start(bf16[4,2,2,64,256]{4,3,2,1,0:T(8,128)(2,1)S(1)} %get-tuple-element.49), channel_id=1, source_target_pairs={{0,1},{1,0},{2,3},{3,2},{4,5},{5,4},{6,7},{7,6},{8,9},{9,8},{10,11... | collective-permute-start | bytes 1572872 | tf_op jit(solution)/shard_map/ppermute | solution.py:244
  119.4 15.3 %collective-permute-start.19 = (bf16[2,2,2,64,256]{4,3,2,1,0:T(8,128)(2,1)S(1)}, bf16[2,2,2,64,256]{4,3,2,1,0:T(8,128)(2,1)S(1)}, u32[]{:S(2)}, u32[]{:S(2)}) collective-permute-start(bf16[2,2,2,64,256]{4,3,2,1,0:T(8,128)(2,1)S(1)} %pad_maximum_fusion.1), channel_id=1, source_target_pairs={{0,64},{1,65},{2,66},{3,67},{4,68},{5,69},{6,70},{7,71},{8,72},{9,... | collective-permute-start | bytes 786440 | tf_op jit(solution)/shard_map/ppermute | solution.py:244
  124.0 10.7 %collective-permute-start.20 = (bf16[2,2,2,64,256]{4,3,2,1,0:T(8,128)(2,1)S(1)}, bf16[2,2,2,64,256]{4,3,2,1,0:T(8,128)(2,1)S(1)}, u32[]{:S(2)}, u32[]{:S(2)}) collective-permute-start(bf16[2,2,2,64,256]{4,3,2,1,0:T(8,128)(2,1)S(1)} %pad_maximum_fusion.2), channel_id=1, source_target_pairs={{0,128},{1,129},{2,130},{3,131},{4,132},{5,133},{6,134},{7,135},{8... | collective-permute-start | bytes 786440 | tf_op jit(solution)/shard_map/ppermute | solution.py:244
  125.9 15.3 %collective-permute-start.21 = (bf16[2,2,2,64,256]{4,3,2,1,0:T(8,128)(2,1)S(1)}, bf16[2,2,2,64,256]{4,3,2,1,0:T(8,128)(2,1)S(1)}, u32[]{:S(2)}, u32[]{:S(2)}) collective-permute-start(bf16[2,2,2,64,256]{4,3,2,1,0:T(8,128)(2,1)S(1)} %pad_maximum_fusion.3), channel_id=1, source_target_pairs={{0,192},{1,193},{2,194},{3,195},{4,196},{5,197},{6,198},{7,199},{8... | collective-permute-start | bytes 786440 | tf_op jit(solution)/shard_map/ppermute | solution.py:244
  (5 other events, 33.9 us)

commit v8 on v7

--- a/solution.py
+++ b/solution.py
@@ -32,27 +32,6 @@
                 for source, owner in ((pieces[at], core), (pieces[at + 1], 1 - core)):
                     for rows, block in (quarters if distance == 2 else whole)(source):
                         pltpu.make_async_copy(block, weights.at[layer, owner, rows], sems.at[layer]).start()
-
-
-def gather_kernel(meta, *refs):
-    pieces, weights, sems = refs[:8], refs[8], refs[9]
-    fetch_weights(meta, pieces, weights, sems)
-    for layer in range(DEPTH):
-        pltpu.make_async_copy(weights.at[layer], weights.at[layer], sems.at[layer]).wait()
-
-
-def gather(meta, kernels):
-    taps, chans = kernels[0].shape
-    return pl.pallas_call(
-        gather_kernel,
-        out_shape=jax.ShapeDtypeStruct((DEPTH, 2, taps, chans), jnp.bfloat16),
-        in_specs=[pl.BlockSpec(memory_space=pltpu.SMEM)] + [pl.BlockSpec(memory_space=pl.ANY)] * 8,
-        out_specs=pl.BlockSpec(memory_space=pltpu.VMEM),
-        scratch_shapes=[pltpu.SemaphoreType.DMA((DEPTH,))],
-        compiler_params=pltpu.CompilerParams(vmem_limit_bytes=LIMIT * 1024 * 1024),
-        cost_estimate=pl.CostEstimate(flops=0, bytes_accessed=19 * 10**6, transcendentals=0),
-        name="gather",
-    )(meta, *kernels)
 
 
 def frame_kernel(frame, builds, slabs, meta, *refs):
@@ -287,13 +266,15 @@
     mine = lax.dynamic_index_in_dim(own, core, 0, keepdims=False)
     theirs = lax.dynamic_index_in_dim(own, 1 - core, 0, keepdims=False)
     mid = jnp.where(core == 0, jnp.concatenate([keep, got], 1), jnp.concatenate([got, keep], 1))
-    top = send(mid, next_chip(1))
     bot = send(mid, next_chip(-1))
 
     far, mine, bot = lax.optimization_barrier((far, mine, bot))
     left_mine = send(mine, along_x(1))
     right_mine = send(mine, along_x(-1))
     parts = (far, send(far, along_y(1)), send(far, along_y(-1)), send(far, two_along_y))
+    early, center = lax.optimization_barrier((parts[2], mid))
+    top = send(center, next_chip(1))
+    parts = (parts[0], parts[1], early, parts[3])
     *parts, top = lax.optimization_barrier((*parts, top))
     far_mine = jnp.stack(parts)
     far_theirs = send(far_mine, sibling)
@@ -309,12 +290,9 @@
     first.append(kept)
     mid_1 = send(reached, hop)
 
-    later_meta, _ = lax.optimization_barrier((meta, mid_0))
-    weights = gather(later_meta, kernels)
-    mid_1, weights = lax.optimization_barrier((mid_1, weights))
     second = []
     top, bot = send(mid_0, next_chip(1), is_upper), send(mid_0, next_chip(-1), is_upper)
-    kept, _, older = run_frame(0, meta, (top, mid_0, bot), weights)
+    kept, _, older, weights = run_frame(0, meta, (top, mid_0, bot), kernels)
     second.append(kept)
     top, bot = send(mid_1, next_chip(1), is_upper), send(mid_1, next_chip(-1), is_upper)
     kept, _ = run_frame(1, meta, (top, mid_1, bot), weights, older)

time: 144 us -> 143 us (level)
  waiting for transfers between devices: 38.9 us -> 43.9 us
  starting transfers between devices: 67.3 us -> 62.4 us
    ppermute x22, waiting for transfers between devices: 38.9 us -> 43.9 us  [send(): return lax.ppermute(array, ('section', 'rows'), route(move, keep))]
    ppermute x22, starting transfers between devices: 67.3 us -> 62.4 us  [send(): return lax.ppermute(array, ('section', 'rows'), route(move, keep))]
    pallas_call x1 -> x0, Pallas kernels: 3.37 us -> none  [gather(): pl.pallas_call(gather_kernel, out_shape=jax.ShapeDtypeStruct((DEPTH, 2, t...]
    pallas_call x4, Pallas kernels: 24.9 us -> 27.2 us  [run_frame(): pl.pallas_call(functools.partial(frame_kernel, frame, builds, len(inputs)...]
  transfers between devices with their start and end apart: 22 -> 22, of which waited for: 11 -> 13; matrix products, arithmetic and copies ran while one was open for 3% -> 3% of each run, Pallas kernels for 10% -> 10%
where the time goes in v8:
time: 143 us; the launch traced here: 142 us
  starting transfers between devices  62.4 us (44%)
  waiting for transfers between devices  43.9 us (31%)
  Pallas kernels  28.8 us (20%)
  local copies, waits for them, and re-layouts  4.82 us (3%)
  other arithmetic  1.5 us (1%)
    ppermute x22, starting transfers between devices, send(): return lax.ppermute(array, ('section', 'rows'), route(move, keep))  62.4 us
    ppermute x22, waiting for transfers between devices, send(): return lax.ppermute(array, ('section', 'rows'), route(move, keep))  43.9 us
    pallas_call x4, Pallas kernels, run_frame(): pl.pallas_call(functools.partial(frame_kernel, frame, builds, len(inputs)...  27.2 us
  transfers between devices with their start and end apart: 22, of which 13 were waited for; matrix products, arithmetic and copies ran while one was open for 3% of the time, Pallas kernels for 10%

profile of v8, /device:TPU:327, one launch (start us, length us, event | category | flops | bytes accessed | tf_op | source)
XLA Modules:
  0.0 142.0 jit_solution(1451087469853745500)
XLA Ops:
  1.0 2.6 %collective-permute-start.1 = (bf16[2,2,64,256]{3,2,1,0:T(8,128)(2,1)S(1)}, bf16[2,2,64,256]{3,2,1,0:T(8,128)(2,1)S(1)}, u32[]{:S(2)}, u32[]{:S(2)}) collective-permute-start(bf16[2,2,64,256]{3,2,1,0:T(8,128)(2,1)S(1)} %get-tuple-element.52), channel_id=1, source_target_pairs={{0,1},{1,0},{2,3},{3,2},{4,5},{5,4},{6,7},{7,6},{8,9},{9,8},{10,11... | collective-permute-start | bytes 393224 | tf_op jit(solution)/shard_map/ppermute | solution.py:223
  4.6 3.0 %collective-permute-start = (bf16[576,256]{1,0:T(8,128)(2,1)S(1)}, bf16[576,256]{1,0:T(8,128)(2,1)S(1)}, u32[]{:S(2)}, u32[]{:S(2)}) collective-permute-start(bf16[576,256]{1,0:T(8,128)(2,1)S(1)} %dynamic-slice_bitcast_fusion.2), channel_id=1, source_target_pairs={{0,128},{1,129},{2,130},{3,131},{4,132},{5,133},{6,134},{7,135},{8... | collective-permute-start | bytes 884744 | tf_op jit(solution)/shard_map/ppermute | solution.py:223
  7.7 5.1 %collective-permute-start.2 = (bf16[2,4,64,256]{3,2,1,0:T(8,128)(2,1)S(1)}, bf16[2,4,64,256]{3,2,1,0:T(8,128)(2,1)S(1)}, u32[]{:S(2)}, u32[]{:S(2)}) collective-permute-start(bf16[2,4,64,256]{3,2,1,0:T(8,128)(2,1)S(1)} %maximum_select_fusion.1.refs_1_), channel_id=1, source_target_pairs={{2,0},{3,1},{4,2},{5,3},{6,4},{7,5},{8,6},{9,7},{10,8},{11,9},{12,... | collective-permute-start | bytes 786440 | tf_op jit(solution)/shard_map/ppermute | solution.py:223
  20.1 4.6 %collective-permute-start.7 = (bf16[2304,256]{1,0:T(8,128)(2,1)S(1)}, bf16[2304,256]{1,0:T(8,128)(2,1)}, u32[]{:S(2)}, u32[]{:S(2)}) collective-permute-start(bf16[2304,256]{1,0:T(8,128)(2,1)S(1)} %get-tuple-element.31.refs_3_), channel_id=1, source_target_pairs={{0,64},{1,65},{2,66},{3,67},{4,68},{5,69},{6,70},{7,71},{8,72},{9,... | collective-permute-start | bytes 3538952 | tf_op jit(solution)/shard_map/ppermute | solution.py:223
  24.7 6.2 %collective-permute-start.4 = (bf16[576,256]{1,0:T(8,128)(2,1)S(1)}, bf16[576,256]{1,0:T(8,128)(2,1)S(1)}, u32[]{:S(2)}, u32[]{:S(2)}) collective-permute-start(bf16[576,256]{1,0:T(8,128)(2,1)S(1)} %collective-permute-done), channel_id=1, source_target_pairs={{0,14},{1,15},{2,0},{3,1},{4,2},{5,3},{6,4},{7,5},{8,6},{9,7},{10,... | collective-permute-start | bytes 884744 | tf_op jit(solution)/shard_map/ppermute | solution.py:223
  32.9 3.1 %collective-permute-start.3 = (bf16[576,256]{1,0:T(8,128)(2,1)S(1)}, bf16[576,256]{1,0:T(8,128)(2,1)S(1)}, u32[]{:S(2)}, u32[]{:S(2)}) collective-permute-start(bf16[576,256]{1,0:T(8,128)(2,1)S(1)} %collective-permute-done), channel_id=1, source_target_pairs={{0,2},{1,3},{2,4},{3,5},{4,6},{5,7},{6,8},{7,9},{8,10},{9,11},{10,... | collective-permute-start | bytes 884744 | tf_op jit(solution)/shard_map/ppermute | solution.py:223
  36.0 5.8 %collective-permute-done.4 = bf16[576,256]{1,0:T(8,128)(2,1)S(1)} collective-permute-done((bf16[576,256]{1,0:T(8,128)(2,1)S(1)}, bf16[576,256]{1,0:T(8,128)(2,1)S(1)}, u32[]{:S(2)}, u32[]{:S(2)}) %collective-permute-start.4) | collective-permute-done | bytes 294944 | tf_op jit(solution)/shard_map/ppermute | solution.py:223
  43.7 6.5 %collective-permute-done.3 = bf16[576,256]{1,0:T(8,128)(2,1)S(1)} collective-permute-done((bf16[576,256]{1,0:T(8,128)(2,1)S(1)}, bf16[576,256]{1,0:T(8,128)(2,1)S(1)}, u32[]{:S(2)}, u32[]{:S(2)}) %collective-permute-start.3) | collective-permute-done | bytes 294944 | tf_op jit(solution)/shard_map/ppermute | solution.py:223
  50.2 4.3 %collective-permute-done.6.refs_0_ = bf16[2,4,64,256]{3,2,1,0:T(8,128)(2,1)S(1)} collective-permute-done((bf16[2,4,64,256]{3,2,1,0:T(8,128)(2,1)S(1)}, bf16[2,4,64,256]{3,2,1,0:T(8,128)(2,1)S(1)}, u32[]{:S(2)}, u32[]{:S(2)}) %collective-permute-start.6) | collective-permute-done | bytes 262176 | tf_op jit(solution)/shard_map/ppermute | solution.py:223
  55.7 3.7 %collective-permute-start.11 = (bf16[4,576,256]{2,1,0:T(8,128)(2,1)S(1)}, bf16[4,576,256]{2,1,0:T(8,128)(2,1)}, u32[]{:S(2)}, u32[]{:S(2)}) collective-permute-start(bf16[4,576,256]{2,1,0:T(8,128)(2,1)S(1)} %pad_maximum_fusion.refs_9_), channel_id=1, source_target_pairs={{0,1},{1,0},{2,3},{3,2},{4,5},{5,4},{6,7},{7,6},{8,9},{9,8},{10,11... | collective-permute-start | bytes 3538952 | tf_op jit(solution)/shard_map/ppermute | solution.py:223
  61.4 2.4 %collective-permute-start.8 = (bf16[2304,256]{1,0:T(8,128)(2,1)}, bf16[2304,256]{1,0:T(8,128)(2,1)}, u32[]{:S(2)}, u32[]{:S(2)}) collective-permute-start(bf16[2304,256]{1,0:T(8,128)(2,1)} %collective-permute-done.7.refs_5_), channel_id=1, source_target_pairs={{0,1},{1,0},{2,3},{3,2},{4,5},{5,4},{6,7},{7,6},{8,9},{9,8},{10,11... | collective-permute-start | bytes 3538952 | tf_op jit(solution)/shard_map/ppermute | solution.py:223
  66.6 8.1 %frame0.2 = (bf16[2,4,2,64,256]{4,3,2,1,0:T(8,128)(2,1)S(1)}, bf16[1,4,64,256]{3,2,1,0:T(8,128)(2,1)S(1)}, f32[28,64,256]{2,1,0:T(8,128)S(1)}, bf16[4,2,2304,256...) custom-call(s32[5]{0:T(128)S(1)} %stack.67.meta, bf16[2,4,64,256]{3,2,1,0:T(8,128)(2,1)} %copy-done.7, ...), custom_call_target="tpu_custom_call" | custom-call | flops 4227858432 | bytes 8000000 | tf_op jit(solution)/shard_map/frame0/pallas_call | solution.py:159
  76.0 4.9 %frame1.2 = (bf16[2,4,2,64,256]{4,3,2,1,0:T(8,128)(2,1)S(1)}, bf16[1,4,64,256]{3,2,1,0:T(8,128)(2,1)}) custom-call(s32[5]{0:T(128)S(1)} %stack.67.meta, bf16[1,12,64,256]{3,2,1,0:T(8,128)(2,1)S(1)} %get-tuple-element.37.refs_0_, bf16[4,2,2304,256]{3,2,1,0:T(8,128)(2,1)S(1)} %get-tuple-element.38.refs_1_, f32[28,64,256]{2,1,0:T(8,128)S(1)} %get-tuple-element.39.refs_2_), custom_call_target="tpu_custom_call" | custom-call | flops 2113929216 | bytes 8000000 | tf_op jit(solution)/shard_map/frame1/pallas_call | solution.py:159
  83.0 5.1 %collective-permute-done.12.refs_1_ = bf16[1,4,64,256]{3,2,1,0:T(8,128)(2,1)} collective-permute-done((bf16[1,4,64,256]{3,2,1,0:T(8,128)(2,1)S(1)}, bf16[1,4,64,256]{3,2,1,0:T(8,128)(2,1)}, u32[]{:S(2)}, u32[]{:S(2)}) %collective-permute-start.12) | collective-permute-done | bytes 131104 | tf_op jit(solution)/shard_map/ppermute | solution.py:223
  90.0 3.4 %collective-permute-start.13 = (bf16[1,4,64,256]{3,2,1,0:T(8,128)(2,1)}, bf16[1,4,64,256]{3,2,1,0:T(8,128)(2,1)}, u32[]{:S(2)}, u32[]{:S(2)}) collective-permute-start(bf16[1,4,64,256]{3,2,1,0:T(8,128)(2,1)} %collective-permute-done.12.refs_1_), channel_id=1, source_target_pairs={{256,258},{257,259},{258,260},{259,261},{260,262},{261,263},{262,2... | collective-permute-start | bytes 393224 | tf_op jit(solution)/shard_map/ppermute | solution.py:223
  93.4 2.6 %collective-permute-done.15.refs_1_ = bf16[1,4,64,256]{3,2,1,0:T(8,128)(2,1)} collective-permute-done((bf16[1,4,64,256]{3,2,1,0:T(8,128)(2,1)}, bf16[1,4,64,256]{3,2,1,0:T(8,128)(2,1)}, u32[]{:S(2)}, u32[]{:S(2)}) %collective-permute-start.15) | collective-permute-done | bytes 131104 | tf_op jit(solution)/shard_map/ppermute | solution.py:223
  97.9 3.4 %collective-permute-start.16 = (bf16[1,4,64,256]{3,2,1,0:T(8,128)(2,1)}, bf16[1,4,64,256]{3,2,1,0:T(8,128)(2,1)S(1)}, u32[]{:S(2)}, u32[]{:S(2)}) collective-permute-start(bf16[1,4,64,256]{3,2,1,0:T(8,128)(2,1)} %collective-permute-done.15.refs_1_), channel_id=1, source_target_pairs={{256,258},{257,259},{258,260},{259,261},{260,262},{261,263},{262,2... | collective-permute-start | bytes 393224 | tf_op jit(solution)/shard_map/ppermute | solution.py:223
  101.3 8.9 %frame0.3 = (bf16[2,4,2,64,256]{4,3,2,1,0:T(8,128)(2,1)S(1)}, bf16[1,4,64,256]{3,2,1,0:T(8,128)(2,1)}, f32[28,64,256]{2,1,0:T(8,128)S(1)}, bf16[4,2,2304,256]{3,2,1,0:T(8,128)(2,1)S(1)}) custom-call(s32[5]{0:T(128)S(1)} %stack.67.meta, bf16[1,4,64,256]{3,2,1,0:T(8,128)(2,1)} %collective-permute-done.13.refs_0_, ...), custom_call_target="tpu_custom_call" | custom-call | flops 4227858432 | bytes 8000000 | tf_op jit(solution)/shard_map/frame0/pallas_call | solution.py:159
  110.2 5.3 %frame1.3 = (bf16[2,4,2,64,256]{4,3,2,1,0:T(8,128)(2,1)S(1)}, bf16[1,4,64,256]{3,2,1,0:T(8,128)(2,1)}) custom-call(s32[5]{0:T(128)S(1)} %stack.67.meta, bf16[1,4,64,256]{3,2,1,0:T(8,128)(2,1)S(1)} %collective-permute-done.16.refs_0_, bf16[1,4,64,256]{3,2,1,0:T(8,128)(2,1)} %collective-permute-done.15.refs_1_, ...), custom_call_target="tpu_custom_call" | custom-call | flops 2113929216 | bytes 8000000 | tf_op jit(solution)/shard_map/frame1/pallas_call | solution.py:159
  115.9 3.7 %collective-permute-start.18 = (bf16[4,2,2,64,256]{4,3,2,1,0:T(8,128)(2,1)S(1)}, bf16[4,2,2,64,256]{4,3,2,1,0:T(8,128)(2,1)S(1)}, u32[]{:S(2)}, u32[]{:S(2)}) collective-permute-start(bf16[4,2,2,64,256]{4,3,2,1,0:T(8,128)(2,1)S(1)} %get-tuple-element.49), channel_id=1, source_target_pairs={{0,1},{1,0},{2,3},{3,2},{4,5},{5,4},{6,7},{7,6},{8,9},{9,8},{10,11... | collective-permute-start | bytes 1572872 | tf_op jit(solution)/shard_map/ppermute | solution.py:223
  123.1 2.5 %collective-permute-start.20 = (bf16[2,2,2,64,256]{4,3,2,1,0:T(8,128)(2,1)S(1)}, bf16[2,2,2,64,256]{4,3,2,1,0:T(8,128)(2,1)S(1)}, u32[]{:S(2)}, u32[]{:S(2)}) collective-permute-start(bf16[2,2,2,64,256]{4,3,2,1,0:T(8,128)(2,1)S(1)} %pad_maximum_fusion.2), channel_id=1, source_target_pairs={{0,128},{1,129},{2,130},{3,131},{4,132},{5,133},{6,134},{7,135},{8... | collective-permute-start | bytes 786440 | tf_op jit(solution)/shard_map/ppermute | solution.py:223
  125.7 2.8 %collective-permute-start.21 = (bf16[2,2,2,64,256]{4,3,2,1,0:T(8,128)(2,1)S(1)}, bf16[2,2,2,64,256]{4,3,2,1,0:T(8,128)(2,1)S(1)}, u32[]{:S(2)}, u32[]{:S(2)}) collective-permute-start(bf16[2,2,2,64,256]{4,3,2,1,0:T(8,128)(2,1)S(1)} %pad_maximum_fusion.3), channel_id=1, source_target_pairs={{0,192},{1,193},{2,194},{3,195},{4,196},{5,197},{6,198},{7,199},{8... | collective-permute-start | bytes 786440 | tf_op jit(solution)/shard_map/ppermute | solution.py:223
  130.6 3.5 %collective-permute-done.20.refs_1_ = bf16[2,2,2,64,256]{4,3,2,1,0:T(8,128)(2,1)S(1)} collective-permute-done((bf16[2,2,2,64,256]{4,3,2,1,0:T(8,128)(2,1)S(1)}, bf16[2,2,2,64,256]{4,3,2,1,0:T(8,128)(2,1)S(1)}, u32[]{:S(2)}, u32[]{:S(2)}) %collective-permute-start.20) | collective-permute-done | bytes 262176 | tf_op jit(solution)/shard_map/ppermute | solution.py:223
  134.1 6.3 %collective-permute-done.21.refs_2_ = bf16[2,2,2,64,256]{4,3,2,1,0:T(8,128)(2,1)S(1)} collective-permute-done((bf16[2,2,2,64,256]{4,3,2,1,0:T(8,128)(2,1)S(1)}, bf16[2,2,2,64,256]{4,3,2,1,0:T(8,128)(2,1)S(1)}, u32[]{:S(2)}, u32[]{:S(2)}) %collective-permute-start.21) | collective-permute-done | bytes 262176 | tf_op jit(solution)/shard_map/ppermute | solution.py:223
  (54 shorter events, 33.7 us)
Async XLA Ops:
  1.0 6.7 %collective-permute-start.1 = (bf16[2,2,64,256]{3,2,1,0:T(8,128)(2,1)S(1)}, bf16[2,2,64,256]{3,2,1,0:T(8,128)(2,1)S(1)}, u32[]{:S(2)}, u32[]{:S(2)}) collective-permute-start(bf16[2,2,64,256]{3,2,1,0:T(8,128)(2,1)S(1)} %get-tuple-element.52), channel_id=1, source_target_pairs={{0,1},{1,0},{2,3},{3,2},{4,5},{5,4},{6,7},{7,6},{8,9},{9,8},{10,11... | collective-permute-start | bytes 393224 | tf_op jit(solution)/shard_map/ppermute | solution.py:223
  4.6 12.0 %collective-permute-start = (bf16[576,256]{1,0:T(8,128)(2,1)S(1)}, bf16[576,256]{1,0:T(8,128)(2,1)S(1)}, u32[]{:S(2)}, u32[]{:S(2)}) collective-permute-start(bf16[576,256]{1,0:T(8,128)(2,1)S(1)} %dynamic-slice_bitcast_fusion.2), channel_id=1, source_target_pairs={{0,128},{1,129},{2,130},{3,131},{4,132},{5,133},{6,134},{7,135},{8... | collective-permute-start | bytes 884744 | tf_op jit(solution)/shard_map/ppermute | solution.py:223
  7.7 10.5 %collective-permute-start.2 = (bf16[2,4,64,256]{3,2,1,0:T(8,128)(2,1)S(1)}, bf16[2,4,64,256]{3,2,1,0:T(8,128)(2,1)S(1)}, u32[]{:S(2)}, u32[]{:S(2)}) collective-permute-start(bf16[2,4,64,256]{3,2,1,0:T(8,128)(2,1)S(1)} %maximum_select_fusion.1.refs_1_), channel_id=1, source_target_pairs={{2,0},{3,1},{4,2},{5,3},{6,4},{7,5},{8,6},{9,7},{10,8},{11,9},{12,... | collective-permute-start | bytes 786440 | tf_op jit(solution)/shard_map/ppermute | solution.py:223
  16.6 37.9 %copy-start.4 = (bf16[576,256]{1,0:T(8,128)(2,1)}, bf16[576,256]{1,0:T(8,128)(2,1)S(1)}, u32[]{:S(2)}) copy-start(bf16[576,256]{1,0:T(8,128)(2,1)S(1)} %collective-permute-done) | copy-start | bytes 884740
  18.2 37.5 %copy-start.6 = (bf16[2,4,64,256]{3,2,1,0:T(8,128)(2,1)}, bf16[2,4,64,256]{3,2,1,0:T(8,128)(2,1)S(1)}, u32[]{:S(2)}) copy-start(bf16[2,4,64,256]{3,2,1,0:T(8,128)(2,1)S(1)} %collective-permute-done.2.refs_2_) | copy-start | bytes 786436
  18.2 41.2 %collective-permute-start.9 = (bf16[2304,256]{1,0:T(8,128)(2,1)S(1)}, bf16[2304,256]{1,0:T(8,128)(2,1)}, u32[]{:S(2)}, u32[]{:S(2)}) collective-permute-start(bf16[2304,256]{1,0:T(8,128)(2,1)S(1)} %get-tuple-element.31.refs_3_), channel_id=1, source_target_pairs={{0,192},{1,193},{2,194},{3,195},{4,196},{5,197},{6,198},{7,199},{8... | collective-permute-start | bytes 3538952 | tf_op jit(solution)/shard_map/ppermute | solution.py:223
  20.1 41.3 %collective-permute-start.7 = (bf16[2304,256]{1,0:T(8,128)(2,1)S(1)}, bf16[2304,256]{1,0:T(8,128)(2,1)}, u32[]{:S(2)}, u32[]{:S(2)}) collective-permute-start(bf16[2304,256]{1,0:T(8,128)(2,1)S(1)} %get-tuple-element.31.refs_3_), channel_id=1, source_target_pairs={{0,64},{1,65},{2,66},{3,67},{4,68},{5,69},{6,70},{7,71},{8,72},{9,... | collective-permute-start | bytes 3538952 | tf_op jit(solution)/shard_map/ppermute | solution.py:223
  24.7 17.0 %collective-permute-start.4 = (bf16[576,256]{1,0:T(8,128)(2,1)S(1)}, bf16[576,256]{1,0:T(8,128)(2,1)S(1)}, u32[]{:S(2)}, u32[]{:S(2)}) collective-permute-start(bf16[576,256]{1,0:T(8,128)(2,1)S(1)} %collective-permute-done), channel_id=1, source_target_pairs={{0,14},{1,15},{2,0},{3,1},{4,2},{5,3},{6,4},{7,5},{8,6},{9,7},{10,... | collective-permute-start | bytes 884744 | tf_op jit(solution)/shard_map/ppermute | solution.py:223
  30.9 12.7 %collective-permute-start.5 = (bf16[576,256]{1,0:T(8,128)(2,1)S(1)}, bf16[576,256]{1,0:T(8,128)(2,1)S(1)}, u32[]{:S(2)}, u32[]{:S(2)}) collective-permute-start(bf16[576,256]{1,0:T(8,128)(2,1)S(1)} %collective-permute-done), channel_id=1, source_target_pairs={{0,4},{1,5},{2,14},{3,15},{4,8},{5,9},{6,2},{7,3},{8,12},{9,13},{1... | collective-permute-start | bytes 884744 | tf_op jit(solution)/shard_map/ppermute | solution.py:223
  32.9 17.3 %collective-permute-start.3 = (bf16[576,256]{1,0:T(8,128)(2,1)S(1)}, bf16[576,256]{1,0:T(8,128)(2,1)S(1)}, u32[]{:S(2)}, u32[]{:S(2)}) collective-permute-start(bf16[576,256]{1,0:T(8,128)(2,1)S(1)} %collective-permute-done), channel_id=1, source_target_pairs={{0,2},{1,3},{2,4},{3,5},{4,6},{5,7},{6,8},{7,9},{8,10},{9,11},{10,... | collective-permute-start | bytes 884744 | tf_op jit(solution)/shard_map/ppermute | solution.py:223
  41.7 12.8 %collective-permute-start.6 = (bf16[2,4,64,256]{3,2,1,0:T(8,128)(2,1)S(1)}, bf16[2,4,64,256]{3,2,1,0:T(8,128)(2,1)S(1)}, u32[]{:S(2)}, u32[]{:S(2)}) collective-permute-start(bf16[2,4,64,256]{3,2,1,0:T(8,128)(2,1)S(1)} %maximum_select_fusion.1.refs_1_), channel_id=1, source_target_pairs={{0,2},{1,3},{2,4},{3,5},{4,6},{5,7},{6,8},{7,9},{8,10},{9,11},{10,... | collective-permute-start | bytes 786440 | tf_op jit(solution)/shard_map/ppermute | solution.py:223
  55.7 8.2 %collective-permute-start.11 = (bf16[4,576,256]{2,1,0:T(8,128)(2,1)S(1)}, bf16[4,576,256]{2,1,0:T(8,128)(2,1)}, u32[]{:S(2)}, u32[]{:S(2)}) collective-permute-start(bf16[4,576,256]{2,1,0:T(8,128)(2,1)S(1)} %pad_maximum_fusion.refs_9_), channel_id=1, source_target_pairs={{0,1},{1,0},{2,3},{3,2},{4,5},{5,4},{6,7},{7,6},{8,9},{9,8},{10,11... | collective-permute-start | bytes 3538952 | tf_op jit(solution)/shard_map/ppermute | solution.py:223
  59.5 5.1 %collective-permute-start.10 = (bf16[2304,256]{1,0:T(8,128)(2,1)}, bf16[2304,256]{1,0:T(8,128)(2,1)}, u32[]{:S(2)}, u32[]{:S(2)}) collective-permute-start(bf16[2304,256]{1,0:T(8,128)(2,1)} %collective-permute-done.9.refs_7_), channel_id=1, source_target_pairs={{0,1},{1,0},{2,3},{3,2},{4,5},{5,4},{6,7},{7,6},{8,9},{9,8},{10,11... | collective-permute-start | bytes 3538952 | tf_op jit(solution)/shard_map/ppermute | solution.py:223
  61.4 5.2 %collective-permute-start.8 = (bf16[2304,256]{1,0:T(8,128)(2,1)}, bf16[2304,256]{1,0:T(8,128)(2,1)}, u32[]{:S(2)}, u32[]{:S(2)}) collective-permute-start(bf16[2304,256]{1,0:T(8,128)(2,1)} %collective-permute-done.7.refs_5_), channel_id=1, source_target_pairs={{0,1},{1,0},{2,3},{3,2},{4,5},{5,4},{6,7},{7,6},{8,9},{9,8},{10,11... | collective-permute-start | bytes 3538952 | tf_op jit(solution)/shard_map/ppermute | solution.py:223
  74.7 13.4 %collective-permute-start.12 = (bf16[1,4,64,256]{3,2,1,0:T(8,128)(2,1)S(1)}, bf16[1,4,64,256]{3,2,1,0:T(8,128)(2,1)}, u32[]{:S(2)}, u32[]{:S(2)}) collective-permute-start(bf16[1,4,64,256]{3,2,1,0:T(8,128)(2,1)S(1)} %get-tuple-element.41), channel_id=1, source_target_pairs={{0,256},{1,257},{2,258},{3,259},{4,260},{5,261},{6,262},{7,263},{8... | collective-permute-start | bytes 393224 | tf_op jit(solution)/shard_map/ppermute | solution.py:223
  81.7 14.3 %collective-permute-start.15 = (bf16[1,4,64,256]{3,2,1,0:T(8,128)(2,1)}, bf16[1,4,64,256]{3,2,1,0:T(8,128)(2,1)}, u32[]{:S(2)}, u32[]{:S(2)}) collective-permute-start(bf16[1,4,64,256]{3,2,1,0:T(8,128)(2,1)} %get-tuple-element.43), channel_id=1, source_target_pairs={{0,256},{1,257},{2,258},{3,259},{4,260},{5,261},{6,262},{7,263},{8... | collective-permute-start | bytes 393224 | tf_op jit(solution)/shard_map/ppermute | solution.py:223
  88.1 13.2 %collective-permute-start.14 = (bf16[1,4,64,256]{3,2,1,0:T(8,128)(2,1)}, bf16[1,4,64,256]{3,2,1,0:T(8,128)(2,1)}, u32[]{:S(2)}, u32[]{:S(2)}) collective-permute-start(bf16[1,4,64,256]{3,2,1,0:T(8,128)(2,1)} %collective-permute-done.12.refs_1_), channel_id=1, source_target_pairs={{258,256},{259,257},{260,258},{261,259},{262,260},{263,261},{264,2... | collective-permute-start | bytes 393224 | tf_op jit(solution)/shard_map/ppermute | solution.py:223
  90.0 11.3 %collective-permute-start.13 = (bf16[1,4,64,256]{3,2,1,0:T(8,128)(2,1)}, bf16[1,4,64,256]{3,2,1,0:T(8,128)(2,1)}, u32[]{:S(2)}, u32[]{:S(2)}) collective-permute-start(bf16[1,4,64,256]{3,2,1,0:T(8,128)(2,1)} %collective-permute-done.12.refs_1_), channel_id=1, source_target_pairs={{256,258},{257,259},{258,260},{259,261},{260,262},{261,263},{262,2... | collective-permute-start | bytes 393224 | tf_op jit(solution)/shard_map/ppermute | solution.py:223
  96.0 14.2 %collective-permute-start.17 = (bf16[1,4,64,256]{3,2,1,0:T(8,128)(2,1)}, bf16[1,4,64,256]{3,2,1,0:T(8,128)(2,1)S(1)}, u32[]{:S(2)}, u32[]{:S(2)}) collective-permute-start(bf16[1,4,64,256]{3,2,1,0:T(8,128)(2,1)} %collective-permute-done.15.refs_1_), channel_id=1, source_target_pairs={{258,256},{259,257},{260,258},{261,259},{262,260},{263,261},{264,2... | collective-permute-start | bytes 393224 | tf_op jit(solution)/shard_map/ppermute | solution.py:223
  97.9 12.3 %collective-permute-start.16 = (bf16[1,4,64,256]{3,2,1,0:T(8,128)(2,1)}, bf16[1,4,64,256]{3,2,1,0:T(8,128)(2,1)S(1)}, u32[]{:S(2)}, u32[]{:S(2)}) collective-permute-start(bf16[1,4,64,256]{3,2,1,0:T(8,128)(2,1)} %collective-permute-done.15.refs_1_), channel_id=1, source_target_pairs={{256,258},{257,259},{258,260},{259,261},{260,262},{261,263},{262,2... | collective-permute-start | bytes 393224 | tf_op jit(solution)/shard_map/ppermute | solution.py:223
  115.9 5.2 %collective-permute-start.18 = (bf16[4,2,2,64,256]{4,3,2,1,0:T(8,128)(2,1)S(1)}, bf16[4,2,2,64,256]{4,3,2,1,0:T(8,128)(2,1)S(1)}, u32[]{:S(2)}, u32[]{:S(2)}) collective-permute-start(bf16[4,2,2,64,256]{4,3,2,1,0:T(8,128)(2,1)S(1)} %get-tuple-element.49), channel_id=1, source_target_pairs={{0,1},{1,0},{2,3},{3,2},{4,5},{5,4},{6,7},{7,6},{8,9},{9,8},{10,11... | collective-permute-start | bytes 1572872 | tf_op jit(solution)/shard_map/ppermute | solution.py:223
  121.2 9.4 %collective-permute-start.19 = (bf16[2,2,2,64,256]{4,3,2,1,0:T(8,128)(2,1)S(1)}, bf16[2,2,2,64,256]{4,3,2,1,0:T(8,128)(2,1)S(1)}, u32[]{:S(2)}, u32[]{:S(2)}) collective-permute-start(bf16[2,2,2,64,256]{4,3,2,1,0:T(8,128)(2,1)S(1)} %pad_maximum_fusion.1), channel_id=1, source_target_pairs={{0,64},{1,65},{2,66},{3,67},{4,68},{5,69},{6,70},{7,71},{8,72},{9,... | collective-permute-start | bytes 786440 | tf_op jit(solution)/shard_map/ppermute | solution.py:223
  123.1 10.9 %collective-permute-start.20 = (bf16[2,2,2,64,256]{4,3,2,1,0:T(8,128)(2,1)S(1)}, bf16[2,2,2,64,256]{4,3,2,1,0:T(8,128)(2,1)S(1)}, u32[]{:S(2)}, u32[]{:S(2)}) collective-permute-start(bf16[2,2,2,64,256]{4,3,2,1,0:T(8,128)(2,1)S(1)} %pad_maximum_fusion.2), channel_id=1, source_target_pairs={{0,128},{1,129},{2,130},{3,131},{4,132},{5,133},{6,134},{7,135},{8... | collective-permute-start | bytes 786440 | tf_op jit(solution)/shard_map/ppermute | solution.py:223
  125.7 14.7 %collective-permute-start.21 = (bf16[2,2,2,64,256]{4,3,2,1,0:T(8,128)(2,1)S(1)}, bf16[2,2,2,64,256]{4,3,2,1,0:T(8,128)(2,1)S(1)}, u32[]{:S(2)}, u32[]{:S(2)}) collective-permute-start(bf16[2,2,2,64,256]{4,3,2,1,0:T(8,128)(2,1)S(1)} %pad_maximum_fusion.3), channel_id=1, source_target_pairs={{0,192},{1,193},{2,194},{3,195},{4,196},{5,197},{6,198},{7,199},{8... | collective-permute-start | bytes 786440 | tf_op jit(solution)/shard_map/ppermute | solution.py:223
  (6 other events, 53.0 us)

commit v9 on v8

--- a/solution.py
+++ b/solution.py
@@ -10,6 +10,7 @@
 DEPTH = 4
 SPLIT = 4
 LIMIT = 24
+SHIFTS = (2, 1, 3)
 
 
 def fetch_weights(meta, pieces, weights, sems):
@@ -180,7 +181,7 @@
     x, core = meta[0], meta[1]
     out[2 * x + core] = home[...]
     out[2 * x + 1 - core] = away[...]
-    for shift, pair in enumerate(arrived, 1):
+    for shift, pair in zip(SHIFTS, arrived):
         group = lax.rem(x - shift + 4, 4)
         out[2 * group + core] = pair[0]
         out[2 * group + 1 - core] = pair[1]
@@ -275,10 +276,10 @@
     early, center = lax.optimization_barrier((parts[2], mid))
     top = send(center, next_chip(1))
     parts = (parts[0], parts[1], early, parts[3])
-    *parts, top = lax.optimization_barrier((*parts, top))
     far_mine = jnp.stack(parts)
     far_theirs = send(far_mine, sibling)
     left_theirs = send(left_mine, sibling)
+    right_mine, top = lax.optimization_barrier((right_mine, top))
     right_theirs = send(right_mine, sibling)
     kernels = (mine, theirs, left_mine, left_theirs, right_mine, right_theirs, far_mine, far_theirs)
 
@@ -303,7 +304,7 @@
     both = (done[0], send(done[1], sibling))
     home, away = [lax.dynamic_index_in_dim(one, x, 0, keepdims=False) for one in both]
     arrived = []
-    for step in (1, 2, 3):
+    for step in SHIFTS:
         layer = (x + step) % 4
         pair = jnp.stack([lax.dynamic_index_in_dim(one, layer, 0, keepdims=False) for one in both])
         arrived.append(send(pair, along_x(step)))

time: 143 us -> 138 us (0.965)
  the two profiles are of different devices: /device:TPU:327 before, /device:TPU:441 now
where the time goes in v9:
time: 138 us; the launch traced here: 137 us
  starting transfers between devices  65.2 us (47%)
  waiting for transfers between devices  37.2 us (27%)
  Pallas kernels  27.9 us (20%)
  local copies, waits for them, and re-layouts  4.83 us (4%)
  other arithmetic  1.4 us (1%)
    ppermute x22, starting transfers between devices, send(): return lax.ppermute(array, ('section', 'rows'), route(move, keep))  65.2 us
    ppermute x22, waiting for transfers between devices, send(): return lax.ppermute(array, ('section', 'rows'), route(move, keep))  37.2 us
    pallas_call x4, Pallas kernels, run_frame(): pl.pallas_call(functools.partial(frame_kernel, frame, builds, len(inputs)...  26.3 us
  transfers between devices with their start and end apart: 22, of which 12 were waited for; matrix products, arithmetic and copies ran while one was open for 3% of the time, Pallas kernels for 10%

profile of v9, /device:TPU:441, one launch (start us, length us, event | category | flops | bytes accessed | tf_op | source)
XLA Modules:
  0.0 137.1 jit_solution(10247608831091526553)
XLA Ops:
  1.0 2.6 %collective-permute-start.1 = (bf16[2,2,64,256]{3,2,1,0:T(8,128)(2,1)S(1)}, bf16[2,2,64,256]{3,2,1,0:T(8,128)(2,1)S(1)}, u32[]{:S(2)}, u32[]{:S(2)}) collective-permute-start(bf16[2,2,64,256]{3,2,1,0:T(8,128)(2,1)S(1)} %get-tuple-element.46), channel_id=1, source_target_pairs={{0,1},{1,0},{2,3},{3,2},{4,5},{5,4},{6,7},{7,6},{8,9},{9,8},{10,11... | collective-permute-start | bytes 393224 | tf_op jit(solution)/shard_map/ppermute | solution.py:224
  4.6 4.7 %collective-permute-start = (bf16[576,256]{1,0:T(8,128)(2,1)S(1)}, bf16[576,256]{1,0:T(8,128)(2,1)S(1)}, u32[]{:S(2)}, u32[]{:S(2)}) collective-permute-start(bf16[576,256]{1,0:T(8,128)(2,1)S(1)} %dynamic-slice_bitcast_fusion.2), channel_id=1, source_target_pairs={{0,128},{1,129},{2,130},{3,131},{4,132},{5,133},{6,134},{7,135},{8... | collective-permute-start | bytes 884744 | tf_op jit(solution)/shard_map/ppermute | solution.py:224
  9.3 3.0 %collective-permute-start.2 = (bf16[2,4,64,256]{3,2,1,0:T(8,128)(2,1)S(1)}, bf16[2,4,64,256]{3,2,1,0:T(8,128)(2,1)S(1)}, u32[]{:S(2)}, u32[]{:S(2)}) collective-permute-start(bf16[2,4,64,256]{3,2,1,0:T(8,128)(2,1)S(1)} %maximum_select_fusion.1.refs_1_), channel_id=1, source_target_pairs={{2,0},{3,1},{4,2},{5,3},{6,4},{7,5},{8,6},{9,7},{10,8},{11,9},{12,... | collective-permute-start | bytes 786440 | tf_op jit(solution)/shard_map/ppermute | solution.py:224
  14.1 2.5 %collective-permute-done = bf16[576,256]{1,0:T(8,128)(2,1)S(1)} collective-permute-done((bf16[576,256]{1,0:T(8,128)(2,1)S(1)}, bf16[576,256]{1,0:T(8,128)(2,1)S(1)}, u32[]{:S(2)}, u32[]{:S(2)}) %collective-permute-start) | collective-permute-done | bytes 294944 | tf_op jit(solution)/shard_map/ppermute | solution.py:224
  16.6 4.3 %collective-permute-done.2.refs_2_ = bf16[2,4,64,256]{3,2,1,0:T(8,128)(2,1)S(1)} collective-permute-done((bf16[2,4,64,256]{3,2,1,0:T(8,128)(2,1)S(1)}, bf16[2,4,64,256]{3,2,1,0:T(8,128)(2,1)S(1)}, u32[]{:S(2)}, u32[]{:S(2)}) %collective-permute-start.2) | collective-permute-done | bytes 262176 | tf_op jit(solution)/shard_map/ppermute | solution.py:224
  21.0 2.8 %collective-permute-start.3 = (bf16[2304,256]{1,0:T(8,128)(2,1)S(1)}, bf16[2304,256]{1,0:T(8,128)(2,1)}, u32[]{:S(2)}, u32[]{:S(2)}) collective-permute-start(bf16[2304,256]{1,0:T(8,128)(2,1)S(1)} %get-tuple-element.23.refs_3_), channel_id=1, source_target_pairs={{0,192},{1,193},{2,194},{3,195},{4,196},{5,197},{6,198},{7,199},{8... | collective-permute-start | bytes 3538952 | tf_op jit(solution)/shard_map/ppermute | solution.py:224
  23.7 2.5 %collective-permute-start.6 = (bf16[2304,256]{1,0:T(8,128)(2,1)S(1)}, bf16[2304,256]{1,0:T(8,128)(2,1)}, u32[]{:S(2)}, u32[]{:S(2)}) collective-permute-start(bf16[2304,256]{1,0:T(8,128)(2,1)S(1)} %get-tuple-element.23.refs_3_), channel_id=1, source_target_pairs={{0,64},{1,65},{2,66},{3,67},{4,68},{5,69},{6,70},{7,71},{8,72},{9,... | collective-permute-start | bytes 3538952 | tf_op jit(solution)/shard_map/ppermute | solution.py:224
  28.2 2.7 %collective-permute-start.10 = (bf16[576,256]{1,0:T(8,128)(2,1)S(1)}, bf16[576,256]{1,0:T(8,128)(2,1)S(1)}, u32[]{:S(2)}, u32[]{:S(2)}) collective-permute-start(bf16[576,256]{1,0:T(8,128)(2,1)S(1)} %collective-permute-done), channel_id=1, source_target_pairs={{0,4},{1,5},{2,14},{3,15},{4,8},{5,9},{6,2},{7,3},{8,12},{9,13},{1... | collective-permute-start | bytes 884744 | tf_op jit(solution)/shard_map/ppermute | solution.py:224
  30.9 3.8 %collective-permute-start.9 = (bf16[576,256]{1,0:T(8,128)(2,1)S(1)}, bf16[576,256]{1,0:T(8,128)(2,1)S(1)}, u32[]{:S(2)}, u32[]{:S(2)}) collective-permute-start(bf16[576,256]{1,0:T(8,128)(2,1)S(1)} %collective-permute-done), channel_id=1, source_target_pairs={{0,2},{1,3},{2,4},{3,5},{4,6},{5,7},{6,8},{7,9},{8,10},{9,11},{10,... | collective-permute-start | bytes 884744 | tf_op jit(solution)/shard_map/ppermute | solution.py:224
  34.7 7.9 %collective-permute-done.4 = bf16[576,256]{1,0:T(8,128)(2,1)S(1)} collective-permute-done((bf16[576,256]{1,0:T(8,128)(2,1)S(1)}, bf16[576,256]{1,0:T(8,128)(2,1)S(1)}, u32[]{:S(2)}, u32[]{:S(2)}) %collective-permute-start.4) | collective-permute-done | bytes 294944 | tf_op jit(solution)/shard_map/ppermute | solution.py:224
  47.8 4.0 %collective-permute-start.11 = (bf16[4,576,256]{2,1,0:T(8,128)(2,1)S(1)}, bf16[4,576,256]{2,1,0:T(8,128)(2,1)}, u32[]{:S(2)}, u32[]{:S(2)}) collective-permute-start(bf16[4,576,256]{2,1,0:T(8,128)(2,1)S(1)} %pad_maximum_fusion.refs_9_), channel_id=1, source_target_pairs={{0,1},{1,0},{2,3},{3,2},{4,5},{5,4},{6,7},{7,6},{8,9},{9,8},{10,11... | collective-permute-start | bytes 3538952 | tf_op jit(solution)/shard_map/ppermute | solution.py:224
  53.0 4.2 %collective-permute-start.7 = (bf16[2304,256]{1,0:T(8,128)(2,1)}, bf16[2304,256]{1,0:T(8,128)(2,1)}, u32[]{:S(2)}, u32[]{:S(2)}) collective-permute-start(bf16[2304,256]{1,0:T(8,128)(2,1)} %collective-permute-done.6.refs_5_), channel_id=1, source_target_pairs={{0,1},{1,0},{2,3},{3,2},{4,5},{5,4},{6,7},{7,6},{8,9},{9,8},{10,11... | collective-permute-start | bytes 3538952 | tf_op jit(solution)/shard_map/ppermute | solution.py:224
  62.3 7.6 %frame0.2 = (bf16[2,4,2,64,256]{4,3,2,1,0:T(8,128)(2,1)S(1)}, bf16[1,4,64,256]{3,2,1,0:T(8,128)(2,1)S(1)}, f32[28,64,256]{2,1,0:T(8,128)S(1)}, bf16[4,2,2304,256...) custom-call(s32[5]{0:T(128)S(1)} %stack.67.meta, bf16[2,4,64,256]{3,2,1,0:T(8,128)(2,1)} %copy-done.7, ...), custom_call_target="tpu_custom_call" | custom-call | flops 4227858432 | bytes 8000000 | tf_op jit(solution)/shard_map/frame0/pallas_call | solution.py:160
  71.2 4.9 %frame1.2 = (bf16[2,4,2,64,256]{4,3,2,1,0:T(8,128)(2,1)S(1)}, bf16[1,4,64,256]{3,2,1,0:T(8,128)(2,1)}) custom-call(s32[5]{0:T(128)S(1)} %stack.67.meta, bf16[1,12,64,256]{3,2,1,0:T(8,128)(2,1)S(1)} %get-tuple-element.31.refs_0_, bf16[4,2,2304,256]{3,2,1,0:T(8,128)(2,1)S(1)} %get-tuple-element.32.refs_1_, f32[28,64,256]{2,1,0:T(8,128)S(1)} %get-tuple-element.33.refs_2_), custom_call_target="tpu_custom_call" | custom-call | flops 2113929216 | bytes 8000000 | tf_op jit(solution)/shard_map/frame1/pallas_call | solution.py:160
  78.2 5.9 %collective-permute-done.12.refs_1_ = bf16[1,4,64,256]{3,2,1,0:T(8,128)(2,1)} collective-permute-done((bf16[1,4,64,256]{3,2,1,0:T(8,128)(2,1)S(1)}, bf16[1,4,64,256]{3,2,1,0:T(8,128)(2,1)}, u32[]{:S(2)}, u32[]{:S(2)}) %collective-permute-start.12) | collective-permute-done | bytes 131104 | tf_op jit(solution)/shard_map/ppermute | solution.py:224
  86.0 5.5 %collective-permute-start.13 = (bf16[1,4,64,256]{3,2,1,0:T(8,128)(2,1)}, bf16[1,4,64,256]{3,2,1,0:T(8,128)(2,1)}, u32[]{:S(2)}, u32[]{:S(2)}) collective-permute-start(bf16[1,4,64,256]{3,2,1,0:T(8,128)(2,1)} %collective-permute-done.12.refs_1_), channel_id=1, source_target_pairs={{256,258},{257,259},{258,260},{259,261},{260,262},{261,263},{262,2... | collective-permute-start | bytes 393224 | tf_op jit(solution)/shard_map/ppermute | solution.py:224
  93.8 5.5 %collective-permute-start.16 = (bf16[1,4,64,256]{3,2,1,0:T(8,128)(2,1)}, bf16[1,4,64,256]{3,2,1,0:T(8,128)(2,1)S(1)}, u32[]{:S(2)}, u32[]{:S(2)}) collective-permute-start(bf16[1,4,64,256]{3,2,1,0:T(8,128)(2,1)} %collective-permute-done.15.refs_1_), channel_id=1, source_target_pairs={{256,258},{257,259},{258,260},{259,261},{260,262},{261,263},{262,2... | collective-permute-start | bytes 393224 | tf_op jit(solution)/shard_map/ppermute | solution.py:224
  99.3 8.6 %frame0.3 = (bf16[2,4,2,64,256]{4,3,2,1,0:T(8,128)(2,1)S(1)}, bf16[1,4,64,256]{3,2,1,0:T(8,128)(2,1)}, f32[28,64,256]{2,1,0:T(8,128)S(1)}, bf16[4,2,2304,256]{3,2,1,0:T(8,128)(2,1)S(1)}) custom-call(s32[5]{0:T(128)S(1)} %stack.67.meta, bf16[1,4,64,256]{3,2,1,0:T(8,128)(2,1)} %collective-permute-done.13.refs_0_, ...), custom_call_target="tpu_custom_call" | custom-call | flops 4227858432 | bytes 8000000 | tf_op jit(solution)/shard_map/frame0/pallas_call | solution.py:160
  107.9 5.3 %frame1.3 = (bf16[2,4,2,64,256]{4,3,2,1,0:T(8,128)(2,1)S(1)}, bf16[1,4,64,256]{3,2,1,0:T(8,128)(2,1)}) custom-call(s32[5]{0:T(128)S(1)} %stack.67.meta, bf16[1,4,64,256]{3,2,1,0:T(8,128)(2,1)S(1)} %collective-permute-done.16.refs_0_, bf16[1,4,64,256]{3,2,1,0:T(8,128)(2,1)} %collective-permute-done.15.refs_1_, ...), custom_call_target="tpu_custom_call" | custom-call | flops 2113929216 | bytes 8000000 | tf_op jit(solution)/shard_map/frame1/pallas_call | solution.py:160
  113.6 3.1 %collective-permute-start.18 = (bf16[4,2,2,64,256]{4,3,2,1,0:T(8,128)(2,1)S(1)}, bf16[4,2,2,64,256]{4,3,2,1,0:T(8,128)(2,1)S(1)}, u32[]{:S(2)}, u32[]{:S(2)}) collective-permute-start(bf16[4,2,2,64,256]{4,3,2,1,0:T(8,128)(2,1)S(1)} %get-tuple-element.43), channel_id=1, source_target_pairs={{0,1},{1,0},{2,3},{3,2},{4,5},{5,4},{6,7},{7,6},{8,9},{9,8},{10,11... | collective-permute-start | bytes 1572872 | tf_op jit(solution)/shard_map/ppermute | solution.py:224
  118.2 2.3 %collective-permute-start.19 = (bf16[2,2,2,64,256]{4,3,2,1,0:T(8,128)(2,1)S(1)}, bf16[2,2,2,64,256]{4,3,2,1,0:T(8,128)(2,1)S(1)}, u32[]{:S(2)}, u32[]{:S(2)}) collective-permute-start(bf16[2,2,2,64,256]{4,3,2,1,0:T(8,128)(2,1)S(1)} %pad_maximum_fusion.1), channel_id=1, source_target_pairs={{0,128},{1,129},{2,130},{3,131},{4,132},{5,133},{6,134},{7,135},{8... | collective-permute-start | bytes 786440 | tf_op jit(solution)/shard_map/ppermute | solution.py:224
  120.6 3.6 %collective-permute-start.20 = (bf16[2,2,2,64,256]{4,3,2,1,0:T(8,128)(2,1)S(1)}, bf16[2,2,2,64,256]{4,3,2,1,0:T(8,128)(2,1)S(1)}, u32[]{:S(2)}, u32[]{:S(2)}) collective-permute-start(bf16[2,2,2,64,256]{4,3,2,1,0:T(8,128)(2,1)S(1)} %pad_maximum_fusion.2), channel_id=1, source_target_pairs={{0,64},{1,65},{2,66},{3,67},{4,68},{5,69},{6,70},{7,71},{8,72},{9,... | collective-permute-start | bytes 786440 | tf_op jit(solution)/shard_map/ppermute | solution.py:224
  124.2 2.9 %collective-permute-start.21 = (bf16[2,2,2,64,256]{4,3,2,1,0:T(8,128)(2,1)S(1)}, bf16[2,2,2,64,256]{4,3,2,1,0:T(8,128)(2,1)S(1)}, u32[]{:S(2)}, u32[]{:S(2)}) collective-permute-start(bf16[2,2,2,64,256]{4,3,2,1,0:T(8,128)(2,1)S(1)} %pad_maximum_fusion.3), channel_id=1, source_target_pairs={{0,192},{1,193},{2,194},{3,195},{4,196},{5,197},{6,198},{7,199},{8... | collective-permute-start | bytes 786440 | tf_op jit(solution)/shard_map/ppermute | solution.py:224
  129.2 6.3 %collective-permute-done.20.refs_1_ = bf16[2,2,2,64,256]{4,3,2,1,0:T(8,128)(2,1)S(1)} collective-permute-done((bf16[2,2,2,64,256]{4,3,2,1,0:T(8,128)(2,1)S(1)}, bf16[2,2,2,64,256]{4,3,2,1,0:T(8,128)(2,1)S(1)}, u32[]{:S(2)}, u32[]{:S(2)}) %collective-permute-start.20) | collective-permute-done | bytes 262176 | tf_op jit(solution)/shard_map/ppermute | solution.py:224
  (54 shorter events, 30.2 us)
Async XLA Ops:
  1.0 8.3 %collective-permute-start.1 = (bf16[2,2,64,256]{3,2,1,0:T(8,128)(2,1)S(1)}, bf16[2,2,64,256]{3,2,1,0:T(8,128)(2,1)S(1)}, u32[]{:S(2)}, u32[]{:S(2)}) collective-permute-start(bf16[2,2,64,256]{3,2,1,0:T(8,128)(2,1)S(1)} %get-tuple-element.46), channel_id=1, source_target_pairs={{0,1},{1,0},{2,3},{3,2},{4,5},{5,4},{6,7},{7,6},{8,9},{9,8},{10,11... | collective-permute-start | bytes 393224 | tf_op jit(solution)/shard_map/ppermute | solution.py:224
  4.6 12.0 %collective-permute-start = (bf16[576,256]{1,0:T(8,128)(2,1)S(1)}, bf16[576,256]{1,0:T(8,128)(2,1)S(1)}, u32[]{:S(2)}, u32[]{:S(2)}) collective-permute-start(bf16[576,256]{1,0:T(8,128)(2,1)S(1)} %dynamic-slice_bitcast_fusion.2), channel_id=1, source_target_pairs={{0,128},{1,129},{2,130},{3,131},{4,132},{5,133},{6,134},{7,135},{8... | collective-permute-start | bytes 884744 | tf_op jit(solution)/shard_map/ppermute | solution.py:224
  9.3 33.3 %copy-start.5 = (bf16[2,4,64,256]{3,2,1,0:T(8,128)(2,1)}, bf16[2,4,64,256]{3,2,1,0:T(8,128)(2,1)S(1)}, u32[]{:S(2)}) copy-start(bf16[2,4,64,256]{3,2,1,0:T(8,128)(2,1)S(1)} %maximum_select_fusion.1.refs_1_) | copy-start | bytes 786436
  9.3 11.6 %collective-permute-start.2 = (bf16[2,4,64,256]{3,2,1,0:T(8,128)(2,1)S(1)}, bf16[2,4,64,256]{3,2,1,0:T(8,128)(2,1)S(1)}, u32[]{:S(2)}, u32[]{:S(2)}) collective-permute-start(bf16[2,4,64,256]{3,2,1,0:T(8,128)(2,1)S(1)} %maximum_select_fusion.1.refs_1_), channel_id=1, source_target_pairs={{2,0},{3,1},{4,2},{5,3},{6,4},{7,5},{8,6},{9,7},{10,8},{11,9},{12,... | collective-permute-start | bytes 786440 | tf_op jit(solution)/shard_map/ppermute | solution.py:224
  16.6 30.0 %copy-start.4 = (bf16[576,256]{1,0:T(8,128)(2,1)}, bf16[576,256]{1,0:T(8,128)(2,1)S(1)}, u32[]{:S(2)}) copy-start(bf16[576,256]{1,0:T(8,128)(2,1)S(1)} %collective-permute-done) | copy-start | bytes 884740
  21.0 30.9 %collective-permute-start.3 = (bf16[2304,256]{1,0:T(8,128)(2,1)S(1)}, bf16[2304,256]{1,0:T(8,128)(2,1)}, u32[]{:S(2)}, u32[]{:S(2)}) collective-permute-start(bf16[2304,256]{1,0:T(8,128)(2,1)S(1)} %get-tuple-element.23.refs_3_), channel_id=1, source_target_pairs={{0,192},{1,193},{2,194},{3,195},{4,196},{5,197},{6,198},{7,199},{8... | collective-permute-start | bytes 3538952 | tf_op jit(solution)/shard_map/ppermute | solution.py:224
  23.7 29.3 %collective-permute-start.6 = (bf16[2304,256]{1,0:T(8,128)(2,1)S(1)}, bf16[2304,256]{1,0:T(8,128)(2,1)}, u32[]{:S(2)}, u32[]{:S(2)}) collective-permute-start(bf16[2304,256]{1,0:T(8,128)(2,1)S(1)} %get-tuple-element.23.refs_3_), channel_id=1, source_target_pairs={{0,64},{1,65},{2,66},{3,67},{4,68},{5,69},{6,70},{7,71},{8,72},{9,... | collective-permute-start | bytes 3538952 | tf_op jit(solution)/shard_map/ppermute | solution.py:224
  26.2 16.4 %collective-permute-start.4 = (bf16[576,256]{1,0:T(8,128)(2,1)S(1)}, bf16[576,256]{1,0:T(8,128)(2,1)S(1)}, u32[]{:S(2)}, u32[]{:S(2)}) collective-permute-start(bf16[576,256]{1,0:T(8,128)(2,1)S(1)} %collective-permute-done), channel_id=1, source_target_pairs={{0,14},{1,15},{2,0},{3,1},{4,2},{5,3},{6,4},{7,5},{8,6},{9,7},{10,... | collective-permute-start | bytes 884744 | tf_op jit(solution)/shard_map/ppermute | solution.py:224
  28.2 16.4 %collective-permute-start.10 = (bf16[576,256]{1,0:T(8,128)(2,1)S(1)}, bf16[576,256]{1,0:T(8,128)(2,1)S(1)}, u32[]{:S(2)}, u32[]{:S(2)}) collective-permute-start(bf16[576,256]{1,0:T(8,128)(2,1)S(1)} %collective-permute-done), channel_id=1, source_target_pairs={{0,4},{1,5},{2,14},{3,15},{4,8},{5,9},{6,2},{7,3},{8,12},{9,13},{1... | collective-permute-start | bytes 884744 | tf_op jit(solution)/shard_map/ppermute | solution.py:224
  30.9 15.8 %collective-permute-start.9 = (bf16[576,256]{1,0:T(8,128)(2,1)S(1)}, bf16[576,256]{1,0:T(8,128)(2,1)S(1)}, u32[]{:S(2)}, u32[]{:S(2)}) collective-permute-start(bf16[576,256]{1,0:T(8,128)(2,1)S(1)} %collective-permute-done), channel_id=1, source_target_pairs={{0,2},{1,3},{2,4},{3,5},{4,6},{5,7},{6,8},{7,9},{8,10},{9,11},{10,... | collective-permute-start | bytes 884744 | tf_op jit(solution)/shard_map/ppermute | solution.py:224
  42.6 9.2 %collective-permute-start.5 = (bf16[2,4,64,256]{3,2,1,0:T(8,128)(2,1)S(1)}, bf16[2,4,64,256]{3,2,1,0:T(8,128)(2,1)S(1)}, u32[]{:S(2)}, u32[]{:S(2)}) collective-permute-start(bf16[2,4,64,256]{3,2,1,0:T(8,128)(2,1)S(1)} %maximum_select_fusion.1.refs_1_), channel_id=1, source_target_pairs={{0,2},{1,3},{2,4},{3,5},{4,6},{5,7},{6,8},{7,9},{8,10},{9,11},{10,... | collective-permute-start | bytes 786440 | tf_op jit(solution)/shard_map/ppermute | solution.py:224
  47.8 11.4 %collective-permute-start.11 = (bf16[4,576,256]{2,1,0:T(8,128)(2,1)S(1)}, bf16[4,576,256]{2,1,0:T(8,128)(2,1)}, u32[]{:S(2)}, u32[]{:S(2)}) collective-permute-start(bf16[4,576,256]{2,1,0:T(8,128)(2,1)S(1)} %pad_maximum_fusion.refs_9_), channel_id=1, source_target_pairs={{0,1},{1,0},{2,3},{3,2},{4,5},{5,4},{6,7},{7,6},{8,9},{9,8},{10,11... | collective-permute-start | bytes 3538952 | tf_op jit(solution)/shard_map/ppermute | solution.py:224
  53.0 7.0 %collective-permute-start.7 = (bf16[2304,256]{1,0:T(8,128)(2,1)}, bf16[2304,256]{1,0:T(8,128)(2,1)}, u32[]{:S(2)}, u32[]{:S(2)}) collective-permute-start(bf16[2304,256]{1,0:T(8,128)(2,1)} %collective-permute-done.6.refs_5_), channel_id=1, source_target_pairs={{0,1},{1,0},{2,3},{3,2},{4,5},{5,4},{6,7},{7,6},{8,9},{9,8},{10,11... | collective-permute-start | bytes 3538952 | tf_op jit(solution)/shard_map/ppermute | solution.py:224
  57.2 5.1 %collective-permute-start.8 = (bf16[2304,256]{1,0:T(8,128)(2,1)}, bf16[2304,256]{1,0:T(8,128)(2,1)}, u32[]{:S(2)}, u32[]{:S(2)}) collective-permute-start(bf16[2304,256]{1,0:T(8,128)(2,1)} %collective-permute-done.3.refs_7_), channel_id=1, source_target_pairs={{0,1},{1,0},{2,3},{3,2},{4,5},{5,4},{6,7},{7,6},{8,9},{9,8},{10,11... | collective-permute-start | bytes 3538952 | tf_op jit(solution)/shard_map/ppermute | solution.py:224
  69.9 14.2 %collective-permute-start.12 = (bf16[1,4,64,256]{3,2,1,0:T(8,128)(2,1)S(1)}, bf16[1,4,64,256]{3,2,1,0:T(8,128)(2,1)}, u32[]{:S(2)}, u32[]{:S(2)}) collective-permute-start(bf16[1,4,64,256]{3,2,1,0:T(8,128)(2,1)S(1)} %get-tuple-element.35), channel_id=1, source_target_pairs={{0,256},{1,257},{2,258},{3,259},{4,260},{5,261},{6,262},{7,263},{8... | collective-permute-start | bytes 393224 | tf_op jit(solution)/shard_map/ppermute | solution.py:224
  76.9 15.0 %collective-permute-start.15 = (bf16[1,4,64,256]{3,2,1,0:T(8,128)(2,1)}, bf16[1,4,64,256]{3,2,1,0:T(8,128)(2,1)}, u32[]{:S(2)}, u32[]{:S(2)}) collective-permute-start(bf16[1,4,64,256]{3,2,1,0:T(8,128)(2,1)} %get-tuple-element.37), channel_id=1, source_target_pairs={{0,256},{1,257},{2,258},{3,259},{4,260},{5,261},{6,262},{7,263},{8... | collective-permute-start | bytes 393224 | tf_op jit(solution)/shard_map/ppermute | solution.py:224
  84.0 15.3 %collective-permute-start.14 = (bf16[1,4,64,256]{3,2,1,0:T(8,128)(2,1)}, bf16[1,4,64,256]{3,2,1,0:T(8,128)(2,1)}, u32[]{:S(2)}, u32[]{:S(2)}) collective-permute-start(bf16[1,4,64,256]{3,2,1,0:T(8,128)(2,1)} %collective-permute-done.12.refs_1_), channel_id=1, source_target_pairs={{258,256},{259,257},{260,258},{261,259},{262,260},{263,261},{264,2... | collective-permute-start | bytes 393224 | tf_op jit(solution)/shard_map/ppermute | solution.py:224
  86.0 13.4 %collective-permute-start.13 = (bf16[1,4,64,256]{3,2,1,0:T(8,128)(2,1)}, bf16[1,4,64,256]{3,2,1,0:T(8,128)(2,1)}, u32[]{:S(2)}, u32[]{:S(2)}) collective-permute-start(bf16[1,4,64,256]{3,2,1,0:T(8,128)(2,1)} %collective-permute-done.12.refs_1_), channel_id=1, source_target_pairs={{256,258},{257,259},{258,260},{259,261},{260,262},{261,263},{262,2... | collective-permute-start | bytes 393224 | tf_op jit(solution)/shard_map/ppermute | solution.py:224
  91.9 16.0 %collective-permute-start.17 = (bf16[1,4,64,256]{3,2,1,0:T(8,128)(2,1)}, bf16[1,4,64,256]{3,2,1,0:T(8,128)(2,1)S(1)}, u32[]{:S(2)}, u32[]{:S(2)}) collective-permute-start(bf16[1,4,64,256]{3,2,1,0:T(8,128)(2,1)} %collective-permute-done.15.refs_1_), channel_id=1, source_target_pairs={{258,256},{259,257},{260,258},{261,259},{262,260},{263,261},{264,2... | collective-permute-start | bytes 393224 | tf_op jit(solution)/shard_map/ppermute | solution.py:224
  93.8 14.1 %collective-permute-start.16 = (bf16[1,4,64,256]{3,2,1,0:T(8,128)(2,1)}, bf16[1,4,64,256]{3,2,1,0:T(8,128)(2,1)S(1)}, u32[]{:S(2)}, u32[]{:S(2)}) collective-permute-start(bf16[1,4,64,256]{3,2,1,0:T(8,128)(2,1)} %collective-permute-done.15.refs_1_), channel_id=1, source_target_pairs={{256,258},{257,259},{258,260},{259,261},{260,262},{261,263},{262,2... | collective-permute-start | bytes 393224 | tf_op jit(solution)/shard_map/ppermute | solution.py:224
  113.6 4.6 %collective-permute-start.18 = (bf16[4,2,2,64,256]{4,3,2,1,0:T(8,128)(2,1)S(1)}, bf16[4,2,2,64,256]{4,3,2,1,0:T(8,128)(2,1)S(1)}, u32[]{:S(2)}, u32[]{:S(2)}) collective-permute-start(bf16[4,2,2,64,256]{4,3,2,1,0:T(8,128)(2,1)S(1)} %get-tuple-element.43), channel_id=1, source_target_pairs={{0,1},{1,0},{2,3},{3,2},{4,5},{5,4},{6,7},{7,6},{8,9},{9,8},{10,11... | collective-permute-start | bytes 1572872 | tf_op jit(solution)/shard_map/ppermute | solution.py:224
  118.2 11.0 %collective-permute-start.19 = (bf16[2,2,2,64,256]{4,3,2,1,0:T(8,128)(2,1)S(1)}, bf16[2,2,2,64,256]{4,3,2,1,0:T(8,128)(2,1)S(1)}, u32[]{:S(2)}, u32[]{:S(2)}) collective-permute-start(bf16[2,2,2,64,256]{4,3,2,1,0:T(8,128)(2,1)S(1)} %pad_maximum_fusion.1), channel_id=1, source_target_pairs={{0,128},{1,129},{2,130},{3,131},{4,132},{5,133},{6,134},{7,135},{8... | collective-permute-start | bytes 786440 | tf_op jit(solution)/shard_map/ppermute | solution.py:224
  120.6 14.9 %collective-permute-start.20 = (bf16[2,2,2,64,256]{4,3,2,1,0:T(8,128)(2,1)S(1)}, bf16[2,2,2,64,256]{4,3,2,1,0:T(8,128)(2,1)S(1)}, u32[]{:S(2)}, u32[]{:S(2)}) collective-permute-start(bf16[2,2,2,64,256]{4,3,2,1,0:T(8,128)(2,1)S(1)} %pad_maximum_fusion.2), channel_id=1, source_target_pairs={{0,64},{1,65},{2,66},{3,67},{4,68},{5,69},{6,70},{7,71},{8,72},{9,... | collective-permute-start | bytes 786440 | tf_op jit(solution)/shard_map/ppermute | solution.py:224
  124.2 11.3 %collective-permute-start.21 = (bf16[2,2,2,64,256]{4,3,2,1,0:T(8,128)(2,1)S(1)}, bf16[2,2,2,64,256]{4,3,2,1,0:T(8,128)(2,1)S(1)}, u32[]{:S(2)}, u32[]{:S(2)}) collective-permute-start(bf16[2,2,2,64,256]{4,3,2,1,0:T(8,128)(2,1)S(1)} %pad_maximum_fusion.3), channel_id=1, source_target_pairs={{0,192},{1,193},{2,194},{3,195},{4,196},{5,197},{6,198},{7,199},{8... | collective-permute-start | bytes 786440 | tf_op jit(solution)/shard_map/ppermute | solution.py:224
  (6 other events, 51.9 us)

commit v10 on v9

--- a/solution.py
+++ b/solution.py
@@ -8,7 +8,7 @@
 from jax.sharding import PartitionSpec as P
 
 DEPTH = 4
-SPLIT = 4
+SPLIT = 2
 LIMIT = 24
 SHIFTS = (2, 1, 3)
 

time: 138 us -> 138 us (level)
  no operation moved by 1% of the time
where the time goes in v10:
time: 138 us; the launch traced here: 137 us
  starting transfers between devices  65.5 us (47%)
  waiting for transfers between devices  37.2 us (27%)
  Pallas kernels  27.3 us (20%)
  local copies, waits for them, and re-layouts  4.83 us (4%)
  other arithmetic  1.4 us (1%)
    ppermute x22, starting transfers between devices, send(): return lax.ppermute(array, ('section', 'rows'), route(move, keep))  65.5 us
    ppermute x22, waiting for transfers between devices, send(): return lax.ppermute(array, ('section', 'rows'), route(move, keep))  37.2 us
    pallas_call x4, Pallas kernels, run_frame(): pl.pallas_call(functools.partial(frame_kernel, frame, builds, len(inputs)...  25.7 us
  transfers between devices with their start and end apart: 22, of which 12 were waited for; matrix products, arithmetic and copies ran while one was open for 3% of the time, Pallas kernels for 10%

profile of v10, /device:TPU:441, one launch (start us, length us, event | category | flops | bytes accessed | tf_op | source)
XLA Modules:
  0.0 136.7 jit_solution(5981076728393063509)
XLA Ops:
  1.0 2.6 %collective-permute-start.1 = (bf16[2,2,64,256]{3,2,1,0:T(8,128)(2,1)S(1)}, bf16[2,2,64,256]{3,2,1,0:T(8,128)(2,1)S(1)}, u32[]{:S(2)}, u32[]{:S(2)}) collective-permute-start(bf16[2,2,64,256]{3,2,1,0:T(8,128)(2,1)S(1)} %get-tuple-element.46), channel_id=1, source_target_pairs={{0,1},{1,0},{2,3},{3,2},{4,5},{5,4},{6,7},{7,6},{8,9},{9,8},{10,11... | collective-permute-start | bytes 393224 | tf_op jit(solution)/shard_map/ppermute | solution.py:224
  4.6 4.7 %collective-permute-start = (bf16[576,256]{1,0:T(8,128)(2,1)S(1)}, bf16[576,256]{1,0:T(8,128)(2,1)S(1)}, u32[]{:S(2)}, u32[]{:S(2)}) collective-permute-start(bf16[576,256]{1,0:T(8,128)(2,1)S(1)} %dynamic-slice_bitcast_fusion.2), channel_id=1, source_target_pairs={{0,128},{1,129},{2,130},{3,131},{4,132},{5,133},{6,134},{7,135},{8... | collective-permute-start | bytes 884744 | tf_op jit(solution)/shard_map/ppermute | solution.py:224
  9.3 3.0 %collective-permute-start.2 = (bf16[2,4,64,256]{3,2,1,0:T(8,128)(2,1)S(1)}, bf16[2,4,64,256]{3,2,1,0:T(8,128)(2,1)S(1)}, u32[]{:S(2)}, u32[]{:S(2)}) collective-permute-start(bf16[2,4,64,256]{3,2,1,0:T(8,128)(2,1)S(1)} %maximum_select_fusion.1.refs_1_), channel_id=1, source_target_pairs={{2,0},{3,1},{4,2},{5,3},{6,4},{7,5},{8,6},{9,7},{10,8},{11,9},{12,... | collective-permute-start | bytes 786440 | tf_op jit(solution)/shard_map/ppermute | solution.py:224
  14.1 2.5 %collective-permute-done = bf16[576,256]{1,0:T(8,128)(2,1)S(1)} collective-permute-done((bf16[576,256]{1,0:T(8,128)(2,1)S(1)}, bf16[576,256]{1,0:T(8,128)(2,1)S(1)}, u32[]{:S(2)}, u32[]{:S(2)}) %collective-permute-start) | collective-permute-done | bytes 294944 | tf_op jit(solution)/shard_map/ppermute | solution.py:224
  16.6 4.3 %collective-permute-done.2.refs_2_ = bf16[2,4,64,256]{3,2,1,0:T(8,128)(2,1)S(1)} collective-permute-done((bf16[2,4,64,256]{3,2,1,0:T(8,128)(2,1)S(1)}, bf16[2,4,64,256]{3,2,1,0:T(8,128)(2,1)S(1)}, u32[]{:S(2)}, u32[]{:S(2)}) %collective-permute-start.2) | collective-permute-done | bytes 262176 | tf_op jit(solution)/shard_map/ppermute | solution.py:224
  21.0 2.8 %collective-permute-start.3 = (bf16[2304,256]{1,0:T(8,128)(2,1)S(1)}, bf16[2304,256]{1,0:T(8,128)(2,1)}, u32[]{:S(2)}, u32[]{:S(2)}) collective-permute-start(bf16[2304,256]{1,0:T(8,128)(2,1)S(1)} %get-tuple-element.23.refs_3_), channel_id=1, source_target_pairs={{0,192},{1,193},{2,194},{3,195},{4,196},{5,197},{6,198},{7,199},{8... | collective-permute-start | bytes 3538952 | tf_op jit(solution)/shard_map/ppermute | solution.py:224
  23.7 2.5 %collective-permute-start.6 = (bf16[2304,256]{1,0:T(8,128)(2,1)S(1)}, bf16[2304,256]{1,0:T(8,128)(2,1)}, u32[]{:S(2)}, u32[]{:S(2)}) collective-permute-start(bf16[2304,256]{1,0:T(8,128)(2,1)S(1)} %get-tuple-element.23.refs_3_), channel_id=1, source_target_pairs={{0,64},{1,65},{2,66},{3,67},{4,68},{5,69},{6,70},{7,71},{8,72},{9,... | collective-permute-start | bytes 3538952 | tf_op jit(solution)/shard_map/ppermute | solution.py:224
  28.2 2.7 %collective-permute-start.10 = (bf16[576,256]{1,0:T(8,128)(2,1)S(1)}, bf16[576,256]{1,0:T(8,128)(2,1)S(1)}, u32[]{:S(2)}, u32[]{:S(2)}) collective-permute-start(bf16[576,256]{1,0:T(8,128)(2,1)S(1)} %collective-permute-done), channel_id=1, source_target_pairs={{0,4},{1,5},{2,14},{3,15},{4,8},{5,9},{6,2},{7,3},{8,12},{9,13},{1... | collective-permute-start | bytes 884744 | tf_op jit(solution)/shard_map/ppermute | solution.py:224
  30.9 3.8 %collective-permute-start.9 = (bf16[576,256]{1,0:T(8,128)(2,1)S(1)}, bf16[576,256]{1,0:T(8,128)(2,1)S(1)}, u32[]{:S(2)}, u32[]{:S(2)}) collective-permute-start(bf16[576,256]{1,0:T(8,128)(2,1)S(1)} %collective-permute-done), channel_id=1, source_target_pairs={{0,2},{1,3},{2,4},{3,5},{4,6},{5,7},{6,8},{7,9},{8,10},{9,11},{10,... | collective-permute-start | bytes 884744 | tf_op jit(solution)/shard_map/ppermute | solution.py:224
  34.7 7.9 %collective-permute-done.4 = bf16[576,256]{1,0:T(8,128)(2,1)S(1)} collective-permute-done((bf16[576,256]{1,0:T(8,128)(2,1)S(1)}, bf16[576,256]{1,0:T(8,128)(2,1)S(1)}, u32[]{:S(2)}, u32[]{:S(2)}) %collective-permute-start.4) | collective-permute-done | bytes 294944 | tf_op jit(solution)/shard_map/ppermute | solution.py:224
  47.8 4.0 %collective-permute-start.11 = (bf16[4,576,256]{2,1,0:T(8,128)(2,1)S(1)}, bf16[4,576,256]{2,1,0:T(8,128)(2,1)}, u32[]{:S(2)}, u32[]{:S(2)}) collective-permute-start(bf16[4,576,256]{2,1,0:T(8,128)(2,1)S(1)} %pad_maximum_fusion.refs_9_), channel_id=1, source_target_pairs={{0,1},{1,0},{2,3},{3,2},{4,5},{5,4},{6,7},{7,6},{8,9},{9,8},{10,11... | collective-permute-start | bytes 3538952 | tf_op jit(solution)/shard_map/ppermute | solution.py:224
  53.0 4.2 %collective-permute-start.7 = (bf16[2304,256]{1,0:T(8,128)(2,1)}, bf16[2304,256]{1,0:T(8,128)(2,1)}, u32[]{:S(2)}, u32[]{:S(2)}) collective-permute-start(bf16[2304,256]{1,0:T(8,128)(2,1)} %collective-permute-done.6.refs_5_), channel_id=1, source_target_pairs={{0,1},{1,0},{2,3},{3,2},{4,5},{5,4},{6,7},{7,6},{8,9},{9,8},{10,11... | collective-permute-start | bytes 3538952 | tf_op jit(solution)/shard_map/ppermute | solution.py:224
  62.3 7.6 %frame0.2 = (bf16[2,4,2,64,256]{4,3,2,1,0:T(8,128)(2,1)S(1)}, bf16[1,4,64,256]{3,2,1,0:T(8,128)(2,1)S(1)}, f32[28,64,256]{2,1,0:T(8,128)S(1)}, bf16[4,2,2304,256...) custom-call(s32[5]{0:T(128)S(1)} %stack.67.meta, bf16[2,4,64,256]{3,2,1,0:T(8,128)(2,1)} %copy-done.7, ...), custom_call_target="tpu_custom_call" | custom-call | flops 4227858432 | bytes 8000000 | tf_op jit(solution)/shard_map/frame0/pallas_call | solution.py:160
  71.2 4.6 %frame1.2 = (bf16[2,4,2,64,256]{4,3,2,1,0:T(8,128)(2,1)S(1)}, bf16[1,4,64,256]{3,2,1,0:T(8,128)(2,1)}) custom-call(s32[5]{0:T(128)S(1)} %stack.67.meta, bf16[1,12,64,256]{3,2,1,0:T(8,128)(2,1)S(1)} %get-tuple-element.31.refs_0_, bf16[4,2,2304,256]{3,2,1,0:T(8,128)(2,1)S(1)} %get-tuple-element.32.refs_1_, f32[28,64,256]{2,1,0:T(8,128)S(1)} %get-tuple-element.33.refs_2_), custom_call_target="tpu_custom_call" | custom-call | flops 2113929216 | bytes 8000000 | tf_op jit(solution)/shard_map/frame1/pallas_call | solution.py:160
  77.8 6.2 %collective-permute-done.12.refs_1_ = bf16[1,4,64,256]{3,2,1,0:T(8,128)(2,1)} collective-permute-done((bf16[1,4,64,256]{3,2,1,0:T(8,128)(2,1)S(1)}, bf16[1,4,64,256]{3,2,1,0:T(8,128)(2,1)}, u32[]{:S(2)}, u32[]{:S(2)}) %collective-permute-start.12) | collective-permute-done | bytes 131104 | tf_op jit(solution)/shard_map/ppermute | solution.py:224
  86.0 5.5 %collective-permute-start.13 = (bf16[1,4,64,256]{3,2,1,0:T(8,128)(2,1)}, bf16[1,4,64,256]{3,2,1,0:T(8,128)(2,1)}, u32[]{:S(2)}, u32[]{:S(2)}) collective-permute-start(bf16[1,4,64,256]{3,2,1,0:T(8,128)(2,1)} %collective-permute-done.12.refs_1_), channel_id=1, source_target_pairs={{256,258},{257,259},{258,260},{259,261},{260,262},{261,263},{262,2... | collective-permute-start | bytes 393224 | tf_op jit(solution)/shard_map/ppermute | solution.py:224
  93.5 5.5 %collective-permute-start.16 = (bf16[1,4,64,256]{3,2,1,0:T(8,128)(2,1)}, bf16[1,4,64,256]{3,2,1,0:T(8,128)(2,1)S(1)}, u32[]{:S(2)}, u32[]{:S(2)}) collective-permute-start(bf16[1,4,64,256]{3,2,1,0:T(8,128)(2,1)} %collective-permute-done.15.refs_1_), channel_id=1, source_target_pairs={{256,258},{257,259},{258,260},{259,261},{260,262},{261,263},{262,2... | collective-permute-start | bytes 393224 | tf_op jit(solution)/shard_map/ppermute | solution.py:224
  99.0 8.6 %frame0.3 = (bf16[2,4,2,64,256]{4,3,2,1,0:T(8,128)(2,1)S(1)}, bf16[1,4,64,256]{3,2,1,0:T(8,128)(2,1)}, f32[28,64,256]{2,1,0:T(8,128)S(1)}, bf16[4,2,2304,256]{3,2,1,0:T(8,128)(2,1)S(1)}) custom-call(s32[5]{0:T(128)S(1)} %stack.67.meta, bf16[1,4,64,256]{3,2,1,0:T(8,128)(2,1)} %collective-permute-done.13.refs_0_, ...), custom_call_target="tpu_custom_call" | custom-call | flops 4227858432 | bytes 8000000 | tf_op jit(solution)/shard_map/frame0/pallas_call | solution.py:160
  107.6 5.0 %frame1.3 = (bf16[2,4,2,64,256]{4,3,2,1,0:T(8,128)(2,1)S(1)}, bf16[1,4,64,256]{3,2,1,0:T(8,128)(2,1)}) custom-call(s32[5]{0:T(128)S(1)} %stack.67.meta, bf16[1,4,64,256]{3,2,1,0:T(8,128)(2,1)S(1)} %collective-permute-done.16.refs_0_, bf16[1,4,64,256]{3,2,1,0:T(8,128)(2,1)} %collective-permute-done.15.refs_1_, ...), custom_call_target="tpu_custom_call" | custom-call | flops 2113929216 | bytes 8000000 | tf_op jit(solution)/shard_map/frame1/pallas_call | solution.py:160
  112.9 3.4 %collective-permute-start.18 = (bf16[4,2,2,64,256]{4,3,2,1,0:T(8,128)(2,1)S(1)}, bf16[4,2,2,64,256]{4,3,2,1,0:T(8,128)(2,1)S(1)}, u32[]{:S(2)}, u32[]{:S(2)}) collective-permute-start(bf16[4,2,2,64,256]{4,3,2,1,0:T(8,128)(2,1)S(1)} %get-tuple-element.43), channel_id=1, source_target_pairs={{0,1},{1,0},{2,3},{3,2},{4,5},{5,4},{6,7},{7,6},{8,9},{9,8},{10,11... | collective-permute-start | bytes 1572872 | tf_op jit(solution)/shard_map/ppermute | solution.py:224
  117.9 2.3 %collective-permute-start.19 = (bf16[2,2,2,64,256]{4,3,2,1,0:T(8,128)(2,1)S(1)}, bf16[2,2,2,64,256]{4,3,2,1,0:T(8,128)(2,1)S(1)}, u32[]{:S(2)}, u32[]{:S(2)}) collective-permute-start(bf16[2,2,2,64,256]{4,3,2,1,0:T(8,128)(2,1)S(1)} %pad_maximum_fusion.1), channel_id=1, source_target_pairs={{0,128},{1,129},{2,130},{3,131},{4,132},{5,133},{6,134},{7,135},{8... | collective-permute-start | bytes 786440 | tf_op jit(solution)/shard_map/ppermute | solution.py:224
  120.3 3.6 %collective-permute-start.20 = (bf16[2,2,2,64,256]{4,3,2,1,0:T(8,128)(2,1)S(1)}, bf16[2,2,2,64,256]{4,3,2,1,0:T(8,128)(2,1)S(1)}, u32[]{:S(2)}, u32[]{:S(2)}) collective-permute-start(bf16[2,2,2,64,256]{4,3,2,1,0:T(8,128)(2,1)S(1)} %pad_maximum_fusion.2), channel_id=1, source_target_pairs={{0,64},{1,65},{2,66},{3,67},{4,68},{5,69},{6,70},{7,71},{8,72},{9,... | collective-permute-start | bytes 786440 | tf_op jit(solution)/shard_map/ppermute | solution.py:224
  123.9 2.9 %collective-permute-start.21 = (bf16[2,2,2,64,256]{4,3,2,1,0:T(8,128)(2,1)S(1)}, bf16[2,2,2,64,256]{4,3,2,1,0:T(8,128)(2,1)S(1)}, u32[]{:S(2)}, u32[]{:S(2)}) collective-permute-start(bf16[2,2,2,64,256]{4,3,2,1,0:T(8,128)(2,1)S(1)} %pad_maximum_fusion.3), channel_id=1, source_target_pairs={{0,192},{1,193},{2,194},{3,195},{4,196},{5,197},{6,198},{7,199},{8... | collective-permute-start | bytes 786440 | tf_op jit(solution)/shard_map/ppermute | solution.py:224
  128.9 6.3 %collective-permute-done.20.refs_1_ = bf16[2,2,2,64,256]{4,3,2,1,0:T(8,128)(2,1)S(1)} collective-permute-done((bf16[2,2,2,64,256]{4,3,2,1,0:T(8,128)(2,1)S(1)}, bf16[2,2,2,64,256]{4,3,2,1,0:T(8,128)(2,1)S(1)}, u32[]{:S(2)}, u32[]{:S(2)}) %collective-permute-start.20) | collective-permute-done | bytes 262176 | tf_op jit(solution)/shard_map/ppermute | solution.py:224
  (54 shorter events, 29.9 us)
Async XLA Ops:
  1.0 8.3 %collective-permute-start.1 = (bf16[2,2,64,256]{3,2,1,0:T(8,128)(2,1)S(1)}, bf16[2,2,64,256]{3,2,1,0:T(8,128)(2,1)S(1)}, u32[]{:S(2)}, u32[]{:S(2)}) collective-permute-start(bf16[2,2,64,256]{3,2,1,0:T(8,128)(2,1)S(1)} %get-tuple-element.46), channel_id=1, source_target_pairs={{0,1},{1,0},{2,3},{3,2},{4,5},{5,4},{6,7},{7,6},{8,9},{9,8},{10,11... | collective-permute-start | bytes 393224 | tf_op jit(solution)/shard_map/ppermute | solution.py:224
  4.6 12.0 %collective-permute-start = (bf16[576,256]{1,0:T(8,128)(2,1)S(1)}, bf16[576,256]{1,0:T(8,128)(2,1)S(1)}, u32[]{:S(2)}, u32[]{:S(2)}) collective-permute-start(bf16[576,256]{1,0:T(8,128)(2,1)S(1)} %dynamic-slice_bitcast_fusion.2), channel_id=1, source_target_pairs={{0,128},{1,129},{2,130},{3,131},{4,132},{5,133},{6,134},{7,135},{8... | collective-permute-start | bytes 884744 | tf_op jit(solution)/shard_map/ppermute | solution.py:224
  9.3 33.3 %copy-start.5 = (bf16[2,4,64,256]{3,2,1,0:T(8,128)(2,1)}, bf16[2,4,64,256]{3,2,1,0:T(8,128)(2,1)S(1)}, u32[]{:S(2)}) copy-start(bf16[2,4,64,256]{3,2,1,0:T(8,128)(2,1)S(1)} %maximum_select_fusion.1.refs_1_) | copy-start | bytes 786436
  9.3 11.6 %collective-permute-start.2 = (bf16[2,4,64,256]{3,2,1,0:T(8,128)(2,1)S(1)}, bf16[2,4,64,256]{3,2,1,0:T(8,128)(2,1)S(1)}, u32[]{:S(2)}, u32[]{:S(2)}) collective-permute-start(bf16[2,4,64,256]{3,2,1,0:T(8,128)(2,1)S(1)} %maximum_select_fusion.1.refs_1_), channel_id=1, source_target_pairs={{2,0},{3,1},{4,2},{5,3},{6,4},{7,5},{8,6},{9,7},{10,8},{11,9},{12,... | collective-permute-start | bytes 786440 | tf_op jit(solution)/shard_map/ppermute | solution.py:224
  16.6 30.0 %copy-start.4 = (bf16[576,256]{1,0:T(8,128)(2,1)}, bf16[576,256]{1,0:T(8,128)(2,1)S(1)}, u32[]{:S(2)}) copy-start(bf16[576,256]{1,0:T(8,128)(2,1)S(1)} %collective-permute-done) | copy-start | bytes 884740
  21.0 30.9 %collective-permute-start.3 = (bf16[2304,256]{1,0:T(8,128)(2,1)S(1)}, bf16[2304,256]{1,0:T(8,128)(2,1)}, u32[]{:S(2)}, u32[]{:S(2)}) collective-permute-start(bf16[2304,256]{1,0:T(8,128)(2,1)S(1)} %get-tuple-element.23.refs_3_), channel_id=1, source_target_pairs={{0,192},{1,193},{2,194},{3,195},{4,196},{5,197},{6,198},{7,199},{8... | collective-permute-start | bytes 3538952 | tf_op jit(solution)/shard_map/ppermute | solution.py:224
  23.7 29.3 %collective-permute-start.6 = (bf16[2304,256]{1,0:T(8,128)(2,1)S(1)}, bf16[2304,256]{1,0:T(8,128)(2,1)}, u32[]{:S(2)}, u32[]{:S(2)}) collective-permute-start(bf16[2304,256]{1,0:T(8,128)(2,1)S(1)} %get-tuple-element.23.refs_3_), channel_id=1, source_target_pairs={{0,64},{1,65},{2,66},{3,67},{4,68},{5,69},{6,70},{7,71},{8,72},{9,... | collective-permute-start | bytes 3538952 | tf_op jit(solution)/shard_map/ppermute | solution.py:224
  26.2 16.4 %collective-permute-start.4 = (bf16[576,256]{1,0:T(8,128)(2,1)S(1)}, bf16[576,256]{1,0:T(8,128)(2,1)S(1)}, u32[]{:S(2)}, u32[]{:S(2)}) collective-permute-start(bf16[576,256]{1,0:T(8,128)(2,1)S(1)} %collective-permute-done), channel_id=1, source_target_pairs={{0,14},{1,15},{2,0},{3,1},{4,2},{5,3},{6,4},{7,5},{8,6},{9,7},{10,... | collective-permute-start | bytes 884744 | tf_op jit(solution)/shard_map/ppermute | solution.py:224
  28.2 16.4 %collective-permute-start.10 = (bf16[576,256]{1,0:T(8,128)(2,1)S(1)}, bf16[576,256]{1,0:T(8,128)(2,1)S(1)}, u32[]{:S(2)}, u32[]{:S(2)}) collective-permute-start(bf16[576,256]{1,0:T(8,128)(2,1)S(1)} %collective-permute-done), channel_id=1, source_target_pairs={{0,4},{1,5},{2,14},{3,15},{4,8},{5,9},{6,2},{7,3},{8,12},{9,13},{1... | collective-permute-start | bytes 884744 | tf_op jit(solution)/shard_map/ppermute | solution.py:224
  30.9 15.8 %collective-permute-start.9 = (bf16[576,256]{1,0:T(8,128)(2,1)S(1)}, bf16[576,256]{1,0:T(8,128)(2,1)S(1)}, u32[]{:S(2)}, u32[]{:S(2)}) collective-permute-start(bf16[576,256]{1,0:T(8,128)(2,1)S(1)} %collective-permute-done), channel_id=1, source_target_pairs={{0,2},{1,3},{2,4},{3,5},{4,6},{5,7},{6,8},{7,9},{8,10},{9,11},{10,... | collective-permute-start | bytes 884744 | tf_op jit(solution)/shard_map/ppermute | solution.py:224
  42.6 9.2 %collective-permute-start.5 = (bf16[2,4,64,256]{3,2,1,0:T(8,128)(2,1)S(1)}, bf16[2,4,64,256]{3,2,1,0:T(8,128)(2,1)S(1)}, u32[]{:S(2)}, u32[]{:S(2)}) collective-permute-start(bf16[2,4,64,256]{3,2,1,0:T(8,128)(2,1)S(1)} %maximum_select_fusion.1.refs_1_), channel_id=1, source_target_pairs={{0,2},{1,3},{2,4},{3,5},{4,6},{5,7},{6,8},{7,9},{8,10},{9,11},{10,... | collective-permute-start | bytes 786440 | tf_op jit(solution)/shard_map/ppermute | solution.py:224
  47.8 11.4 %collective-permute-start.11 = (bf16[4,576,256]{2,1,0:T(8,128)(2,1)S(1)}, bf16[4,576,256]{2,1,0:T(8,128)(2,1)}, u32[]{:S(2)}, u32[]{:S(2)}) collective-permute-start(bf16[4,576,256]{2,1,0:T(8,128)(2,1)S(1)} %pad_maximum_fusion.refs_9_), channel_id=1, source_target_pairs={{0,1},{1,0},{2,3},{3,2},{4,5},{5,4},{6,7},{7,6},{8,9},{9,8},{10,11... | collective-permute-start | bytes 3538952 | tf_op jit(solution)/shard_map/ppermute | solution.py:224
  53.0 7.0 %collective-permute-start.7 = (bf16[2304,256]{1,0:T(8,128)(2,1)}, bf16[2304,256]{1,0:T(8,128)(2,1)}, u32[]{:S(2)}, u32[]{:S(2)}) collective-permute-start(bf16[2304,256]{1,0:T(8,128)(2,1)} %collective-permute-done.6.refs_5_), channel_id=1, source_target_pairs={{0,1},{1,0},{2,3},{3,2},{4,5},{5,4},{6,7},{7,6},{8,9},{9,8},{10,11... | collective-permute-start | bytes 3538952 | tf_op jit(solution)/shard_map/ppermute | solution.py:224
  57.2 5.1 %collective-permute-start.8 = (bf16[2304,256]{1,0:T(8,128)(2,1)}, bf16[2304,256]{1,0:T(8,128)(2,1)}, u32[]{:S(2)}, u32[]{:S(2)}) collective-permute-start(bf16[2304,256]{1,0:T(8,128)(2,1)} %collective-permute-done.3.refs_7_), channel_id=1, source_target_pairs={{0,1},{1,0},{2,3},{3,2},{4,5},{5,4},{6,7},{7,6},{8,9},{9,8},{10,11... | collective-permute-start | bytes 3538952 | tf_op jit(solution)/shard_map/ppermute | solution.py:224
  69.9 14.2 %collective-permute-start.12 = (bf16[1,4,64,256]{3,2,1,0:T(8,128)(2,1)S(1)}, bf16[1,4,64,256]{3,2,1,0:T(8,128)(2,1)}, u32[]{:S(2)}, u32[]{:S(2)}) collective-permute-start(bf16[1,4,64,256]{3,2,1,0:T(8,128)(2,1)S(1)} %get-tuple-element.35), channel_id=1, source_target_pairs={{0,256},{1,257},{2,258},{3,259},{4,260},{5,261},{6,262},{7,263},{8... | collective-permute-start | bytes 393224 | tf_op jit(solution)/shard_map/ppermute | solution.py:224
  76.6 15.0 %collective-permute-start.15 = (bf16[1,4,64,256]{3,2,1,0:T(8,128)(2,1)}, bf16[1,4,64,256]{3,2,1,0:T(8,128)(2,1)}, u32[]{:S(2)}, u32[]{:S(2)}) collective-permute-start(bf16[1,4,64,256]{3,2,1,0:T(8,128)(2,1)} %get-tuple-element.37), channel_id=1, source_target_pairs={{0,256},{1,257},{2,258},{3,259},{4,260},{5,261},{6,262},{7,263},{8... | collective-permute-start | bytes 393224 | tf_op jit(solution)/shard_map/ppermute | solution.py:224
  84.0 14.9 %collective-permute-start.14 = (bf16[1,4,64,256]{3,2,1,0:T(8,128)(2,1)}, bf16[1,4,64,256]{3,2,1,0:T(8,128)(2,1)}, u32[]{:S(2)}, u32[]{:S(2)}) collective-permute-start(bf16[1,4,64,256]{3,2,1,0:T(8,128)(2,1)} %collective-permute-done.12.refs_1_), channel_id=1, source_target_pairs={{258,256},{259,257},{260,258},{261,259},{262,260},{263,261},{264,2... | collective-permute-start | bytes 393224 | tf_op jit(solution)/shard_map/ppermute | solution.py:224
  86.0 13.0 %collective-permute-start.13 = (bf16[1,4,64,256]{3,2,1,0:T(8,128)(2,1)}, bf16[1,4,64,256]{3,2,1,0:T(8,128)(2,1)}, u32[]{:S(2)}, u32[]{:S(2)}) collective-permute-start(bf16[1,4,64,256]{3,2,1,0:T(8,128)(2,1)} %collective-permute-done.12.refs_1_), channel_id=1, source_target_pairs={{256,258},{257,259},{258,260},{259,261},{260,262},{261,263},{262,2... | collective-permute-start | bytes 393224 | tf_op jit(solution)/shard_map/ppermute | solution.py:224
  91.6 16.0 %collective-permute-start.17 = (bf16[1,4,64,256]{3,2,1,0:T(8,128)(2,1)}, bf16[1,4,64,256]{3,2,1,0:T(8,128)(2,1)S(1)}, u32[]{:S(2)}, u32[]{:S(2)}) collective-permute-start(bf16[1,4,64,256]{3,2,1,0:T(8,128)(2,1)} %collective-permute-done.15.refs_1_), channel_id=1, source_target_pairs={{258,256},{259,257},{260,258},{261,259},{262,260},{263,261},{264,2... | collective-permute-start | bytes 393224 | tf_op jit(solution)/shard_map/ppermute | solution.py:224
  93.5 14.1 %collective-permute-start.16 = (bf16[1,4,64,256]{3,2,1,0:T(8,128)(2,1)}, bf16[1,4,64,256]{3,2,1,0:T(8,128)(2,1)S(1)}, u32[]{:S(2)}, u32[]{:S(2)}) collective-permute-start(bf16[1,4,64,256]{3,2,1,0:T(8,128)(2,1)} %collective-permute-done.15.refs_1_), channel_id=1, source_target_pairs={{256,258},{257,259},{258,260},{259,261},{260,262},{261,263},{262,2... | collective-permute-start | bytes 393224 | tf_op jit(solution)/shard_map/ppermute | solution.py:224
  112.9 4.9 %collective-permute-start.18 = (bf16[4,2,2,64,256]{4,3,2,1,0:T(8,128)(2,1)S(1)}, bf16[4,2,2,64,256]{4,3,2,1,0:T(8,128)(2,1)S(1)}, u32[]{:S(2)}, u32[]{:S(2)}) collective-permute-start(bf16[4,2,2,64,256]{4,3,2,1,0:T(8,128)(2,1)S(1)} %get-tuple-element.43), channel_id=1, source_target_pairs={{0,1},{1,0},{2,3},{3,2},{4,5},{5,4},{6,7},{7,6},{8,9},{9,8},{10,11... | collective-permute-start | bytes 1572872 | tf_op jit(solution)/shard_map/ppermute | solution.py:224
  117.9 11.0 %collective-permute-start.19 = (bf16[2,2,2,64,256]{4,3,2,1,0:T(8,128)(2,1)S(1)}, bf16[2,2,2,64,256]{4,3,2,1,0:T(8,128)(2,1)S(1)}, u32[]{:S(2)}, u32[]{:S(2)}) collective-permute-start(bf16[2,2,2,64,256]{4,3,2,1,0:T(8,128)(2,1)S(1)} %pad_maximum_fusion.1), channel_id=1, source_target_pairs={{0,128},{1,129},{2,130},{3,131},{4,132},{5,133},{6,134},{7,135},{8... | collective-permute-start | bytes 786440 | tf_op jit(solution)/shard_map/ppermute | solution.py:224
  120.3 14.9 %collective-permute-start.20 = (bf16[2,2,2,64,256]{4,3,2,1,0:T(8,128)(2,1)S(1)}, bf16[2,2,2,64,256]{4,3,2,1,0:T(8,128)(2,1)S(1)}, u32[]{:S(2)}, u32[]{:S(2)}) collective-permute-start(bf16[2,2,2,64,256]{4,3,2,1,0:T(8,128)(2,1)S(1)} %pad_maximum_fusion.2), channel_id=1, source_target_pairs={{0,64},{1,65},{2,66},{3,67},{4,68},{5,69},{6,70},{7,71},{8,72},{9,... | collective-permute-start | bytes 786440 | tf_op jit(solution)/shard_map/ppermute | solution.py:224
  123.9 11.3 %collective-permute-start.21 = (bf16[2,2,2,64,256]{4,3,2,1,0:T(8,128)(2,1)S(1)}, bf16[2,2,2,64,256]{4,3,2,1,0:T(8,128)(2,1)S(1)}, u32[]{:S(2)}, u32[]{:S(2)}) collective-permute-start(bf16[2,2,2,64,256]{4,3,2,1,0:T(8,128)(2,1)S(1)} %pad_maximum_fusion.3), channel_id=1, source_target_pairs={{0,192},{1,193},{2,194},{3,195},{4,196},{5,197},{6,198},{7,199},{8... | collective-permute-start | bytes 786440 | tf_op jit(solution)/shard_map/ppermute | solution.py:224
  (6 other events, 50.9 us)

commit v11 on v10

--- a/solution.py
+++ b/solution.py
@@ -259,11 +259,11 @@
     own = layer_weights.reshape(2, 9 * chans, chans)
     part = own.shape[1] // 4
     quarter = lax.dynamic_slice(own, (core, piece * part, 0), (1, part, chans))[0]
-    far = send(quarter, along_x(2))
-
     give = lax.dynamic_index_in_dim(frames_in, 2 * x + 1 - core, 0, keepdims=False)
     keep = lax.dynamic_index_in_dim(frames_in, 2 * x + core, 0, keepdims=False)
     got = send(give, sibling)
+    quarter, got = lax.optimization_barrier((quarter, got))
+    far = send(quarter, along_x(2))
     mine = lax.dynamic_index_in_dim(own, core, 0, keepdims=False)
     theirs = lax.dynamic_index_in_dim(own, 1 - core, 0, keepdims=False)
     mid = jnp.where(core == 0, jnp.concatenate([keep, got], 1), jnp.concatenate([got, keep], 1))

time: 138 us -> 138 us (level)
  the two profiles are of different devices: /device:TPU:441 before, /device:TPU:377 now
where the time goes in v11:
time: 138 us; the launch traced here: 137 us
  starting transfers between devices  70.9 us (51%)
  waiting for transfers between devices  32.9 us (24%)
  Pallas kernels  27.7 us (20%)
  local copies, waits for them, and re-layouts  4.82 us (3%)
    ppermute x22, starting transfers between devices, send(): return lax.ppermute(array, ('section', 'rows'), route(move, keep))  70.9 us
    ppermute x22, waiting for transfers between devices, send(): return lax.ppermute(array, ('section', 'rows'), route(move, keep))  32.9 us
    pallas_call x4, Pallas kernels, run_frame(): pl.pallas_call(functools.partial(frame_kernel, frame, builds, len(inputs)...  26.1 us
  transfers between devices with their start and end apart: 22, of which 13 were waited for; matrix products, arithmetic and copies ran while one was open for 2% of the time, Pallas kernels for 10%

profile of v11, /device:TPU:377, one launch (start us, length us, event | category | flops | bytes accessed | tf_op | source)
XLA Modules:
  0.0 137.3 jit_solution(4983295231054641786)
XLA Ops:
  4.7 3.0 %collective-permute-start.2 = (bf16[2,4,64,256]{3,2,1,0:T(8,128)(2,1)S(1)}, bf16[2,4,64,256]{3,2,1,0:T(8,128)(2,1)S(1)}, u32[]{:S(2)}, u32[]{:S(2)}) collective-permute-start(bf16[2,4,64,256]{3,2,1,0:T(8,128)(2,1)S(1)} %maximum_select_fusion.1.refs_1_), channel_id=1, source_target_pairs={{2,0},{3,1},{4,2},{5,3},{6,4},{7,5},{8,6},{9,7},{10,8},{11,9},{12,... | collective-permute-start | bytes 786440 | tf_op jit(solution)/shard_map/ppermute | solution.py:224
  7.7 4.7 %collective-permute-start.1 = (bf16[576,256]{1,0:T(8,128)(2,1)S(1)}, bf16[576,256]{1,0:T(8,128)(2,1)S(1)}, u32[]{:S(2)}, u32[]{:S(2)}) collective-permute-start(bf16[576,256]{1,0:T(8,128)(2,1)S(1)} %dynamic-slice_bitcast_fusion.2), channel_id=1, source_target_pairs={{0,128},{1,129},{2,130},{3,131},{4,132},{5,133},{6,134},{7,135},{8... | collective-permute-start | bytes 884744 | tf_op jit(solution)/shard_map/ppermute | solution.py:224
  16.3 2.8 %collective-permute-done.1 = bf16[576,256]{1,0:T(8,128)(2,1)S(1)} collective-permute-done((bf16[576,256]{1,0:T(8,128)(2,1)S(1)}, bf16[576,256]{1,0:T(8,128)(2,1)S(1)}, u32[]{:S(2)}, u32[]{:S(2)}) %collective-permute-start.1) | collective-permute-done | bytes 294944 | tf_op jit(solution)/shard_map/ppermute | solution.py:224
  19.1 4.4 %collective-permute-start.3 = (bf16[2304,256]{1,0:T(8,128)(2,1)S(1)}, bf16[2304,256]{1,0:T(8,128)(2,1)}, u32[]{:S(2)}, u32[]{:S(2)}) collective-permute-start(bf16[2304,256]{1,0:T(8,128)(2,1)S(1)} %get-tuple-element.27.refs_3_), channel_id=1, source_target_pairs={{0,192},{1,193},{2,194},{3,195},{4,196},{5,197},{6,198},{7,199},{8... | collective-permute-start | bytes 3538952 | tf_op jit(solution)/shard_map/ppermute | solution.py:224
  25.4 3.0 %collective-permute-start.4 = (bf16[576,256]{1,0:T(8,128)(2,1)S(1)}, bf16[576,256]{1,0:T(8,128)(2,1)S(1)}, u32[]{:S(2)}, u32[]{:S(2)}) collective-permute-start(bf16[576,256]{1,0:T(8,128)(2,1)S(1)} %collective-permute-done.1), channel_id=1, source_target_pairs={{0,14},{1,15},{2,0},{3,1},{4,2},{5,3},{6,4},{7,5},{8,6},{9,7},{10,... | collective-permute-start | bytes 884744 | tf_op jit(solution)/shard_map/ppermute | solution.py:224
  28.4 2.9 %collective-permute-start.10 = (bf16[576,256]{1,0:T(8,128)(2,1)S(1)}, bf16[576,256]{1,0:T(8,128)(2,1)S(1)}, u32[]{:S(2)}, u32[]{:S(2)}) collective-permute-start(bf16[576,256]{1,0:T(8,128)(2,1)S(1)} %collective-permute-done.1), channel_id=1, source_target_pairs={{0,4},{1,5},{2,14},{3,15},{4,8},{5,9},{6,2},{7,3},{8,12},{9,13},{1... | collective-permute-start | bytes 884744 | tf_op jit(solution)/shard_map/ppermute | solution.py:224
  35.4 3.5 %collective-permute-start.5 = (bf16[2,4,64,256]{3,2,1,0:T(8,128)(2,1)S(1)}, bf16[2,4,64,256]{3,2,1,0:T(8,128)(2,1)S(1)}, u32[]{:S(2)}, u32[]{:S(2)}) collective-permute-start(bf16[2,4,64,256]{3,2,1,0:T(8,128)(2,1)S(1)} %maximum_select_fusion.1.refs_1_), channel_id=1, source_target_pairs={{0,2},{1,3},{2,4},{3,5},{4,6},{5,7},{6,8},{7,9},{8,10},{9,11},{10,... | collective-permute-start | bytes 786440 | tf_op jit(solution)/shard_map/ppermute | solution.py:224
  38.9 2.8 %collective-permute-done.10 = bf16[576,256]{1,0:T(8,128)(2,1)S(1)} collective-permute-done((bf16[576,256]{1,0:T(8,128)(2,1)S(1)}, bf16[576,256]{1,0:T(8,128)(2,1)S(1)}, u32[]{:S(2)}, u32[]{:S(2)}) %collective-permute-start.10) | collective-permute-done | bytes 294944 | tf_op jit(solution)/shard_map/ppermute | solution.py:224
  41.7 4.1 %collective-permute-done.9 = bf16[576,256]{1,0:T(8,128)(2,1)S(1)} collective-permute-done((bf16[576,256]{1,0:T(8,128)(2,1)S(1)}, bf16[576,256]{1,0:T(8,128)(2,1)S(1)}, u32[]{:S(2)}, u32[]{:S(2)}) %collective-permute-start.9) | collective-permute-done | bytes 294944 | tf_op jit(solution)/shard_map/ppermute | solution.py:224
  46.0 5.9 %collective-permute-start.11 = (bf16[4,576,256]{2,1,0:T(8,128)(2,1)S(1)}, bf16[4,576,256]{2,1,0:T(8,128)(2,1)}, u32[]{:S(2)}, u32[]{:S(2)}) collective-permute-start(bf16[4,576,256]{2,1,0:T(8,128)(2,1)S(1)} %pad_maximum_fusion.refs_9_), channel_id=1, source_target_pairs={{0,1},{1,0},{2,3},{3,2},{4,5},{5,4},{6,7},{7,6},{8,9},{9,8},{10,11... | collective-permute-start | bytes 3538952 | tf_op jit(solution)/shard_map/ppermute | solution.py:224
  52.5 4.5 %collective-permute-start.7 = (bf16[2304,256]{1,0:T(8,128)(2,1)}, bf16[2304,256]{1,0:T(8,128)(2,1)}, u32[]{:S(2)}, u32[]{:S(2)}) collective-permute-start(bf16[2304,256]{1,0:T(8,128)(2,1)} %collective-permute-done.6.refs_5_), channel_id=1, source_target_pairs={{0,1},{1,0},{2,3},{3,2},{4,5},{5,4},{6,7},{7,6},{8,9},{9,8},{10,11... | collective-permute-start | bytes 3538952 | tf_op jit(solution)/shard_map/ppermute | solution.py:224
  62.0 7.7 %frame0.2 = (bf16[2,4,2,64,256]{4,3,2,1,0:T(8,128)(2,1)S(1)}, bf16[1,4,64,256]{3,2,1,0:T(8,128)(2,1)S(1)}, f32[28,64,256]{2,1,0:T(8,128)S(1)}, bf16[4,2,2304,256...) custom-call(s32[5]{0:T(128)S(1)} %stack.67.meta, bf16[2,4,64,256]{3,2,1,0:T(8,128)(2,1)} %copy-done.6, ...), custom_call_target="tpu_custom_call" | custom-call | flops 4227858432 | bytes 8000000 | tf_op jit(solution)/shard_map/frame0/pallas_call | solution.py:160
  71.0 4.6 %frame1.2 = (bf16[2,4,2,64,256]{4,3,2,1,0:T(8,128)(2,1)S(1)}, bf16[1,4,64,256]{3,2,1,0:T(8,128)(2,1)}) custom-call(s32[5]{0:T(128)S(1)} %stack.67.meta, bf16[1,12,64,256]{3,2,1,0:T(8,128)(2,1)S(1)} %get-tuple-element.35.refs_0_, bf16[4,2,2304,256]{3,2,1,0:T(8,128)(2,1)S(1)} %get-tuple-element.36.refs_1_, f32[28,64,256]{2,1,0:T(8,128)S(1)} %get-tuple-element.37.refs_2_), custom_call_target="tpu_custom_call" | custom-call | flops 2113929216 | bytes 8000000 | tf_op jit(solution)/shard_map/frame1/pallas_call | solution.py:160
  77.8 5.6 %collective-permute-done.12.refs_1_ = bf16[1,4,64,256]{3,2,1,0:T(8,128)(2,1)} collective-permute-done((bf16[1,4,64,256]{3,2,1,0:T(8,128)(2,1)S(1)}, bf16[1,4,64,256]{3,2,1,0:T(8,128)(2,1)}, u32[]{:S(2)}, u32[]{:S(2)}) %collective-permute-start.12) | collective-permute-done | bytes 131104 | tf_op jit(solution)/shard_map/ppermute | solution.py:224
  83.4 3.0 %collective-permute-start.14 = (bf16[1,4,64,256]{3,2,1,0:T(8,128)(2,1)}, bf16[1,4,64,256]{3,2,1,0:T(8,128)(2,1)}, u32[]{:S(2)}, u32[]{:S(2)}) collective-permute-start(bf16[1,4,64,256]{3,2,1,0:T(8,128)(2,1)} %collective-permute-done.12.refs_1_), channel_id=1, source_target_pairs={{258,256},{259,257},{260,258},{261,259},{262,260},{263,261},{264,2... | collective-permute-start | bytes 393224 | tf_op jit(solution)/shard_map/ppermute | solution.py:224
  86.4 4.4 %collective-permute-start.13 = (bf16[1,4,64,256]{3,2,1,0:T(8,128)(2,1)}, bf16[1,4,64,256]{3,2,1,0:T(8,128)(2,1)}, u32[]{:S(2)}, u32[]{:S(2)}) collective-permute-start(bf16[1,4,64,256]{3,2,1,0:T(8,128)(2,1)} %collective-permute-done.12.refs_1_), channel_id=1, source_target_pairs={{256,258},{257,259},{258,260},{259,261},{260,262},{261,263},{262,2... | collective-permute-start | bytes 393224 | tf_op jit(solution)/shard_map/ppermute | solution.py:224
  91.0 3.0 %collective-permute-start.17 = (bf16[1,4,64,256]{3,2,1,0:T(8,128)(2,1)}, bf16[1,4,64,256]{3,2,1,0:T(8,128)(2,1)S(1)}, u32[]{:S(2)}, u32[]{:S(2)}) collective-permute-start(bf16[1,4,64,256]{3,2,1,0:T(8,128)(2,1)} %collective-permute-done.15.refs_1_), channel_id=1, source_target_pairs={{258,256},{259,257},{260,258},{261,259},{262,260},{263,261},{264,2... | collective-permute-start | bytes 393224 | tf_op jit(solution)/shard_map/ppermute | solution.py:224
  94.0 4.4 %collective-permute-start.16 = (bf16[1,4,64,256]{3,2,1,0:T(8,128)(2,1)}, bf16[1,4,64,256]{3,2,1,0:T(8,128)(2,1)S(1)}, u32[]{:S(2)}, u32[]{:S(2)}) collective-permute-start(bf16[1,4,64,256]{3,2,1,0:T(8,128)(2,1)} %collective-permute-done.15.refs_1_), channel_id=1, source_target_pairs={{256,258},{257,259},{258,260},{259,261},{260,262},{261,263},{262,2... | collective-permute-start | bytes 393224 | tf_op jit(solution)/shard_map/ppermute | solution.py:224
  98.4 8.7 %frame0.3 = (bf16[2,4,2,64,256]{4,3,2,1,0:T(8,128)(2,1)S(1)}, bf16[1,4,64,256]{3,2,1,0:T(8,128)(2,1)}, f32[28,64,256]{2,1,0:T(8,128)S(1)}, bf16[4,2,2304,256]{3,2,1,0:T(8,128)(2,1)S(1)}) custom-call(s32[5]{0:T(128)S(1)} %stack.67.meta, bf16[1,4,64,256]{3,2,1,0:T(8,128)(2,1)} %collective-permute-done.13.refs_0_, ...), custom_call_target="tpu_custom_call" | custom-call | flops 4227858432 | bytes 8000000 | tf_op jit(solution)/shard_map/frame0/pallas_call | solution.py:160
  107.2 5.1 %frame1.3 = (bf16[2,4,2,64,256]{4,3,2,1,0:T(8,128)(2,1)S(1)}, bf16[1,4,64,256]{3,2,1,0:T(8,128)(2,1)}) custom-call(s32[5]{0:T(128)S(1)} %stack.67.meta, bf16[1,4,64,256]{3,2,1,0:T(8,128)(2,1)S(1)} %collective-permute-done.16.refs_0_, bf16[1,4,64,256]{3,2,1,0:T(8,128)(2,1)} %collective-permute-done.15.refs_1_, ...), custom_call_target="tpu_custom_call" | custom-call | flops 2113929216 | bytes 8000000 | tf_op jit(solution)/shard_map/frame1/pallas_call | solution.py:160
  112.6 4.3 %collective-permute-start.18 = (bf16[4,2,2,64,256]{4,3,2,1,0:T(8,128)(2,1)S(1)}, bf16[4,2,2,64,256]{4,3,2,1,0:T(8,128)(2,1)S(1)}, u32[]{:S(2)}, u32[]{:S(2)}) collective-permute-start(bf16[4,2,2,64,256]{4,3,2,1,0:T(8,128)(2,1)S(1)} %get-tuple-element.47), channel_id=1, source_target_pairs={{0,1},{1,0},{2,3},{3,2},{4,5},{5,4},{6,7},{7,6},{8,9},{9,8},{10,11... | collective-permute-start | bytes 1572872 | tf_op jit(solution)/shard_map/ppermute | solution.py:224
  120.5 3.9 %collective-permute-start.20 = (bf16[2,2,2,64,256]{4,3,2,1,0:T(8,128)(2,1)S(1)}, bf16[2,2,2,64,256]{4,3,2,1,0:T(8,128)(2,1)S(1)}, u32[]{:S(2)}, u32[]{:S(2)}) collective-permute-start(bf16[2,2,2,64,256]{4,3,2,1,0:T(8,128)(2,1)S(1)} %pad_maximum_fusion.2), channel_id=1, source_target_pairs={{0,64},{1,65},{2,66},{3,67},{4,68},{5,69},{6,70},{7,71},{8,72},{9,... | collective-permute-start | bytes 786440 | tf_op jit(solution)/shard_map/ppermute | solution.py:224
  124.4 2.6 %collective-permute-start.21 = (bf16[2,2,2,64,256]{4,3,2,1,0:T(8,128)(2,1)S(1)}, bf16[2,2,2,64,256]{4,3,2,1,0:T(8,128)(2,1)S(1)}, u32[]{:S(2)}, u32[]{:S(2)}) collective-permute-start(bf16[2,2,2,64,256]{4,3,2,1,0:T(8,128)(2,1)S(1)} %pad_maximum_fusion.3), channel_id=1, source_target_pairs={{0,192},{1,193},{2,194},{3,195},{4,196},{5,197},{6,198},{7,199},{8... | collective-permute-start | bytes 786440 | tf_op jit(solution)/shard_map/ppermute | solution.py:224
  129.4 6.3 %collective-permute-done.20.refs_1_ = bf16[2,2,2,64,256]{4,3,2,1,0:T(8,128)(2,1)S(1)} collective-permute-done((bf16[2,2,2,64,256]{4,3,2,1,0:T(8,128)(2,1)S(1)}, bf16[2,2,2,64,256]{4,3,2,1,0:T(8,128)(2,1)S(1)}, u32[]{:S(2)}, u32[]{:S(2)}) %collective-permute-start.20) | collective-permute-done | bytes 262176 | tf_op jit(solution)/shard_map/ppermute | solution.py:224
  (52 shorter events, 31.7 us)
Async XLA Ops:
  1.0 3.6 %collective-permute-start = (bf16[2,2,64,256]{3,2,1,0:T(8,128)(2,1)S(1)}, bf16[2,2,64,256]{3,2,1,0:T(8,128)(2,1)S(1)}, u32[]{:S(2)}, u32[]{:S(2)}) collective-permute-start(bf16[2,2,64,256]{3,2,1,0:T(8,128)(2,1)S(1)} %get-tuple-element.50), channel_id=1, source_target_pairs={{0,1},{1,0},{2,3},{3,2},{4,5},{5,4},{6,7},{7,6},{8,9},{9,8},{10,11... | collective-permute-start | bytes 393224 | tf_op jit(solution)/shard_map/ppermute | solution.py:224
  4.7 30.8 %copy-start.4 = (bf16[2,4,64,256]{3,2,1,0:T(8,128)(2,1)}, bf16[2,4,64,256]{3,2,1,0:T(8,128)(2,1)S(1)}, u32[]{:S(2)}) copy-start(bf16[2,4,64,256]{3,2,1,0:T(8,128)(2,1)S(1)} %maximum_select_fusion.1.refs_1_) | copy-start | bytes 786436
  4.7 11.6 %collective-permute-start.2 = (bf16[2,4,64,256]{3,2,1,0:T(8,128)(2,1)S(1)}, bf16[2,4,64,256]{3,2,1,0:T(8,128)(2,1)S(1)}, u32[]{:S(2)}, u32[]{:S(2)}) collective-permute-start(bf16[2,4,64,256]{3,2,1,0:T(8,128)(2,1)S(1)} %maximum_select_fusion.1.refs_1_), channel_id=1, source_target_pairs={{2,0},{3,1},{4,2},{5,3},{6,4},{7,5},{8,6},{9,7},{10,8},{11,9},{12,... | collective-permute-start | bytes 786440 | tf_op jit(solution)/shard_map/ppermute | solution.py:224
  7.7 11.4 %collective-permute-start.1 = (bf16[576,256]{1,0:T(8,128)(2,1)S(1)}, bf16[576,256]{1,0:T(8,128)(2,1)S(1)}, u32[]{:S(2)}, u32[]{:S(2)}) collective-permute-start(bf16[576,256]{1,0:T(8,128)(2,1)S(1)} %dynamic-slice_bitcast_fusion.2), channel_id=1, source_target_pairs={{0,128},{1,129},{2,130},{3,131},{4,132},{5,133},{6,134},{7,135},{8... | collective-permute-start | bytes 884744 | tf_op jit(solution)/shard_map/ppermute | solution.py:224
  16.3 29.7 %copy-start.5 = (bf16[2,4,64,256]{3,2,1,0:T(8,128)(2,1)}, bf16[2,4,64,256]{3,2,1,0:T(8,128)(2,1)S(1)}, u32[]{:S(2)}) copy-start(bf16[2,4,64,256]{3,2,1,0:T(8,128)(2,1)S(1)} %collective-permute-done.2.refs_2_) | copy-start | bytes 786436
  19.1 32.9 %collective-permute-start.3 = (bf16[2304,256]{1,0:T(8,128)(2,1)S(1)}, bf16[2304,256]{1,0:T(8,128)(2,1)}, u32[]{:S(2)}, u32[]{:S(2)}) collective-permute-start(bf16[2304,256]{1,0:T(8,128)(2,1)S(1)} %get-tuple-element.27.refs_3_), channel_id=1, source_target_pairs={{0,192},{1,193},{2,194},{3,195},{4,196},{5,197},{6,198},{7,199},{8... | collective-permute-start | bytes 3538952 | tf_op jit(solution)/shard_map/ppermute | solution.py:224
  23.5 29.0 %collective-permute-start.6 = (bf16[2304,256]{1,0:T(8,128)(2,1)S(1)}, bf16[2304,256]{1,0:T(8,128)(2,1)}, u32[]{:S(2)}, u32[]{:S(2)}) collective-permute-start(bf16[2304,256]{1,0:T(8,128)(2,1)S(1)} %get-tuple-element.27.refs_3_), channel_id=1, source_target_pairs={{0,64},{1,65},{2,66},{3,67},{4,68},{5,69},{6,70},{7,71},{8,72},{9,... | collective-permute-start | bytes 3538952 | tf_op jit(solution)/shard_map/ppermute | solution.py:224
  25.4 10.0 %collective-permute-start.4 = (bf16[576,256]{1,0:T(8,128)(2,1)S(1)}, bf16[576,256]{1,0:T(8,128)(2,1)S(1)}, u32[]{:S(2)}, u32[]{:S(2)}) collective-permute-start(bf16[576,256]{1,0:T(8,128)(2,1)S(1)} %collective-permute-done.1), channel_id=1, source_target_pairs={{0,14},{1,15},{2,0},{3,1},{4,2},{5,3},{6,4},{7,5},{8,6},{9,7},{10,... | collective-permute-start | bytes 884744 | tf_op jit(solution)/shard_map/ppermute | solution.py:224
  28.4 13.4 %collective-permute-start.10 = (bf16[576,256]{1,0:T(8,128)(2,1)S(1)}, bf16[576,256]{1,0:T(8,128)(2,1)S(1)}, u32[]{:S(2)}, u32[]{:S(2)}) collective-permute-start(bf16[576,256]{1,0:T(8,128)(2,1)S(1)} %collective-permute-done.1), channel_id=1, source_target_pairs={{0,4},{1,5},{2,14},{3,15},{4,8},{5,9},{6,2},{7,3},{8,12},{9,13},{1... | collective-permute-start | bytes 884744 | tf_op jit(solution)/shard_map/ppermute | solution.py:224
  31.2 14.6 %collective-permute-start.9 = (bf16[576,256]{1,0:T(8,128)(2,1)S(1)}, bf16[576,256]{1,0:T(8,128)(2,1)S(1)}, u32[]{:S(2)}, u32[]{:S(2)}) collective-permute-start(bf16[576,256]{1,0:T(8,128)(2,1)S(1)} %collective-permute-done.1), channel_id=1, source_target_pairs={{0,2},{1,3},{2,4},{3,5},{4,6},{5,7},{6,8},{7,9},{8,10},{9,11},{10,... | collective-permute-start | bytes 884744 | tf_op jit(solution)/shard_map/ppermute | solution.py:224
  35.4 16.5 %collective-permute-start.5 = (bf16[2,4,64,256]{3,2,1,0:T(8,128)(2,1)S(1)}, bf16[2,4,64,256]{3,2,1,0:T(8,128)(2,1)S(1)}, u32[]{:S(2)}, u32[]{:S(2)}) collective-permute-start(bf16[2,4,64,256]{3,2,1,0:T(8,128)(2,1)S(1)} %maximum_select_fusion.1.refs_1_), channel_id=1, source_target_pairs={{0,2},{1,3},{2,4},{3,5},{4,6},{5,7},{6,8},{7,9},{8,10},{9,11},{10,... | collective-permute-start | bytes 786440 | tf_op jit(solution)/shard_map/ppermute | solution.py:224
  46.0 13.0 %collective-permute-start.11 = (bf16[4,576,256]{2,1,0:T(8,128)(2,1)S(1)}, bf16[4,576,256]{2,1,0:T(8,128)(2,1)}, u32[]{:S(2)}, u32[]{:S(2)}) collective-permute-start(bf16[4,576,256]{2,1,0:T(8,128)(2,1)S(1)} %pad_maximum_fusion.refs_9_), channel_id=1, source_target_pairs={{0,1},{1,0},{2,3},{3,2},{4,5},{5,4},{6,7},{7,6},{8,9},{9,8},{10,11... | collective-permute-start | bytes 3538952 | tf_op jit(solution)/shard_map/ppermute | solution.py:224
  52.5 7.3 %collective-permute-start.7 = (bf16[2304,256]{1,0:T(8,128)(2,1)}, bf16[2304,256]{1,0:T(8,128)(2,1)}, u32[]{:S(2)}, u32[]{:S(2)}) collective-permute-start(bf16[2304,256]{1,0:T(8,128)(2,1)} %collective-permute-done.6.refs_5_), channel_id=1, source_target_pairs={{0,1},{1,0},{2,3},{3,2},{4,5},{5,4},{6,7},{7,6},{8,9},{9,8},{10,11... | collective-permute-start | bytes 3538952 | tf_op jit(solution)/shard_map/ppermute | solution.py:224
  57.0 5.1 %collective-permute-start.8 = (bf16[2304,256]{1,0:T(8,128)(2,1)}, bf16[2304,256]{1,0:T(8,128)(2,1)}, u32[]{:S(2)}, u32[]{:S(2)}) collective-permute-start(bf16[2304,256]{1,0:T(8,128)(2,1)} %collective-permute-done.3.refs_7_), channel_id=1, source_target_pairs={{0,1},{1,0},{2,3},{3,2},{4,5},{5,4},{6,7},{7,6},{8,9},{9,8},{10,11... | collective-permute-start | bytes 3538952 | tf_op jit(solution)/shard_map/ppermute | solution.py:224
  69.7 13.7 %collective-permute-start.12 = (bf16[1,4,64,256]{3,2,1,0:T(8,128)(2,1)S(1)}, bf16[1,4,64,256]{3,2,1,0:T(8,128)(2,1)}, u32[]{:S(2)}, u32[]{:S(2)}) collective-permute-start(bf16[1,4,64,256]{3,2,1,0:T(8,128)(2,1)S(1)} %get-tuple-element.39), channel_id=1, source_target_pairs={{0,256},{1,257},{2,258},{3,259},{4,260},{5,261},{6,262},{7,263},{8... | collective-permute-start | bytes 393224 | tf_op jit(solution)/shard_map/ppermute | solution.py:224
  76.5 14.5 %collective-permute-start.15 = (bf16[1,4,64,256]{3,2,1,0:T(8,128)(2,1)}, bf16[1,4,64,256]{3,2,1,0:T(8,128)(2,1)}, u32[]{:S(2)}, u32[]{:S(2)}) collective-permute-start(bf16[1,4,64,256]{3,2,1,0:T(8,128)(2,1)} %get-tuple-element.41), channel_id=1, source_target_pairs={{0,256},{1,257},{2,258},{3,259},{4,260},{5,261},{6,262},{7,263},{8... | collective-permute-start | bytes 393224 | tf_op jit(solution)/shard_map/ppermute | solution.py:224
  83.4 15.0 %collective-permute-start.14 = (bf16[1,4,64,256]{3,2,1,0:T(8,128)(2,1)}, bf16[1,4,64,256]{3,2,1,0:T(8,128)(2,1)}, u32[]{:S(2)}, u32[]{:S(2)}) collective-permute-start(bf16[1,4,64,256]{3,2,1,0:T(8,128)(2,1)} %collective-permute-done.12.refs_1_), channel_id=1, source_target_pairs={{258,256},{259,257},{260,258},{261,259},{262,260},{263,261},{264,2... | collective-permute-start | bytes 393224 | tf_op jit(solution)/shard_map/ppermute | solution.py:224
  86.4 12.0 %collective-permute-start.13 = (bf16[1,4,64,256]{3,2,1,0:T(8,128)(2,1)}, bf16[1,4,64,256]{3,2,1,0:T(8,128)(2,1)}, u32[]{:S(2)}, u32[]{:S(2)}) collective-permute-start(bf16[1,4,64,256]{3,2,1,0:T(8,128)(2,1)} %collective-permute-done.12.refs_1_), channel_id=1, source_target_pairs={{256,258},{257,259},{258,260},{259,261},{260,262},{261,263},{262,2... | collective-permute-start | bytes 393224 | tf_op jit(solution)/shard_map/ppermute | solution.py:224
  91.0 16.1 %collective-permute-start.17 = (bf16[1,4,64,256]{3,2,1,0:T(8,128)(2,1)}, bf16[1,4,64,256]{3,2,1,0:T(8,128)(2,1)S(1)}, u32[]{:S(2)}, u32[]{:S(2)}) collective-permute-start(bf16[1,4,64,256]{3,2,1,0:T(8,128)(2,1)} %collective-permute-done.15.refs_1_), channel_id=1, source_target_pairs={{258,256},{259,257},{260,258},{261,259},{262,260},{263,261},{264,2... | collective-permute-start | bytes 393224 | tf_op jit(solution)/shard_map/ppermute | solution.py:224
  94.0 13.1 %collective-permute-start.16 = (bf16[1,4,64,256]{3,2,1,0:T(8,128)(2,1)}, bf16[1,4,64,256]{3,2,1,0:T(8,128)(2,1)S(1)}, u32[]{:S(2)}, u32[]{:S(2)}) collective-permute-start(bf16[1,4,64,256]{3,2,1,0:T(8,128)(2,1)} %collective-permute-done.15.refs_1_), channel_id=1, source_target_pairs={{256,258},{257,259},{258,260},{259,261},{260,262},{261,263},{262,2... | collective-permute-start | bytes 393224 | tf_op jit(solution)/shard_map/ppermute | solution.py:224
  112.6 5.8 %collective-permute-start.18 = (bf16[4,2,2,64,256]{4,3,2,1,0:T(8,128)(2,1)S(1)}, bf16[4,2,2,64,256]{4,3,2,1,0:T(8,128)(2,1)S(1)}, u32[]{:S(2)}, u32[]{:S(2)}) collective-permute-start(bf16[4,2,2,64,256]{4,3,2,1,0:T(8,128)(2,1)S(1)} %get-tuple-element.47), channel_id=1, source_target_pairs={{0,1},{1,0},{2,3},{3,2},{4,5},{5,4},{6,7},{7,6},{8,9},{9,8},{10,11... | collective-permute-start | bytes 1572872 | tf_op jit(solution)/shard_map/ppermute | solution.py:224
  118.5 11.0 %collective-permute-start.19 = (bf16[2,2,2,64,256]{4,3,2,1,0:T(8,128)(2,1)S(1)}, bf16[2,2,2,64,256]{4,3,2,1,0:T(8,128)(2,1)S(1)}, u32[]{:S(2)}, u32[]{:S(2)}) collective-permute-start(bf16[2,2,2,64,256]{4,3,2,1,0:T(8,128)(2,1)S(1)} %pad_maximum_fusion.1), channel_id=1, source_target_pairs={{0,128},{1,129},{2,130},{3,131},{4,132},{5,133},{6,134},{7,135},{8... | collective-permute-start | bytes 786440 | tf_op jit(solution)/shard_map/ppermute | solution.py:224
  120.5 15.2 %collective-permute-start.20 = (bf16[2,2,2,64,256]{4,3,2,1,0:T(8,128)(2,1)S(1)}, bf16[2,2,2,64,256]{4,3,2,1,0:T(8,128)(2,1)S(1)}, u32[]{:S(2)}, u32[]{:S(2)}) collective-permute-start(bf16[2,2,2,64,256]{4,3,2,1,0:T(8,128)(2,1)S(1)} %pad_maximum_fusion.2), channel_id=1, source_target_pairs={{0,64},{1,65},{2,66},{3,67},{4,68},{5,69},{6,70},{7,71},{8,72},{9,... | collective-permute-start | bytes 786440 | tf_op jit(solution)/shard_map/ppermute | solution.py:224
  124.4 11.3 %collective-permute-start.21 = (bf16[2,2,2,64,256]{4,3,2,1,0:T(8,128)(2,1)S(1)}, bf16[2,2,2,64,256]{4,3,2,1,0:T(8,128)(2,1)S(1)}, u32[]{:S(2)}, u32[]{:S(2)}) collective-permute-start(bf16[2,2,2,64,256]{4,3,2,1,0:T(8,128)(2,1)S(1)} %pad_maximum_fusion.3), channel_id=1, source_target_pairs={{0,192},{1,193},{2,194},{3,195},{4,196},{5,197},{6,198},{7,199},{8... | collective-permute-start | bytes 786440 | tf_op jit(solution)/shard_map/ppermute | solution.py:224
  (5 other events, 24.0 us)
